TPU v7x, 32 devices: a whole 2x2x4 slice. The times are simulated.
32 devices in a mesh: dp: 8 (over z, x), seq: 4 (over y, core).
Axes of the slice: x: 2, y: 2, z: 4, core: 2. Of those that a mesh axis runs over, the one named last changes fastest.
Arguments:
- tokens: bfloat16 [2, 8, 2048, 768], P(None, 'dp', 'seq'), may hold values from -6 to 6
- qkv_weight: bfloat16 [768, 2304], P(('dp', 'seq')), may hold values from -0.21875 to 0.21875
- query_bias: bfloat16 [768], P(('dp', 'seq')), may hold values from -1.796875 to 1.796875
- value_bias: bfloat16 [768], P(('dp', 'seq')), may hold values from -1.796875 to 1.796875
- proj_weight: bfloat16 [768, 768], P(('dp', 'seq')), may hold values from -0.875 to 0.875
- proj_bias: bfloat16 [768], P(('dp', 'seq')), may hold values from -1.796875 to 1.796875
- attn_gain: bfloat16 [768], P(('dp', 'seq')), may hold values from 0.5 to 1.5
- attn_shift: bfloat16 [768], P(('dp', 'seq')), may hold values from -1.796875 to 1.796875
- inner_weight: bfloat16 [768, 3072], P(('dp', 'seq')), may hold values from -0.21875 to 0.21875
- inner_bias: bfloat16 [3072], P(('dp', 'seq')), may hold values from -1.796875 to 1.796875
- down_weight: bfloat16 [3072, 768], P(('dp', 'seq')), may hold values from -0.109375 to 0.109375
- down_bias: bfloat16 [768], P(('dp', 'seq')), may hold values from -1.796875 to 1.796875
- ffn_gain: bfloat16 [768], P(('dp', 'seq')), may hold values from 0.5 to 1.5
- ffn_shift: bfloat16 [768], P(('dp', 'seq')), may hold values from -1.796875 to 1.796875
- seg_ids: int32 [2, 8, 2048], P(None, 'dp'), may hold values from 0 to 3, never falling along the last dimension, each value on 1 to 1024 neighbouring positions
- rand_blocks: int32 [2, 8, 12, 32, 3], P(None, 'dp', 'seq'), may hold values from 0 to 31
- glob_blocks: int32 [2, 8, 2], P(None, 'dp'), may hold values from 0 to 31, as said below
- d_out: bfloat16 [2, 8, 2048, 768], P(None, 'dp', 'seq'), may hold values from -6 to 6
Outputs:
- layer_out: bfloat16 [2, 8, 2048, 768], P(None, 'dp', 'seq')
- grad_input: bfloat16 [2, 8, 2048, 768], P(None, 'dp', 'seq')
- grad_qkv_weight: float32 [768, 2304], P(('dp', 'seq'))
- grad_query_bias: float32 [768], P(('dp', 'seq'))
- grad_value_bias: float32 [768], P(('dp', 'seq'))
- grad_proj_weight: float32 [768, 768], P(('dp', 'seq'))
- grad_proj_bias: float32 [768], P(('dp', 'seq'))
- grad_attn_gain: float32 [768], P(('dp', 'seq'))
- grad_attn_shift: float32 [768], P(('dp', 'seq'))
- grad_inner_weight: float32 [768, 3072], P(('dp', 'seq'))
- grad_inner_bias: float32 [3072], P(('dp', 'seq'))
- grad_down_weight: float32 [3072, 768], P(('dp', 'seq'))
- grad_down_bias: float32 [768], P(('dp', 'seq'))
- grad_ffn_gain: float32 [768], P(('dp', 'seq'))
- grad_ffn_shift: float32 [768], P(('dp', 'seq'))
Inputs may be any that keep to these rules, and one draw needn't show every extreme that they name: `seg_ids`: document numbers never fall along a sequence; each document holds at most 1024 tokens, and one holds exactly that many. `rand_blocks`: block numbers of the whole sequence. `glob_blocks`: the two global blocks of a sequence are different.
All inputs are finite; a program needn't handle non-finite values.
Results may differ from a plain program's by a relative error of at most 0.015.
Values may be sent and summed in bfloat16 or wider, within the bound.
No kernel may reach another device: no remote copies, remote signals or barrier semaphores. Data moves between devices by JAX's collectives and lax.ppermute only.
A program may use at most 256 MiB of HBM per device.

v0:
```python
import jax
import jax.numpy as jnp
from jax import lax
from jax.sharding import PartitionSpec as P

HD = 64
BLOCK = 64


EPSILON = 1e-06


def layer_norm(value, gain, shift):
    centred = value - jnp.mean(value, axis=-1, keepdims=True)
    normed = centred * lax.rsqrt(jnp.mean(centred * centred, axis=-1, keepdims=True) + EPSILON)
    return normed * gain + shift


def gelu_exact(value):
    return jax.nn.gelu(value, approximate=False)


def outer_sum(left, right):
    return lax.dot_general(
        left, right, (((0,), (0,)), ((), ())), preferred_element_type=jnp.float32
    )


def regroup(matrix, groups):
    return (
        matrix.reshape(matrix.shape[0], 3, groups, -1)
        .transpose(0, 2, 1, 3)
        .reshape(matrix.shape[0], -1)
    )


def ungroup(matrix, groups):
    return (
        matrix.reshape(matrix.shape[0], groups, 3, -1)
        .transpose(0, 2, 1, 3)
        .reshape(matrix.shape[0], -1)
    )


def block_lists(table, globals_pair, block_count):
    head_count = table.shape[0]
    blocks = jnp.arange(block_count, dtype=jnp.int32)
    first_global = jnp.broadcast_to(globals_pair[0], (block_count,))
    second_global = jnp.broadcast_to(globals_pair[1], (block_count,))
    fixed_part = jnp.stack([blocks - 1, blocks, blocks + 1, first_global, second_global], axis=1)
    fixed_part = jnp.broadcast_to(fixed_part[None], (head_count, block_count, 5))
    listed = jnp.concatenate([fixed_part, table], axis=2)
    inside = (listed >= 0) & (listed < block_count)
    entries = listed.shape[2]
    equal = listed[..., :, None] == listed[..., None, :]
    earlier = jnp.tril(jnp.ones((entries, entries), dtype=bool), -1)
    repeated = jnp.any(equal & earlier & inside[..., None, :], axis=-1)
    return (jnp.clip(listed, 0, block_count - 1), inside & ~repeated)


def prepare(heads, segment, table, globals_pair):
    length = heads.shape[0]
    block_count = length // BLOCK
    head_count = table.shape[0]
    packed = heads.reshape(block_count, BLOCK, 3, head_count, HD)
    queries = packed[:, :, 0]
    key_heads = packed[:, :, 1].transpose(2, 0, 1, 3)
    value_heads = packed[:, :, 2].transpose(2, 0, 1, 3)
    listed, usable = block_lists(table, globals_pair, block_count)
    seg_blocks = segment.reshape(block_count, BLOCK)
    return (queries, key_heads, value_heads, listed, usable, seg_blocks)


def gather_step(queries, key_heads, value_heads, listed, usable, seg_blocks, number, span):
    block_count = key_heads.shape[1]
    first = number * span
    query_step = lax.dynamic_slice_in_dim(queries, first, span, 0)
    picked = lax.dynamic_slice_in_dim(listed, first, span, 1)
    allowed = lax.dynamic_slice_in_dim(usable, first, span, 1)
    choose = (picked[..., None] == jnp.arange(block_count, dtype=jnp.int32)).astype(jnp.bfloat16)
    key_step = jnp.einsum(
        "hqkn,hnse->hqkse", choose, key_heads, preferred_element_type=jnp.float32
    ).astype(jnp.bfloat16)
    value_step = jnp.einsum(
        "hqkn,hnse->hqkse", choose, value_heads, preferred_element_type=jnp.float32
    ).astype(jnp.bfloat16)
    query_segs = lax.dynamic_slice_in_dim(seg_blocks, first, span, 0)
    key_segs = seg_blocks[picked].transpose(1, 0, 2, 3)
    scores = jnp.einsum(
        "qthe,hqkse->qthks", query_step, key_step, preferred_element_type=jnp.float32
    ) * HD ** (-0.5)
    visible = allowed.transpose(1, 0, 2)[:, None, :, :, None] & (
        query_segs[:, :, None, None, None] == key_segs[:, None]
    )
    scores = jnp.where(visible, scores, -1e30)
    return (query_step, key_step, value_step, scores, picked, choose)


def global_scores(queries, key_heads, seg_blocks, segment, globals_pair):
    head_count = key_heads.shape[0]
    length = segment.shape[0]
    global_queries = queries[globals_pair]
    key_flat = key_heads.reshape(head_count, length, HD)
    scores = jnp.einsum(
        "gthe,hje->gthj", global_queries, key_flat, preferred_element_type=jnp.float32
    ) * HD ** (-0.5)
    visible = seg_blocks[globals_pair][:, :, None, None] == segment[None, None, None, :]
    return (global_queries, key_flat, jnp.where(visible, scores, -1e30))


def attend(heads, segment, table, globals_pair):
    length = heads.shape[0]
    block_count = length // BLOCK
    head_count = table.shape[0]
    queries, key_heads, value_heads, listed, usable, seg_blocks = prepare(
        heads, segment, table, globals_pair
    )
    span = min(8, block_count)

    def one_step(number):
        query_step, key_step, value_step, scores, picked, choose = gather_step(
            queries, key_heads, value_heads, listed, usable, seg_blocks, number, span
        )
        largest = jnp.max(scores, axis=(3, 4), keepdims=True)
        expo = jnp.exp(scores - largest)
        totals = jnp.sum(expo, axis=(3, 4), keepdims=True)
        weights = (expo / totals).astype(jnp.bfloat16)
        result = jnp.einsum(
            "qthks,hqkse->qthe", weights, value_step, preferred_element_type=jnp.float32
        )
        return (result, (largest + jnp.log(totals))[..., 0, 0])

    results, logsums = lax.map(one_step, jnp.arange(block_count // span, dtype=jnp.int32))
    results = results.reshape(block_count, BLOCK, head_count, HD)
    logsums = logsums.reshape(block_count, BLOCK, head_count)
    global_queries, key_flat, scores = global_scores(
        queries, key_heads, seg_blocks, segment, globals_pair
    )
    largest = jnp.max(scores, axis=-1, keepdims=True)
    expo = jnp.exp(scores - largest)
    totals = jnp.sum(expo, axis=-1, keepdims=True)
    weights = (expo / totals).astype(jnp.bfloat16)
    value_flat = value_heads.reshape(head_count, length, HD)
    global_result = jnp.einsum(
        "gthj,hje->gthe", weights, value_flat, preferred_element_type=jnp.float32
    )
    results = results.at[globals_pair].set(global_result)
    logsums = logsums.at[globals_pair].set((largest + jnp.log(totals))[..., 0])
    return (results.astype(jnp.bfloat16).reshape(length, head_count * HD), logsums)


def attend_back(heads, logsums, grad_context, segment, table, globals_pair):
    length = heads.shape[0]
    block_count = length // BLOCK
    head_count = table.shape[0]
    queries, key_heads, value_heads, listed, usable, seg_blocks = prepare(
        heads, segment, table, globals_pair
    )
    span = min(8, block_count)
    grad_rows = grad_context.reshape(block_count, BLOCK, head_count, HD)
    blocks = jnp.arange(block_count, dtype=jnp.int32)
    global_row = (blocks == globals_pair[0]) | (blocks == globals_pair[1])
    grad_sparse = jnp.where(global_row[:, None, None, None], jnp.zeros_like(grad_rows), grad_rows)

    def back_step(carry, number):
        key_grads, value_grads = carry
        query_step, key_step, value_step, scores, picked, choose = gather_step(
            queries, key_heads, value_heads, listed, usable, seg_blocks, number, span
        )
        logsum_step = lax.dynamic_slice_in_dim(logsums, number * span, span, 0)
        weights = jnp.exp(scores - logsum_step[..., None, None])
        grad_step = lax.dynamic_slice_in_dim(grad_sparse, number * span, span, 0)
        grad_weights = jnp.einsum(
            "qthe,hqkse->qthks", grad_step, value_step, preferred_element_type=jnp.float32
        )
        inner = jnp.sum(weights * grad_weights, axis=(3, 4), keepdims=True)
        grad_scores = (weights * (grad_weights - inner)).astype(jnp.bfloat16)
        grad_query = jnp.einsum(
            "qthks,hqkse->qthe", grad_scores, key_step, preferred_element_type=jnp.float32
        ) * HD ** (-0.5)
        grad_key = jnp.einsum(
            "qthks,qthe->hqkse", grad_scores, query_step, preferred_element_type=jnp.float32
        ) * HD ** (-0.5)
        grad_value = jnp.einsum(
            "qthks,qthe->hqkse",
            weights.astype(jnp.bfloat16),
            grad_step,
            preferred_element_type=jnp.float32,
        )
        choose_wide = choose.astype(jnp.float32)
        key_grads = key_grads + jnp.einsum(
            "hqkn,hqkse->hnse",
            choose_wide,
            grad_key,
            precision=lax.Precision.HIGHEST,
            preferred_element_type=jnp.float32,
        )
        value_grads = value_grads + jnp.einsum(
            "hqkn,hqkse->hnse",
            choose_wide,
            grad_value,
            precision=lax.Precision.HIGHEST,
            preferred_element_type=jnp.float32,
        )
        return ((key_grads, value_grads), grad_query)

    empty = jnp.zeros((head_count, block_count, BLOCK, HD), jnp.float32)
    (key_grads, value_grads), query_grads = lax.scan(
        back_step, (empty, empty), jnp.arange(block_count // span, dtype=jnp.int32)
    )
    query_grads = query_grads.reshape(block_count, BLOCK, head_count, HD)
    global_queries, key_flat, scores = global_scores(
        queries, key_heads, seg_blocks, segment, globals_pair
    )
    weights = jnp.exp(scores - logsums[globals_pair][..., None])
    grad_global = grad_rows[globals_pair]
    value_flat = value_heads.reshape(head_count, length, HD)
    grad_weights = jnp.einsum(
        "gthe,hje->gthj", grad_global, value_flat, preferred_element_type=jnp.float32
    )
    inner = jnp.sum(weights * grad_weights, axis=-1, keepdims=True)
    grad_scores = (weights * (grad_weights - inner)).astype(jnp.bfloat16)
    global_query_grad = jnp.einsum(
        "gthj,hje->gthe", grad_scores, key_flat, preferred_element_type=jnp.float32
    ) * HD ** (-0.5)
    key_extra = jnp.einsum(
        "gthj,gthe->hje", grad_scores, global_queries, preferred_element_type=jnp.float32
    ) * HD ** (-0.5)
    value_extra = jnp.einsum(
        "gthj,gthe->hje",
        weights.astype(jnp.bfloat16),
        grad_global,
        preferred_element_type=jnp.float32,
    )
    key_grads = key_grads + key_extra.reshape(head_count, block_count, BLOCK, HD)
    value_grads = value_grads + value_extra.reshape(head_count, block_count, BLOCK, HD)
    query_grads = query_grads.at[globals_pair].add(global_query_grad)
    stacked = jnp.stack(
        [query_grads, key_grads.transpose(1, 2, 0, 3), value_grads.transpose(1, 2, 0, 3)], axis=2
    )
    return stacked.reshape(length, 3 * head_count * HD).astype(jnp.bfloat16)


def run_batch(weights, tokens, segment, table, globals_pair, grad_out):
    (
        qkv_weight,
        query_bias,
        value_bias,
        proj_weight,
        proj_bias,
        attn_gain,
        attn_shift,
        inner_weight,
        inner_bias,
        down_weight,
        down_bias,
        ffn_gain,
        ffn_shift,
    ) = weights
    groups = lax.axis_size("seq")
    rows_here = tokens.shape[0]
    model_width = qkv_weight.shape[0]
    length = segment.shape[0]
    grouped_weight = regroup(qkv_weight, groups)
    bias_all = jnp.concatenate([query_bias, jnp.zeros_like(query_bias), value_bias]).astype(
        jnp.float32
    )
    grouped_bias = regroup(bias_all[None], groups)[0]
    projected = jnp.dot(tokens, grouped_weight, preferred_element_type=jnp.float32) + grouped_bias
    packed = projected.astype(jnp.bfloat16).reshape(rows_here, groups, -1)
    heads = lax.all_to_all(packed, "seq", split_axis=1, concat_axis=0, tiled=True).reshape(
        length, -1
    )
    context, logsums = attend(heads, segment, table, globals_pair)
    gathered = lax.all_to_all(
        context.reshape(length, 1, -1), "seq", split_axis=0, concat_axis=1, tiled=True
    ).reshape(rows_here, model_width)
    attn = jnp.dot(gathered, proj_weight, preferred_element_type=jnp.float32) + proj_bias.astype(
        jnp.float32
    )
    residual = tokens.astype(jnp.float32) + attn
    first_out, pull_first = jax.vjp(
        layer_norm, residual, attn_gain.astype(jnp.float32), attn_shift.astype(jnp.float32)
    )
    first_low = first_out.astype(jnp.bfloat16)
    pre = jnp.dot(first_low, inner_weight, preferred_element_type=jnp.float32) + inner_bias.astype(
        jnp.float32
    )
    activated, pull_gelu = jax.vjp(gelu_exact, pre)
    hidden = activated.astype(jnp.bfloat16)
    ffn = jnp.dot(hidden, down_weight, preferred_element_type=jnp.float32) + down_bias.astype(
        jnp.float32
    )
    output, pull_second = jax.vjp(
        layer_norm, first_out + ffn, ffn_gain.astype(jnp.float32), ffn_shift.astype(jnp.float32)
    )
    grad_second, grad_ffn_gain, grad_ffn_shift = pull_second(grad_out.astype(jnp.float32))
    grad_ffn = grad_second.astype(jnp.bfloat16)
    grad_down_weight = outer_sum(hidden, grad_ffn)
    grad_down_bias = jnp.sum(grad_ffn.astype(jnp.float32), axis=0)
    grad_hidden = jnp.dot(grad_ffn, down_weight.T, preferred_element_type=jnp.float32)
    (grad_pre_full,) = pull_gelu(grad_hidden)
    grad_pre = grad_pre_full.astype(jnp.bfloat16)
    grad_inner_weight = outer_sum(first_low, grad_pre)
    grad_inner_bias = jnp.sum(grad_pre.astype(jnp.float32), axis=0)
    grad_first = grad_second + jnp.dot(grad_pre, inner_weight.T, preferred_element_type=jnp.float32)
    grad_residual, grad_attn_gain, grad_attn_shift = pull_first(grad_first)
    grad_attn = grad_residual.astype(jnp.bfloat16)
    grad_proj_weight = outer_sum(gathered, grad_attn)
    grad_proj_bias = jnp.sum(grad_attn.astype(jnp.float32), axis=0)
    grad_context = jnp.dot(grad_attn, proj_weight.T, preferred_element_type=jnp.float32).astype(
        jnp.bfloat16
    )
    grad_heads_in = lax.all_to_all(
        grad_context.reshape(rows_here, groups, -1), "seq", split_axis=1, concat_axis=0, tiled=True
    )
    grad_heads = attend_back(
        heads, logsums, grad_heads_in.reshape(length, -1), segment, table, globals_pair
    )
    grad_projected = lax.all_to_all(
        grad_heads.reshape(length, 1, -1), "seq", split_axis=0, concat_axis=1, tiled=True
    )
    grad_projected = grad_projected.reshape(rows_here, 3 * model_width)
    grad_grouped = outer_sum(tokens, grad_projected)
    grad_bias_grouped = jnp.sum(grad_projected.astype(jnp.float32), axis=0)
    grad_tokens = grad_residual + jnp.dot(
        grad_projected, grouped_weight.T, preferred_element_type=jnp.float32
    )
    grad_qkv_weight = ungroup(grad_grouped, groups)
    grad_bias_all = ungroup(grad_bias_grouped[None], groups)[0]
    grads = (
        grad_qkv_weight,
        grad_bias_all[:model_width],
        grad_bias_all[2 * model_width :],
        grad_proj_weight,
        grad_proj_bias,
        grad_attn_gain,
        grad_attn_shift,
        grad_inner_weight,
        grad_inner_bias,
        grad_down_weight,
        grad_down_bias,
        grad_ffn_gain,
        grad_ffn_shift,
    )
    return (output.astype(jnp.bfloat16), grad_tokens.astype(jnp.bfloat16), grads)


def body(
    tokens,
    qkv_weight,
    query_bias,
    value_bias,
    proj_weight,
    proj_bias,
    attn_gain,
    attn_shift,
    inner_weight,
    inner_bias,
    down_weight,
    down_bias,
    ffn_gain,
    ffn_shift,
    seg_ids,
    rand_blocks,
    glob_blocks,
    d_out,
):
    running = None
    outputs = []
    input_grads = []
    for number in range(tokens.shape[0]):
        current = (
            lax.all_gather(qkv_weight, ("dp", "seq"), axis=0, tiled=True),
            lax.all_gather(query_bias, ("dp", "seq"), axis=0, tiled=True),
            lax.all_gather(value_bias, ("dp", "seq"), axis=0, tiled=True),
            lax.all_gather(proj_weight, ("dp", "seq"), axis=0, tiled=True),
            lax.all_gather(proj_bias, ("dp", "seq"), axis=0, tiled=True),
            lax.all_gather(attn_gain, ("dp", "seq"), axis=0, tiled=True),
            lax.all_gather(attn_shift, ("dp", "seq"), axis=0, tiled=True),
            lax.all_gather(inner_weight, ("dp", "seq"), axis=0, tiled=True),
            lax.all_gather(inner_bias, ("dp", "seq"), axis=0, tiled=True),
            lax.all_gather(down_weight, ("dp", "seq"), axis=0, tiled=True),
            lax.all_gather(down_bias, ("dp", "seq"), axis=0, tiled=True),
            lax.all_gather(ffn_gain, ("dp", "seq"), axis=0, tiled=True),
            lax.all_gather(ffn_shift, ("dp", "seq"), axis=0, tiled=True),
        )
        output, grad_tokens, grads = run_batch(
            current,
            tokens[number, 0],
            seg_ids[number, 0],
            rand_blocks[number, 0],
            glob_blocks[number, 0],
            d_out[number, 0],
        )
        outputs.append(output)
        input_grads.append(grad_tokens)
        running = (
            grads
            if running is None
            else tuple((left + right for left, right in zip(running, grads)))
        )
    summed = lax.psum_scatter(tuple(running), ("dp", "seq"), scatter_dimension=0, tiled=True)
    layer_out = jnp.stack(outputs)[:, None]
    grad_input = jnp.stack(input_grads)[:, None]
    return (
        layer_out,
        grad_input,
        summed[0],
        summed[1],
        summed[2],
        summed[3],
        summed[4],
        summed[5],
        summed[6],
        summed[7],
        summed[8],
        summed[9],
        summed[10],
        summed[11],
        summed[12],
    )


def solution(mesh):
    return jax.shard_map(
        body,
        mesh=mesh,
        in_specs=(
            P(None, "dp", "seq", None),
            P(("dp", "seq"), None),
            P(("dp", "seq")),
            P(("dp", "seq")),
            P(("dp", "seq"), None),
            P(("dp", "seq")),
            P(("dp", "seq")),
            P(("dp", "seq")),
            P(("dp", "seq"), None),
            P(("dp", "seq")),
            P(("dp", "seq"), None),
            P(("dp", "seq")),
            P(("dp", "seq")),
            P(("dp", "seq")),
            P(None, "dp", None),
            P(None, "dp", "seq", None, None),
            P(None, "dp", None),
            P(None, "dp", "seq", None),
        ),
        out_specs=(
            P(None, "dp", "seq", None),
            P(None, "dp", "seq", None),
            P(("dp", "seq"), None),
            P(("dp", "seq")),
            P(("dp", "seq")),
            P(("dp", "seq"), None),
            P(("dp", "seq")),
            P(("dp", "seq")),
            P(("dp", "seq")),
            P(("dp", "seq"), None),
            P(("dp", "seq")),
            P(("dp", "seq"), None),
            P(("dp", "seq")),
            P(("dp", "seq")),
            P(("dp", "seq")),
        ),
        check_vma=False,
    )
```

profile of v0, /device:TPU:0, one launch (start us, length us, event | category | flops | bytes accessed | tf_op | source)
XLA Modules:
  0.0 2053.5 jit_solution(61349227883006377)
XLA Ops:
  17.6 42.6 %all-reduce.19 = (bf16[768]{0:T(1024)(128)(2,1)S(1)}, bf16[768]{0:T(1024)(128)(2,1)S(1)}, bf16[768]{0:T(1024)(128)(2,1)}, bf16[768]{0:T(1024)(128)(2,1)}, bf16[7...) all-reduce(bf16[768]{0:T(1024)(128)(2,1)S(1)} %dynamic-update-slice, ...), channel_id=1, replica_groups=mesh['dp'=8,'seq'=4] {'dp','seq'}, use_global_device_ids=true, to_apply=%add.1 | all-reduce | flops 9216 | bytes 36864
  105.5 12.2 all-to-all-done
  167.6 14.1 copy.487
  201.5 111.6 %while.54 = (s32[]{:T(128)}, f32[4,8,64,3,64]{4,2,3,1,0:T(8,128)}, f32[4,8,64,3]{2,3,1,0:T(4,128)S(1)}, s32[4]{0:T(128)S(1)}, s32[3,32,8]{2,1,0:T(8,128)}, /*ind...) while((s32[]{:T(128)}, f32[4,8,64,3,64]{4,2,3,1,0:T(8,128)}, ...), condition=%wide.region_4.5_spmd, body=%wide.region_1.4_spmd.sunk | while | flops 317730880 | bytes 24040040 | solution.py:133
  320.4 9.1 reshape.842
  330.0 13.7 reduce.19
  363.9 111.2 %while.55 = (s32[]{:T(128)}, f32[4,8,64,3,64]{4,2,3,1,0:T(8,128)}, f32[4,8,64,3]{2,3,1,0:T(4,128)}, s32[4]{0:T(128)S(1)}, s32[3,32,8]{2,1,0:T(8,128)}, /*index=5...) while((s32[]{:T(128)}, f32[4,8,64,3,64]{4,2,3,1,0:T(8,128)}, ...), condition=%wide.region_16.17_spmd, body=%wide.region_13.16_spmd.sunk | while | flops 317730880 | bytes 20874128 | solution.py:133
  490.7 13.7 reduce.18
  551.0 35.0 %multiply_convert_fusion.1 = (bf16[512,3072]{1,0:T(8,128)(2,1)}, f32[512,3072]{1,0:T(8,128)}, bf16[512,3072]{1,0:T(8,128)(2,1)}, f32[512,3072]{1,0:T(8,128)}, f32[512,3072]{1,0:T(8,128)}) fusion(f32[3072]{0:T(1024)S(1)} %copy-done.134, f32[512,3072]{1,0:T(8,128)S(1)} %fusion.218, bf16[768,3072]{1,0:T(8,128)(2,1)S(1)} %copy-done.161, ...), kind=kOutput, calls=%fused_computation.207 | convolution fusion | flops 2625503232 | bytes 37771264 | tf_op jit(solution)/shard_map/dot_general | solution.py:286
  607.7 18.2 convert_reduce_fusion.1
  690.2 318.5 %while.56 = (s32[]{:T(128)}, f32[3,32,64,64]{3,1,2,0:T(8,128)}, f32[3,32,64,64]{3,1,2,0:T(8,128)}, f32[4,8,64,3,64]{4,2,3,1,0:T(8,128)}, s32[4]{0:T(128)S(1)}, /...) while((s32[]{:T(128)}, f32[3,32,64,64]{3,1,2,0:T(8,128)}, ...), condition=%wide.region_31.32_spmd.clone, body=%wide.region_29.31_spmd.clone.sunk | while | flops 1220665344 | bytes 97837528 | solution.py:208
  715.7 10.4 fusion.407
  746.8 10.4 bitcast_add_fusion.9
  759.1 9.5 bitcast_add_fusion.8
  793.5 10.3 fusion.407
  824.5 11.3 bitcast_add_fusion.9
  837.7 10.9 bitcast_add_fusion.8
  873.5 10.3 fusion.407
  904.4 11.3 bitcast_add_fusion.9
  917.7 10.9 bitcast_add_fusion.8
  953.5 10.3 fusion.407
  984.4 11.3 bitcast_add_fusion.9
  997.7 10.9 bitcast_add_fusion.8
  1038.3 20.4 reshape.846
  1058.7 56.1 %reduce.21 = bf16[2048,576]{1,0:T(8,128)(2,1)S(1)} reduce(bf16[2048,1,576]{2,1,0:T(2,128)(2,1)} %reshape.846, bf16[]{:T(256)} %broadcast.892), dimensions={1}, to_apply=%reshape.846.reduce_sub_computation | reduce | bytes 4718594 | tf_op jit(solution)/shard_map/convert_element_type | solution.py:241
  1143.4 317.8 %while.57 = (s32[]{:T(128)}, f32[3,32,64,64]{3,1,2,0:T(8,128)}, f32[3,32,64,64]{3,1,2,0:T(8,128)}, f32[4,8,64,3,64]{4,2,3,1,0:T(8,128)}, s32[4]{0:T(128)S(1)}, /...) while((s32[]{:T(128)}, f32[3,32,64,64]{3,1,2,0:T(8,128)}, ...), condition=%wide.region_41.42_spmd.clone, body=%wide.region_39.41_spmd.clone.sunk | while | flops 1220665344 | bytes 97837528 | solution.py:208
  1168.5 10.3 fusion.431
  1178.8 9.0 fusion.432
  1199.4 10.3 bitcast_add_fusion.11
  1211.7 9.5 bitcast_add_fusion.10
  1246.1 10.3 fusion.431
  1277.0 11.2 bitcast_add_fusion.11
  1290.2 10.8 bitcast_add_fusion.10
  1325.9 10.3 fusion.431
  1336.3 9.0 fusion.432
  1356.9 11.2 bitcast_add_fusion.11
  1370.1 10.8 bitcast_add_fusion.10
  1405.8 10.3 fusion.431
  1416.2 9.0 fusion.432
  1436.7 11.2 bitcast_add_fusion.11
  1450.0 10.8 bitcast_add_fusion.10
  1495.7 20.4 reshape.849
  1516.2 56.1 %reduce.20 = bf16[2048,576]{1,0:T(8,128)(2,1)S(1)} reduce(bf16[2048,1,576]{2,1,0:T(2,128)(2,1)} %reshape.849, bf16[]{:T(256)} %broadcast.892), dimensions={1}, to_apply=%reshape.849.reduce_sub_computation | reduce | bytes 4718594 | tf_op jit(solution)/shard_map/convert_element_type | solution.py:241
  1596.7 12.9 all-to-all-done.7
  1676.8 40.0 %all-reduce.18 = (f32[768]{0:T(1024)S(1)}, f32[768]{0:T(1024)S(1)}, f32[768]{0:T(1024)S(1)}, f32[768]{0:T(1024)S(1)}, f32[768]{0:T(1024)S(1)}, /*index=5*/f32[30...) all-reduce(f32[768]{0:T(1024)S(1)} %add.483, ...), channel_id=3, replica_groups=mesh['dp'=8,'seq'=4] {'dp','seq'}, use_global_device_ids=true, to_apply=%region_47.48.clone | all-reduce | flops 9216 | bytes 73728
  1730.2 32.8 %reduce-scatter.13.cloned.1.call-done = f32[24,2304]{1,0:T(8,128)} async-done(((f32[768,2304]{1,0:T(8,128)}), f32[24,2304]{1,0:T(8,128)}) %reduce-scatter.13.cloned.1.call-update) | async-done | bytes 221200
  1763.0 141.3 %reduce-scatter.11.cloned.1.call-done = f32[96,768]{1,0:T(8,128)} async-done(((f32[3072,768]{1,0:T(8,128)}), f32[96,768]{1,0:T(8,128)}) %reduce-scatter.11.cloned.1.call-update) | async-done | bytes 294928 | tf_op jit(solution)/shard_map/reduce_scatter | solution.py:403
  1904.4 142.1 %reduce-scatter.9.cloned.1.call-done = f32[24,3072]{1,0:T(8,128)} async-done(((f32[768,3072]{1,0:T(8,128)}), f32[24,3072]{1,0:T(8,128)}) %reduce-scatter.9.cloned.1.call-update) | async-done | bytes 294928 | tf_op jit(solution)/shard_map/reduce_scatter | solution.py:403
  (1127 shorter events, 1060.9 us)
Async XLA Ops:
  7.2 66.7 %all-gather.5.cloned.1.call-start = ((), (), s32[]{:S(2)}) async-start(), calls=%async_computation.12 | async-start | bytes 3649536 | tf_op jit(solution)/shard_map/all_gather | solution.py:374
  7.9 523.4 %all-gather.7.cloned.1.call-start = ((), (), s32[]{:S(2)}) async-start(), calls=%async_computation.13 | async-start | bytes 1216512 | tf_op jit(solution)/shard_map/all_gather | solution.py:377
  8.7 534.8 %all-gather.9.cloned.1.call-start = ((), (), s32[]{:S(2)}) async-start(), calls=%async_computation.14 | async-start | bytes 4866048 | tf_op jit(solution)/shard_map/all_gather | solution.py:381
  9.4 576.6 %all-gather.11.cloned.1.call-start = ((), (), s32[]{:S(2)}) async-start(), calls=%async_computation.15 | async-start | bytes 4866048 | tf_op jit(solution)/shard_map/all_gather | solution.py:383
  85.1 32.6 %all-to-all-start = ((bf16[512,4,576]{0,2,1:T(8,128)(2,1)}), bf16[512,4,576]{0,2,1:T(8,128)(2,1)S(1)}, u32[]{:S(2)}, u32[]{:S(2)}) async-start(bf16[512,4,576]{0,2,1:T(8,128)(2,1)} %bitcast.820), calls=%async_computation | async-start | bytes 4718592 | tf_op jit(solution)/shard_map/all_to_all | solution.py:271
  90.6 32.7 %copy-start = (s32[32,64]{1,0:T(8,128)}, s32[32,64]{1,0:T(8,128)S(1)}, u32[]{:S(2)}) copy-start(s32[32,64]{1,0:T(8,128)S(1)} %reshape_squeeze.9) | copy-start | bytes 24580
  105.5 17.1 copy-start.139
  105.5 22.0 %copy-start.109 = (s32[1,1,2048]{2,1,0:T(1,128)S(1)}, s32[1,1,2048]{2,1,0:T(1,128)}, u32[]{:S(2)}) copy-start(s32[1,1,2048]{2,1,0:T(1,128)} %get-tuple-element.847) | copy-start | bytes 24580
  105.5 22.2 %copy-start.108 = (s32[1,1,2048]{2,1,0:T(1,128)S(1)}, s32[1,1,2048]{2,1,0:T(1,128)}, u32[]{:S(2)}) copy-start(s32[1,1,2048]{2,1,0:T(1,128)} %get-tuple-element.848) | copy-start | bytes 24580
  117.7 11.0 copy-start.43
  117.7 34.5 %all-to-all-start.2 = ((bf16[512,4,576]{0,2,1:T(8,128)(2,1)}), bf16[512,4,576]{0,2,1:T(8,128)(2,1)}, u32[]{:S(2)}, u32[]{:S(2)}) async-start(bf16[512,4,576]{0,2,1:T(8,128)(2,1)} %bitcast.821), calls=%async_computation.2 | async-start | bytes 4718592 | tf_op jit(solution)/shard_map/all_to_all | solution.py:271
  122.7 13.9 copy-start.123
  122.7 13.9 copy-start.126
  122.7 13.8 copy-start.137
  122.7 67.8 %copy-start.138 = (s32[1024]{0:T(1024)}, s32[1024]{0:T(1024)S(1)}, u32[]{:S(2)}) copy-start(s32[1024]{0:T(1024)S(1)} %get-tuple-element.881) | copy-start | bytes 12292
  127.8 67.9 %copy-start.47 = (pred[2,64,2048]{2,1,0:T(8,128)(4,1)}, pred[2,64,2048]{2,1,0:T(8,128)(4,1)S(1)}, u32[]{:S(2)}) copy-start(pred[2,64,2048]{2,1,0:T(8,128)(4,1)S(1)} %broadcast_compare_fusion.1) | copy-start | bytes 786436
  164.4 17.2 copy-start.25
  347.6 161.1 %all-to-all-start.1 = ((bf16[4,2,49152]{2,1,0:T(2,128)(2,1)}), bf16[4,2,49152]{2,1,0:T(2,128)(2,1)}, u32[]{:S(2)}, u32[]{:S(2)}) async-start(bf16[4,2,49152]{2,1,0:T(2,128)(2,1)} %reshape.870), calls=%async_computation.1 | async-start | bytes 1572864 | tf_op jit(solution)/shard_map/all_to_all | solution.py:275
  490.7 17.9 copy-start.112
  490.7 18.0 copy-start.130
  490.7 22.2 %copy-start.24 = (bf16[3,32,64,64]{2,1,3,0:T(8,128)(2,1)S(1)}, bf16[3,32,64,64]{2,1,3,0:T(8,128)(2,1)}, u32[]{:S(2)}) copy-start(bf16[3,32,64,64]{2,1,3,0:T(8,128)(2,1)} %copy-done.23) | copy-start | bytes 2359300
  508.7 26.4 %all-to-all-start.3 = ((bf16[4,2,49152]{2,1,0:T(2,128)(2,1)}), bf16[4,2,49152]{2,1,0:T(2,128)(2,1)}, u32[]{:S(2)}, u32[]{:S(2)}) async-start(bf16[4,2,49152]{2,1,0:T(2,128)(2,1)} %reshape.868), calls=%async_computation.3 | async-start | bytes 1572864 | tf_op jit(solution)/shard_map/all_to_all | solution.py:275
  535.0 103.8 %copy-start.113 = (f32[512]{0:T(512)}, f32[512]{0:T(512)S(1)}, u32[]{:S(2)}) copy-start(f32[512]{0:T(512)S(1)} %broadcast_multiply_fusion.5) | copy-start | bytes 6148
  542.7 96.1 %copy-start.29 = (f32[512,768]{1,0:T(8,128)}, f32[512,768]{1,0:T(8,128)S(1)}, u32[]{:S(2)}) copy-start(f32[512,768]{1,0:T(8,128)S(1)} %get-tuple-element.869) | copy-start | bytes 4718596
  542.8 96.1 %copy-start.100 = (f32[512]{0:T(512)}, f32[512]{0:T(512)S(1)}, u32[]{:S(2)}) copy-start(f32[512]{0:T(512)S(1)} %broadcast_multiply_fusion.3) | copy-start | bytes 6148
  543.4 95.5 %copy-start.140 = (f32[512]{0:T(512)}, f32[512]{0:T(512)S(1)}, u32[]{:S(2)}) copy-start(f32[512]{0:T(512)S(1)} %fusion.199) | copy-start | bytes 6148
  543.4 95.5 %copy-start.106 = (f32[512]{0:T(512)}, f32[512]{0:T(512)S(1)}, u32[]{:S(2)}) copy-start(f32[512]{0:T(512)S(1)} %fusion.201) | copy-start | bytes 6148
  551.0 35.0 %copy-start.151 = (f32[768]{0:T(1024)S(1)}, f32[768]{0:T(1024)}, u32[]{:S(2)}) copy-start(f32[768]{0:T(1024)} %convert_element_type.239) | copy-start | bytes 9220
  647.0 15.9 all-to-all-start.4
  651.2 1079.0 %reduce-scatter.7.cloned.1.call-start = ((), (), s32[]{:S(2)}) async-start(), calls=%async_computation.16 | async-start | bytes 2433024 | tf_op jit(solution)/shard_map/reduce_scatter | solution.py:403
  662.9 456.0 %all-to-all-start.6 = ((bf16[512,4,192]{0,2,1:T(8,128)(2,1)}), bf16[512,4,192]{0,2,1:T(8,128)(2,1)}, u32[]{:S(2)}, u32[]{:S(2)}) async-start(bf16[512,4,192]{0,2,1:T(8,128)(2,1)} %bitcast.125), calls=%async_computation.6 | async-start | bytes 1572864 | tf_op jit(solution)/shard_map/all_to_all | solution.py:314
  709.2 17.0 copy-start.5
  787.0 16.9 copy-start.5
  837.7 10.9 copy-start.167
  866.9 16.9 copy-start.5
  917.7 10.9 copy-start.167
  946.9 16.9 copy-start.5
  1118.9 457.5 %all-to-all-start.5 = ((bf16[4,2,147456]{2,1,0:T(2,128)(2,1)}), bf16[4,2,147456]{2,1,0:T(2,128)(2,1)}, u32[]{:S(2)}, u32[]{:S(2)}) async-start(bf16[4,2,147456]{2,1,0:T(2,128)(2,1)} %reshape.874), calls=%async_computation.5 | async-start | bytes 4718592 | tf_op jit(solution)/shard_map/all_to_all | solution.py:320
  1161.9 16.9 copy-start.7
  1239.5 16.9 copy-start.7
  1319.3 16.9 copy-start.7
  1399.2 16.9 copy-start.7
  1576.3 33.3 %all-to-all-start.7 = ((bf16[4,2,147456]{2,1,0:T(2,128)(2,1)}), bf16[4,2,147456]{2,1,0:T(2,128)(2,1)}, u32[]{:S(2)}, u32[]{:S(2)}) async-start(bf16[4,2,147456]{2,1,0:T(2,128)(2,1)} %reshape.872), calls=%async_computation.7 | async-start | bytes 4718592 | tf_op jit(solution)/shard_map/all_to_all | solution.py:320
  1581.1 181.9 %reduce-scatter.13.cloned.1.call-start = ((), (), s32[]{:S(2)}) async-start(), calls=%async_computation.19 | async-start | bytes 7299072
  1644.7 259.6 %reduce-scatter.11.cloned.1.call-start = ((), (), s32[]{:S(2)}) async-start(), calls=%async_computation.18 | async-start | bytes 9732096 | tf_op jit(solution)/shard_map/reduce_scatter | solution.py:403
  1655.6 390.9 %reduce-scatter.9.cloned.1.call-start = ((), (), s32[]{:S(2)}) async-start(), calls=%async_computation.17 | async-start | bytes 9732096 | tf_op jit(solution)/shard_map/reduce_scatter | solution.py:403
  1672.2 49.9 %copy-start.143 = (f32[512]{0:T(512)S(1)}, f32[512]{0:T(512)}, u32[]{:S(2)}) copy-start(f32[512]{0:T(512)} %copy-done.142) | copy-start | bytes 6148
  1673.2 48.8 %copy-start.42 = (bf16[512,4,1,576]{0,3,1,2:T(8,128)(2,1)S(1)}, bf16[512,4,1,576]{0,3,1,2:T(8,128)(2,1)}, u32[]{:S(2)}) copy-start(bf16[512,4,1,576]{0,3,1,2:T(8,128)(2,1)} %copy-done.41) | copy-start | bytes 7077892
  (214 other events, 1005.9 us)
Sparse Core Ops, SparseCore 0:
  10.9 62.9 all-gather.4
  76.8 53.1 all-gather.6
  132.9 62.4 all-gather.8
  198.2 62.3 all-gather.10
  657.6 99.2 reduce-scatter.6
  1644.8 118.1 reduce-scatter.12
  1769.5 134.8 reduce-scatter.10
  1911.8 134.6 reduce-scatter.8
where the time goes:
time: 2080 us; the launch traced here: 2050 us
  matrix products  690 us (33%)
  local copies, waits for them, and re-layouts  530 us (25%)
  waiting for transfers between devices  351 us (17%)
  other arithmetic  333 us (16%)
  blocking collectives  82.6 us (4%)
  starting transfers between devices  36.3 us (2%)
    reduce_scatter x3, waiting for transfers between devices, body(): lax.psum_scatter(tuple(running), ('dp', 'seq'), scatter_dimension=0, tile...  283 us
    dot_general x16, matrix products, gather_step(): jnp.einsum('qthe,hqkse->qthks', query_step, key_step, preferred_element_t...  136 us
    convert_element_type x2, other arithmetic, attend_back(): return stacked.reshape(length, 3 * head_count * HD).astype(jnp.bfloat16)  112 us
    dot_general x8, matrix products, back_step(): jnp.einsum('hqkn,hqkse->hnse', choose_wide, grad_value, precision=lax.Pre...  88.3 us
    dot_general x8, matrix products, back_step(): jnp.einsum('hqkn,hqkse->hnse', choose_wide, grad_key, precision=lax.Preci...  84 us
    unnamed x2, blocking collectives  82.6 us
    unnamed x346, local copies, waits for them, and re-layouts  78 us
    convert_element_type x8, other arithmetic, back_step(): weights.astype(jnp.bfloat16)  71.9 us
  transfers between devices with their start and end apart: 16, of which 8 were waited for; matrix products, arithmetic and copies ran while one was open for 72% of the time, Pallas kernels for 0%

commit v1 on v0

v1 whole, which is shorter than its diff:
```python
import jax
import jax.numpy as jnp
from jax import lax
from jax.experimental import pallas as pl
from jax.experimental.pallas import tpu as pltpu
from jax.sharding import PartitionSpec as P

HD = 64
BLOCK = 64
EPSILON = 1e-06
BIG = float(2.0**100)
LOWEST = -3.0e38
TQ = 256
TK = 512
CHIPS = 16
TILE = 256
BF = jnp.bfloat16
F32 = jnp.float32
VMEM_LIMIT = 60 << 20


def nn(left, right):
    return lax.dot_general(left, right, (((1,), (0,)), ((), ())), preferred_element_type=F32)


def nt(left, right):
    return lax.dot_general(left, right, (((1,), (1,)), ((), ())), preferred_element_type=F32)


def tn(left, right):
    return lax.dot_general(left, right, (((0,), (0,)), ((), ())), preferred_element_type=F32)


def smem():
    return pl.BlockSpec(memory_space=pltpu.SMEM)


def anywhere():
    return pl.BlockSpec(memory_space=pl.ANY)


def shape(dims, kind):
    return jax.ShapeDtypeStruct(dims, kind)


def swap(value, dim):
    bit = 1 if dim == "core" else 2
    return lax.ppermute(value, "seq", [(s, s ^ bit) for s in range(4)])


DIMS = {"x": (1, 2), "z": (2, 4)}


def shift(value, dim, by):
    stride, size = DIMS[dim]
    pairs = []
    for d in range(lax.axis_size("dp")):
        at = d // stride % size
        pairs.append((d, d + ((at + by) % size - at) * stride))
    return lax.ppermute(value, "dp", pairs)


def extent(dim):
    return 2 if dim == "y" else DIMS[dim][1]


def others(value, dim):
    if dim == "y":
        return [swap(value, "y")]
    return [shift(value, dim, by) for by in range(1, extent(dim))]


def gather(chunk, order):
    current = chunk[None]
    for dim in order[:-1]:
        current = jnp.concatenate([current] + others(current, dim), axis=0)
    return [current] + others(current, order[-1])


def scatter_sum(pieces, order):
    for step, dim in enumerate(order):
        total = pieces[0].astype(F32)
        for r in range(1, extent(dim)):
            if dim == "y":
                came = swap(pieces[r], "y")
            else:
                came = shift(pieces[r], dim, extent(dim) - r)
            total = total + came.astype(F32)
        if step + 1 < len(order):
            ways = extent(order[step + 1])
            total = total.astype(BF).reshape((ways, -1) + total.shape[1:])
            pieces = [total[r] for r in range(ways)]
    return total[0]


def chip_at(order, piece, index, here):
    rel = {order[-1]: piece}
    for dim in order[:-1]:
        rel[dim] = index % extent(dim)
        index //= extent(dim)
    z = lax.rem(here["z"] - rel["z"] + 4, 4)
    x = lax.rem(here["x"] + rel["x"], 2)
    y = lax.rem(here["y"] + rel["y"], 2)
    return z * 4 + x * 2 + y


def placed(meta):
    return {"c": meta[0], "x": meta[1], "y": meta[2], "z": meta[3]}


class Plan:
    def __init__(self, parts):
        self.parts = parts

    def counts(self):
        return [1 if order is None else extent(order[-1]) for _, _, order in self.parts]

    def entries(self):
        return sum(
            CHIPS for _ in self.parts
        )

    def walk(self, here):
        number = 0
        for (first, end, order), count in zip(self.parts, self.counts()):
            for p in range(count):
                for m in range(CHIPS // count):
                    chip = m if order is None else chip_at(order, p, m, here)
                    yield number + p, m, chip, first, end
            number += count


def qkv_kernel(plan, pieces_n, *refs):
    meta = refs[0]
    pieces = refs[1 : 1 + pieces_n]
    x_ref, bias_ref, out_ref, w_ref, sems = refs[1 + pieces_n :]
    here = placed(meta)
    width = w_ref.shape[2]
    depth = w_ref.shape[1] // 3

    @pl.when(pl.program_id(0) == 0)
    def _():
        copies = []
        for i, (p, m, chip, first, end) in enumerate(plan.walk(here)):
            copies.append(
                pltpu.make_async_copy(pieces[p].at[m], w_ref.at[chip, first:end, :], sems.at[i])
            )
        for copy in copies:
            copy.start()
        for copy in copies:
            copy.wait()

    x = x_ref[...]
    for w in range(3):
        weight = w_ref[:, depth * w : depth * w + depth, :].reshape(CHIPS * depth, width)
        cols = slice(width * w, width * w + width)
        out_ref[:, cols] = (nn(x, weight) + bias_ref[0:1, cols]).astype(BF)


def project_qkv(plan, meta, pieces, x_full, bias):
    rows, model = x_full.shape
    wide = bias.shape[1]
    width, depth = wide // 3, model // CHIPS
    tile = 512
    return pl.pallas_call(
        lambda *refs: qkv_kernel(plan, len(pieces), *refs),
        grid=(rows // tile,),
        in_specs=[smem()]
        + [anywhere()] * len(pieces)
        + [pl.BlockSpec((tile, model), lambda i: (i, 0)), pl.BlockSpec((1, wide), lambda i: (0, 0))],
        out_specs=[
            pl.BlockSpec((tile, wide), lambda i: (i, 0)),
            pl.BlockSpec((CHIPS, 3 * depth, width), lambda i: (0, 0, 0)),
        ],
        out_shape=[shape((rows, wide), BF), shape((CHIPS, 3 * depth, width), BF)],
        scratch_shapes=[pltpu.SemaphoreType.DMA((plan.entries(),))],
        compiler_params=pltpu.CompilerParams(vmem_limit_bytes=VMEM_LIMIT),
        cost_estimate=pl.CostEstimate(
            flops=2 * rows * model * wide, bytes_accessed=2 * rows * (model + wide), transcendentals=0
        ),
        name="project_qkv",
    )(meta, *pieces, x_full, bias)


def fill_features(seg_ref, rand_ref, first_global, second_global, key_ref, query_ref):
    heads, _, length = key_ref.shape
    blocks = length // BLOCK
    at = lax.broadcasted_iota(jnp.int32, (blocks, length), 1) // BLOCK
    row = lax.broadcasted_iota(jnp.int32, (blocks, length), 0)
    seen = jnp.abs(at - row) <= 1
    for chosen in (first_global, second_global):
        seen = seen | (at == chosen) | (row == chosen)
    same = lax.broadcasted_iota(jnp.int32, (HD - blocks, length), 0) == seg_ref[...]
    for h in range(heads):
        picked = seen
        for r in range(rand_ref.shape[2]):
            picked = picked | (at == rand_ref[h, :, r : r + 1])
        key_ref[h, 0:blocks, :] = jnp.where(picked, 0.0, 1.0).astype(BF)
        key_ref[h, blocks:HD, :] = jnp.where(same, 0.0, 1.0).astype(BF)
    query_ref[0:blocks, :] = jnp.where(at == row, -BIG, 0.0).astype(BF)
    query_ref[blocks:HD, :] = jnp.where(same, -BIG, 0.0).astype(BF)


def widen_pair(p, q_ref, k_ref, key_feat, query_feat, key_wide, query_wide):
    cols = slice(128 * p, 128 * p + 128)
    scaled = q_ref[:, cols] * BF(HD**-0.5)
    queries, keys = scaled.T, k_ref[:, cols].T
    a, b = 2 * p, 2 * p + 1
    query_wide[a, 0:HD, :] = queries[0:HD]
    query_wide[a, HD:128, :] = query_feat[...]
    query_wide[b, 0:HD, :] = query_feat[...]
    query_wide[b, HD:128, :] = queries[HD:128]
    key_wide[a] = jnp.concatenate([keys[0:HD], key_feat[a]], axis=0).T
    key_wide[b] = jnp.concatenate([key_feat[b], keys[HD:128]], axis=0).T
    return scaled, keys


def attend_kernel(meta, lo_ref, n_ref, glob_ref, q_ref, k_ref, v_ref, seg_ref, rand_ref, out_ref, lse_ref,
                  key_feat, query_feat, key_wide, query_wide, values, turned, store):
    heads, length = lse_ref.shape
    fill_features(seg_ref, rand_ref, glob_ref[0], glob_ref[1], key_feat, query_feat)
    for p in range(heads // 2):
        widen_pair(p, q_ref, k_ref, key_feat, query_feat, key_wide, query_wide)
        values[128 * p : 128 * p + 128, :] = v_ref[:, 128 * p : 128 * p + 128].T

    def tile(i, _):
        qs = pl.ds(pl.multiple_of(i * TQ, TQ), TQ)
        start = lo_ref[i]

        def scan(j, tops):
            ks = pl.ds(pl.multiple_of(start + j * TK, 128), TK)
            to = pl.ds(pl.multiple_of(j * TK, TK), TK)
            raised = []
            for h in range(heads):
                scores = nn(key_wide[h, ks, :], query_wide[h, :, qs])
                store[h, to, :] = scores
                raised.append(jnp.maximum(tops[h], jnp.max(scores.reshape(TK // 8, 8, TQ), axis=0)))
            return tuple(raised)

        tops = lax.fori_loop(0, n_ref[i], scan, (jnp.full((8, TQ), LOWEST, F32),) * heads)
        tops = [jnp.max(top, axis=0, keepdims=True) for top in tops]

        def collect(j, carry):
            ks = pl.ds(pl.multiple_of(start + j * TK, 128), TK)
            at = pl.ds(pl.multiple_of(j * TK, TK), TK)
            new = []
            for h in range(heads):
                total, summed = carry[h]
                expo = jnp.exp(store[h, at, :] - tops[h])
                total = total + jnp.sum(expo.reshape(TK // 8, 8, TQ), axis=0)
                summed = summed + nn(values[HD * h : HD * h + HD, ks], expo.astype(BF))
                new.append((total, summed))
            return tuple(new)

        none = (jnp.zeros((8, TQ), F32), jnp.zeros((HD, TQ), F32))
        found = lax.fori_loop(0, n_ref[i], collect, (none,) * heads)
        for h in range(heads):
            total, summed = found[h]
            total = jnp.sum(total, axis=0, keepdims=True)
            turned[HD * h : HD * h + HD, qs] = (summed / total).astype(BF)
            lse_ref[h : h + 1, qs] = tops[h] + jnp.log(total)
        return 0

    lax.fori_loop(0, length // TQ, tile, 0)
    quarter = length // 4
    for p in range(heads // 2):
        result = turned[128 * p : 128 * p + 128, :].T
        for n in range(4):
            rel = lax.rem(meta[0] + n, 2)
            out_ref[rel, quarter * (n // 2) : quarter * (n // 2) + quarter, 128 * p : 128 * p + 128] = result[
                quarter * n : quarter * n + quarter
            ]


def whole(dims):
    return pl.BlockSpec(dims, lambda *_: (0,) * len(dims))


def attend(meta, qkv, seg_row, table, globs, lo, n):
    length = qkv.shape[0]
    heads, blocks = table.shape[:2]
    wide = heads * HD
    third = lambda w: pl.BlockSpec((length, wide), lambda i: (0, w))
    return pl.pallas_call(
        attend_kernel,
        grid=(1,),
        in_specs=[smem()] * 4 + [third(0), third(1), third(2), whole((1, length)), whole((heads, blocks, 3))],
        out_specs=[whole((2, length // 2, wide)), whole((heads, length))],
        out_shape=[shape((2, length // 2, wide), BF), shape((heads, length), F32)],
        scratch_shapes=[
            pltpu.VMEM((heads, HD, length), BF),
            pltpu.VMEM((HD, length), BF),
            pltpu.VMEM((heads, length, 128), BF),
            pltpu.VMEM((heads, 128, length), BF),
            pltpu.VMEM((wide, length), BF),
            pltpu.VMEM((wide, length), BF),
            pltpu.VMEM((heads, length, TQ), F32),
        ],
        compiler_params=pltpu.CompilerParams(vmem_limit_bytes=VMEM_LIMIT),
        cost_estimate=pl.CostEstimate(
            flops=heads * length * length * 512, bytes_accessed=10 * length * wide, transcendentals=heads * length * length // 2
        ),
        name="attend",
    )(meta, lo, n, globs, qkv, qkv, qkv, seg_row, table)


def attend_back_kernel(meta, lo_ref, n_ref, glob_ref, q_ref, k_ref, v_ref, own_ref, oth_ref, ctx_ref, lse_ref, seg_ref,
                       rand_ref, dq_ref, dk_ref, dv_ref, key_feat, query_feat, key_wide, query_wide, value_one,
                       grad_turned, keys_turned, query_one, grad_one, inner_ref, dk, dv, dqt, grads):
    heads, length = lse_ref.shape
    quarter = length // 4
    fill_features(seg_ref, rand_ref, glob_ref[0], glob_ref[1], key_feat, query_feat)
    for rel, source in ((0, own_ref), (1, oth_ref)):
        for n in range(2):
            at = 2 * n + lax.rem(meta[0] + rel, 2)
            rows = pl.ds(pl.multiple_of(at * quarter, quarter), quarter)
            grads[0, rows, :] = source[quarter * n : quarter * n + quarter, :]
            grads[1, rows, :] = ctx_ref[rel, quarter * n : quarter * n + quarter, :]
    low = lax.broadcasted_iota(jnp.int32, (length, 128), 1) < HD
    zero = jnp.zeros((length, 128), BF)
    for p in range(heads // 2):
        cols = slice(128 * p, 128 * p + 128)
        scaled, keys = widen_pair(p, q_ref, k_ref, key_feat, query_feat, key_wide, query_wide)
        keys_turned[cols, :] = keys
        grad, value = grads[0, :, cols], v_ref[:, cols]
        for e in range(2):
            keep = low if e == 0 else ~low
            value_one[2 * p + e] = jnp.where(keep, value, zero)
            query_one[2 * p + e] = jnp.where(keep, scaled, zero)
            grad_one[2 * p + e] = jnp.where(keep, grad, zero)
        turned = grad.T
        grad_turned[cols, :] = turned
        product = turned.astype(F32) * grads[1, :, cols].T.astype(F32)
        for e in range(2):
            h = 2 * p + e
            inner_ref[h : h + 1, :] = jnp.sum(product[HD * e : HD * e + HD], axis=0, keepdims=True)
    dk[...] = jnp.zeros_like(dk)
    dv[...] = jnp.zeros_like(dv)

    def tile(i, _):
        qs = pl.ds(pl.multiple_of(i * TQ, TQ), TQ)
        start = lo_ref[i]

        def body(j, carry):
            ks = pl.ds(pl.multiple_of(start + j * TK, 128), TK)
            new = []
            for p in range(heads // 2):
                cols = slice(128 * p, 128 * p + 128)
                more_k, more_v = [], []
                for h in (2 * p, 2 * p + 1):
                    scores = nn(key_wide[h, ks, :], query_wide[h, :, qs])
                    prob = jnp.exp(scores - lse_ref[h : h + 1, qs])
                    grad_prob = nn(value_one[h, ks, :], grad_turned[cols, qs])
                    grad_scores = (prob * (grad_prob - inner_ref[h : h + 1, qs])).astype(BF)
                    new.append(carry[h] + nn(keys_turned[HD * h : HD * h + HD, ks], grad_scores))
                    more_k.append(nn(grad_scores, query_one[h, qs, :]))
                    more_v.append(nn(prob.astype(BF), grad_one[h, qs, :]))
                dk[ks, cols] += more_k[0] + more_k[1]
                dv[ks, cols] += more_v[0] + more_v[1]
            return tuple(new)

        found = lax.fori_loop(0, n_ref[i], body, (jnp.zeros((HD, TQ), F32),) * heads)
        for h in range(heads):
            dqt[HD * h : HD * h + HD, qs] = (found[h] * HD**-0.5).astype(BF)
        return 0

    lax.fori_loop(0, length // TQ, tile, 0)
    for p in range(heads // 2):
        cols = slice(128 * p, 128 * p + 128)
        dq_ref[:, cols] = dqt[cols, :].T
    dk_ref[...] = dk[...].astype(BF)
    dv_ref[...] = dv[...].astype(BF)


def attend_back(meta, qkv, own, oth, ctx, lse, seg_row, table, globs, lo, n):
    length = qkv.shape[0]
    heads, blocks = table.shape[:2]
    wide = heads * HD
    third = lambda w: pl.BlockSpec((length, wide), lambda i: (0, w))
    half = whole((length // 2, wide))
    return pl.pallas_call(
        attend_back_kernel,
        grid=(1,),
        in_specs=[smem()] * 4
        + [third(0), third(1), third(2), half, half, whole((2, length // 2, wide)), whole((heads, length))]
        + [whole((1, length)), whole((heads, blocks, 3))],
        out_specs=[whole((length, wide))] * 3,
        out_shape=[shape((length, wide), BF)] * 3,
        scratch_shapes=[
            pltpu.VMEM((heads, HD, length), BF),
            pltpu.VMEM((HD, length), BF),
            pltpu.VMEM((heads, length, 128), BF),
            pltpu.VMEM((heads, 128, length), BF),
            pltpu.VMEM((heads, length, 128), BF),
            pltpu.VMEM((wide, length), BF),
            pltpu.VMEM((wide, length), BF),
            pltpu.VMEM((heads, length, 128), BF),
            pltpu.VMEM((heads, length, 128), BF),
            pltpu.VMEM((heads, length), F32),
            pltpu.VMEM((length, wide), F32),
            pltpu.VMEM((length, wide), F32),
            pltpu.VMEM((wide, length), BF),
            pltpu.VMEM((2, length, wide), BF),
        ],
        compiler_params=pltpu.CompilerParams(vmem_limit_bytes=VMEM_LIMIT),
        cost_estimate=pl.CostEstimate(
            flops=heads * length * length * 1280, bytes_accessed=20 * length * wide, transcendentals=heads * length * length // 2
        ),
        name="attend_back",
    )(meta, lo, n, globs, qkv, qkv, qkv, own, oth, ctx, lse, seg_row, table)


def key_ranges(segment):
    length = segment.shape[0]
    first, last = segment[::TQ], segment[TQ - 1 :: TQ]
    lo = jnp.sum(segment[None, :] < first[:, None], axis=1, dtype=jnp.int32) // 128 * 128
    hi = jnp.sum(segment[None, :] <= last[:, None], axis=1, dtype=jnp.int32)
    n = (hi - lo + TK - 1) // TK
    return jnp.minimum(lo, length - n * TK), n


def centre(value):
    centred = value - jnp.mean(value, axis=1, keepdims=True)
    rate = lax.rsqrt(jnp.mean(centred * centred, axis=1, keepdims=True) + EPSILON)
    return centred * rate, rate


def norm_back(grad, normed, rate):
    return rate * (
        grad
        - jnp.mean(grad, axis=1, keepdims=True)
        - normed * jnp.mean(grad * normed, axis=1, keepdims=True)
    )


def cut(value):
    half = value.shape[1] // 2
    return value[:, :half], value[:, half:]


class Packed:
    def __init__(self, ref):
        self.ref = ref
        self.width = ref.shape[3]
        self.depth = 2 * self.width // CHIPS
        self.groups = (ref.shape[2] - self.depth) // (2 * self.depth)
        self.low = self.depth * (1 + self.groups)
        self.deep = ref.shape[2] - self.low
        self.span = self.width // self.deep

    def at_proj(self, h, hc):
        return (hc, slice(CHIPS // 2 * h, CHIPS // 2 * h + CHIPS // 2), slice(0, self.depth), slice(None))

    def at_inner(self, h, g):
        return (h, slice(0, CHIPS), slice(self.depth * (1 + g), self.depth * (2 + g)), slice(None))

    def at_down(self, h, g, hc):
        first = CHIPS // 2 * h + self.span * g
        return (hc, slice(first, first + self.span), slice(self.low, self.low + self.deep), slice(None))

    def read(self, where):
        value = self.ref[where]
        return value.reshape(-1, self.width)

    def write(self, where, value):
        a, b = where[1], where[2]
        self.ref[where] = value.reshape(a.stop - a.start, b.stop - b.start, self.width).astype(self.ref.dtype)


def ffn_kernel(plan, pieces_n, *refs):
    meta = refs[0]
    own_pieces = refs[1 : 1 + pieces_n]
    oth_pieces = refs[1 + pieces_n : 1 + 2 * pieces_n]
    (ctx_own, ctx_oth, x_ref, dout_ref, vec_ref, bias_ref,
     out_ref, hid_ref, gf_ref, low_ref, gp_ref, gr_ref, ga_ref, gc_own, gc_oth, vg_ref, bg_ref,
     w_ref, slope, sems) = refs[1 + 2 * pieces_n :]
    here = placed(meta)
    c = here["c"]
    step = pl.program_id(0)

    @pl.when(step == 0)
    def _():
        copies = []
        for rel, pieces in ((0, own_pieces), (1, oth_pieces)):
            for p, m, chip, first, end in plan.walk(here):
                copies.append(
                    pltpu.make_async_copy(
                        pieces[p].at[m], w_ref.at[lax.rem(c + rel, 2), chip, first:end, :], sems.at[len(copies)]
                    )
                )
        for copy in copies:
            copy.start()
        for copy in copies:
            copy.wait()
        vg_ref[...] = jnp.zeros_like(vg_ref)
        bg_ref[...] = jnp.zeros_like(bg_ref)

    w = Packed(w_ref)
    wide = w.width
    vec = lambda n: vec_ref[n : n + 1, :]
    own, oth = ctx_own[...], ctx_oth[...]
    context = (jnp.where(c == 0, own, oth), jnp.where(c == 0, oth, own))
    attn = jnp.concatenate(
        [nn(context[0], w.read(w.at_proj(0, hc))) + nn(context[1], w.read(w.at_proj(1, hc))) for hc in range(2)], axis=1
    )
    n1, rate1 = centre(x_ref[...].astype(F32) + (attn + vec(0)))
    x1 = n1 * vec(1) + vec(2)
    low = x1.astype(BF)
    low_ref[...] = low
    ffn = [None, None]
    chunks = [(h, g) for h in range(2) for g in range(w.groups)]
    for number, (h, g) in enumerate(chunks):
        cols = slice(wide * number, wide * number + wide)
        pre = nn(low, w.read(w.at_inner(h, g))) + bias_ref[0:1, cols]
        below = 0.5 + 0.5 * lax.erf(pre * 0.7071067811865476)
        slope[:, cols] = below + pre * (jnp.exp(-0.5 * (pre * pre)) * 0.3989422804014327)
        hidden = (pre * below).astype(BF)
        hid_ref[:, cols] = hidden
        for hc in range(2):
            more = nn(hidden, w.read(w.at_down(h, g, hc)))
            ffn[hc] = more if ffn[hc] is None else ffn[hc] + more
    n2, rate2 = centre(x1 + (jnp.concatenate(ffn, axis=1) + vec(3)))
    out_ref[...] = (n2 * vec(4) + vec(5)).astype(BF)

    total = lambda value: jnp.sum(value, axis=0, keepdims=True)
    grad = dout_ref[...].astype(F32)
    gr2 = norm_back(grad * vec(4), n2, rate2)
    gf = gr2.astype(BF)
    gf_ref[...] = gf
    vg_ref[4:5, :] += total(grad * n2)
    vg_ref[5:6, :] += total(grad)
    vg_ref[3:4, :] += total(gf.astype(F32))
    gf_halves = cut(gf)
    gx1 = gr2
    for number, (h, g) in enumerate(chunks):
        cols = slice(wide * number, wide * number + wide)
        grad_hidden = nt(gf_halves[0], w.read(w.at_down(h, g, 0))) + nt(gf_halves[1], w.read(w.at_down(h, g, 1)))
        gp = (grad_hidden * slope[:, cols]).astype(BF)
        gp_ref[:, cols] = gp
        bg_ref[0:1, cols] += total(gp.astype(F32))
        gx1 = gx1 + nt(gp, w.read(w.at_inner(h, g)))
    gr1 = norm_back(gx1 * vec(1), n1, rate1)
    gr_ref[...] = gr1
    ga = gr1.astype(BF)
    ga_ref[...] = ga
    vg_ref[1:2, :] += total(gx1 * n1)
    vg_ref[2:3, :] += total(gx1)
    vg_ref[0:1, :] += total(ga.astype(F32))
    ga_halves = cut(ga)
    gc = [nt(ga_halves[0], w.read(w.at_proj(h, 0))) + nt(ga_halves[1], w.read(w.at_proj(h, 1))) for h in range(2)]
    gc_own[...] = jnp.where(c == 0, gc[0], gc[1]).astype(BF)
    gc_oth[...] = jnp.where(c == 0, gc[1], gc[0]).astype(BF)


def feed_forward(plan, meta, own_pieces, oth_pieces, ctx, ctx_oth, x_own, d_own, vectors, inner_bias):
    rows, model = x_own.shape
    wide = inner_bias.shape[1]
    half = model // 2
    packed = (2, CHIPS, model // CHIPS * (1 + wide // 2 // half) + wide // CHIPS, half)
    tile = lambda n: pl.BlockSpec((TILE, n), lambda i: (i, 0))
    return pl.pallas_call(
        lambda *refs: ffn_kernel(plan, len(own_pieces), *refs),
        grid=(rows // TILE,),
        in_specs=[smem()]
        + [anywhere()] * (2 * len(own_pieces))
        + [pl.BlockSpec((None, TILE, half), lambda i: (0, i, 0)), tile(half), tile(model), tile(model)]
        + [whole(vectors.shape), whole(inner_bias.shape)],
        out_specs=[tile(model), tile(wide), tile(model), tile(model), tile(wide), tile(model), tile(model), tile(half), tile(half)]
        + [whole((8, model)), whole((8, wide))],
        out_shape=[
            shape((rows, model), BF),
            shape((rows, wide), BF),
            shape((rows, model), BF),
            shape((rows, model), BF),
            shape((rows, wide), BF),
            shape((rows, model), F32),
            shape((rows, model), BF),
            shape((rows, half), BF),
            shape((rows, half), BF),
            shape((8, model), F32),
            shape((8, wide), F32),
        ],
        scratch_shapes=[
            pltpu.VMEM(packed, BF),
            pltpu.VMEM((TILE, wide), F32),
            pltpu.SemaphoreType.DMA((2 * plan.entries(),)),
        ],
        compiler_params=pltpu.CompilerParams(vmem_limit_bytes=VMEM_LIMIT),
        cost_estimate=pl.CostEstimate(
            flops=4 * rows * model * (model + 2 * wide), bytes_accessed=rows * (8 * wide + 20 * model), transcendentals=2 * rows * wide
        ),
        name="feed_forward",
    )(meta, *own_pieces, *oth_pieces, ctx, ctx_oth, x_own, d_own, vectors, inner_bias)


def weight_grads_kernel(plan, pieces_n, *refs):
    meta, hid_ref, gp_ref, gf_ref, low_ref, ctx_own, ctx_oth, ga_ref = refs[:8]
    own_pieces = refs[8 : 8 + pieces_n]
    oth_pieces = refs[8 + pieces_n : 8 + 2 * pieces_n]
    g_ref, sems = refs[8 + 2 * pieces_n :]
    here = placed(meta)
    c = here["c"]
    step = pl.program_id(0)
    w = Packed(g_ref)

    @pl.when(step == 0)
    def _():
        own, oth = ctx_own[...], ctx_oth[...]
        context = (jnp.where(c == 0, own, oth), jnp.where(c == 0, oth, own))
        for hc, part in enumerate(cut(ga_ref[...])):
            for h in range(2):
                w.write(w.at_proj(h, hc), tn(context[h], part))

    inner = tn(low_ref[...], gp_ref[...])
    down = cut(tn(hid_ref[...], gf_ref[...]))
    for number in range(2 * w.groups):

        @pl.when(step == number)
        def _():
            h, g = divmod(number, w.groups)
            w.write(w.at_inner(h, g), inner)
            for hc in range(2):
                w.write(w.at_down(h, g, hc), down[hc])

    @pl.when(step == 2 * w.groups - 1)
    def _():
        copies = []
        for rel, pieces in ((0, own_pieces), (1, oth_pieces)):
            for p, m, chip, first, end in plan.walk(here):
                copies.append(
                    pltpu.make_async_copy(
                        g_ref.at[lax.rem(c + rel, 2), chip, first:end, :], pieces[p].at[m], sems.at[len(copies)]
                    )
                )
        for copy in copies:
            copy.start()
        for copy in copies:
            copy.wait()


def piece_shapes(plan, width):
    made = []
    for (first, end, _), count in zip(plan.parts, plan.counts()):
        made += [shape((CHIPS // count, end - first, width), BF)] * count
    return made


def weight_grads(plan, meta, hid, gp, gf, low, ctx, ctx_oth, ga):
    rows, model = gf.shape
    wide, half = hid.shape[1], model // 2
    packed = (2, CHIPS, model // CHIPS * (1 + wide // 2 // half) + wide // CHIPS, half)
    pieces = piece_shapes(plan, half)
    cols = pl.BlockSpec((rows, half), lambda i: (0, i))
    found = pl.pallas_call(
        lambda *refs: weight_grads_kernel(plan, len(pieces), *refs),
        grid=(wide // half,),
        in_specs=[smem(), cols, cols, whole((rows, model)), whole((rows, model))]
        + [pl.BlockSpec((None, rows, half), lambda i: (0, 0, 0)), whole((rows, half)), whole((rows, model))],
        out_specs=[anywhere()] * (2 * len(pieces)),
        out_shape=pieces * 2,
        scratch_shapes=[pltpu.VMEM(packed, BF), pltpu.SemaphoreType.DMA((2 * plan.entries(),))],
        compiler_params=pltpu.CompilerParams(vmem_limit_bytes=VMEM_LIMIT),
        cost_estimate=pl.CostEstimate(
            flops=2 * rows * model * (model + 2 * wide), bytes_accessed=rows * (4 * wide + 8 * model), transcendentals=0
        ),
        name="weight_grads",
    )(meta, hid, gp, gf, low, ctx, ctx_oth, ga)
    return found[: len(pieces)], found[len(pieces) :]


def qkv_grads_kernel(plan, pieces_n, *refs):
    meta, x_ref, dq_ref, dk_ref, dv_ref = refs[:5]
    pieces = refs[5 : 5 + pieces_n]
    sums_ref, g_ref, sems = refs[5 + pieces_n :]
    here = placed(meta)
    depth, width = g_ref.shape[1] // 3, g_ref.shape[2]
    x = x_ref[...]
    for w, source in enumerate((dq_ref, dk_ref, dv_ref)):
        grad = source[...]
        g_ref[:, depth * w : depth * w + depth, :] = tn(x, grad).reshape(CHIPS, depth, width).astype(BF)
        sums_ref[w : w + 1, :] = jnp.sum(grad.astype(F32), axis=0, keepdims=True)
    copies = []
    for i, (p, m, chip, first, end) in enumerate(plan.walk(here)):
        copies.append(pltpu.make_async_copy(g_ref.at[chip, first:end, :], pieces[p].at[m], sems.at[i]))
    for copy in copies:
        copy.start()
    for copy in copies:
        copy.wait()


def qkv_grads(plan, meta, x_full, dq, dk, dv):
    rows, model = x_full.shape
    width, depth = dq.shape[1], model // CHIPS
    pieces = piece_shapes(plan, width)
    found = pl.pallas_call(
        lambda *refs: qkv_grads_kernel(plan, len(pieces), *refs),
        grid=(1,),
        in_specs=[smem(), whole((rows, model))] + [whole((rows, width))] * 3,
        out_specs=[anywhere()] * len(pieces) + [whole((8, width))],
        out_shape=pieces + [shape((8, width), F32)],
        scratch_shapes=[pltpu.VMEM((CHIPS, 3 * depth, width), BF), pltpu.SemaphoreType.DMA((plan.entries(),))],
        compiler_params=pltpu.CompilerParams(vmem_limit_bytes=VMEM_LIMIT),
        cost_estimate=pl.CostEstimate(
            flops=6 * rows * model * width, bytes_accessed=2 * rows * (model + 3 * width), transcendentals=0
        ),
        name="qkv_grads",
    )(meta, x_full, dq, dk, dv)
    return found[:-1], found[-1]


def input_grads_kernel(meta, dq_ref, dk_ref, dv_ref, w_ref, out_ref):
    depth, width = w_ref.shape[1] // 3, w_ref.shape[2]
    total = None
    for w, source in enumerate((dq_ref, dk_ref, dv_ref)):
        weight = w_ref[:, depth * w : depth * w + depth, :].reshape(CHIPS * depth, width)
        more = nt(source[...], weight)
        total = more if total is None else total + more
    out_ref[...] = total.astype(BF)


def input_grads(meta, dq, dk, dv, weights):
    rows, width = dq.shape
    chips, deep, _ = weights.shape
    model = chips * deep // 3
    quarter = rows // 4
    part = pl.BlockSpec((quarter, width), lambda i, meta: (i, 0))
    return pl.pallas_call(
        input_grads_kernel,
        grid_spec=pltpu.PrefetchScalarGridSpec(
            num_scalar_prefetch=1,
            grid=(4,),
            in_specs=[part, part, part, whole(weights.shape)],
            out_specs=pl.BlockSpec(
                (None, quarter, model), lambda i, meta: (lax.rem(meta[0] + i, 2), i // 2, 0)
            ),
        ),
        out_shape=shape((2, 2 * quarter, model), BF),
        compiler_params=pltpu.CompilerParams(vmem_limit_bytes=VMEM_LIMIT),
        cost_estimate=pl.CostEstimate(
            flops=6 * rows * model * width, bytes_accessed=2 * rows * (model + 3 * width), transcendentals=0
        ),
        name="input_grads",
    )(meta, dq, dk, dv, weights)


def pack_vectors(vectors, inner_bias):
    row = jnp.concatenate(list(vectors) + [inner_bias])
    return jnp.pad(row, (0, -row.shape[0] % 128))


def body(
    tokens,
    qkv_weight,
    query_bias,
    value_bias,
    proj_weight,
    proj_bias,
    attn_gain,
    attn_shift,
    inner_weight,
    inner_bias,
    down_weight,
    down_bias,
    ffn_gain,
    ffn_shift,
    seg_ids,
    rand_blocks,
    glob_blocks,
    d_out,
):
    dp, seq = lax.axis_index("dp"), lax.axis_index("seq")
    members = lax.axis_size("dp") * lax.axis_size("seq")
    near = lax.axis_size("dp") == 8
    y, c = seq // 2, seq % 2
    even = c == 0
    meta = jnp.stack([c, dp % 2, y, dp // 2]).astype(jnp.int32)
    model = tokens.shape[3]
    half = model // 2
    ffw = inner_weight.shape[1]
    share = qkv_weight.shape[0]
    share_f = down_weight.shape[0]
    groups = ffw // 2 // half
    depth, deep = model // CHIPS, ffw // CHIPS
    low = depth * (1 + groups)

    vectors = (query_bias, value_bias, proj_bias, attn_gain, attn_shift, down_bias, ffn_gain, ffn_shift)
    row = pack_vectors(vectors, inner_bias)
    if near:
        plan_a = Plan([(0, 64, "zxy"), (64, 3 * depth, "yzx")])
        plan_b = Plan([(0, 208, "zxy"), (208, low + deep, "yzx")])

        def sections(h):
            col = lambda w, first: w[:, first : first + half]
            found = [col(qkv_weight, model * w + half * h) for w in range(3)] + [col(proj_weight, half * h)]
            found += [col(inner_weight, ffw // 2 * h + half * g) for g in range(groups)]
            found += [col(down_weight, half * h)]
            return jnp.concatenate(found, axis=0)

        zero, one = sections(0), sections(1)
        mine, theirs = jnp.where(even, zero, one), jnp.where(even, one, zero)
        came = swap(theirs, "core")
        first, second = jnp.where(even, mine, came), jnp.where(even, came, mine)
        laid, at = [], 0
        for length in [share] * (4 + groups) + [share_f]:
            laid += [first[at : at + length], second[at : at + length]]
            at += length
        chunk_a = jnp.concatenate(laid[:6], axis=0)
        chunk_b = jnp.concatenate(laid[6:], axis=0)
        came = swap(row, "core")
        rows = jnp.where(even, jnp.stack([row, came]), jnp.stack([came, row]))
        for dim in "yxz":
            rows = jnp.concatenate([rows] + others(rows, dim), axis=0)
        entry = jnp.arange(CHIPS)
        y_rel, x_rel, z_rel = entry % 2, entry // 2 % 2, entry // 4
        source = (meta[3] - z_rel) % 4 * 4 + (meta[1] ^ x_rel) * 2 + (meta[2] ^ y_rel)
        order = (source[None, :] == jnp.arange(CHIPS)[:, None]).astype(BF)
        rows = nn(order, rows.reshape(CHIPS, -1)).reshape(members, -1)
        pieces_a = []
        for start, end, way in plan_a.parts:
            pieces_a += gather(chunk_a[start:end], way)
    else:
        plan_a = Plan([(0, 3 * depth, None)])
        plan_b = Plan([(0, low + deep, None)])
        everyone = lambda w: lax.all_gather(w, ("dp", "seq"), axis=0, tiled=True)
        full_qkv, full_proj, full_inner, full_down = map(everyone, (qkv_weight, proj_weight, inner_weight, down_weight))
        rows = everyone(row[None]).astype(F32)

        def packed(h):
            col = lambda w, first: lax.dynamic_slice_in_dim(w, first, half, 1).reshape(CHIPS, -1, half)
            a = jnp.concatenate([col(full_qkv, model * w + half * h) for w in range(3)], axis=1)
            b = [col(full_proj, half * h)] + [col(full_inner, ffw // 2 * h + half * g) for g in range(groups)]
            return a, jnp.concatenate(b + [col(full_down, half * h)], axis=1)

        chunk_a, own_b = packed(c)
        pieces_a, own_b, oth_b = [chunk_a], [own_b], [packed(1 - c)[1]]
    spread = rows[:, : 8 * share].reshape(members, 8, share).transpose(1, 0, 2).reshape(8, model)
    hidden_bias = rows[:, 8 * share : 8 * share + share_f * 1].reshape(1, ffw)
    pick = lambda v: lax.dynamic_slice_in_dim(v, c * half, half, 0)
    bias = jnp.concatenate([pick(spread[0]), jnp.zeros((half,), F32), pick(spread[1])])[None]

    low_y = y == 0
    pair = lambda kept, came: jnp.where(low_y, jnp.stack([kept, came]), jnp.stack([came, kept]))

    def to_chip(value):
        kept = jnp.where(low_y, value[0], value[1])
        return pair(kept, swap(jnp.where(low_y, value[1], value[0]), "y"))

    def from_chip(value):
        kept = jnp.where(low_y, value[0], value[1])
        return pair(kept, swap(jnp.where(low_y, value[1], value[0]), "y"))

    x_own = to_chip(tokens[:, 0])
    x_oth = swap(x_own, "core")
    x_full = jnp.where(even, jnp.stack([x_own, x_oth], 1), jnp.stack([x_oth, x_own], 1)).reshape(-1, model)
    x_own = x_own.reshape(-1, model)
    segment = jnp.where(low_y, seg_ids[0, 0], seg_ids[1, 0])
    globs = jnp.where(low_y, glob_blocks[0, 0], glob_blocks[1, 0])
    tables = rand_blocks[:, 0]
    turn = lambda v, to: lax.ppermute(v, "seq", to)
    spot = lambda a, b: 2 * a + b
    one = turn(jnp.where(even, tables[0], tables[1]), [(spot(a, b), spot(b, a)) for a in range(2) for b in range(2)])
    two = turn(jnp.where(even, tables[1], tables[0]), [(spot(a, b), spot(1 - b, a)) for a in range(2) for b in range(2)])
    table = jnp.where(low_y, jnp.concatenate([one, two]), jnp.concatenate([two, one]))
    lo, n = key_ranges(segment)

    qkv, w_qkv = project_qkv(plan_a, meta, pieces_a, x_full, bias)
    d_own = to_chip(d_out[:, 0]).reshape(-1, model)
    if near:
        own_b = []
        for start, end, way in plan_b.parts:
            own_b += gather(chunk_b[start:end], way)
        oth_b = [swap(piece, "core") for piece in own_b]
    ctx, lse = attend(meta, qkv, segment[None], table, globs, lo, n)
    ctx_oth = swap(ctx[1], "core")
    found = feed_forward(plan_b, meta, own_b, oth_b, ctx, ctx_oth, x_own, d_own, spread[2:], hidden_bias)
    out, hid, gf, x1_low, gp, gr1, ga, gc_own, gc_oth, vg, bg = found
    layer_out = from_chip(out.reshape(2, -1, model))[:, None]

    gc_came = swap(gc_oth, "core")
    grads_own, grads_oth = weight_grads(plan_b, meta, hid, gp, gf, x1_low, ctx, ctx_oth, ga)
    dq, dk, dv = attend_back(meta, qkv, gc_own, gc_came, ctx, lse, segment[None], table, globs, lo, n)
    grads_qkv, sums = qkv_grads(plan_a, meta, x_full, dq, dk, dv)
    back = input_grads(meta, dq, dk, dv, w_qkv)
    grad_own = gr1 + (back[0].astype(F32) + swap(back[1], "core").astype(F32))
    grad_input = from_chip(grad_own.astype(BF).reshape(2, -1, model))[:, None]

    nil = jnp.zeros((half,), F32)
    across = lambda v: jnp.where(even, jnp.concatenate([v, nil]), jnp.concatenate([nil, v]))
    small = jnp.concatenate([across(sums[0])[None], across(sums[2])[None], vg[:6]], axis=0)
    small = small.reshape(8, members, share).transpose(1, 0, 2).reshape(members, 8 * share)
    small = jnp.concatenate([small, bg[0].reshape(members, share_f)], axis=1)
    if near:
        small = small + swap(small, "core")
        for dim in "yxz":
            total = small
            for came in others(small, dim):
                total = total + came
            small = total
        small = lax.dynamic_slice_in_dim(small, dp * 4 + seq, 1, 0)[0]

        def chip_sum(pieces, plan):
            sums, at = [], 0
            for (_, _, way), count in zip(plan.parts, plan.counts()):
                turned = [p.reshape((-1,) + p.shape[1:]) for p in pieces[at : at + count]]
                sums.append(scatter_sum(turned, way[::-1]))
                at += count
            return jnp.concatenate(sums, axis=0)

        both = [a + swap(b, "core") for a, b in zip(grads_own, grads_oth)]
        total = jnp.concatenate([chip_sum(grads_qkv, plan_a), chip_sum(both, plan_b)], axis=0)
        mine, theirs, at = [], [], 0
        for length in [share] * (4 + groups) + [share_f]:
            first, second = total[at : at + length], total[at + length : at + 2 * length]
            mine.append(jnp.where(even, first, second))
            theirs.append(jnp.where(even, second, first))
            at += 2 * length
        mine = jnp.concatenate(mine, axis=0)
        came = swap(jnp.concatenate(theirs, axis=0).astype(BF), "core").astype(F32)
        halves = jnp.where(even, jnp.stack([mine, came]), jnp.stack([came, mine]))
        cuts, at = [], 0
        for length in [share] * (4 + groups) + [share_f]:
            cuts.append(halves[:, at : at + length])
            at += length
        side = lambda v: [v[0], v[1]]
        grad_qkv = jnp.concatenate([v for w in range(3) for v in side(cuts[w])], axis=1)
        grad_proj = jnp.concatenate(side(cuts[3]), axis=1)
        grad_inner = jnp.concatenate([cuts[4 + g][h] for h in range(2) for g in range(groups)], axis=1)
        grad_down = jnp.concatenate(side(cuts[4 + groups]), axis=1)
    else:
        scatter = lambda v: lax.psum_scatter(v.astype(F32), ("dp", "seq"), scatter_dimension=0, tiled=True)
        small = scatter(small)[0]
        full = jnp.where(even, jnp.stack([grads_own[0], grads_oth[0]]), jnp.stack([grads_oth[0], grads_own[0]]))
        part = lambda h, a, b: full[h, :, a:b].reshape(-1, half)
        zero = jnp.zeros((model, half), BF)
        third = lambda w: grads_qkv[0][:, depth * w : depth * w + depth].reshape(-1, half)
        place = lambda v: jnp.where(even, jnp.concatenate([v, zero], axis=1), jnp.concatenate([zero, v], axis=1))
        grad_qkv = scatter(jnp.concatenate([place(third(w)) for w in range(3)], axis=1))
        grad_proj = scatter(jnp.concatenate([part(h, 0, depth) for h in range(2)], axis=1))
        grad_inner = scatter(
            jnp.concatenate(
                [part(h, depth * (1 + g), depth * (2 + g)) for h in range(2) for g in range(groups)], axis=1
            )
        )
        grad_down = scatter(jnp.concatenate([part(h, low, low + deep) for h in range(2)], axis=1))
    vector = [small[share * i : share * i + share] for i in range(8)]
    return (
        layer_out,
        grad_input,
        grad_qkv,
        vector[0],
        vector[1],
        grad_proj,
        vector[2],
        vector[3],
        vector[4],
        grad_inner,
        small[8 * share : 8 * share + share_f],
        grad_down,
        vector[5],
        vector[6],
        vector[7],
    )


def solution(mesh):
    row, vec = P(("dp", "seq"), None), P(("dp", "seq"))
    wide = P(None, "dp", "seq", None)
    return jax.shard_map(
        body,
        mesh=mesh,
        in_specs=(wide, row, vec, vec, row, vec, vec, vec, row, vec, row, vec, vec, vec)
        + (P(None, "dp", None), P(None, "dp", "seq", None, None), P(None, "dp", None), wide),
        out_specs=(wide, wide, row, vec, vec, row, vec, vec, vec, row, vec, row, vec, vec, vec),
        check_vma=False,
    )
```

time: 2080 us -> 565 us (0.27)
  matrix products: 690 us -> 0.13 us
  local copies, waits for them, and re-layouts: 530 us -> 38.5 us
  other arithmetic: 333 us -> 24.8 us
  Pallas kernels: 0 us -> 216 us
  waiting for transfers between devices: 351 us -> 189 us
  blocking collectives: 82.6 us -> 0 us
  starting transfers between devices: 36.3 us -> 87.1 us
    dot_general x136 -> x1, matrix products: 684 us -> 0.13 us  [nn(): lax.dot_general(left, right, (((1,), (0,)), ((), ())), preferred_element_...]
    reduce_scatter x3 -> x0, waiting for transfers between devices: 283 us -> none  [body(): lax.psum_scatter(tuple(running), ('dp', 'seq'), scatter_dimension=0, tile...]
    pallas_call x0 -> x7, Pallas kernels: none -> 216 us  [the longest x1 73.2 us: attend_back(): pl.pallas_call(attend_back_kernel, grid=(1,), in_specs=[smem()] * 4 + [th...]
    convert_element_type x21 -> x9, other arithmetic: 195 us -> 2.22 us  [the longest x8 1.74 us: scatter_sum(): total = total.astype(BF).reshape((ways, -1) + total.shape[1:])]
    ppermute x0 -> x72, waiting for transfers between devices: none -> 189 us  [the longest x40 134 us: shift(): return lax.ppermute(value, 'dp', pairs)]
    convert_element_type x16 -> x0, local copies, waits for them, and re-layouts: 95.6 us -> none  [the longest x4 55.1 us: attend_back(): return stacked.reshape(length, 3 * head_count * HD).astype(jnp.bfloat16)]
    ppermute x0 -> x72, starting transfers between devices: none -> 87.1 us  [the longest x40 65.8 us: shift(): return lax.ppermute(value, 'dp', pairs)]
    unnamed x2 -> x0, blocking collectives: 82.6 us -> none
  transfers between devices with their start and end apart: 16 -> 72, of which waited for: 8 -> 34; matrix products, arithmetic and copies ran while one was open for 72% -> 9% of each run, Pallas kernels for 0% -> 29%
where the time goes in v1:
time: 565 us; the launch traced here: 558 us
  Pallas kernels  216 us (38%)
  waiting for transfers between devices  189 us (33%)
  starting transfers between devices  87.1 us (15%)
  local copies, waits for them, and re-layouts  38.5 us (7%)
  other arithmetic  24.8 us (4%)
    ppermute x40, waiting for transfers between devices, shift(): return lax.ppermute(value, 'dp', pairs)  134 us
    pallas_call x1, Pallas kernels, attend_back(): pl.pallas_call(attend_back_kernel, grid=(1,), in_specs=[smem()] * 4 + [th...  73.2 us
    ppermute x40, starting transfers between devices, shift(): return lax.ppermute(value, 'dp', pairs)  65.8 us
    ppermute x30, waiting for transfers between devices, swap(): return lax.ppermute(value, 'seq', [(s, s ^ bit) for s in range(4)])  55.9 us
    pallas_call x1, Pallas kernels, feed_forward(): pl.pallas_call(lambda *refs: ffn_kernel(plan, len(own_pieces), *refs), gr...  54.7 us
    pallas_call x1, Pallas kernels, attend(): pl.pallas_call(attend_kernel, grid=(1,), in_specs=[smem()] * 4 + [third(0...  34.7 us
    pallas_call x1, Pallas kernels, weight_grads(): pl.pallas_call(lambda *refs: weight_grads_kernel(plan, len(pieces), *refs...  24.3 us
    unnamed x91, local copies, waits for them, and re-layouts  18.3 us
  transfers between devices with their start and end apart: 72, of which 34 were waited for; matrix products, arithmetic and copies ran while one was open for 9% of the time, Pallas kernels for 29%

profile of v1, /device:TPU:0, one launch (start us, length us, event | category | flops | bytes accessed | tf_op | source)
XLA Modules:
  0.0 558.3 jit_solution(9444597012431402639)
XLA Ops:
  0.7 6.2 %concatenate.177 = bf16[288]{0:T(512)(128)(2,1)S(1)} concatenate(bf16[24]{0:T(256)(128)(2,1)} %param.20, bf16[24]{0:T(256)(128)(2,1)} %param.21, bf16[24]{0:T(256)(128)(2,1)} %param.23, bf16[24]{0:T(256)(128)(2,1)} %param.24, bf16[24]{0:T(256)(128)(2,1)} %param.25, bf16[24]{0:T(256)(128)(2,1)} %param.29, bf16[24]{0:T(256)(128)(2,1)} %param.30, bf16[24]{0:T(256)(128)(2,1)} %param.31, ...), dimensions={0} | concatenate | bytes 1152 | tf_op jit(solution)/shard_map/concatenate | solution.py:747
  8.8 3.8 collective-permute-start.34
  28.0 2.4 select_bitcast_fusion.3
  32.2 12.8 %collective-permute-done.28 = bf16[2,384]{1,0:T(2,128)(2,1)S(1)} collective-permute-done((bf16[2,384]{1,0:T(2,128)(2,1)S(1)}, bf16[2,384]{1,0:T(2,128)(2,1)S(1)}, u32[]{:S(2)}, u32[]{:S(2)}) %collective-permute-start.28) | collective-permute-done | bytes 1568 | tf_op jit(solution)/shard_map/ppermute | solution.py:48
  45.1 2.1 collective-permute-start.29
  48.8 4.2 collective-permute-start.32
  54.6 2.9 collective-permute-done.31
  66.5 6.0 %collective-permute-done.15 = bf16[1,64,384]{2,1,0:T(8,128)(2,1)S(1)} collective-permute-done((bf16[1,64,384]{2,1,0:T(8,128)(2,1)S(1)}, bf16[1,64,384]{2,1,0:T(8,128)(2,1)S(1)}, u32[]{:S(2)}, u32[]{:S(2)}) %collective-permute-start.15) | collective-permute-done | bytes 49184 | tf_op jit(solution)/shard_map/ppermute | solution.py:60
  72.5 4.9 collective-permute-start.16
  77.5 2.1 collective-permute-done.16
  80.0 3.6 collective-permute-done.17
  87.0 2.0 collective-permute-done.6
  89.1 3.3 collective-permute-start.8
  93.5 3.8 collective-permute-start.9
  98.1 9.4 %collective-permute-done.7 = bf16[2,224,384]{2,1,0:T(8,128)(2,1)S(1)} collective-permute-done((bf16[2,224,384]{2,1,0:T(8,128)(2,1)S(1)}, bf16[2,224,384]{2,1,0:T(8,128)(2,1)S(1)}, u32[]{:S(2)}, u32[]{:S(2)}) %collective-permute-start.7) | collective-permute-done | bytes 344096 | tf_op jit(solution)/shard_map/ppermute | solution.py:60
  108.6 2.7 collective-permute-done.8
  112.1 3.1 collective-permute-done.9
  118.8 5.9 %collective-permute-start.21 = (bf16[2,80,384]{2,1,0:T(8,128)(2,1)S(1)}, bf16[2,80,384]{2,1,0:T(8,128)(2,1)S(1)}, u32[]{:S(2)}, u32[]{:S(2)}) collective-permute-start(bf16[2,80,384]{2,1,0:T(8,128)(2,1)S(1)} %pad_maximum_fusion.7), channel_id=1, source_target_pairs={{0,8},{4,12},{8,16},{12,20},{16,24},{20,28},{24,0},{28,4},{1,9},{5... | collective-permute-start | bytes 368648 | tf_op jit(solution)/shard_map/ppermute | solution.py:60
  124.7 2.0 collective-permute-start.22
  127.6 4.1 collective-permute-start.23
  132.3 4.1 collective-permute-done.23
  137.1 16.4 %collective-permute-done.18 = bf16[4,64,384]{2,1,0:T(8,128)(2,1)S(1)} collective-permute-done((bf16[4,64,384]{2,1,0:T(8,128)(2,1)S(1)}, bf16[4,64,384]{2,1,0:T(8,128)(2,1)S(1)}, u32[]{:S(2)}, u32[]{:S(2)}) %collective-permute-start.18) | collective-permute-done | bytes 196640 | tf_op jit(solution)/shard_map/ppermute | solution.py:60
  156.7 1.9 maximum_select_fusion
  158.7 6.9 %collective-permute-done.19.refs_2_ = bf16[8,64,384]{2,1,0:T(8,128)(2,1)S(1)} collective-permute-done((bf16[8,64,384]{2,1,0:T(8,128)(2,1)S(1)}, bf16[8,64,384]{2,1,0:T(8,128)(2,1)S(1)}, u32[]{:S(2)}, u32[]{:S(2)}) %collective-permute-start.19) | collective-permute-done | bytes 393248 | tf_op jit(solution)/shard_map/ppermute | solution.py:48
  167.4 9.7 %project_qkv.1 = (bf16[2048,1152]{1,0:T(8,128)(2,1)}, bf16[16,144,384]{2,1,0:T(8,128)(2,1)}) custom-call(s32[4]{0:T(128)} %pad_add_fusion.2.refs_0_.meta, bf16[8,64,384]{2,1,0:T(8,128)(2,1)} %copy-done.15, bf16[8,64,384]{2,1,0:T(8,128)(2,1)} %copy-done.25, bf16[8,80,384]{2,1,0:T(8,128)(2,1)} %copy-done.14, bf16[8,80,384]{2,1,0:T(8,128)(2,1)} %copy-done.23, ...), custom_call_target="tpu_custom_call" | custom-call | flops 3623878656 | bytes 7864320 | tf_op jit(solution)/shard_map/project_qkv/pallas_call | solution.py:165
  177.1 34.7 %attend.1 = (bf16[2,1024,384]{2,1,0:T(8,128)(2,1)}, f32[6,2048]{1,0:T(8,128)}) custom-call(s32[4]{0:T(128)} %pad_add_fusion.2.refs_0_.meta, s32[8]{0:T(128)} %get-tuple-element.91.lo_ref, s32[8]{0:T(128)} %get-tuple-element.92.n_ref, s32[2]{0:T(128)} %fusion.18.glob_ref, bf16[2048,1152]{1,0:T(8,128)(2,1)} %get-tuple-element.46.q_ref.k_ref.v_ref, ...), custom_call_target="tpu_custom_call" | custom-call | flops 12884901888 | bytes 7864320 | tf_op jit(solution)/shard_map/attend/pallas_call | solution.py:284
  216.1 54.7 %feed_forward.1 = (bf16[1024,768]{1,0:T(8,128)(2,1)}, bf16[1024,3072]{1,0:T(8,128)(2,1)}, bf16[1024,768]{1,0:T(8,128)(2,1)}, bf16[1024,768]{1,0:T(8,128)(2,1)}, ...) custom-call(s32[4]{0:T(128)} %pad_add_fusion.2.refs_0_.meta, ...), custom_call_target="tpu_custom_call" | custom-call | flops 21743271936 | bytes 40894464 | tf_op jit(solution)/shard_map/feed_forward/pallas_call | solution.py:561
  273.2 2.3 select_bitcast_fusion.1
  277.0 73.2 %attend_back.1 = (bf16[2048,384]{1,0:T(8,128)(2,1)}, bf16[2048,384]{1,0:T(8,128)(2,1)}, bf16[2048,384]{1,0:T(8,128)(2,1)}) custom-call(s32[4]{0:T(128)} %pad_add_fusion.2.refs_0_.meta, s32[8]{0:T(128)} %get-tuple-element.91.lo_ref, s32[8]{0:T(128)} %get-tuple-element.92.n_ref, s32[2]{0:T(128)} %fusion.18.glob_ref, ...), custom_call_target="tpu_custom_call" | custom-call | flops 32212254720 | bytes 15728640 | tf_op jit(solution)/shard_map/attend_back/pallas_call | solution.py:381
  350.2 10.4 %qkv_grads.1 = (bf16[8,64,384]{2,1,0:T(8,128)(2,1)}, bf16[8,64,384]{2,1,0:T(8,128)(2,1)}, bf16[8,80,384]{2,1,0:T(8,128)(2,1)}, bf16[8,80,384]{2,1,0:T(8,128)(2,1)}, f32[8,384]{1,0:T(8,128)}) custom-call(s32[4]{0:T(128)} %pad_add_fusion.2.refs_0_.meta, bf16[2048,768]{1,0:T(8,128)(2,1)} %bitcast.213, bf16[2048,384]{1,0:T(8,128)(2,1)} %get-tuple-element.53.dq_ref.refs_2_, ...), custom_call_target="tpu_custom_call" | custom-call | flops 3623878656 | bytes 7864320 | tf_op jit(solution)/shard_map/qkv_grads/pallas_call | solution.py:695
  362.0 24.3 %weight_grads.1 = (bf16[8,208,384]{2,1,0:T(8,128)(2,1)}, bf16[8,208,384]{2,1,0:T(8,128)(2,1)}, bf16[8,224,384]{2,1,0:T(8,128)(2,1)}, bf16[8,224,384]{2,1,0:T(8,1...) custom-call(s32[4]{0:T(128)} %pad_add_fusion.2.refs_0_.meta, ...), custom_call_target="tpu_custom_call" | custom-call | flops 10871635968 | bytes 18874368 | tf_op jit(solution)/shard_map/weight_grads/pallas_call | solution.py:654
  388.4 9.3 %input_grads.1 = bf16[2,1024,768]{2,1,0:T(8,128)(2,1)} custom-call(s32[4]{0:T(128)} %pad_add_fusion.2.refs_0_.meta, bf16[2048,384]{1,0:T(8,128)(2,1)} %get-tuple-element.53.dq_ref.refs_2_, bf16[2048,384]{1,0:T(8,128)(2,1)} %get-tuple-element.54.dk_ref.refs_3_, bf16[2048,384]{1,0:T(8,128)(2,1)} %get-tuple-element.55.dv_ref.refs_4_, ...), custom_call_target="tpu_custom_call" | custom-call | flops 3623878656 | bytes 7864320 | tf_op jit(solution)/shard_map/input_grads/pallas_call | solution.py:727
  399.3 2.5 collective-permute-done.68
  404.2 2.9 maximum_select_fusion.4
  409.1 2.0 collective-permute-start.46
  412.3 6.5 %collective-permute-done.41 = bf16[8,64,384]{2,1,0:T(8,128)(2,1)S(1)} collective-permute-done((bf16[8,64,384]{2,1,0:T(8,128)(2,1)S(1)}, bf16[8,64,384]{2,1,0:T(8,128)(2,1)S(1)}, u32[]{:S(2)}, u32[]{:S(2)}) %collective-permute-start.41) | collective-permute-done | bytes 393248 | tf_op jit(solution)/shard_map/ppermute | solution.py:48
  418.9 3.7 collective-permute-done.46
  424.6 2.2 collective-permute-start.47
  430.6 4.3 collective-permute-start.43
  435.7 3.2 collective-permute-done.48
  445.0 25.8 %collective-permute-done.50 = bf16[1,80,384]{2,1,0:T(8,128)(2,1)S(1)} collective-permute-done((bf16[1,80,384]{2,1,0:T(8,128)(2,1)S(1)}, bf16[1,80,384]{2,1,0:T(8,128)(2,1)S(1)}, u32[]{:S(2)}, u32[]{:S(2)}) %collective-permute-start.50) | collective-permute-done | bytes 61472 | tf_op jit(solution)/shard_map/ppermute | solution.py:48
  473.4 27.4 %collective-permute-done.60 = bf16[8,224,384]{2,1,0:T(8,128)(2,1)S(1)} collective-permute-done((bf16[8,224,384]{2,1,0:T(8,128)(2,1)S(1)}, bf16[8,224,384]{2,1,0:T(8,128)(2,1)S(1)}, u32[]{:S(2)}, u32[]{:S(2)}) %collective-permute-start.60) | collective-permute-done | bytes 1376288 | tf_op jit(solution)/shard_map/ppermute | solution.py:60
  501.4 4.3 collective-permute-start.61
  509.7 6.8 %collective-permute-done.61 = bf16[2,224,384]{2,1,0:T(8,128)(2,1)S(1)} collective-permute-done((bf16[2,224,384]{2,1,0:T(8,128)(2,1)S(1)}, bf16[2,224,384]{2,1,0:T(8,128)(2,1)S(1)}, u32[]{:S(2)}, u32[]{:S(2)}) %collective-permute-start.61) | collective-permute-done | bytes 344096 | tf_op jit(solution)/shard_map/ppermute | solution.py:60
  516.5 7.6 %collective-permute-done.63 = bf16[2,224,384]{2,1,0:T(8,128)(2,1)S(1)} collective-permute-done((bf16[2,224,384]{2,1,0:T(8,128)(2,1)S(1)}, bf16[2,224,384]{2,1,0:T(8,128)(2,1)S(1)}, u32[]{:S(2)}, u32[]{:S(2)}) %collective-permute-start.63) | collective-permute-done | bytes 344096 | tf_op jit(solution)/shard_map/ppermute | solution.py:60
  524.1 12.4 %collective-permute-done.62 = bf16[2,224,384]{2,1,0:T(8,128)(2,1)S(1)} collective-permute-done((bf16[2,224,384]{2,1,0:T(8,128)(2,1)S(1)}, bf16[2,224,384]{2,1,0:T(8,128)(2,1)S(1)}, u32[]{:S(2)}, u32[]{:S(2)}) %collective-permute-start.62) | collective-permute-done | bytes 344096 | tf_op jit(solution)/shard_map/ppermute | solution.py:60
  542.2 5.9 %collective-permute-done.55 = bf16[1,208,384]{2,1,0:T(8,128)(2,1)S(1)} collective-permute-done((bf16[1,208,384]{2,1,0:T(8,128)(2,1)S(1)}, bf16[1,208,384]{2,1,0:T(8,128)(2,1)S(1)}, u32[]{:S(2)}, u32[]{:S(2)}) %collective-permute-start.55) | collective-permute-done | bytes 159776 | tf_op jit(solution)/shard_map/ppermute | solution.py:60
  550.0 4.4 collective-permute-done.56
  (331 shorter events, 99.1 us)
Async XLA Ops:
  6.9 24.3 %collective-permute-start.27 = (bf16[384]{0:T(512)(128)(2,1)S(1)}, bf16[384]{0:T(512)(128)(2,1)S(1)}, u32[]{:S(2)}, u32[]{:S(2)}) collective-permute-start(bf16[384]{0:T(512)(128)(2,1)S(1)} %pad.8), channel_id=1, source_target_pairs={{0,1},{1,0},{2,3},{3,2},{4,5},{5,4},{6,7},{7,6},{8,9},{9,8},{10,11... | collective-permute-start | bytes 2312 | tf_op jit(solution)/shard_map/ppermute | solution.py:48
  8.1 39.1 %collective-permute-start.33 = (s32[3,32,3]{1,0,2:T(4,128)S(1)}, s32[3,32,3]{1,0,2:T(4,128)S(1)}, u32[]{:S(2)}, u32[]{:S(2)}) collective-permute-start(s32[3,32,3]{1,0,2:T(4,128)S(1)} %get-tuple-element.159), channel_id=1, source_target_pairs={{0,0},{1,2},{2,1},{3,3},{4,4},{5,6},{6,5},{7,7},{8,8},{9,10},{10,9... | collective-permute-start | bytes 3464 | tf_op jit(solution)/shard_map/ppermute | solution.py:859
  8.8 38.4 %collective-permute-start.34 = (s32[3,32,3]{1,0,2:T(4,128)S(1)}, s32[3,32,3]{1,0,2:T(4,128)S(1)}, u32[]{:S(2)}, u32[]{:S(2)}) collective-permute-start(s32[3,32,3]{1,0,2:T(4,128)S(1)} %get-tuple-element.160), channel_id=1, source_target_pairs={{0,2},{1,0},{2,3},{3,1},{4,6},{5,4},{6,7},{7,5},{8,10},{9,8},{10,1... | collective-permute-start | bytes 3464 | tf_op jit(solution)/shard_map/ppermute | solution.py:859
  23.8 35.9 %collective-permute-start = (bf16[288,384]{1,0:T(8,128)(2,1)}, bf16[288,384]{1,0:T(8,128)(2,1)}, u32[]{:S(2)}, u32[]{:S(2)}) collective-permute-start(bf16[288,384]{1,0:T(8,128)(2,1)} %broadcast_select_fusion.5), channel_id=1, source_target_pairs={{0,1},{1,0},{2,3},{3,2},{4,5},{5,4},{6,7},{7,6},{8,9},{9,8},{10,11... | collective-permute-start | bytes 663560 | tf_op jit(solution)/shard_map/ppermute | solution.py:48
  24.9 67.5 %collective-permute-start.25 = (bf16[512,768]{1,0:T(8,128)(2,1)}, bf16[512,768]{1,0:T(8,128)(2,1)S(1)}, u32[]{:S(2)}, u32[]{:S(2)}) collective-permute-start(bf16[512,768]{1,0:T(8,128)(2,1)} %get-tuple-element.102), channel_id=1, source_target_pairs={{0,2},{1,3},{2,0},{3,1},{4,6},{5,7},{6,4},{7,5},{8,10},{9,11},{10,... | collective-permute-start | bytes 2359304 | tf_op jit(solution)/shard_map/ppermute | solution.py:48
  31.2 13.8 %collective-permute-start.28 = (bf16[2,384]{1,0:T(2,128)(2,1)S(1)}, bf16[2,384]{1,0:T(2,128)(2,1)S(1)}, u32[]{:S(2)}, u32[]{:S(2)}) collective-permute-start(bf16[2,384]{1,0:T(2,128)(2,1)S(1)} %broadcast_select_fusion.9), channel_id=1, source_target_pairs={{0,2},{1,3},{2,0},{3,1},{4,6},{5,7},{6,4},{7,5},{8,10},{9,11},{10,... | collective-permute-start | bytes 4616 | tf_op jit(solution)/shard_map/ppermute | solution.py:48
  61.0 23.0 %collective-permute-start.3 = (bf16[1,208,384]{2,1,0:T(8,128)(2,1)S(1)}, bf16[1,208,384]{2,1,0:T(8,128)(2,1)S(1)}, u32[]{:S(2)}, u32[]{:S(2)}) collective-permute-start(bf16[1,208,384]{2,1,0:T(8,128)(2,1)S(1)} %slice_bitcast_fusion.3), channel_id=1, source_target_pairs={{0,24},{4,28},{8,0},{12,4},{16,8},{20,12},{24,16},{28,20},{1,25},{... | collective-permute-start | bytes 479240 | tf_op jit(solution)/shard_map/ppermute | solution.py:60
  61.6 22.3 %collective-permute-start.2 = (bf16[1,208,384]{2,1,0:T(8,128)(2,1)S(1)}, bf16[1,208,384]{2,1,0:T(8,128)(2,1)S(1)}, u32[]{:S(2)}, u32[]{:S(2)}) collective-permute-start(bf16[1,208,384]{2,1,0:T(8,128)(2,1)S(1)} %slice_bitcast_fusion.3), channel_id=1, source_target_pairs={{0,16},{4,20},{8,24},{12,28},{16,0},{20,4},{24,8},{28,12},{1,17},{... | collective-permute-start | bytes 479240 | tf_op jit(solution)/shard_map/ppermute | solution.py:60
  62.2 21.7 %collective-permute-start.1 = (bf16[1,208,384]{2,1,0:T(8,128)(2,1)S(1)}, bf16[1,208,384]{2,1,0:T(8,128)(2,1)S(1)}, u32[]{:S(2)}, u32[]{:S(2)}) collective-permute-start(bf16[1,208,384]{2,1,0:T(8,128)(2,1)S(1)} %slice_bitcast_fusion.3), channel_id=1, source_target_pairs={{0,8},{4,12},{8,16},{12,20},{16,24},{20,28},{24,0},{28,4},{1,9},{5... | collective-permute-start | bytes 479240 | tf_op jit(solution)/shard_map/ppermute | solution.py:60
  84.1 33.4 %collective-permute-start.4 = (bf16[4,208,384]{2,1,0:T(8,128)(2,1)S(1)}, bf16[4,208,384]{2,1,0:T(8,128)(2,1)S(1)}, u32[]{:S(2)}, u32[]{:S(2)}) collective-permute-start(bf16[4,208,384]{2,1,0:T(8,128)(2,1)S(1)} %pad_maximum_fusion), channel_id=1, source_target_pairs={{0,4},{4,0},{8,12},{12,8},{16,20},{20,16},{24,28},{28,24},{1,5},{5... | collective-permute-start | bytes 1916936 | tf_op jit(solution)/shard_map/ppermute | solution.py:60
  89.1 22.2 %collective-permute-start.8 = (bf16[2,224,384]{2,1,0:T(8,128)(2,1)S(1)}, bf16[2,224,384]{2,1,0:T(8,128)(2,1)S(1)}, u32[]{:S(2)}, u32[]{:S(2)}) collective-permute-start(bf16[2,224,384]{2,1,0:T(8,128)(2,1)S(1)} %pad_maximum_fusion.1), channel_id=1, source_target_pairs={{0,16},{4,20},{8,24},{12,28},{16,0},{20,4},{24,8},{28,12},{1,17},{... | collective-permute-start | bytes 1032200 | tf_op jit(solution)/shard_map/ppermute | solution.py:60
  92.4 15.1 %collective-permute-start.7 = (bf16[2,224,384]{2,1,0:T(8,128)(2,1)S(1)}, bf16[2,224,384]{2,1,0:T(8,128)(2,1)S(1)}, u32[]{:S(2)}, u32[]{:S(2)}) collective-permute-start(bf16[2,224,384]{2,1,0:T(8,128)(2,1)S(1)} %pad_maximum_fusion.1), channel_id=1, source_target_pairs={{0,8},{4,12},{8,16},{12,20},{16,24},{20,28},{24,0},{28,4},{1,9},{5... | collective-permute-start | bytes 1032200 | tf_op jit(solution)/shard_map/ppermute | solution.py:60
  92.7 61.7 %collective-permute-start.26 = (bf16[2,512,768]{2,1,0:T(8,128)(2,1)S(1)}, bf16[2,512,768]{2,1,0:T(8,128)(2,1)S(1)}, u32[]{:S(2)}, u32[]{:S(2)}) collective-permute-start(bf16[2,512,768]{2,1,0:T(8,128)(2,1)S(1)} %maximum_select_fusion.2), channel_id=1, source_target_pairs={{0,1},{1,0},{2,3},{3,2},{4,5},{5,4},{6,7},{7,6},{8,9},{9,8},{10,11... | collective-permute-start | bytes 4718600 | tf_op jit(solution)/shard_map/ppermute | solution.py:48
  93.5 21.6 %collective-permute-start.9 = (bf16[2,224,384]{2,1,0:T(8,128)(2,1)S(1)}, bf16[2,224,384]{2,1,0:T(8,128)(2,1)S(1)}, u32[]{:S(2)}, u32[]{:S(2)}) collective-permute-start(bf16[2,224,384]{2,1,0:T(8,128)(2,1)S(1)} %pad_maximum_fusion.1), channel_id=1, source_target_pairs={{0,24},{4,28},{8,0},{12,4},{16,8},{20,12},{24,16},{28,20},{1,25},{... | collective-permute-start | bytes 1032200 | tf_op jit(solution)/shard_map/ppermute | solution.py:60
  107.5 11.3 %collective-permute-start.20 = (bf16[1,80,384]{2,1,0:T(8,128)(2,1)S(1)}, bf16[1,80,384]{2,1,0:T(8,128)(2,1)S(1)}, u32[]{:S(2)}, u32[]{:S(2)}) collective-permute-start(bf16[1,80,384]{2,1,0:T(8,128)(2,1)S(1)} %get-tuple-element.88), channel_id=1, source_target_pairs={{0,2},{1,3},{2,0},{3,1},{4,6},{5,7},{6,4},{7,5},{8,10},{9,11},{10,... | collective-permute-start | bytes 184328 | tf_op jit(solution)/shard_map/ppermute | solution.py:48
  115.9 51.0 %collective-permute-start.10 = (bf16[8,224,384]{2,1,0:T(8,128)(2,1)}, bf16[8,224,384]{2,1,0:T(8,128)(2,1)}, u32[]{:S(2)}, u32[]{:S(2)}) collective-permute-start(bf16[8,224,384]{2,1,0:T(8,128)(2,1)} %constant_dynamic-update-slice_fusion.32.refs_3_), channel_id=1, source_target_pairs={{0,4},{4,0},{8,12},{12,8},{16,20},{20,16},{24,28},{28,24},{1,5},{5... | collective-permute-start | bytes 4128776 | tf_op jit(solution)/shard_map/ppermute | solution.py:60
  118.3 48.6 %collective-permute-start.5 = (bf16[8,208,384]{2,1,0:T(8,128)(2,1)}, bf16[8,208,384]{2,1,0:T(8,128)(2,1)}, u32[]{:S(2)}, u32[]{:S(2)}) collective-permute-start(bf16[8,208,384]{2,1,0:T(8,128)(2,1)} %constant_dynamic-update-slice_fusion.27.refs_1_), channel_id=1, source_target_pairs={{0,2},{1,3},{2,0},{3,1},{4,6},{5,7},{6,4},{7,5},{8,10},{9,11},{10,... | collective-permute-start | bytes 3833864 | tf_op jit(solution)/shard_map/ppermute | solution.py:48
  127.6 8.9 %collective-permute-start.23 = (bf16[2,80,384]{2,1,0:T(8,128)(2,1)S(1)}, bf16[2,80,384]{2,1,0:T(8,128)(2,1)S(1)}, u32[]{:S(2)}, u32[]{:S(2)}) collective-permute-start(bf16[2,80,384]{2,1,0:T(8,128)(2,1)S(1)} %pad_maximum_fusion.7), channel_id=1, source_target_pairs={{0,24},{4,28},{8,0},{12,4},{16,8},{20,12},{24,16},{28,20},{1,25},{... | collective-permute-start | bytes 368648 | tf_op jit(solution)/shard_map/ppermute | solution.py:60
  131.7 21.7 %collective-permute-start.18 = (bf16[4,64,384]{2,1,0:T(8,128)(2,1)S(1)}, bf16[4,64,384]{2,1,0:T(8,128)(2,1)S(1)}, u32[]{:S(2)}, u32[]{:S(2)}) collective-permute-start(bf16[4,64,384]{2,1,0:T(8,128)(2,1)S(1)} %pad_maximum_fusion.3), channel_id=1, source_target_pairs={{0,4},{4,0},{8,12},{12,8},{16,20},{20,16},{24,28},{28,24},{1,5},{5... | collective-permute-start | bytes 589832 | tf_op jit(solution)/shard_map/ppermute | solution.py:60
  136.5 29.1 %collective-permute-start.24 = (bf16[8,80,384]{2,1,0:T(8,128)(2,1)S(1)}, bf16[8,80,384]{2,1,0:T(8,128)(2,1)S(1)}, u32[]{:S(2)}, u32[]{:S(2)}) collective-permute-start(bf16[8,80,384]{2,1,0:T(8,128)(2,1)S(1)} %constant_dynamic-update-slice_fusion.42.refs_3_), channel_id=1, source_target_pairs={{0,4},{4,0},{8,12},{12,8},{16,20},{20,16},{24,28},{28,24},{1,5},{5... | collective-permute-start | bytes 1474568 | tf_op jit(solution)/shard_map/ppermute | solution.py:60
  153.5 12.1 %collective-permute-start.19 = (bf16[8,64,384]{2,1,0:T(8,128)(2,1)S(1)}, bf16[8,64,384]{2,1,0:T(8,128)(2,1)S(1)}, u32[]{:S(2)}, u32[]{:S(2)}) collective-permute-start(bf16[8,64,384]{2,1,0:T(8,128)(2,1)S(1)} %constant_dynamic-update-slice_fusion.37.refs_1_), channel_id=1, source_target_pairs={{0,2},{1,3},{2,0},{3,1},{4,6},{5,7},{6,4},{7,5},{8,10},{9,11},{10,... | collective-permute-start | bytes 1179656 | tf_op jit(solution)/shard_map/ppermute | solution.py:48
  155.2 57.9 %collective-permute-start.36 = (bf16[512,768]{1,0:T(8,128)(2,1)S(1)}, bf16[512,768]{1,0:T(8,128)(2,1)S(1)}, u32[]{:S(2)}, u32[]{:S(2)}) collective-permute-start(bf16[512,768]{1,0:T(8,128)(2,1)S(1)} %copy-done.10), channel_id=1, source_target_pairs={{0,2},{1,3},{2,0},{3,1},{4,6},{5,7},{6,4},{7,5},{8,10},{9,11},{10,... | collective-permute-start | bytes 2359304 | tf_op jit(solution)/shard_map/ppermute | solution.py:48
  165.6 50.5 %collective-permute-start.13 = (bf16[8,224,384]{2,1,0:T(8,128)(2,1)}, bf16[8,224,384]{2,1,0:T(8,128)(2,1)}, u32[]{:S(2)}, u32[]{:S(2)}) collective-permute-start(bf16[8,224,384]{2,1,0:T(8,128)(2,1)} %constant_dynamic-update-slice_fusion.32.refs_3_), channel_id=1, source_target_pairs={{0,1},{1,0},{2,3},{3,2},{4,5},{5,4},{6,7},{7,6},{8,9},{9,8},{10,11... | collective-permute-start | bytes 4128776 | tf_op jit(solution)/shard_map/ppermute | solution.py:48
  166.4 49.7 %collective-permute-start.11 = (bf16[8,208,384]{2,1,0:T(8,128)(2,1)}, bf16[8,208,384]{2,1,0:T(8,128)(2,1)}, u32[]{:S(2)}, u32[]{:S(2)}) collective-permute-start(bf16[8,208,384]{2,1,0:T(8,128)(2,1)} %constant_dynamic-update-slice_fusion.27.refs_1_), channel_id=1, source_target_pairs={{0,1},{1,0},{2,3},{3,2},{4,5},{5,4},{6,7},{7,6},{8,9},{9,8},{10,11... | collective-permute-start | bytes 3833864 | tf_op jit(solution)/shard_map/ppermute | solution.py:48
  166.9 49.2 %collective-permute-start.14 = (bf16[8,224,384]{2,1,0:T(8,128)(2,1)}, bf16[8,224,384]{2,1,0:T(8,128)(2,1)}, u32[]{:S(2)}, u32[]{:S(2)}) collective-permute-start(bf16[8,224,384]{2,1,0:T(8,128)(2,1)} %collective-permute-done.10.refs_4_), channel_id=1, source_target_pairs={{0,1},{1,0},{2,3},{3,2},{4,5},{5,4},{6,7},{7,6},{8,9},{9,8},{10,11... | collective-permute-start | bytes 4128776 | tf_op jit(solution)/shard_map/ppermute | solution.py:48
  167.0 49.1 %collective-permute-start.12 = (bf16[8,208,384]{2,1,0:T(8,128)(2,1)}, bf16[8,208,384]{2,1,0:T(8,128)(2,1)}, u32[]{:S(2)}, u32[]{:S(2)}) collective-permute-start(bf16[8,208,384]{2,1,0:T(8,128)(2,1)} %collective-permute-done.5.refs_2_), channel_id=1, source_target_pairs={{0,1},{1,0},{2,3},{3,2},{4,5},{5,4},{6,7},{7,6},{8,9},{9,8},{10,11... | collective-permute-start | bytes 3833864 | tf_op jit(solution)/shard_map/ppermute | solution.py:48
  275.6 127.6 %collective-permute-start.37 = (bf16[512,768]{1,0:T(8,128)(2,1)}, bf16[512,768]{1,0:T(8,128)(2,1)}, u32[]{:S(2)}, u32[]{:S(2)}) collective-permute-start(bf16[512,768]{1,0:T(8,128)(2,1)} %get-tuple-element.98), channel_id=1, source_target_pairs={{0,2},{1,3},{2,0},{3,1},{4,6},{5,7},{6,4},{7,5},{8,10},{9,11},{10,... | collective-permute-start | bytes 2359304 | tf_op jit(solution)/shard_map/ppermute | solution.py:48
  362.0 24.9 %collective-permute-start.66 = (f32[32,288]{1,0:T(8,128)S(1)}, f32[32,288]{1,0:T(8,128)S(1)}, u32[]{:S(2)}, u32[]{:S(2)}) collective-permute-start(f32[32,288]{1,0:T(8,128)S(1)} %pad_maximum_fusion.14), channel_id=1, source_target_pairs={{0,1},{1,0},{2,3},{3,2},{4,5},{5,4},{6,7},{7,6},{8,9},{9,8},{10,11... | collective-permute-start | bytes 110600 | tf_op jit(solution)/shard_map/ppermute | solution.py:48
  386.3 120.0 %collective-permute-start.51 = (bf16[8,208,384]{2,1,0:T(8,128)(2,1)}, bf16[8,208,384]{2,1,0:T(8,128)(2,1)S(1)}, u32[]{:S(2)}, u32[]{:S(2)}) collective-permute-start(bf16[8,208,384]{2,1,0:T(8,128)(2,1)} %get-tuple-element.67), channel_id=1, source_target_pairs={{0,1},{1,0},{2,3},{3,2},{4,5},{5,4},{6,7},{7,6},{8,9},{9,8},{10,11... | collective-permute-start | bytes 3833864 | tf_op jit(solution)/shard_map/ppermute | solution.py:48
  386.8 40.3 %collective-permute-start.59 = (bf16[8,224,384]{2,1,0:T(8,128)(2,1)}, bf16[8,224,384]{2,1,0:T(8,128)(2,1)S(1)}, u32[]{:S(2)}, u32[]{:S(2)}) collective-permute-start(bf16[8,224,384]{2,1,0:T(8,128)(2,1)} %get-tuple-element.73), channel_id=1, source_target_pairs={{0,1},{1,0},{2,3},{3,2},{4,5},{5,4},{6,7},{7,6},{8,9},{9,8},{10,11... | collective-permute-start | bytes 4128776 | tf_op jit(solution)/shard_map/ppermute | solution.py:48
  386.9 10.7 %collective-permute-start.67 = (f32[32,288]{1,0:T(8,128)S(1)}, f32[32,288]{1,0:T(8,128)S(1)}, u32[]{:S(2)}, u32[]{:S(2)}) collective-permute-start(f32[32,288]{1,0:T(8,128)S(1)} %fusion.27), channel_id=1, source_target_pairs={{0,2},{1,3},{2,0},{3,1},{4,6},{5,7},{6,4},{7,5},{8,10},{9,11},{10,... | collective-permute-start | bytes 110600 | tf_op jit(solution)/shard_map/ppermute | solution.py:48
  407.2 17.4 %collective-permute-start.52 = (bf16[8,208,384]{2,1,0:T(8,128)(2,1)S(1)}, bf16[8,208,384]{2,1,0:T(8,128)(2,1)S(1)}, u32[]{:S(2)}, u32[]{:S(2)}) collective-permute-start(bf16[8,208,384]{2,1,0:T(8,128)(2,1)S(1)} %copy-done.20), channel_id=1, source_target_pairs={{0,1},{1,0},{2,3},{3,2},{4,5},{5,4},{6,7},{7,6},{8,9},{9,8},{10,11... | collective-permute-start | bytes 3833864 | tf_op jit(solution)/shard_map/ppermute | solution.py:48
  407.5 11.3 %collective-permute-start.41 = (bf16[8,64,384]{2,1,0:T(8,128)(2,1)S(1)}, bf16[8,64,384]{2,1,0:T(8,128)(2,1)S(1)}, u32[]{:S(2)}, u32[]{:S(2)}) collective-permute-start(bf16[8,64,384]{2,1,0:T(8,128)(2,1)S(1)} %copy-done.24), channel_id=1, source_target_pairs={{0,2},{1,3},{2,0},{3,1},{4,6},{5,7},{6,4},{7,5},{8,10},{9,11},{10,... | collective-permute-start | bytes 1179656 | tf_op jit(solution)/shard_map/ppermute | solution.py:48
  409.1 13.5 %collective-permute-start.46 = (bf16[8,80,384]{2,1,0:T(8,128)(2,1)S(1)}, bf16[8,80,384]{2,1,0:T(8,128)(2,1)S(1)}, u32[]{:S(2)}, u32[]{:S(2)}) collective-permute-start(bf16[8,80,384]{2,1,0:T(8,128)(2,1)S(1)} %copy-done.22), channel_id=1, source_target_pairs={{0,4},{4,0},{8,12},{12,8},{16,20},{20,16},{24,28},{28,24},{1,5},{5... | collective-permute-start | bytes 1474568 | tf_op jit(solution)/shard_map/ppermute | solution.py:60
  418.8 54.6 %collective-permute-start.58 = (bf16[8,224,384]{2,1,0:T(8,128)(2,1)S(1)}, bf16[8,224,384]{2,1,0:T(8,128)(2,1)S(1)}, u32[]{:S(2)}, u32[]{:S(2)}) collective-permute-start(bf16[8,224,384]{2,1,0:T(8,128)(2,1)S(1)} %copy-done.19), channel_id=1, source_target_pairs={{0,1},{1,0},{2,3},{3,2},{4,5},{5,4},{6,7},{7,6},{8,9},{9,8},{10,11... | collective-permute-start | bytes 4128776 | tf_op jit(solution)/shard_map/ppermute | solution.py:48
  429.0 9.8 %collective-permute-start.48 = (bf16[2,80,384]{2,1,0:T(8,128)(2,1)S(1)}, bf16[2,80,384]{2,1,0:T(8,128)(2,1)S(1)}, u32[]{:S(2)}, u32[]{:S(2)}) collective-permute-start(bf16[2,80,384]{2,1,0:T(8,128)(2,1)S(1)} %get-tuple-element.131), channel_id=1, source_target_pairs={{0,16},{4,20},{8,24},{12,28},{16,0},{20,4},{24,8},{28,12},{1,17},{... | collective-permute-start | bytes 368648 | tf_op jit(solution)/shard_map/ppermute | solution.py:60
  438.9 32.7 %collective-permute-start.39 = (bf16[1024,768]{1,0:T(8,128)(2,1)S(1)}, bf16[1024,768]{1,0:T(8,128)(2,1)S(1)}, u32[]{:S(2)}, u32[]{:S(2)}) collective-permute-start(bf16[1024,768]{1,0:T(8,128)(2,1)S(1)} %slice_bitcast_fusion), channel_id=1, source_target_pairs={{0,1},{1,0},{2,3},{3,2},{4,5},{5,4},{6,7},{7,6},{8,9},{9,8},{10,11... | collective-permute-start | bytes 4718600 | tf_op jit(solution)/shard_map/ppermute | solution.py:48
  440.8 67.4 %collective-permute-start.53 = (bf16[8,208,384]{2,1,0:T(8,128)(2,1)S(1)}, bf16[8,208,384]{2,1,0:T(8,128)(2,1)S(1)}, u32[]{:S(2)}, u32[]{:S(2)}) collective-permute-start(bf16[8,208,384]{2,1,0:T(8,128)(2,1)S(1)} %add.202), channel_id=1, source_target_pairs={{0,2},{1,3},{2,0},{3,1},{4,6},{5,7},{6,4},{7,5},{8,10},{9,11},{10,... | collective-permute-start | bytes 3833864 | tf_op jit(solution)/shard_map/ppermute | solution.py:48
  443.8 27.0 %collective-permute-start.50 = (bf16[1,80,384]{2,1,0:T(8,128)(2,1)S(1)}, bf16[1,80,384]{2,1,0:T(8,128)(2,1)S(1)}, u32[]{:S(2)}, u32[]{:S(2)}) collective-permute-start(bf16[1,80,384]{2,1,0:T(8,128)(2,1)S(1)} %slice.728), channel_id=1, source_target_pairs={{0,2},{1,3},{2,0},{3,1},{4,6},{5,7},{6,4},{7,5},{8,10},{9,11},{10,... | collective-permute-start | bytes 184328 | tf_op jit(solution)/shard_map/ppermute | solution.py:48
  470.8 29.9 %collective-permute-start.60 = (bf16[8,224,384]{2,1,0:T(8,128)(2,1)S(1)}, bf16[8,224,384]{2,1,0:T(8,128)(2,1)S(1)}, u32[]{:S(2)}, u32[]{:S(2)}) collective-permute-start(bf16[8,224,384]{2,1,0:T(8,128)(2,1)S(1)} %add.209), channel_id=1, source_target_pairs={{0,4},{4,0},{8,12},{12,8},{16,20},{20,16},{24,28},{28,24},{1,5},{5... | collective-permute-start | bytes 4128776 | tf_op jit(solution)/shard_map/ppermute | solution.py:60
  472.3 65.4 %collective-permute-start.40 = (bf16[512,768]{1,0:T(8,128)(2,1)S(1)}, bf16[512,768]{1,0:T(8,128)(2,1)S(1)}, u32[]{:S(2)}, u32[]{:S(2)}) collective-permute-start(bf16[512,768]{1,0:T(8,128)(2,1)S(1)} %get-tuple-element.96), channel_id=1, source_target_pairs={{0,2},{1,3},{2,0},{3,1},{4,6},{5,7},{6,4},{7,5},{8,10},{9,11},{10,... | collective-permute-start | bytes 2359304 | tf_op jit(solution)/shard_map/ppermute | solution.py:48
  501.4 15.2 %collective-permute-start.61 = (bf16[2,224,384]{2,1,0:T(8,128)(2,1)S(1)}, bf16[2,224,384]{2,1,0:T(8,128)(2,1)S(1)}, u32[]{:S(2)}, u32[]{:S(2)}) collective-permute-start(bf16[2,224,384]{2,1,0:T(8,128)(2,1)S(1)} %get-tuple-element.103), channel_id=1, source_target_pairs={{0,24},{4,28},{8,0},{12,4},{16,8},{20,12},{24,16},{28,20},{1,25},{... | collective-permute-start | bytes 1032200 | tf_op jit(solution)/shard_map/ppermute | solution.py:60
  505.7 18.4 %collective-permute-start.63 = (bf16[2,224,384]{2,1,0:T(8,128)(2,1)S(1)}, bf16[2,224,384]{2,1,0:T(8,128)(2,1)S(1)}, u32[]{:S(2)}, u32[]{:S(2)}) collective-permute-start(bf16[2,224,384]{2,1,0:T(8,128)(2,1)S(1)} %get-tuple-element.104), channel_id=1, source_target_pairs={{0,8},{4,12},{8,16},{12,20},{16,24},{20,28},{24,0},{28,4},{1,9},{5... | collective-permute-start | bytes 1032200 | tf_op jit(solution)/shard_map/ppermute | solution.py:60
  506.3 30.2 %collective-permute-start.62 = (bf16[2,224,384]{2,1,0:T(8,128)(2,1)S(1)}, bf16[2,224,384]{2,1,0:T(8,128)(2,1)S(1)}, u32[]{:S(2)}, u32[]{:S(2)}) collective-permute-start(bf16[2,224,384]{2,1,0:T(8,128)(2,1)S(1)} %get-tuple-element.105), channel_id=1, source_target_pairs={{0,16},{4,20},{8,24},{12,28},{16,0},{20,4},{24,8},{28,12},{1,17},{... | collective-permute-start | bytes 1032200 | tf_op jit(solution)/shard_map/ppermute | solution.py:60
  508.8 30.2 %collective-permute-start.54 = (bf16[4,208,384]{2,1,0:T(8,128)(2,1)S(1)}, bf16[4,208,384]{2,1,0:T(8,128)(2,1)S(1)}, u32[]{:S(2)}, u32[]{:S(2)}) collective-permute-start(bf16[4,208,384]{2,1,0:T(8,128)(2,1)S(1)} %slice.733), channel_id=1, source_target_pairs={{0,4},{4,0},{8,12},{12,8},{16,20},{20,16},{24,28},{28,24},{1,5},{5... | collective-permute-start | bytes 1916936 | tf_op jit(solution)/shard_map/ppermute | solution.py:60
  539.3 8.9 %collective-permute-start.55 = (bf16[1,208,384]{2,1,0:T(8,128)(2,1)S(1)}, bf16[1,208,384]{2,1,0:T(8,128)(2,1)S(1)}, u32[]{:S(2)}, u32[]{:S(2)}) collective-permute-start(bf16[1,208,384]{2,1,0:T(8,128)(2,1)S(1)} %get-tuple-element.124), channel_id=1, source_target_pairs={{0,24},{4,28},{8,0},{12,4},{16,8},{20,12},{24,16},{28,20},{1,25},{... | collective-permute-start | bytes 479240 | tf_op jit(solution)/shard_map/ppermute | solution.py:60
  541.1 8.9 %collective-permute-start.57 = (bf16[1,208,384]{2,1,0:T(8,128)(2,1)S(1)}, bf16[1,208,384]{2,1,0:T(8,128)(2,1)S(1)}, u32[]{:S(2)}, u32[]{:S(2)}) collective-permute-start(bf16[1,208,384]{2,1,0:T(8,128)(2,1)S(1)} %get-tuple-element.125), channel_id=1, source_target_pairs={{0,8},{4,12},{8,16},{12,20},{16,24},{20,28},{24,0},{28,4},{1,9},{5... | collective-permute-start | bytes 479240 | tf_op jit(solution)/shard_map/ppermute | solution.py:60
  541.4 13.0 %collective-permute-start.56 = (bf16[1,208,384]{2,1,0:T(8,128)(2,1)S(1)}, bf16[1,208,384]{2,1,0:T(8,128)(2,1)S(1)}, u32[]{:S(2)}, u32[]{:S(2)}) collective-permute-start(bf16[1,208,384]{2,1,0:T(8,128)(2,1)S(1)} %get-tuple-element.126), channel_id=1, source_target_pairs={{0,16},{4,20},{8,24},{12,28},{16,0},{20,4},{24,8},{28,12},{1,17},{... | collective-permute-start | bytes 479240 | tf_op jit(solution)/shard_map/ppermute | solution.py:60
  (50 other events, 449.6 us)

commit v2 on v1

v2 whole, which is shorter than its diff:
```python
import jax
import jax.numpy as jnp
from jax import lax
from jax.experimental import pallas as pl
from jax.experimental.pallas import tpu as pltpu
from jax.sharding import PartitionSpec as P

HD = 64
BLOCK = 64
EPSILON = 1e-06
BIG = float(2.0**100)
LOWEST = -3.0e38
TQ = 256
TK = 512
CHIPS = 16
TILE = 256
BF = jnp.bfloat16
F32 = jnp.float32
VMEM_LIMIT = 60 << 20


def nn(left, right):
    return lax.dot_general(left, right, (((1,), (0,)), ((), ())), preferred_element_type=F32)


def nt(left, right):
    return lax.dot_general(left, right, (((1,), (1,)), ((), ())), preferred_element_type=F32)


def tn(left, right):
    return lax.dot_general(left, right, (((0,), (0,)), ((), ())), preferred_element_type=F32)


def smem():
    return pl.BlockSpec(memory_space=pltpu.SMEM)


def anywhere():
    return pl.BlockSpec(memory_space=pl.ANY)


def shape(dims, kind):
    return jax.ShapeDtypeStruct(dims, kind)


def after(value, *ready):
    if not ready:
        return value
    return lax.optimization_barrier((value,) + ready)[0]


def swap(value, dim):
    if dim == "x":
        return lax.ppermute(value, "dp", [(d, d ^ 1) for d in range(lax.axis_size("dp"))])
    bit = 1 if dim == "core" else 2
    return lax.ppermute(value, "seq", [(s, s ^ bit) for s in range(4)])


def shift_z(value, by):
    size = lax.axis_size("dp") // 2
    return lax.ppermute(value, "dp", [(2 * z + x, (z + by) % size * 2 + x) for z in range(size) for x in range(2)])


ZS = 4


def gather_z(chunk):
    return jnp.stack([chunk] + [shift_z(chunk, by) for by in range(1, ZS)])


def scatter_z(total, *late):
    summed = total[0].astype(F32)
    for r in range(1, ZS):
        summed = summed + after(shift_z(total[r].astype(BF), ZS - r), *late).astype(F32)
    return summed


def add(a, b):
    return (a.astype(F32) + b.astype(F32)).astype(BF)


def fold_first(a_far, b_far, a_near, b_near, *late):
    a, b = after(swap(a_far, "y"), *late), after(swap(b_far, "x"), *late)
    return add(a_near, a), add(b_near, b)


def fold_second(a, b, *late):
    a_came, b_came = after(swap(a[ZS:], "x"), *late), after(swap(b[ZS:], "y"), *late)
    return jnp.concatenate([add(b[:ZS], b_came), add(a[:ZS], a_came)], axis=1), (a_came, b_came)


def chip_at(order, other, index, here):
    z = lax.rem(here["z"] - index % ZS + ZS, ZS)
    near = {order[0]: index // ZS, order[1]: other}
    return z * 4 + lax.rem(here["x"] + near["x"], 2) * 2 + lax.rem(here["y"] + near["y"], 2)


def placed(meta):
    return {"c": meta[0], "x": meta[1], "y": meta[2], "z": meta[3]}


class Plan:
    def __init__(self, sections, cut):
        self.sections, self.cut = sections, cut
        self.rows = sum(sections)

    def parts(self):
        if self.cut is None:
            return [(0, self.rows, None)]
        return [(self.cut, self.rows, "xy"), (0, self.cut, "yx")]

    def shapes(self, width):
        if self.cut is None:
            return [shape((CHIPS, self.rows, width), BF)]
        return [shape((CHIPS // 2, end - first, width), BF) for first, end, _ in self.parts() for _ in range(2)]

    def walk(self, here):
        piece = 0
        for first, end, order in self.parts():
            for other in range(1 if order is None else 2):
                for m in range(CHIPS if order is None else CHIPS // 2):
                    chip = m if order is None else chip_at(order, other, m, here)
                    start = 0
                    for number, length in enumerate(self.sections):
                        lo, hi = max(start, first), min(start + length, end)
                        if lo < hi:
                            yield piece, m, lo - first, hi - first, chip, number, lo - start
                        start += length
                piece += 1

    def entries(self):
        return sum(1 for _ in self.walk({"c": 0, "x": 0, "y": 0, "z": 0}))


def move(plan, here, pieces, target, sems, base, back=False):
    copies = []
    for i, (p, m, lo, hi, chip, number, at) in enumerate(plan.walk(here)):
        near, far = pieces[p].at[m, lo:hi, :], target(number, chip, slice(at, at + hi - lo))
        if back:
            near, far = far, near
        copies.append(pltpu.make_async_copy(near, far, sems.at[base + i]))
    for copy in copies:
        copy.start()
    return copies


def spread_vectors(rows, first, second, marks, hidden_marks):
    count = rows.shape[0]
    number = lax.broadcasted_iota(jnp.int32, (9 * CHIPS, count), 0)
    entry = lax.broadcasted_iota(jnp.int32, (9 * CHIPS, count), 1)
    picker = (entry == lax.rem(number, CHIPS) * 16 + number // CHIPS).astype(F32).astype(BF)
    picked = nn(picker, rows).astype(BF)
    model = first.shape[1]
    vectors = nn(picked[: 8 * CHIPS], first).reshape(8, CHIPS, model) * marks[None]
    hidden = nn(picked[8 * CHIPS :], second).reshape(4, 4, model) * hidden_marks[None]
    return jnp.sum(vectors, axis=1), jnp.sum(hidden, axis=1)


def spread_tables(model, share, share_f, *ready):
    lane, col = jnp.arange(384)[:, None], jnp.arange(model)[None, :]
    if ready:
        lane = after(lane, *ready)
    first = (lane == 128 * (col // share % 2) + col % share).astype(BF)
    second = (lane == 128 * (col // share_f % 2) + col % share_f).astype(BF)
    marks = (jnp.arange(CHIPS)[:, None] == col // (2 * share)).astype(F32)
    hidden_marks = (jnp.arange(4)[:, None] == col // (2 * share_f)).astype(F32)
    return first, second, marks, hidden_marks


def pack_kernel(meta, qkv_ref, proj_ref, inner_ref, down_ref, mine_ref, theirs_ref):
    model = proj_ref.shape[1]
    half, share = model // 2, proj_ref.shape[0]
    for rel, out in ((0, mine_ref), (1, theirs_ref)):
        h = lax.rem(meta[0] + rel, 2)
        lanes = lambda first, n: pl.ds(pl.multiple_of(first, 128), n)
        at = 0
        for p in range(half // 128):
            for w in range(3):
                out[at : at + share, 128 * w : 128 * w + 128] = qkv_ref[:, lanes(model * w + half * h + 128 * p, 128)]
            at += share
        out[at : at + share, :] = proj_ref[:, lanes(half * h, half)]
        at += share
        for g in range(inner_ref.shape[1] // 2 // half):
            out[at : at + share, :] = inner_ref[:, lanes(inner_ref.shape[1] // 2 * h + half * g, half)]
            at += share
        out[at : at + down_ref.shape[0], :] = down_ref[:, lanes(half * h, half)]


def pack(meta, qkv, proj, inner, down):
    half = proj.shape[1] // 2
    rows = proj.shape[0] * (half // 128 + 1 + inner.shape[1] // 2 // half) + down.shape[0]
    return pl.pallas_call(
        pack_kernel,
        in_specs=[smem()] + [pl.BlockSpec(memory_space=pltpu.VMEM)] * 4,
        out_specs=[pl.BlockSpec(memory_space=pltpu.VMEM)] * 2,
        out_shape=[shape((rows, half), BF)] * 2,
        cost_estimate=pl.CostEstimate(flops=0, bytes_accessed=8 * rows * half, transcendentals=0),
        name="pack",
    )(meta, qkv, proj, inner, down)


def qkv_kernel(plan, pieces_n, *refs):
    meta = refs[0]
    pieces = refs[1 : 1 + pieces_n]
    x_ref, first, second, marks, hidden_marks, out_ref, w_ref, vec_ref, rows_ref, bias_ref, sems = refs[1 + pieces_n :]
    here = placed(meta)
    wide = out_ref.shape[1]
    third = wide // 3

    @pl.when(pl.program_id(0) == 0)
    def _():
        def target(number, chip, rows):
            if number == 3:
                return rows_ref.at[chip, rows, :]
            return w_ref.at[chip, rows, third * number : third * number + third]

        for copy in move(plan, here, pieces, target, sems, 0):
            copy.wait()
        rows = rows_ref[...].reshape(CHIPS * 16, 384)
        vectors, hidden = spread_vectors(rows, first[...], second[...], marks[...], hidden_marks[...])
        vec_ref[0:8, :] = vectors
        vec_ref[8:12, :] = hidden
        vec_ref[12:16, :] = jnp.zeros_like(hidden)
        mine = jnp.where(here["c"] == 0, vectors[:, :third], vectors[:, third:])
        bias_ref[...] = jnp.zeros_like(bias_ref)
        for p in range(3):
            for w, source in ((0, 0), (2, 1)):
                at = third * p + 128 * w
                bias_ref[0:1, at : at + 128] = mine[source : source + 1, 128 * p : 128 * p + 128]

    weight = w_ref[...].reshape(-1, wide)
    out_ref[...] = (nn(x_ref[...], weight) + bias_ref[0:1, :]).astype(BF)


def project_qkv(plan, meta, pieces, x_full, tables):
    rows, model = x_full.shape
    width, depth = model // 2, model // CHIPS
    wide = 3 * width
    tile = 512
    return pl.pallas_call(
        lambda *refs: qkv_kernel(plan, len(pieces), *refs),
        grid=(rows // tile,),
        in_specs=[smem()]
        + [anywhere()] * len(pieces)
        + [pl.BlockSpec((tile, model), lambda i: (i, 0))]
        + [whole(t.shape) for t in tables],
        out_specs=[
            pl.BlockSpec((tile, wide), lambda i: (i, 0)),
            whole((CHIPS, depth, wide)),
            whole((16, model)),
        ],
        out_shape=[shape((rows, wide), BF), shape((CHIPS, depth, wide), BF), shape((16, model), F32)],
        scratch_shapes=[
            pltpu.VMEM((CHIPS, 16, width), BF),
            pltpu.VMEM((8, wide), F32),
            pltpu.SemaphoreType.DMA((plan.entries(),)),
        ],
        compiler_params=pltpu.CompilerParams(vmem_limit_bytes=VMEM_LIMIT),
        cost_estimate=pl.CostEstimate(
            flops=2 * rows * model * wide, bytes_accessed=2 * rows * (model + wide), transcendentals=0
        ),
        name="project_qkv",
    )(meta, *pieces, x_full, *tables)


def fill_features(seg_ref, rand_ref, first_global, second_global, key_ref, query_ref):
    heads, _, length = key_ref.shape
    blocks = length // BLOCK
    at = lax.broadcasted_iota(jnp.int32, (blocks, length), 1) // BLOCK
    row = lax.broadcasted_iota(jnp.int32, (blocks, length), 0)
    seen = jnp.abs(at - row) <= 1
    for chosen in (first_global, second_global):
        seen = seen | (at == chosen) | (row == chosen)
    same = lax.broadcasted_iota(jnp.int32, (HD - blocks, length), 0) == seg_ref[...]
    for h in range(heads):
        picked = seen
        for r in range(rand_ref.shape[2]):
            picked = picked | (at == rand_ref[h, :, r : r + 1])
        key_ref[h, 0:blocks, :] = jnp.where(picked, 0.0, 1.0).astype(BF)
        key_ref[h, blocks:HD, :] = jnp.where(same, 0.0, 1.0).astype(BF)
    query_ref[0:blocks, :] = jnp.where(at == row, -BIG, 0.0).astype(BF)
    query_ref[blocks:HD, :] = jnp.where(same, -BIG, 0.0).astype(BF)


def of_pair(ref, p, w):
    return ref[:, 384 * p + 128 * w : 384 * p + 128 * w + 128]


def widen_pair(p, qkv_ref, key_feat, query_feat, key_wide, query_wide):
    scaled = of_pair(qkv_ref, p, 0) * BF(HD**-0.5)
    queries, keys = scaled.T, of_pair(qkv_ref, p, 1).T
    a, b = 2 * p, 2 * p + 1
    query_wide[a, 0:HD, :] = queries[0:HD]
    query_wide[a, HD:128, :] = query_feat[...]
    query_wide[b, 0:HD, :] = query_feat[...]
    query_wide[b, HD:128, :] = queries[HD:128]
    key_wide[a] = jnp.concatenate([keys[0:HD], key_feat[a]], axis=0).T
    key_wide[b] = jnp.concatenate([key_feat[b], keys[HD:128]], axis=0).T
    return scaled, keys


def attend_kernel(meta, lo_ref, n_ref, glob_ref, qkv_ref, seg_ref, rand_ref, out_ref, lse_ref,
                  key_feat, query_feat, key_wide, query_wide, values, turned, store):
    heads, length = lse_ref.shape
    fill_features(seg_ref, rand_ref, glob_ref[0], glob_ref[1], key_feat, query_feat)
    for p in range(heads // 2):
        widen_pair(p, qkv_ref, key_feat, query_feat, key_wide, query_wide)
        values[128 * p : 128 * p + 128, :] = of_pair(qkv_ref, p, 2).T

    def tile(i, _):
        qs = pl.ds(pl.multiple_of(i * TQ, TQ), TQ)
        start = lo_ref[i]

        def scan(j, tops):
            ks = pl.ds(pl.multiple_of(start + j * TK, 128), TK)
            to = pl.ds(pl.multiple_of(j * TK, TK), TK)
            raised = []
            for h in range(heads):
                scores = nn(key_wide[h, ks, :], query_wide[h, :, qs])
                store[h, to, :] = scores
                raised.append(jnp.maximum(tops[h], jnp.max(scores.reshape(TK // 8, 8, TQ), axis=0)))
            return tuple(raised)

        tops = lax.fori_loop(0, n_ref[i], scan, (jnp.full((8, TQ), LOWEST, F32),) * heads)
        tops = [jnp.max(top, axis=0, keepdims=True) for top in tops]

        def collect(j, carry):
            ks = pl.ds(pl.multiple_of(start + j * TK, 128), TK)
            at = pl.ds(pl.multiple_of(j * TK, TK), TK)
            new = []
            for h in range(heads):
                total, summed = carry[h]
                expo = jnp.exp(store[h, at, :] - tops[h])
                total = total + jnp.sum(expo.reshape(TK // 8, 8, TQ), axis=0)
                summed = summed + nn(values[HD * h : HD * h + HD, ks], expo.astype(BF))
                new.append((total, summed))
            return tuple(new)

        none = (jnp.zeros((8, TQ), F32), jnp.zeros((HD, TQ), F32))
        found = lax.fori_loop(0, n_ref[i], collect, (none,) * heads)
        for h in range(heads):
            total, summed = found[h]
            total = jnp.sum(total, axis=0, keepdims=True)
            turned[HD * h : HD * h + HD, qs] = (summed / total).astype(BF)
            lse_ref[h : h + 1, qs] = tops[h] + jnp.log(total)
        return 0

    lax.fori_loop(0, length // TQ, tile, 0)
    quarter = length // 4
    for p in range(heads // 2):
        result = turned[128 * p : 128 * p + 128, :].T
        for n in range(4):
            rel = lax.rem(meta[0] + n, 2)
            out_ref[rel, quarter * (n // 2) : quarter * (n // 2) + quarter, 128 * p : 128 * p + 128] = result[
                quarter * n : quarter * n + quarter
            ]


def whole(dims):
    return pl.BlockSpec(dims, lambda *_: (0,) * len(dims))


def attend(meta, qkv, number, seg_row, table, globs, lo, n):
    length = qkv.shape[0]
    heads, blocks = table.shape[:2]
    wide = heads * HD
    return pl.pallas_call(
        attend_kernel,
        grid=(1,),
        in_specs=[smem()] * 4
        + [pl.BlockSpec((length, 3 * wide), lambda i: (0, number)), whole((1, length)), whole((heads, blocks, 3))],
        out_specs=[whole((2, length // 2, wide)), whole((heads, length))],
        out_shape=[shape((2, length // 2, wide), BF), shape((heads, length), F32)],
        scratch_shapes=[
            pltpu.VMEM((heads, HD, length), BF),
            pltpu.VMEM((HD, length), BF),
            pltpu.VMEM((heads, length, 128), BF),
            pltpu.VMEM((heads, 128, length), BF),
            pltpu.VMEM((wide, length), BF),
            pltpu.VMEM((wide, length), BF),
            pltpu.VMEM((heads, length, TQ), F32),
        ],
        compiler_params=pltpu.CompilerParams(vmem_limit_bytes=VMEM_LIMIT),
        cost_estimate=pl.CostEstimate(
            flops=heads * length * length * 700, bytes_accessed=10 * length * wide, transcendentals=heads * length * length // 2
        ),
        name="attend",
    )(meta, lo, n, globs, qkv, seg_row, table)


def attend_back_kernel(meta, lo_ref, n_ref, glob_ref, qkv_ref, own_ref, oth_ref, ctx_ref, lse_ref, seg_ref,
                       rand_ref, out_ref, key_feat, query_feat, key_wide, query_wide, value_one,
                       grad_turned, keys_turned, query_one, grad_one, inner_ref, dk, dv, dqt, grads):
    heads, length = lse_ref.shape
    quarter = length // 4
    fill_features(seg_ref, rand_ref, glob_ref[0], glob_ref[1], key_feat, query_feat)
    for rel, source in ((0, own_ref), (1, oth_ref)):
        for n in range(2):
            at = 2 * n + lax.rem(meta[0] + rel, 2)
            rows = pl.ds(pl.multiple_of(at * quarter, quarter), quarter)
            grads[0, rows, :] = source[quarter * n : quarter * n + quarter, :]
            grads[1, rows, :] = ctx_ref[rel, quarter * n : quarter * n + quarter, :]
    low = lax.broadcasted_iota(jnp.int32, (length, 128), 1) < HD
    zero = jnp.zeros((length, 128), BF)
    for p in range(heads // 2):
        cols = slice(128 * p, 128 * p + 128)
        scaled, keys = widen_pair(p, qkv_ref, key_feat, query_feat, key_wide, query_wide)
        keys_turned[cols, :] = keys
        grad, value = grads[0, :, cols], of_pair(qkv_ref, p, 2)
        for e in range(2):
            keep = low if e == 0 else ~low
            value_one[2 * p + e] = jnp.where(keep, value, zero)
            query_one[2 * p + e] = jnp.where(keep, scaled, zero)
            grad_one[2 * p + e] = jnp.where(keep, grad, zero)
        turned = grad.T
        grad_turned[cols, :] = turned
        product = turned.astype(F32) * grads[1, :, cols].T.astype(F32)
        for e in range(2):
            h = 2 * p + e
            inner_ref[h : h + 1, :] = jnp.sum(product[HD * e : HD * e + HD], axis=0, keepdims=True)
    dk[...] = jnp.zeros_like(dk)
    dv[...] = jnp.zeros_like(dv)

    def tile(i, _):
        qs = pl.ds(pl.multiple_of(i * TQ, TQ), TQ)
        start = lo_ref[i]

        def body(j, carry):
            ks = pl.ds(pl.multiple_of(start + j * TK, 128), TK)
            new = []
            for p in range(heads // 2):
                cols = slice(128 * p, 128 * p + 128)
                more_k, more_v = [], []
                for h in (2 * p, 2 * p + 1):
                    scores = nn(key_wide[h, ks, :], query_wide[h, :, qs])
                    prob = jnp.exp(scores - lse_ref[h : h + 1, qs])
                    grad_prob = nn(value_one[h, ks, :], grad_turned[cols, qs])
                    grad_scores = (prob * (grad_prob - inner_ref[h : h + 1, qs])).astype(BF)
                    new.append(carry[h] + nn(keys_turned[HD * h : HD * h + HD, ks], grad_scores))
                    more_k.append(nn(grad_scores, query_one[h, qs, :]))
                    more_v.append(nn(prob.astype(BF), grad_one[h, qs, :]))
                dk[ks, cols] += more_k[0] + more_k[1]
                dv[ks, cols] += more_v[0] + more_v[1]
            return tuple(new)

        found = lax.fori_loop(0, n_ref[i], body, (jnp.zeros((HD, TQ), F32),) * heads)
        for h in range(heads):
            dqt[HD * h : HD * h + HD, qs] = (found[h] * HD**-0.5).astype(BF)
        return 0

    lax.fori_loop(0, length // TQ, tile, 0)
    for p in range(heads // 2):
        cols = slice(128 * p, 128 * p + 128)
        for w, value in enumerate((dqt[cols, :].T, dk[:, cols].astype(BF), dv[:, cols].astype(BF))):
            out_ref[:, 384 * p + 128 * w : 384 * p + 128 * w + 128] = value


def attend_back(meta, qkv, number, own, oth, ctx, lse, part, seg_row, table, globs, lo, n):
    length = qkv.shape[0]
    heads, blocks = table.shape[:2]
    wide = heads * HD
    group = lambda w, i=number: pl.BlockSpec((length, w), lambda _: (0, i))
    half = pl.BlockSpec((length // 2, wide), lambda _: (0, number))
    return pl.pallas_call(
        attend_back_kernel,
        grid=(1,),
        in_specs=[smem()] * 4
        + [group(3 * wide), half, half, pl.BlockSpec((2, length // 2, wide), lambda _: (0, 0, part))]
        + [whole((heads, length)), whole((1, length)), whole((heads, blocks, 3))],
        out_specs=whole((length, 3 * wide)),
        out_shape=shape((length, 3 * wide), BF),
        scratch_shapes=[
            pltpu.VMEM((heads, HD, length), BF),
            pltpu.VMEM((HD, length), BF),
            pltpu.VMEM((heads, length, 128), BF),
            pltpu.VMEM((heads, 128, length), BF),
            pltpu.VMEM((heads, length, 128), BF),
            pltpu.VMEM((wide, length), BF),
            pltpu.VMEM((wide, length), BF),
            pltpu.VMEM((heads, length, 128), BF),
            pltpu.VMEM((heads, length, 128), BF),
            pltpu.VMEM((heads, length), F32),
            pltpu.VMEM((length, wide), F32),
            pltpu.VMEM((length, wide), F32),
            pltpu.VMEM((wide, length), BF),
            pltpu.VMEM((2, length, wide), BF),
        ],
        compiler_params=pltpu.CompilerParams(vmem_limit_bytes=VMEM_LIMIT),
        cost_estimate=pl.CostEstimate(
            flops=heads * length * length * 1500, bytes_accessed=20 * length * wide, transcendentals=heads * length * length // 2
        ),
        name="attend_back",
    )(meta, lo, n, globs, qkv, own, oth, ctx, lse, seg_row, table)


def key_ranges(segment):
    length = segment.shape[0]
    first, last = segment[::TQ], segment[TQ - 1 :: TQ]
    lo = jnp.sum(segment[None, :] < first[:, None], axis=1, dtype=jnp.int32) // 128 * 128
    hi = jnp.sum(segment[None, :] <= last[:, None], axis=1, dtype=jnp.int32)
    n = (hi - lo + TK - 1) // TK
    return jnp.minimum(lo, length - n * TK), n


def centre(value):
    centred = value - jnp.mean(value, axis=1, keepdims=True)
    rate = lax.rsqrt(jnp.mean(centred * centred, axis=1, keepdims=True) + EPSILON)
    return centred * rate, rate


def norm_back(grad, normed, rate):
    return rate * (
        grad
        - jnp.mean(grad, axis=1, keepdims=True)
        - normed * jnp.mean(grad * normed, axis=1, keepdims=True)
    )


def cut(value):
    half = value.shape[1] // 2
    return value[:, :half], value[:, half:]


def wide_target(proj, inner, down, half):
    width = proj.shape[2] // 2
    groups = inner.shape[2] // 2 // width

    def target(number, chip, rows):
        if number == 0:
            return proj.at[chip, rows, pl.ds(pl.multiple_of(half * width, 128), width)]
        if number <= groups:
            first = half * (groups * width) + width * (number - 1)
            return inner.at[chip, rows, pl.ds(pl.multiple_of(first, 128), width)]
        return down.at[chip, rows, pl.ds(pl.multiple_of(half * width, 128), width)]

    return target


def ffn_kernel(plan, pieces_n, ctx_n, *refs):
    meta = refs[0]
    own_pieces = refs[1 : 1 + pieces_n]
    oth_pieces = refs[1 + pieces_n : 1 + 2 * pieces_n]
    refs = refs[1 + 2 * pieces_n :]
    ctx_own, ctx_oth = refs[:ctx_n], refs[ctx_n : 2 * ctx_n]
    (x_ref, dout_ref, vec_ref,
     out_ref, hid_ref, gf_ref, low_ref, gp_ref, gr_ref, ga_ref, gc_own, gc_oth, ctx_ref, vg_ref,
     proj, inner, down, slope, sems) = refs[2 * ctx_n :]
    here = placed(meta)
    c = here["c"]
    step = pl.program_id(0)
    model = x_ref.shape[1]
    wide = hid_ref.shape[1]

    @pl.when(step == 0)
    def _():
        copies = []
        for rel, pieces in ((0, own_pieces), (1, oth_pieces)):
            target = wide_target(proj, inner, down, lax.rem(c + rel, 2))
            copies += move(plan, here, pieces, target, sems, len(copies))
        for copy in copies:
            copy.wait()
        vg_ref[...] = jnp.zeros_like(vg_ref)

    vec = lambda n: vec_ref[n : n + 1, :]
    w_proj = proj[...].reshape(model, model)
    w_inner = lambda j: inner[:, :, model * j : model * j + model].reshape(model, model)
    span = CHIPS * model // wide
    w_down = lambda j: down[span * j : span * j + span].reshape(model, model)
    own = jnp.concatenate([ref[...] for ref in ctx_own], axis=1)
    oth = jnp.concatenate([ref[...] for ref in ctx_oth], axis=1)
    context = jnp.concatenate([jnp.where(c == 0, own, oth), jnp.where(c == 0, oth, own)], axis=1)
    ctx_ref[...] = context
    attn = nn(context, w_proj)
    n1, rate1 = centre(x_ref[...].astype(F32) + (attn + vec(2)))
    x1 = n1 * vec(3) + vec(4)
    low = x1.astype(BF)
    low_ref[...] = low
    ffn = None
    chunks = wide // model
    for j in range(chunks):
        cols = slice(model * j, model * j + model)
        pre = nn(low, w_inner(j)) + vec(8 + j)
        below = 0.5 + 0.5 * lax.erf(pre * 0.7071067811865476)
        slope[:, cols] = below + pre * (jnp.exp(-0.5 * (pre * pre)) * 0.3989422804014327)
        hidden = (pre * below).astype(BF)
        hid_ref[:, cols] = hidden
        more = nn(hidden, w_down(j))
        ffn = more if ffn is None else ffn + more
    n2, rate2 = centre(x1 + (ffn + vec(5)))
    out_ref[...] = (n2 * vec(6) + vec(7)).astype(BF)

    total = lambda value: jnp.sum(value, axis=0, keepdims=True)
    grad = dout_ref[...].astype(F32)
    gr2 = norm_back(grad * vec(6), n2, rate2)
    gf = gr2.astype(BF)
    gf_ref[...] = gf
    vg_ref[6:7, :] += total(grad * n2)
    vg_ref[7:8, :] += total(grad)
    vg_ref[5:6, :] += total(gf.astype(F32))
    gx1 = gr2
    for j in range(chunks):
        cols = slice(model * j, model * j + model)
        gp = (nt(gf, w_down(j)) * slope[:, cols]).astype(BF)
        gp_ref[:, cols] = gp
        vg_ref[8 + j : 9 + j, :] += total(gp.astype(F32))
        gx1 = gx1 + nt(gp, w_inner(j))
    gr1 = norm_back(gx1 * vec(3), n1, rate1)
    gr_ref[...] = gr1
    ga = gr1.astype(BF)
    ga_ref[...] = ga
    vg_ref[3:4, :] += total(gx1 * n1)
    vg_ref[4:5, :] += total(gx1)
    vg_ref[2:3, :] += total(ga.astype(F32))
    gc = cut(nt(ga, w_proj))
    gc_own[...] = jnp.where(c == 0, gc[0], gc[1]).astype(BF)
    gc_oth[...] = jnp.where(c == 0, gc[1], gc[0]).astype(BF)


def feed_forward(plan, meta, own_pieces, oth_pieces, ctx, ctx_oth, x_own, d_own, vectors, wide):
    rows, model = x_own.shape
    half = model // 2
    tile = lambda n: pl.BlockSpec((TILE, n), lambda i: (i, 0))
    return pl.pallas_call(
        lambda *refs: ffn_kernel(plan, len(own_pieces), len(ctx), *refs),
        grid=(rows // TILE,),
        in_specs=[smem()]
        + [anywhere()] * (2 * len(own_pieces))
        + [pl.BlockSpec((None, TILE, v.shape[2]), lambda i: (0, i, 0)) for v in ctx]
        + [tile(v.shape[1]) for v in ctx_oth]
        + [tile(model), tile(model), whole(vectors.shape)],
        out_specs=[tile(model), tile(wide), tile(model), tile(model), tile(wide), tile(model), tile(model)]
        + [tile(half), tile(half), tile(model), whole((16, model))],
        out_shape=[
            shape((rows, model), BF),
            shape((rows, wide), BF),
            shape((rows, model), BF),
            shape((rows, model), BF),
            shape((rows, wide), BF),
            shape((rows, model), F32),
            shape((rows, model), BF),
            shape((rows, half), BF),
            shape((rows, half), BF),
            shape((rows, model), BF),
            shape((16, model), F32),
        ],
        scratch_shapes=[
            pltpu.VMEM((CHIPS, model // CHIPS, model), BF),
            pltpu.VMEM((CHIPS, model // CHIPS, wide), BF),
            pltpu.VMEM((CHIPS, wide // CHIPS, model), BF),
            pltpu.VMEM((TILE, wide), F32),
            pltpu.SemaphoreType.DMA((2 * plan.entries(),)),
        ],
        compiler_params=pltpu.CompilerParams(vmem_limit_bytes=VMEM_LIMIT),
        cost_estimate=pl.CostEstimate(
            flops=4 * rows * model * (model + 2 * wide), bytes_accessed=rows * (8 * wide + 20 * model), transcendentals=2 * rows * wide
        ),
        name="feed_forward",
    )(meta, *own_pieces, *oth_pieces, *ctx, *ctx_oth, x_own, d_own, vectors)


def weight_grads_kernel(plan, pieces_n, *refs):
    meta, hid_ref, gp_ref, gf_ref, low_ref, ctx_ref, ga_ref = refs[:7]
    own_pieces = refs[7 : 7 + pieces_n]
    oth_pieces = refs[7 + pieces_n : 7 + 2 * pieces_n]
    proj, inner, down, sems = refs[7 + 2 * pieces_n :]
    here = placed(meta)
    c = here["c"]
    step = pl.program_id(0)
    model = gf_ref.shape[1]
    span = CHIPS * model // inner.shape[2]
    steps = inner.shape[2] // model

    @pl.when(step == 0)
    def _():
        proj[...] = tn(ctx_ref[...], ga_ref[...]).reshape(proj.shape).astype(BF)

    more_inner = tn(low_ref[...], gp_ref[...])
    inner[:, :, pl.ds(pl.multiple_of(step * model, 128), model)] = more_inner.reshape(CHIPS, -1, model).astype(BF)
    more_down = tn(hid_ref[...], gf_ref[...])
    down[pl.ds(step * span, span)] = more_down.reshape(span, -1, model).astype(BF)

    @pl.when(step == steps - 1)
    def _():
        copies = []
        for rel, pieces in ((0, own_pieces), (1, oth_pieces)):
            target = wide_target(proj, inner, down, lax.rem(c + rel, 2))
            copies += move(plan, here, pieces, target, sems, len(copies), back=True)
        for copy in copies:
            copy.wait()


def weight_grads(plan, meta, hid, gp, gf, low, context, ga):
    rows, model = gf.shape
    wide, half = hid.shape[1], model // 2
    pieces = plan.shapes(half)
    cols = pl.BlockSpec((rows, model), lambda i: (0, i))
    found = pl.pallas_call(
        lambda *refs: weight_grads_kernel(plan, len(pieces), *refs),
        grid=(wide // model,),
        in_specs=[smem(), cols, cols] + [whole((rows, model))] * 4,
        out_specs=[anywhere()] * (2 * len(pieces)),
        out_shape=pieces * 2,
        scratch_shapes=[
            pltpu.VMEM((CHIPS, model // CHIPS, model), BF),
            pltpu.VMEM((CHIPS, model // CHIPS, wide), BF),
            pltpu.VMEM((CHIPS, wide // CHIPS, model), BF),
            pltpu.SemaphoreType.DMA((2 * plan.entries(),)),
        ],
        compiler_params=pltpu.CompilerParams(vmem_limit_bytes=VMEM_LIMIT),
        cost_estimate=pl.CostEstimate(
            flops=2 * rows * model * (model + 2 * wide), bytes_accessed=rows * (4 * wide + 8 * model), transcendentals=0
        ),
        name="weight_grads",
    )(meta, hid, gp, gf, low, context, ga)
    return found[: len(pieces)], found[len(pieces) :]


def gather_vectors(vectors, hidden, first, second, marks, hidden_marks):
    model = first.shape[1]
    one = nt((vectors[:, None, :] * marks[None]).reshape(-1, model).astype(BF), first)
    two = nt((hidden[:, None, :] * hidden_marks[None]).reshape(-1, model).astype(BF), second)
    laid = jnp.concatenate([one, two], axis=0).astype(BF)
    number = lax.broadcasted_iota(jnp.int32, (9 * CHIPS, 16 * CHIPS), 0)
    entry = lax.broadcasted_iota(jnp.int32, (9 * CHIPS, 16 * CHIPS), 1)
    picker = (entry == lax.rem(number, CHIPS) * 16 + number // CHIPS).astype(F32).astype(BF)
    return tn(picker, laid)


def qkv_grads_kernel(plan, pieces_n, groups, *refs):
    meta, x_ref = refs[:2]
    grads = refs[2 : 2 + groups]
    vg_ref, first, second, marks, hidden_marks = refs[2 + groups : 7 + groups]
    pieces = refs[7 + groups : 7 + groups + pieces_n]
    g_ref, rows_ref, vec_ref, sems = refs[7 + groups + pieces_n :]
    here = placed(meta)
    even = here["c"] == 0
    width = x_ref.shape[1] // 2
    x = x_ref[...]
    vec_ref[...] = vg_ref[...]
    none = jnp.zeros((1, 128), F32)
    for p, source in enumerate(grads):
        grad = source[...]
        g_ref[p] = tn(x, grad).reshape(g_ref.shape[1:]).astype(BF)
        summed = jnp.sum(grad.astype(F32), axis=0, keepdims=True)
        for row, w in ((0, 0), (1, 2)):
            value = summed[:, 128 * w : 128 * w + 128]
            vec_ref[row : row + 1, 128 * p : 128 * p + 128] = jnp.where(even, value, none)
            at = width + 128 * p
            vec_ref[row : row + 1, at : at + 128] = jnp.where(even, none, value)
    found = gather_vectors(vec_ref[0:8, :], vec_ref[8:12, :], first[...], second[...], marks[...], hidden_marks[...])
    rows_ref[...] = found.reshape(rows_ref.shape).astype(BF)

    def target(number, chip, rows):
        if number == 3:
            return rows_ref.at[chip, rows, :]
        return g_ref.at[number, chip, rows, :]

    for copy in move(plan, here, pieces, target, sems, 0, back=True):
        copy.wait()


def qkv_grads(plan, meta, x_full, grads, vg, tables):
    rows, model = x_full.shape
    width, depth = grads[0].shape[1], model // CHIPS
    pieces = plan.shapes(width)
    return pl.pallas_call(
        lambda *refs: qkv_grads_kernel(plan, len(pieces), len(grads), *refs),
        grid=(1,),
        in_specs=[smem(), whole((rows, model))]
        + [whole((rows, width))] * len(grads)
        + [whole(vg.shape)]
        + [whole(t.shape) for t in tables],
        out_specs=[anywhere()] * len(pieces),
        out_shape=pieces,
        scratch_shapes=[
            pltpu.VMEM((len(grads), CHIPS, depth, width), BF),
            pltpu.VMEM((CHIPS, 16, width), BF),
            pltpu.VMEM((16, model), F32),
            pltpu.SemaphoreType.DMA((plan.entries(),)),
        ],
        compiler_params=pltpu.CompilerParams(vmem_limit_bytes=VMEM_LIMIT),
        cost_estimate=pl.CostEstimate(
            flops=6 * rows * model * width, bytes_accessed=2 * rows * (model + 3 * width), transcendentals=0
        ),
        name="qkv_grads",
    )(meta, x_full, *grads, vg, *tables)


def input_grads_kernel(meta, *refs):
    *grads, w_ref, out_ref = refs
    width = grads[0].shape[1]
    total = None
    for p, source in enumerate(grads):
        weight = w_ref[:, :, width * p : width * p + width].reshape(-1, width)
        more = nt(source[...], weight)
        total = more if total is None else total + more
    out_ref[...] = total.astype(BF)


def input_grads(meta, grads, weights):
    rows, width = grads[0].shape
    model = weights.shape[0] * weights.shape[1]
    quarter = rows // 4
    part = pl.BlockSpec((quarter, width), lambda i, meta: (i, 0))
    return pl.pallas_call(
        input_grads_kernel,
        grid_spec=pltpu.PrefetchScalarGridSpec(
            num_scalar_prefetch=1,
            grid=(4,),
            in_specs=[part] * len(grads) + [whole(weights.shape)],
            out_specs=pl.BlockSpec(
                (None, quarter, model), lambda i, meta: (lax.rem(meta[0] + i, 2), i // 2, 0)
            ),
        ),
        out_shape=shape((2, 2 * quarter, model), BF),
        compiler_params=pltpu.CompilerParams(vmem_limit_bytes=VMEM_LIMIT),
        cost_estimate=pl.CostEstimate(
            flops=6 * rows * model * width, bytes_accessed=2 * rows * (model + 3 * width), transcendentals=0
        ),
        name="input_grads",
    )(meta, *grads, weights)


def body(
    tokens,
    qkv_weight,
    query_bias,
    value_bias,
    proj_weight,
    proj_bias,
    attn_gain,
    attn_shift,
    inner_weight,
    inner_bias,
    down_weight,
    down_bias,
    ffn_gain,
    ffn_shift,
    seg_ids,
    rand_blocks,
    glob_blocks,
    d_out,
):
    dp, seq = lax.axis_index("dp"), lax.axis_index("seq")
    members = lax.axis_size("dp") * lax.axis_size("seq")
    near = lax.axis_size("dp") == 2 * ZS
    y, c = seq // 2, seq % 2
    even, low_y = c == 0, y == 0
    meta = jnp.stack([c, dp % 2, y, dp // 2]).astype(jnp.int32)
    model = tokens.shape[3]
    half = model // 2
    ffw = inner_weight.shape[1]
    share, share_f = qkv_weight.shape[0], down_weight.shape[0]
    groups = ffw // 2 // half
    depth, deep = model // CHIPS, ffw // CHIPS
    by_parity = lambda mine, other: (jnp.where(even, mine, other), jnp.where(even, other, mine))

    def columns(h):
        qkv = [[model * w + half * h + 128 * p for w in range(3)] for p in range(half // 128)]
        return qkv, half * h, [ffw // 2 * h + half * g for g in range(groups)]

    pair = lambda kept, came: jnp.where(low_y, jnp.stack([kept, came]), jnp.stack([came, kept]))

    def to_chip(value, ready=(), late=()):
        kept = jnp.where(low_y, value[0], value[1])
        given = jnp.where(low_y, value[1], value[0])
        came = swap(after(given, *ready) if ready else given, "y")
        return pair(kept, after(came, *late) if late else came)

    vectors = (query_bias, value_bias, proj_bias, attn_gain, attn_shift, down_bias, ffn_gain, ffn_shift)
    sections_a, sections_b = [depth] * 3 + [16], [depth] * (1 + groups) + [deep]
    if near:
        plan_a = Plan(sections_a, 80)
        plan_b = Plan(sections_b, 256)

        x_own = to_chip(tokens[:, 0])
        mine, theirs = pack(meta, qkv_weight, proj_weight, inner_weight, down_weight)
        came = swap(theirs, "core")
        first, second = by_parity(mine, came)
        small = jnp.concatenate([jnp.pad(jnp.stack(vectors), ((0, 0), (0, 128 - share))),
                                 jnp.pad(inner_bias[None], ((0, 7), (0, 128 - share_f)))])
        small = jnp.concatenate(by_parity(small, swap(small, "core")) + (jnp.zeros_like(small),), axis=1)
        laid, at = [], 0
        for length in [share] * (4 + groups) + [share_f]:
            laid += [first[at : at + length], second[at : at + length]]
            at += length
        chunk_a = jnp.concatenate(laid[:6] + [small], axis=0)
        chunk_b = jnp.concatenate(laid[6:], axis=0)

        def split_z(chunk, plan):
            found = gather_z(chunk)
            return found[:, plan.cut :], found[:, : plan.cut]

        def first_side(a, b, *late):
            a_came, b_came = after(swap(a, "x"), *late), after(swap(b, "y"), *late)
            return jnp.concatenate([a, a_came]), jnp.concatenate([b, b_came])

        def second_side(a, b, *late):
            return [a, after(swap(a, "y"), *late), b, after(swap(b, "x"), *late)]

        za = split_z(chunk_a, plan_a)
        tables = spread_tables(model, depth // 2, deep // 2, chunk_a)
        x_oth = swap(x_own, "core")
        za = [after(v, x_oth) for v in za]
        zb = split_z(after(chunk_b, *za), plan_b)
        pieces_a = second_side(*first_side(*za))
    else:
        plan_a, plan_b = Plan(sections_a, None), Plan(sections_b, None)
        x_own = to_chip(tokens[:, 0])
        x_oth = swap(x_own, "core")
        tables = spread_tables(model, depth // 2, deep // 2)
        everyone = lambda w: lax.all_gather(w, ("dp", "seq"), axis=0, tiled=True)
        full_qkv, full_proj, full_inner, full_down = map(everyone, (qkv_weight, proj_weight, inner_weight, down_weight))
        row = everyone(jnp.concatenate(list(vectors) + [inner_bias])[None])
        full_vectors = row[:, : 8 * share].reshape(members, 8, share).transpose(1, 0, 2).reshape(8, CHIPS, 2, -1)
        full_bias = row[:, 8 * share :].reshape(1, CHIPS, 2, -1)
        padded = lambda v: jnp.pad(v, ((0, 0),) * 3 + ((0, 128 - v.shape[3]),))
        rows = jnp.concatenate([padded(full_vectors), padded(full_bias)], axis=0)
        rows = jnp.pad(rows, ((0, 7), (0, 0), (0, 1), (0, 0))).transpose(1, 0, 2, 3).reshape(CHIPS, 16, 384)

        def packed(h):
            qkv, first, inner = columns(h)
            col = lambda w, at, n=half: w[:, at : at + n].reshape(CHIPS, -1, n)
            a = [jnp.concatenate([col(full_qkv, at, 128) for at in p], axis=2) for p in qkv]
            b = [col(full_proj, first)] + [col(full_inner, at) for at in inner] + [col(full_down, first)]
            return jnp.concatenate(a + [rows], axis=1), jnp.concatenate(b, axis=1)

        zero, one = packed(0), packed(1)
        pieces_a = [jnp.where(even, zero[0], one[0])]
        own_b, oth_b = [[v] for v in by_parity(zero[1], one[1])]
        chunk_a = pieces_a[0]

    x_full = jnp.where(even, jnp.stack([x_own, x_oth], 1), jnp.stack([x_oth, x_own], 1)).reshape(-1, model)
    x_own = x_own.reshape(-1, model)
    segment = jnp.where(low_y, seg_ids[0, 0], seg_ids[1, 0])
    globs = jnp.where(low_y, glob_blocks[0, 0], glob_blocks[1, 0])
    lo, n = key_ranges(segment)
    blocks = rand_blocks[:, 0]
    of_chip = by_parity(blocks, swap(blocks, "core"))
    for_chip = jnp.where(low_y, *(jnp.concatenate([v[m] for v in of_chip]) for m in range(2)))
    for_other = jnp.where(low_y, *(jnp.concatenate([v[1 - m] for v in of_chip]) for m in range(2)))
    table = jnp.where(c == y, for_chip, swap(after(for_other, x_oth), "y"))

    qkv, w_qkv, spread = project_qkv(plan_a, meta, pieces_a, x_full, tables)
    spots = (segment[None], globs, lo, n)
    attention = lambda heads, number, source: attend(meta, source, number, spots[0], table[heads], *spots[1:])
    ctx_b, lse_b = attention(slice(4, 6), 2, qkv)
    ctx_b_oth = swap(ctx_b[1], "core")
    qkv_later = qkv
    if near:
        ones = first_side(*[after(v, x_full, *pieces_a) for v in zb], ctx_b)
        qkv_later = after(qkv, *ones)
    ctx_a, lse_a = attention(slice(0, 4), 0, qkv_later)
    ctx_a_oth = swap(ctx_a[1], "core")
    d_own = to_chip(d_out[:, 0], pieces_a, (ctx_a,)).reshape(-1, model)
    if near:
        own_b = second_side(*ones, ctx_a)
        oth_b = [swap(piece, "core") for piece in own_b]
    found = feed_forward(plan_b, meta, own_b, oth_b, [ctx_a, ctx_b], [ctx_a_oth, ctx_b_oth], x_own, d_own, spread, ffw)
    out, hid, gf, x1_low, gp, gr1, ga, gc_own, gc_oth, context, vg = found

    gc_came = swap(gc_oth, "core")
    grads_own, grads_oth = weight_grads(plan_b, meta, hid, gp, gf, x1_low, context, ga)
    layer_given = out.reshape(2, -1, model)

    def attention_back(p, *ready):
        ctx, lse, part = (ctx_a, lse_a, p) if p < 2 else (ctx_b, lse_b, 0)
        return attend_back(meta, qkv, p, after(gc_own, *ready), gc_came, ctx, lse[2 * part : 2 * part + 2], part, spots[0],
                           table[2 * p : 2 * p + 2], *spots[1:])

    if near:
        far = [add(grads_own[i], swap(grads_oth[i], "core")) for i in (1, 3)]
        grads = [attention_back(0, *far)]
        layer_out = to_chip(layer_given, (), (grads[0],))[:, None]
        close = [add(grads_own[i], after(swap(grads_oth[i], "core"), grads[0])) for i in (0, 2)]
        grads.append(attention_back(1, *close, layer_out))
        down_b = fold_first(*far, *close, grads[1])
        grads.append(attention_back(2, *down_b))
        down_b, ready = fold_second(*down_b, grads[2])
    else:
        grads = [attention_back(p) for p in range(3)]
        layer_out = to_chip(layer_given)[:, None]
        ready = ()
    grads_qkv = qkv_grads(plan_a, meta, x_full, [after(grads[0], *ready)] + grads[1:], vg, tables)
    back = input_grads(meta, [after(grads[0], grads_qkv[0])] + grads[1:], w_qkv)
    grad_own = gr1 + (back[0].astype(F32) + swap(back[1], "core").astype(F32))
    grad_input = to_chip(grad_own.astype(BF).reshape(2, -1, model))[:, None]

    if near:
        down_a = fold_first(*[grads_qkv[i] for i in (1, 3, 0, 2)], back)
        total_b = scatter_z(down_b, *down_a)
        down_a, _ = fold_second(*down_a, grad_own)
        total_a = scatter_z(after(down_a, total_b), grad_input)
        kept, given = by_parity(total_a[3 * depth :, :128], total_a[3 * depth :, 128:256])
        small = kept + swap(given, "core")
        small = jnp.concatenate([small[v, :share] for v in range(8)] + [small[8, :share_f]])

        def finish(total, lengths):
            mine, theirs, at = [], [], 0
            for length in lengths:
                kept, given = by_parity(total[at : at + length], total[at + length : at + 2 * length])
                mine.append(kept)
                theirs.append(given)
                at += 2 * length
            mine = jnp.concatenate(mine, axis=0)
            came = swap(jnp.concatenate(theirs, axis=0).astype(BF), "core").astype(F32)
            halves, cuts, at = by_parity(mine, came), [], 0
            for length in lengths:
                cuts.append([v[at : at + length] for v in halves])
                at += length
            return cuts

        cuts_a = finish(total_a, [share] * 3)
        cuts_b = finish(total_b, [share] * (1 + groups) + [share_f])
    else:
        scatter = lambda v: lax.psum_scatter(v.astype(F32), ("dp", "seq"), scatter_dimension=0, tiled=True)
        found = grads_qkv[0][:, 3 * depth :].astype(F32)
        found = jnp.stack([found[:, :, :128], found[:, :, 128:256]], axis=1).transpose(2, 0, 1, 3)
        small = jnp.concatenate([found[v, :, :, :depth // 2].reshape(-1, 1) for v in range(8)], axis=1)
        small = jnp.concatenate([small.reshape(members, share, 8).transpose(0, 2, 1).reshape(members, -1),
                                 found[8, :, :, : deep // 2].reshape(members, share_f)], axis=1)
        small = scatter(small)[0]
        zero = jnp.zeros((model, half), BF)
        cuts_a, at = [], 0
        for length in sections_a[:3]:
            part = grads_qkv[0][:, at : at + length].reshape(-1, half)
            cuts_a.append([scatter(v) for v in by_parity(part, zero)])
            at += length
        halves = by_parity(grads_own[0], grads_oth[0])
        cuts_b, at = [], 0
        for length in sections_b:
            cuts_b.append([scatter(v[:, at : at + length].reshape(-1, half)) for v in halves])
            at += length
    cut_w = lambda h, p, w: cuts_a[p][h][:, 128 * w : 128 * w + 128]
    grad_qkv = jnp.concatenate([cut_w(h, p, w) for w in range(3) for h in range(2) for p in range(3)], axis=1)
    grad_proj = jnp.concatenate(cuts_b[0], axis=1)
    grad_inner = jnp.concatenate([cuts_b[1 + g][h] for h in range(2) for g in range(groups)], axis=1)
    grad_down = jnp.concatenate(cuts_b[1 + groups], axis=1)
    vector = [small[share * i : share * i + share] for i in range(8)]
    return (
        layer_out,
        grad_input,
        grad_qkv,
        vector[0],
        vector[1],
        grad_proj,
        vector[2],
        vector[3],
        vector[4],
        grad_inner,
        small[8 * share :],
        grad_down,
        vector[5],
        vector[6],
        vector[7],
    )


def solution(mesh):
    row, vec = P(("dp", "seq"), None), P(("dp", "seq"))
    wide = P(None, "dp", "seq", None)
    return jax.shard_map(
        body,
        mesh=mesh,
        in_specs=(wide, row, vec, vec, row, vec, vec, vec, row, vec, row, vec, vec, vec)
        + (P(None, "dp", None), P(None, "dp", "seq", None, None), P(None, "dp", None), wide),
        out_specs=(wide, wide, row, vec, vec, row, vec, vec, vec, row, vec, row, vec, vec, vec),
        check_vma=False,
    )
```

time: 565 us -> 422 us (0.75)
  waiting for transfers between devices: 189 us -> 103 us
  Pallas kernels: 216 us -> 184 us
  local copies, waits for them, and re-layouts: 38.5 us -> 20.5 us
  starting transfers between devices: 87.1 us -> 71.3 us
  other arithmetic: 24.8 us -> 37.4 us
    ppermute x42 -> x20, waiting for transfers between devices: 134 us -> 51.4 us  [the longest x12 38.8 us: shift_z(): lax.ppermute(value, 'dp', [(2 * z + x, (z + by) % size * 2 + x) for z in...]
    pallas_call x4 -> x8, Pallas kernels: 173 us -> 141 us  [the longest x3 57.8 us: attend_back(): pl.pallas_call(attend_back_kernel, grid=(1,), in_specs=[smem()] * 4 + [gr...]
    ppermute x42 -> x20, starting transfers between devices: 70.3 us -> 43.3 us  [the longest x8 27.2 us: swap(): lax.ppermute(value, 'dp', [(d, d ^ 1) for d in range(lax.axis_size('dp'))])]
    convert_element_type x9 -> x15, other arithmetic: 2.22 us -> 15.8 us  [the longest x12 13.2 us: add(): return (a.astype(F32) + b.astype(F32)).astype(BF)]
    ppermute x30 -> x32, starting transfers between devices: 16.8 us -> 28 us  [swap(): return lax.ppermute(value, 'seq', [(s, s ^ bit) for s in range(4)])]
    concatenate x13 -> x10, local copies, waits for them, and re-layouts: 10.2 us -> 2.29 us  [the longest x4 1.13 us: first_side(): return (jnp.concatenate([a, a_came]), jnp.concatenate([b, b_came]))]
    unnamed x91 -> x116, local copies, waits for them, and re-layouts: 18.3 us -> 11.5 us
    ppermute x30 -> x32, waiting for transfers between devices: 55.9 us -> 51.7 us  [swap(): return lax.ppermute(value, 'seq', [(s, s ^ bit) for s in range(4)])]
  transfers between devices with their start and end apart: 72 -> 52, of which waited for: 34 -> 14; matrix products, arithmetic and copies ran while one was open for 9% -> 12% of each run, Pallas kernels for 29% -> 26%
where the time goes in v2:
time: 422 us; the launch traced here: 418 us
  Pallas kernels  184 us (44%)
  waiting for transfers between devices  103 us (24%)
  starting transfers between devices  71.3 us (17%)
  other arithmetic  37.4 us (9%)
  local copies, waits for them, and re-layouts  20.5 us (5%)
    pallas_call x3, Pallas kernels, attend_back(): pl.pallas_call(attend_back_kernel, grid=(1,), in_specs=[smem()] * 4 + [gr...  57.8 us
    ppermute x32, waiting for transfers between devices, swap(): return lax.ppermute(value, 'seq', [(s, s ^ bit) for s in range(4)])  51.7 us
    pallas_call x1, Pallas kernels, feed_forward(): pl.pallas_call(lambda *refs: ffn_kernel(plan, len(own_pieces), len(ctx),...  40.2 us
    ppermute x12, waiting for transfers between devices, shift_z(): lax.ppermute(value, 'dp', [(2 * z + x, (z + by) % size * 2 + x) for z in...  38.8 us
    pallas_call x2, Pallas kernels, attend(): pl.pallas_call(attend_kernel, grid=(1,), in_specs=[smem()] * 4 + [pl.Bloc...  30.3 us
    ppermute x32, starting transfers between devices, swap(): return lax.ppermute(value, 'seq', [(s, s ^ bit) for s in range(4)])  28 us
    ppermute x8, starting transfers between devices, swap(): lax.ppermute(value, 'dp', [(d, d ^ 1) for d in range(lax.axis_size('dp'))])  27.2 us
    pallas_call x1, Pallas kernels, weight_grads(): pl.pallas_call(lambda *refs: weight_grads_kernel(plan, len(pieces), *refs...  22.3 us
  transfers between devices with their start and end apart: 52, of which 14 were waited for; matrix products, arithmetic and copies ran while one was open for 12% of the time, Pallas kernels for 26%

profile of v2, /device:TPU:0, one launch (start us, length us, event | category | flops | bytes accessed | tf_op | source)
XLA Modules:
  0.0 418.1 jit_solution(12881053882040209226)
XLA Ops:
  3.9 1.9 pack.1
  6.3 1.5 broadcast_select_fusion
  7.8 2.6 collective-permute-start.5
  18.1 10.5 %collective-permute-done.5 = bf16[512,768]{1,0:T(8,128)(2,1)S(1)} collective-permute-done((bf16[512,768]{1,0:T(8,128)(2,1)S(1)}, bf16[512,768]{1,0:T(8,128)(2,1)S(1)}, u32[]{:S(2)}, u32[]{:S(2)}) %collective-permute-start.5) | collective-permute-done | bytes 786464 | tf_op jit(solution)/shard_map/ppermute | solution.py:56
  30.3 3.8 collective-permute-start.4
  38.3 7.6 %collective-permute-done.3 = bf16[160,384]{1,0:T(8,128)(2,1)} collective-permute-done((bf16[160,384]{1,0:T(8,128)(2,1)}, bf16[160,384]{1,0:T(8,128)(2,1)}, u32[]{:S(2)}, u32[]{:S(2)}) %collective-permute-start.3) | collective-permute-done | bytes 122912 | tf_op jit(solution)/shard_map/ppermute | solution.py:61
  47.4 1.6 collective-permute-start.10
  48.9 1.5 collective-permute-start.12
  52.7 2.2 collective-permute-start.7
  55.0 3.7 maximum_select_fusion
  60.0 4.0 collective-permute-done.16
  65.8 15.0 %collective-permute-done.8 = bf16[432,384]{1,0:T(8,128)(2,1)S(1)} collective-permute-done((bf16[432,384]{1,0:T(8,128)(2,1)S(1)}, bf16[432,384]{1,0:T(8,128)(2,1)S(1)}, u32[]{:S(2)}, u32[]{:S(2)}) %collective-permute-start.8) | collective-permute-done | bytes 331808 | tf_op jit(solution)/shard_map/ppermute | solution.py:61
  82.9 10.5 %project_qkv.1 = (bf16[2048,1152]{1,0:T(8,128)(2,1)}, bf16[16,48,1152]{2,1,0:T(8,128)(2,1)}, f32[16,768]{1,0:T(8,128)}) custom-call(s32[4]{0:T(128)} %pad_add_fusion.2.meta.refs_0_, bf16[8,80,384]{2,1,0:T(8,128)(2,1)} %copy-done.24, bf16[8,80,384]{2,1,0:T(8,128)(2,1)} %copy-done.37, bf16[8,80,384]{2,1,0:T(8,128)(2,1)} %copy-done.25, ...), custom_call_target="tpu_custom_call" | custom-call | flops 3623878656 | bytes 7864320 | tf_op jit(solution)/shard_map/project_qkv/pallas_call | solution.py:240
  93.4 12.1 %attend.2 = (bf16[2,1024,128]{2,1,0:T(8,128)(2,1)}, f32[2,2048]{1,0:T(2,128)}) custom-call(s32[4]{0:T(128)} %pad_add_fusion.2.meta.refs_0_, s32[8]{0:T(128)} %get-tuple-element.155.lo_ref, s32[8]{0:T(128)} %get-tuple-element.156.n_ref, s32[2]{0:T(128)} %fusion.38.glob_ref, bf16[2048,1152]{1,0:T(8,128)(2,1)} %get-tuple-element.97.qkv_ref, ...), custom_call_target="tpu_custom_call" | custom-call | flops 5872025600 | bytes 2621440 | tf_op jit(solution)/shard_map/attend/pallas_call | solution.py:367
  107.4 4.5 %collective-permute-start.19 = (bf16[8,256,384]{2,1,0:T(8,128)(2,1)}, bf16[8,256,384]{2,1,0:T(8,128)(2,1)}, u32[]{:S(2)}, u32[]{:S(2)}) collective-permute-start(bf16[8,256,384]{2,1,0:T(8,128)(2,1)} %constant_dynamic-update-slice_fusion.25.refs_3_), channel_id=1, source_target_pairs={{0,4},{4,0},{8,12},{12,8},{16,20},{20,16},{24,28},{28,24},{1,5},{5... | collective-permute-start | bytes 4718600 | tf_op jit(solution)/shard_map/ppermute | solution.py:54
  112.2 1.9 collective-permute-start.17
  114.3 18.3 %attend.3 = (bf16[2,1024,256]{2,1,0:T(8,128)(2,1)}, f32[4,2048]{1,0:T(4,128)}) custom-call(s32[4]{0:T(128)} %pad_add_fusion.2.meta.refs_0_, s32[8]{0:T(128)} %get-tuple-element.155.lo_ref, s32[8]{0:T(128)} %get-tuple-element.156.n_ref, s32[2]{0:T(128)} %fusion.38.glob_ref, bf16[2048,1152]{1,0:T(8,128)(2,1)} %get-tuple-element.97.qkv_ref, ...), custom_call_target="tpu_custom_call" | custom-call | flops 11744051200 | bytes 5242880 | tf_op jit(solution)/shard_map/attend/pallas_call | solution.py:367
  132.5 11.8 %collective-permute-done.19.refs_4_ = bf16[8,256,384]{2,1,0:T(8,128)(2,1)} collective-permute-done((bf16[8,256,384]{2,1,0:T(8,128)(2,1)}, bf16[8,256,384]{2,1,0:T(8,128)(2,1)}, u32[]{:S(2)}, u32[]{:S(2)}) %collective-permute-start.19) | collective-permute-done | bytes 1572896 | tf_op jit(solution)/shard_map/ppermute | solution.py:54
  144.4 3.6 collective-permute-start.26
  148.6 17.6 %collective-permute-done.26 = bf16[512,768]{1,0:T(8,128)(2,1)S(1)} collective-permute-done((bf16[512,768]{1,0:T(8,128)(2,1)S(1)}, bf16[512,768]{1,0:T(8,128)(2,1)S(1)}, u32[]{:S(2)}, u32[]{:S(2)}) %collective-permute-start.26) | collective-permute-done | bytes 786464 | tf_op jit(solution)/shard_map/ppermute | solution.py:56
  166.3 1.4 maximum_select_fusion.3
  169.4 40.2 %feed_forward.1 = (bf16[1024,768]{1,0:T(8,128)(2,1)}, bf16[1024,3072]{1,0:T(8,128)(2,1)}, bf16[1024,768]{1,0:T(8,128)(2,1)}, bf16[1024,768]{1,0:T(8,128)(2,1)}, ...) custom-call(s32[4]{0:T(128)} %pad_add_fusion.2.meta.refs_0_, ...), custom_call_target="tpu_custom_call" | custom-call | flops 21743271936 | bytes 40894464 | tf_op jit(solution)/shard_map/feed_forward/pallas_call | solution.py:623
  209.6 22.3 %weight_grads.1 = (bf16[8,176,384]{2,1,0:T(8,128)(2,1)}, bf16[8,176,384]{2,1,0:T(8,128)(2,1)}, bf16[8,256,384]{2,1,0:T(8,128)(2,1)}, bf16[8,256,384]{2,1,0:T(8,1...) custom-call(s32[4]{0:T(128)} %pad_add_fusion.2.meta.refs_0_, ...), custom_call_target="tpu_custom_call" | custom-call | flops 10871635968 | bytes 18874368 | tf_op jit(solution)/shard_map/weight_grads/pallas_call | solution.py:697
  234.3 1.8 collective-permute-start.27
  236.2 2.2 collective-permute-done.28
  239.7 1.8 collective-permute-start.32
  241.5 1.5 add_convert_fusion.2
  243.3 19.1 %attend_back.3.refs_2_.refs_0_ = bf16[2048,384]{1,0:T(8,128)(2,1)} custom-call(s32[4]{0:T(128)} %pad_add_fusion.2.meta.refs_0_, s32[8]{0:T(128)} %get-tuple-element.155.lo_ref, s32[8]{0:T(128)} %get-tuple-element.156.n_ref, s32[2]{0:T(128)} %fusion.38.glob_ref, bf16[2048,1152]{1,0:T(8,128)(2,1)} %get-tuple-element.97.qkv_ref, ...), custom_call_target="tpu_custom_call" | custom-call | flops 12582912000 | bytes 5242880 | tf_op jit(solution)/shard_map/attend_back/pallas_call | solution.py:464
  263.6 2.4 add_convert_fusion.4
  266.2 1.8 add_convert_fusion.1
  268.0 2.8 maximum_select_fusion.4
  270.8 19.4 %attend_back.4.refs_3_.refs_1_ = bf16[2048,384]{1,0:T(8,128)(2,1)} custom-call(s32[4]{0:T(128)} %pad_add_fusion.2.meta.refs_0_, s32[8]{0:T(128)} %get-tuple-element.155.lo_ref, s32[8]{0:T(128)} %get-tuple-element.156.n_ref, s32[2]{0:T(128)} %fusion.38.glob_ref, bf16[2048,1152]{1,0:T(8,128)(2,1)} %get-tuple-element.97.qkv_ref, ...), custom_call_target="tpu_custom_call" | custom-call | flops 12582912000 | bytes 5242880 | tf_op jit(solution)/shard_map/attend_back/pallas_call | solution.py:464
  290.2 1.5 add_convert_fusion.3
  291.8 11.9 %collective-permute-start.34 = (bf16[4,176,384]{2,1,0:T(8,128)(2,1)S(1)}, bf16[4,176,384]{2,1,0:T(8,128)(2,1)}, u32[]{:S(2)}, u32[]{:S(2)}) collective-permute-start(bf16[4,176,384]{2,1,0:T(8,128)(2,1)S(1)} %slice.573), channel_id=1, source_target_pairs={{0,4},{4,0},{8,12},{12,8},{16,20},{20,16},{24,28},{28,24},{1,5},{5... | collective-permute-start | bytes 1622024 | tf_op jit(solution)/shard_map/ppermute | solution.py:54
  303.7 1.8 add_convert_fusion
  306.4 5.7 %collective-permute-start.36 = (bf16[4,256,384]{2,1,0:T(8,128)(2,1)}, bf16[4,256,384]{2,1,0:T(8,128)(2,1)}, u32[]{:S(2)}, u32[]{:S(2)}) collective-permute-start(bf16[4,256,384]{2,1,0:T(8,128)(2,1)} %slice.574), channel_id=1, source_target_pairs={{0,2},{1,3},{2,0},{3,1},{4,6},{5,7},{6,4},{7,5},{8,10},{9,11},{10,... | collective-permute-start | bytes 2359304 | tf_op jit(solution)/shard_map/ppermute | solution.py:56
  312.1 19.3 %attend_back.5.refs_4_.refs_2_ = bf16[2048,384]{1,0:T(8,128)(2,1)} custom-call(s32[4]{0:T(128)} %pad_add_fusion.2.meta.refs_0_, s32[8]{0:T(128)} %get-tuple-element.155.lo_ref, s32[8]{0:T(128)} %get-tuple-element.156.n_ref, s32[2]{0:T(128)} %fusion.38.glob_ref, bf16[2048,1152]{1,0:T(8,128)(2,1)} %get-tuple-element.97.qkv_ref, ...), custom_call_target="tpu_custom_call" | custom-call | flops 12582912000 | bytes 5242880 | tf_op jit(solution)/shard_map/attend_back/pallas_call | solution.py:464
  333.9 11.2 %qkv_grads.1 = (bf16[8,80,384]{2,1,0:T(8,128)(2,1)}, bf16[8,80,384]{2,1,0:T(8,128)(2,1)}, bf16[8,80,384]{2,1,0:T(8,128)(2,1)}, bf16[8,80,384]{2,1,0:T(8,128)(2,1)}) custom-call(s32[4]{0:T(128)} %pad_add_fusion.2.meta.refs_0_, bf16[2048,768]{1,0:T(8,128)(2,1)} %bitcast.112, bf16[2048,384]{1,0:T(8,128)(2,1)} %attend_back.3.refs_2_.refs_0_, ...), custom_call_target="tpu_custom_call" | custom-call | flops 3623878656 | bytes 7864320 | tf_op jit(solution)/shard_map/qkv_grads/pallas_call | solution.py:766
  345.1 6.2 %collective-permute-start.39 = (bf16[8,80,384]{2,1,0:T(8,128)(2,1)}, bf16[8,80,384]{2,1,0:T(8,128)(2,1)S(1)}, u32[]{:S(2)}, u32[]{:S(2)}) collective-permute-start(bf16[8,80,384]{2,1,0:T(8,128)(2,1)} %get-tuple-element.140), channel_id=1, source_target_pairs={{0,4},{4,0},{8,12},{12,8},{16,20},{20,16},{24,28},{28,24},{1,5},{5... | collective-permute-start | bytes 1474568 | tf_op jit(solution)/shard_map/ppermute | solution.py:54
  351.3 2.0 collective-permute-start.41
  354.1 2.5 collective-permute-start.45
  356.7 1.5 collective-permute-start.44
  358.1 9.5 %input_grads.1 = bf16[2,1024,768]{2,1,0:T(8,128)(2,1)} custom-call(s32[4]{0:T(128)} %pad_add_fusion.2.meta.refs_0_, bf16[2048,384]{1,0:T(8,128)(2,1)} %attend_back.3.refs_2_.refs_0_, bf16[2048,384]{1,0:T(8,128)(2,1)} %attend_back.4.refs_3_.refs_1_, bf16[2048,384]{1,0:T(8,128)(2,1)} %attend_back.5.refs_4_.refs_2_, ...), custom_call_target="tpu_custom_call" | custom-call | flops 3623878656 | bytes 7864320 | tf_op jit(solution)/shard_map/input_grads/pallas_call | solution.py:805
  367.6 1.6 slice_bitcast_fusion
  371.2 15.4 %collective-permute-done.44 = bf16[432,384]{1,0:T(8,128)(2,1)S(1)} collective-permute-done((bf16[432,384]{1,0:T(8,128)(2,1)S(1)}, bf16[432,384]{1,0:T(8,128)(2,1)S(1)}, u32[]{:S(2)}, u32[]{:S(2)}) %collective-permute-start.44) | collective-permute-done | bytes 331808 | tf_op jit(solution)/shard_map/ppermute | solution.py:61
  388.0 1.7 collective-permute-start.42
  395.5 2.1 collective-permute-start.46
  398.2 14.9 %collective-permute-done.38 = bf16[512,768]{1,0:T(8,128)(2,1)S(1)} collective-permute-done((bf16[512,768]{1,0:T(8,128)(2,1)S(1)}, bf16[512,768]{1,0:T(8,128)(2,1)S(1)}, u32[]{:S(2)}, u32[]{:S(2)}) %collective-permute-start.38) | collective-permute-done | bytes 786464 | tf_op jit(solution)/shard_map/ppermute | solution.py:56
  (288 shorter events, 54.6 us)
Async XLA Ops:
  2.1 12.7 %collective-permute-start.1 = (bf16[16,128]{1,0:T(8,128)(2,1)S(1)}, bf16[16,128]{1,0:T(8,128)(2,1)S(1)}, u32[]{:S(2)}, u32[]{:S(2)}) collective-permute-start(bf16[16,128]{1,0:T(8,128)(2,1)S(1)} %fusion.34), channel_id=1, source_target_pairs={{0,1},{1,0},{2,3},{3,2},{4,5},{5,4},{6,7},{7,6},{8,9},{9,8},{10,11... | collective-permute-start | bytes 12296 | tf_op jit(solution)/shard_map/ppermute | solution.py:56
  3.3 10.6 %collective-permute-start.15 = (s32[2,3,32,3]{2,1,3,0:T(4,128)S(1)}, s32[2,3,32,3]{2,1,3,0:T(4,128)S(1)}, u32[]{:S(2)}, u32[]{:S(2)}) collective-permute-start(s32[2,3,32,3]{2,1,3,0:T(4,128)S(1)} %bitcast.130), channel_id=1, source_target_pairs={{0,1},{1,0},{2,3},{3,2},{4,5},{5,4},{6,7},{7,6},{8,9},{9,8},{10,11... | collective-permute-start | bytes 6920 | tf_op jit(solution)/shard_map/ppermute | solution.py:56
  5.8 9.0 %collective-permute-start = (bf16[288,384]{1,0:T(8,128)(2,1)}, bf16[288,384]{1,0:T(8,128)(2,1)S(1)}, u32[]{:S(2)}, u32[]{:S(2)}) collective-permute-start(bf16[288,384]{1,0:T(8,128)(2,1)} %get-tuple-element.85), channel_id=1, source_target_pairs={{0,1},{1,0},{2,3},{3,2},{4,5},{5,4},{6,7},{7,6},{8,9},{9,8},{10,11... | collective-permute-start | bytes 663560 | tf_op jit(solution)/shard_map/ppermute | solution.py:56
  7.8 20.8 %collective-permute-start.5 = (bf16[512,768]{1,0:T(8,128)(2,1)S(1)}, bf16[512,768]{1,0:T(8,128)(2,1)S(1)}, u32[]{:S(2)}, u32[]{:S(2)}) collective-permute-start(bf16[512,768]{1,0:T(8,128)(2,1)S(1)} %get-tuple-element.164), channel_id=1, source_target_pairs={{0,2},{1,3},{2,0},{3,1},{4,6},{5,7},{6,4},{7,5},{8,10},{9,11},{10,... | collective-permute-start | bytes 2359304 | tf_op jit(solution)/shard_map/ppermute | solution.py:56
  28.9 18.5 %collective-permute-start.6 = (bf16[2,512,768]{2,1,0:T(8,128)(2,1)S(1)}, bf16[2,512,768]{2,1,0:T(8,128)(2,1)}, u32[]{:S(2)}, u32[]{:S(2)}) collective-permute-start(bf16[2,512,768]{2,1,0:T(8,128)(2,1)S(1)} %maximum_select_fusion.1), channel_id=1, source_target_pairs={{0,1},{1,0},{2,3},{3,2},{4,5},{5,4},{6,7},{7,6},{8,9},{9,8},{10,11... | collective-permute-start | bytes 4718600 | tf_op jit(solution)/shard_map/ppermute | solution.py:56
  30.3 7.9 %collective-permute-start.4 = (bf16[160,384]{1,0:T(8,128)(2,1)}, bf16[160,384]{1,0:T(8,128)(2,1)}, u32[]{:S(2)}, u32[]{:S(2)}) collective-permute-start(bf16[160,384]{1,0:T(8,128)(2,1)} %constant_dynamic-update-slice_fusion.12), channel_id=1, source_target_pairs={{0,24},{4,28},{8,0},{12,4},{16,8},{20,12},{24,16},{28,20},{1,25},{... | collective-permute-start | bytes 368648 | tf_op jit(solution)/shard_map/ppermute | solution.py:61
  34.2 11.7 %collective-permute-start.3 = (bf16[160,384]{1,0:T(8,128)(2,1)}, bf16[160,384]{1,0:T(8,128)(2,1)}, u32[]{:S(2)}, u32[]{:S(2)}) collective-permute-start(bf16[160,384]{1,0:T(8,128)(2,1)} %constant_dynamic-update-slice_fusion.12), channel_id=1, source_target_pairs={{0,16},{4,20},{8,24},{12,28},{16,0},{20,4},{24,8},{28,12},{1,17},{... | collective-permute-start | bytes 368648 | tf_op jit(solution)/shard_map/ppermute | solution.py:61
  34.2 11.7 %collective-permute-start.2 = (bf16[160,384]{1,0:T(8,128)(2,1)}, bf16[160,384]{1,0:T(8,128)(2,1)}, u32[]{:S(2)}, u32[]{:S(2)}) collective-permute-start(bf16[160,384]{1,0:T(8,128)(2,1)} %constant_dynamic-update-slice_fusion.12), channel_id=1, source_target_pairs={{0,8},{4,12},{8,16},{12,20},{16,24},{20,28},{24,0},{28,4},{1,9},{5... | collective-permute-start | bytes 368648 | tf_op jit(solution)/shard_map/ppermute | solution.py:61
  47.4 12.0 %collective-permute-start.10 = (bf16[4,80,384]{2,1,0:T(8,128)(2,1)S(1)}, bf16[4,80,384]{2,1,0:T(8,128)(2,1)S(1)}, u32[]{:S(2)}, u32[]{:S(2)}) collective-permute-start(bf16[4,80,384]{2,1,0:T(8,128)(2,1)S(1)} %get-tuple-element.86), channel_id=1, source_target_pairs={{0,4},{4,0},{8,12},{12,8},{16,20},{20,16},{24,28},{28,24},{1,5},{5... | collective-permute-start | bytes 737288 | tf_op jit(solution)/shard_map/ppermute | solution.py:54
  48.9 9.8 %collective-permute-start.12 = (bf16[4,80,384]{2,1,0:T(8,128)(2,1)S(1)}, bf16[4,80,384]{2,1,0:T(8,128)(2,1)S(1)}, u32[]{:S(2)}, u32[]{:S(2)}) collective-permute-start(bf16[4,80,384]{2,1,0:T(8,128)(2,1)S(1)} %get-tuple-element.87), channel_id=1, source_target_pairs={{0,2},{1,3},{2,0},{3,1},{4,6},{5,7},{6,4},{7,5},{8,10},{9,11},{10,... | collective-permute-start | bytes 737288 | tf_op jit(solution)/shard_map/ppermute | solution.py:56
  50.5 15.3 %collective-permute-start.9 = (bf16[432,384]{1,0:T(8,128)(2,1)S(1)}, bf16[432,384]{1,0:T(8,128)(2,1)S(1)}, u32[]{:S(2)}, u32[]{:S(2)}) collective-permute-start(bf16[432,384]{1,0:T(8,128)(2,1)S(1)} %constant_dynamic-update-slice_fusion), channel_id=1, source_target_pairs={{0,24},{4,28},{8,0},{12,4},{16,8},{20,12},{24,16},{28,20},{1,25},{... | collective-permute-start | bytes 995336 | tf_op jit(solution)/shard_map/ppermute | solution.py:61
  51.8 29.0 %collective-permute-start.8 = (bf16[432,384]{1,0:T(8,128)(2,1)S(1)}, bf16[432,384]{1,0:T(8,128)(2,1)S(1)}, u32[]{:S(2)}, u32[]{:S(2)}) collective-permute-start(bf16[432,384]{1,0:T(8,128)(2,1)S(1)} %constant_dynamic-update-slice_fusion), channel_id=1, source_target_pairs={{0,16},{4,20},{8,24},{12,28},{16,0},{20,4},{24,8},{28,12},{1,17},{... | collective-permute-start | bytes 995336 | tf_op jit(solution)/shard_map/ppermute | solution.py:61
  52.7 28.0 %collective-permute-start.7 = (bf16[432,384]{1,0:T(8,128)(2,1)S(1)}, bf16[432,384]{1,0:T(8,128)(2,1)S(1)}, u32[]{:S(2)}, u32[]{:S(2)}) collective-permute-start(bf16[432,384]{1,0:T(8,128)(2,1)S(1)} %constant_dynamic-update-slice_fusion), channel_id=1, source_target_pairs={{0,8},{4,12},{8,16},{12,20},{16,24},{20,28},{24,0},{28,4},{1,9},{5... | collective-permute-start | bytes 995336 | tf_op jit(solution)/shard_map/ppermute | solution.py:61
  58.7 5.2 %collective-permute-start.16 = (s32[6,32,3]{2,1,0:T(8,128)S(1)}, s32[6,32,3]{2,1,0:T(8,128)S(1)}, u32[]{:S(2)}, u32[]{:S(2)}) collective-permute-start(s32[6,32,3]{2,1,0:T(8,128)S(1)} %copy-done.26), channel_id=1, source_target_pairs={{0,2},{1,3},{2,0},{3,1},{4,6},{5,7},{6,4},{7,5},{8,10},{9,11},{10,... | collective-permute-start | bytes 6920 | tf_op jit(solution)/shard_map/ppermute | solution.py:56
  59.4 21.6 %collective-permute-start.13 = (bf16[8,80,384]{2,1,0:T(8,128)(2,1)S(1)}, bf16[8,80,384]{2,1,0:T(8,128)(2,1)S(1)}, u32[]{:S(2)}, u32[]{:S(2)}) collective-permute-start(bf16[8,80,384]{2,1,0:T(8,128)(2,1)S(1)} %constant_dynamic-update-slice_fusion.21.refs_3_), channel_id=1, source_target_pairs={{0,4},{4,0},{8,12},{12,8},{16,20},{20,16},{24,28},{28,24},{1,5},{5... | collective-permute-start | bytes 1474568 | tf_op jit(solution)/shard_map/ppermute | solution.py:54
  64.0 17.0 %collective-permute-start.11 = (bf16[8,80,384]{2,1,0:T(8,128)(2,1)S(1)}, bf16[8,80,384]{2,1,0:T(8,128)(2,1)S(1)}, u32[]{:S(2)}, u32[]{:S(2)}) collective-permute-start(bf16[8,80,384]{2,1,0:T(8,128)(2,1)S(1)} %constant_dynamic-update-slice_fusion.19.refs_1_), channel_id=1, source_target_pairs={{0,2},{1,3},{2,0},{3,1},{4,6},{5,7},{6,4},{7,5},{8,10},{9,11},{10,... | collective-permute-start | bytes 1474568 | tf_op jit(solution)/shard_map/ppermute | solution.py:56
  81.8 30.2 %collective-permute-start.14 = (bf16[4,176,384]{2,1,0:T(8,128)(2,1)S(1)}, bf16[4,176,384]{2,1,0:T(8,128)(2,1)S(1)}, u32[]{:S(2)}, u32[]{:S(2)}) collective-permute-start(bf16[4,176,384]{2,1,0:T(8,128)(2,1)S(1)} %pad_maximum_fusion.3), channel_id=1, source_target_pairs={{0,4},{4,0},{8,12},{12,8},{16,20},{20,16},{24,28},{28,24},{1,5},{5... | collective-permute-start | bytes 1622024 | tf_op jit(solution)/shard_map/ppermute | solution.py:54
  82.4 24.1 %collective-permute-start.18 = (bf16[4,256,384]{2,1,0:T(8,128)(2,1)S(1)}, bf16[4,256,384]{2,1,0:T(8,128)(2,1)S(1)}, u32[]{:S(2)}, u32[]{:S(2)}) collective-permute-start(bf16[4,256,384]{2,1,0:T(8,128)(2,1)S(1)} %pad_maximum_fusion), channel_id=1, source_target_pairs={{0,2},{1,3},{2,0},{3,1},{4,6},{5,7},{6,4},{7,5},{8,10},{9,11},{10,... | collective-permute-start | bytes 2359304 | tf_op jit(solution)/shard_map/ppermute | solution.py:56
  107.4 36.9 %collective-permute-start.19 = (bf16[8,256,384]{2,1,0:T(8,128)(2,1)}, bf16[8,256,384]{2,1,0:T(8,128)(2,1)}, u32[]{:S(2)}, u32[]{:S(2)}) collective-permute-start(bf16[8,256,384]{2,1,0:T(8,128)(2,1)} %constant_dynamic-update-slice_fusion.25.refs_3_), channel_id=1, source_target_pairs={{0,4},{4,0},{8,12},{12,8},{16,20},{20,16},{24,28},{28,24},{1,5},{5... | collective-permute-start | bytes 4718600 | tf_op jit(solution)/shard_map/ppermute | solution.py:54
  111.9 36.4 %collective-permute-start.25 = (bf16[1024,128]{1,0:T(8,128)(2,1)S(1)}, bf16[1024,128]{1,0:T(8,128)(2,1)}, u32[]{:S(2)}, u32[]{:S(2)}) collective-permute-start(bf16[1024,128]{1,0:T(8,128)(2,1)S(1)} %slice_bitcast_fusion.3), channel_id=1, source_target_pairs={{0,1},{1,0},{2,3},{3,2},{4,5},{5,4},{6,7},{7,6},{8,9},{9,8},{10,11... | collective-permute-start | bytes 786440 | tf_op jit(solution)/shard_map/ppermute | solution.py:56
  112.2 35.9 %collective-permute-start.17 = (bf16[8,176,384]{2,1,0:T(8,128)(2,1)S(1)}, bf16[8,176,384]{2,1,0:T(8,128)(2,1)}, u32[]{:S(2)}, u32[]{:S(2)}) collective-permute-start(bf16[8,176,384]{2,1,0:T(8,128)(2,1)S(1)} %constant_dynamic-update-slice_fusion.23.refs_1_), channel_id=1, source_target_pairs={{0,2},{1,3},{2,0},{3,1},{4,6},{5,7},{6,4},{7,5},{8,10},{9,11},{10,... | collective-permute-start | bytes 3244040 | tf_op jit(solution)/shard_map/ppermute | solution.py:56
  114.1 54.1 %collective-permute-start.22 = (bf16[8,256,384]{2,1,0:T(8,128)(2,1)}, bf16[8,256,384]{2,1,0:T(8,128)(2,1)}, u32[]{:S(2)}, u32[]{:S(2)}) collective-permute-start(bf16[8,256,384]{2,1,0:T(8,128)(2,1)} %constant_dynamic-update-slice_fusion.25.refs_3_), channel_id=1, source_target_pairs={{0,1},{1,0},{2,3},{3,2},{4,5},{5,4},{6,7},{7,6},{8,9},{9,8},{10,11... | collective-permute-start | bytes 4718600 | tf_op jit(solution)/shard_map/ppermute | solution.py:56
  144.3 23.9 %collective-permute-start.23 = (bf16[8,256,384]{2,1,0:T(8,128)(2,1)}, bf16[8,256,384]{2,1,0:T(8,128)(2,1)}, u32[]{:S(2)}, u32[]{:S(2)}) collective-permute-start(bf16[8,256,384]{2,1,0:T(8,128)(2,1)} %collective-permute-done.19.refs_4_), channel_id=1, source_target_pairs={{0,1},{1,0},{2,3},{3,2},{4,5},{5,4},{6,7},{7,6},{8,9},{9,8},{10,11... | collective-permute-start | bytes 4718600 | tf_op jit(solution)/shard_map/ppermute | solution.py:56
  144.4 21.8 %collective-permute-start.26 = (bf16[512,768]{1,0:T(8,128)(2,1)S(1)}, bf16[512,768]{1,0:T(8,128)(2,1)S(1)}, u32[]{:S(2)}, u32[]{:S(2)}) collective-permute-start(bf16[512,768]{1,0:T(8,128)(2,1)S(1)} %get-tuple-element.101), channel_id=1, source_target_pairs={{0,2},{1,3},{2,0},{3,1},{4,6},{5,7},{6,4},{7,5},{8,10},{9,11},{10,... | collective-permute-start | bytes 2359304 | tf_op jit(solution)/shard_map/ppermute | solution.py:56
  148.1 20.1 %collective-permute-start.20 = (bf16[8,176,384]{2,1,0:T(8,128)(2,1)S(1)}, bf16[8,176,384]{2,1,0:T(8,128)(2,1)S(1)}, u32[]{:S(2)}, u32[]{:S(2)}) collective-permute-start(bf16[8,176,384]{2,1,0:T(8,128)(2,1)S(1)} %constant_dynamic-update-slice_fusion.23.refs_1_), channel_id=1, source_target_pairs={{0,1},{1,0},{2,3},{3,2},{4,5},{5,4},{6,7},{7,6},{8,9},{9,8},{10,11... | collective-permute-start | bytes 3244040 | tf_op jit(solution)/shard_map/ppermute | solution.py:56
  148.3 19.9 %collective-permute-start.21 = (bf16[8,176,384]{2,1,0:T(8,128)(2,1)}, bf16[8,176,384]{2,1,0:T(8,128)(2,1)}, u32[]{:S(2)}, u32[]{:S(2)}) collective-permute-start(bf16[8,176,384]{2,1,0:T(8,128)(2,1)} %collective-permute-done.17.refs_2_), channel_id=1, source_target_pairs={{0,1},{1,0},{2,3},{3,2},{4,5},{5,4},{6,7},{7,6},{8,9},{9,8},{10,11... | collective-permute-start | bytes 3244040 | tf_op jit(solution)/shard_map/ppermute | solution.py:56
  232.0 7.8 %collective-permute-start.29 = (bf16[8,256,384]{2,1,0:T(8,128)(2,1)}, bf16[8,256,384]{2,1,0:T(8,128)(2,1)S(1)}, u32[]{:S(2)}, u32[]{:S(2)}) collective-permute-start(bf16[8,256,384]{2,1,0:T(8,128)(2,1)} %get-tuple-element.115), channel_id=1, source_target_pairs={{0,1},{1,0},{2,3},{3,2},{4,5},{5,4},{6,7},{7,6},{8,9},{9,8},{10,11... | collective-permute-start | bytes 4718600 | tf_op jit(solution)/shard_map/ppermute | solution.py:56
  232.2 6.1 %collective-permute-start.28 = (bf16[8,176,384]{2,1,0:T(8,128)(2,1)}, bf16[8,176,384]{2,1,0:T(8,128)(2,1)S(1)}, u32[]{:S(2)}, u32[]{:S(2)}) collective-permute-start(bf16[8,176,384]{2,1,0:T(8,128)(2,1)} %get-tuple-element.113), channel_id=1, source_target_pairs={{0,1},{1,0},{2,3},{3,2},{4,5},{5,4},{6,7},{7,6},{8,9},{9,8},{10,11... | collective-permute-start | bytes 3244040 | tf_op jit(solution)/shard_map/ppermute | solution.py:56
  233.2 9.9 %collective-permute-start.30 = (bf16[1024,384]{1,0:T(8,128)(2,1)}, bf16[1024,384]{1,0:T(8,128)(2,1)}, u32[]{:S(2)}, u32[]{:S(2)}) collective-permute-start(bf16[1024,384]{1,0:T(8,128)(2,1)} %get-tuple-element.117), channel_id=1, source_target_pairs={{0,1},{1,0},{2,3},{3,2},{4,5},{5,4},{6,7},{7,6},{8,9},{9,8},{10,11... | collective-permute-start | bytes 2359304 | tf_op jit(solution)/shard_map/ppermute | solution.py:56
  234.3 28.2 %collective-permute-start.27 = (bf16[512,768]{1,0:T(8,128)(2,1)}, bf16[512,768]{1,0:T(8,128)(2,1)}, u32[]{:S(2)}, u32[]{:S(2)}) collective-permute-start(bf16[512,768]{1,0:T(8,128)(2,1)} %get-tuple-element.160), channel_id=1, source_target_pairs={{0,2},{1,3},{2,0},{3,1},{4,6},{5,7},{6,4},{7,5},{8,10},{9,11},{10,... | collective-permute-start | bytes 2359304 | tf_op jit(solution)/shard_map/ppermute | solution.py:56
  236.1 26.4 %collective-permute-start.31 = (bf16[8,176,384]{2,1,0:T(8,128)(2,1)}, bf16[8,176,384]{2,1,0:T(8,128)(2,1)S(1)}, u32[]{:S(2)}, u32[]{:S(2)}) collective-permute-start(bf16[8,176,384]{2,1,0:T(8,128)(2,1)} %get-tuple-element.122), channel_id=1, source_target_pairs={{0,1},{1,0},{2,3},{3,2},{4,5},{5,4},{6,7},{7,6},{8,9},{9,8},{10,11... | collective-permute-start | bytes 3244040 | tf_op jit(solution)/shard_map/ppermute | solution.py:56
  238.3 24.2 %collective-permute-start.33 = (bf16[8,256,384]{2,1,0:T(8,128)(2,1)}, bf16[8,256,384]{2,1,0:T(8,128)(2,1)S(1)}, u32[]{:S(2)}, u32[]{:S(2)}) collective-permute-start(bf16[8,256,384]{2,1,0:T(8,128)(2,1)} %get-tuple-element.125), channel_id=1, source_target_pairs={{0,1},{1,0},{2,3},{3,2},{4,5},{5,4},{6,7},{7,6},{8,9},{9,8},{10,11... | collective-permute-start | bytes 4718600 | tf_op jit(solution)/shard_map/ppermute | solution.py:56
  239.7 50.4 %collective-permute-start.32 = (bf16[8,176,384]{2,1,0:T(8,128)(2,1)}, bf16[8,176,384]{2,1,0:T(8,128)(2,1)}, u32[]{:S(2)}, u32[]{:S(2)}) collective-permute-start(bf16[8,176,384]{2,1,0:T(8,128)(2,1)} %add_convert_fusion.5), channel_id=1, source_target_pairs={{0,2},{1,3},{2,0},{3,1},{4,6},{5,7},{6,4},{7,5},{8,10},{9,11},{10,... | collective-permute-start | bytes 3244040 | tf_op jit(solution)/shard_map/ppermute | solution.py:56
  243.1 60.6 %collective-permute-start.35 = (bf16[8,256,384]{2,1,0:T(8,128)(2,1)}, bf16[8,256,384]{2,1,0:T(8,128)(2,1)}, u32[]{:S(2)}, u32[]{:S(2)}) collective-permute-start(bf16[8,256,384]{2,1,0:T(8,128)(2,1)} %add_convert_fusion.2), channel_id=1, source_target_pairs={{0,4},{4,0},{8,12},{12,8},{16,20},{20,16},{24,28},{28,24},{1,5},{5... | collective-permute-start | bytes 4718600 | tf_op jit(solution)/shard_map/ppermute | solution.py:54
  291.8 39.6 %collective-permute-start.34 = (bf16[4,176,384]{2,1,0:T(8,128)(2,1)S(1)}, bf16[4,176,384]{2,1,0:T(8,128)(2,1)}, u32[]{:S(2)}, u32[]{:S(2)}) collective-permute-start(bf16[4,176,384]{2,1,0:T(8,128)(2,1)S(1)} %slice.573), channel_id=1, source_target_pairs={{0,4},{4,0},{8,12},{12,8},{16,20},{20,16},{24,28},{28,24},{1,5},{5... | collective-permute-start | bytes 1622024 | tf_op jit(solution)/shard_map/ppermute | solution.py:54
  306.4 26.2 %collective-permute-start.36 = (bf16[4,256,384]{2,1,0:T(8,128)(2,1)}, bf16[4,256,384]{2,1,0:T(8,128)(2,1)}, u32[]{:S(2)}, u32[]{:S(2)}) collective-permute-start(bf16[4,256,384]{2,1,0:T(8,128)(2,1)} %slice.574), channel_id=1, source_target_pairs={{0,2},{1,3},{2,0},{3,1},{4,6},{5,7},{6,4},{7,5},{8,10},{9,11},{10,... | collective-permute-start | bytes 2359304 | tf_op jit(solution)/shard_map/ppermute | solution.py:56
  345.1 24.1 %collective-permute-start.39 = (bf16[8,80,384]{2,1,0:T(8,128)(2,1)}, bf16[8,80,384]{2,1,0:T(8,128)(2,1)S(1)}, u32[]{:S(2)}, u32[]{:S(2)}) collective-permute-start(bf16[8,80,384]{2,1,0:T(8,128)(2,1)} %get-tuple-element.140), channel_id=1, source_target_pairs={{0,4},{4,0},{8,12},{12,8},{16,20},{20,16},{24,28},{28,24},{1,5},{5... | collective-permute-start | bytes 1474568 | tf_op jit(solution)/shard_map/ppermute | solution.py:54
  351.3 18.2 %collective-permute-start.41 = (bf16[8,80,384]{2,1,0:T(8,128)(2,1)}, bf16[8,80,384]{2,1,0:T(8,128)(2,1)S(1)}, u32[]{:S(2)}, u32[]{:S(2)}) collective-permute-start(bf16[8,80,384]{2,1,0:T(8,128)(2,1)} %get-tuple-element.143), channel_id=1, source_target_pairs={{0,2},{1,3},{2,0},{3,1},{4,6},{5,7},{6,4},{7,5},{8,10},{9,11},{10,... | collective-permute-start | bytes 1474568 | tf_op jit(solution)/shard_map/ppermute | solution.py:56
  354.1 17.1 %collective-permute-start.43 = (bf16[432,384]{1,0:T(8,128)(2,1)}, bf16[432,384]{1,0:T(8,128)(2,1)S(1)}, u32[]{:S(2)}, u32[]{:S(2)}) collective-permute-start(bf16[432,384]{1,0:T(8,128)(2,1)} %get-tuple-element.165), channel_id=1, source_target_pairs={{0,24},{4,28},{8,0},{12,4},{16,8},{20,12},{24,16},{28,20},{1,25},{... | collective-permute-start | bytes 995336 | tf_op jit(solution)/shard_map/ppermute | solution.py:61
  354.1 17.1 %collective-permute-start.45 = (bf16[432,384]{1,0:T(8,128)(2,1)S(1)}, bf16[432,384]{1,0:T(8,128)(2,1)S(1)}, u32[]{:S(2)}, u32[]{:S(2)}) collective-permute-start(bf16[432,384]{1,0:T(8,128)(2,1)S(1)} %get-tuple-element.166), channel_id=1, source_target_pairs={{0,8},{4,12},{8,16},{12,20},{16,24},{20,28},{24,0},{28,4},{1,9},{5... | collective-permute-start | bytes 995336 | tf_op jit(solution)/shard_map/ppermute | solution.py:61
  356.7 29.9 %collective-permute-start.44 = (bf16[432,384]{1,0:T(8,128)(2,1)S(1)}, bf16[432,384]{1,0:T(8,128)(2,1)S(1)}, u32[]{:S(2)}, u32[]{:S(2)}) collective-permute-start(bf16[432,384]{1,0:T(8,128)(2,1)S(1)} %get-tuple-element.167), channel_id=1, source_target_pairs={{0,16},{4,20},{8,24},{12,28},{16,0},{20,4},{24,8},{28,12},{1,17},{... | collective-permute-start | bytes 995336 | tf_op jit(solution)/shard_map/ppermute | solution.py:61
  369.2 23.6 %collective-permute-start.37 = (bf16[1024,768]{1,0:T(8,128)(2,1)S(1)}, bf16[1024,768]{1,0:T(8,128)(2,1)S(1)}, u32[]{:S(2)}, u32[]{:S(2)}) collective-permute-start(bf16[1024,768]{1,0:T(8,128)(2,1)S(1)} %slice_bitcast_fusion), channel_id=1, source_target_pairs={{0,1},{1,0},{2,3},{3,2},{4,5},{5,4},{6,7},{7,6},{8,9},{9,8},{10,11... | collective-permute-start | bytes 4718600 | tf_op jit(solution)/shard_map/ppermute | solution.py:56
  386.8 7.5 %collective-permute-start.40 = (bf16[4,80,384]{2,1,0:T(8,128)(2,1)S(1)}, bf16[4,80,384]{2,1,0:T(8,128)(2,1)S(1)}, u32[]{:S(2)}, u32[]{:S(2)}) collective-permute-start(bf16[4,80,384]{2,1,0:T(8,128)(2,1)S(1)} %slice.580), channel_id=1, source_target_pairs={{0,2},{1,3},{2,0},{3,1},{4,6},{5,7},{6,4},{7,5},{8,10},{9,11},{10,... | collective-permute-start | bytes 737288 | tf_op jit(solution)/shard_map/ppermute | solution.py:56
  388.0 6.2 %collective-permute-start.42 = (bf16[4,80,384]{2,1,0:T(8,128)(2,1)S(1)}, bf16[4,80,384]{2,1,0:T(8,128)(2,1)S(1)}, u32[]{:S(2)}, u32[]{:S(2)}) collective-permute-start(bf16[4,80,384]{2,1,0:T(8,128)(2,1)S(1)} %slice.582), channel_id=1, source_target_pairs={{0,4},{4,0},{8,12},{12,8},{16,20},{20,16},{24,28},{28,24},{1,5},{5... | collective-permute-start | bytes 737288 | tf_op jit(solution)/shard_map/ppermute | solution.py:54
  394.3 18.8 %collective-permute-start.38 = (bf16[512,768]{1,0:T(8,128)(2,1)S(1)}, bf16[512,768]{1,0:T(8,128)(2,1)S(1)}, u32[]{:S(2)}, u32[]{:S(2)}) collective-permute-start(bf16[512,768]{1,0:T(8,128)(2,1)S(1)} %get-tuple-element.158), channel_id=1, source_target_pairs={{0,2},{1,3},{2,0},{3,1},{4,6},{5,7},{6,4},{7,5},{8,10},{9,11},{10,... | collective-permute-start | bytes 2359304 | tf_op jit(solution)/shard_map/ppermute | solution.py:56
  395.5 19.0 %collective-permute-start.46 = (bf16[160,384]{1,0:T(8,128)(2,1)S(1)}, bf16[160,384]{1,0:T(8,128)(2,1)S(1)}, u32[]{:S(2)}, u32[]{:S(2)}) collective-permute-start(bf16[160,384]{1,0:T(8,128)(2,1)S(1)} %get-tuple-element.170), channel_id=1, source_target_pairs={{0,24},{4,28},{8,0},{12,4},{16,8},{20,12},{24,16},{28,20},{1,25},{... | collective-permute-start | bytes 368648 | tf_op jit(solution)/shard_map/ppermute | solution.py:61
  397.6 16.9 %collective-permute-start.48 = (bf16[160,384]{1,0:T(8,128)(2,1)S(1)}, bf16[160,384]{1,0:T(8,128)(2,1)S(1)}, u32[]{:S(2)}, u32[]{:S(2)}) collective-permute-start(bf16[160,384]{1,0:T(8,128)(2,1)S(1)} %get-tuple-element.171), channel_id=1, source_target_pairs={{0,8},{4,12},{8,16},{12,20},{16,24},{20,28},{24,0},{28,4},{1,9},{5... | collective-permute-start | bytes 368648 | tf_op jit(solution)/shard_map/ppermute | solution.py:61
  397.6 16.9 %collective-permute-start.47 = (bf16[160,384]{1,0:T(8,128)(2,1)S(1)}, bf16[160,384]{1,0:T(8,128)(2,1)S(1)}, u32[]{:S(2)}, u32[]{:S(2)}) collective-permute-start(bf16[160,384]{1,0:T(8,128)(2,1)S(1)} %get-tuple-element.172), channel_id=1, source_target_pairs={{0,16},{4,20},{8,24},{12,28},{16,0},{20,4},{24,8},{28,12},{1,17},{... | collective-permute-start | bytes 368648 | tf_op jit(solution)/shard_map/ppermute | solution.py:61
  (42 other events, 336.4 us)

commit v3 on v2

v3 whole, which is shorter than its diff:
```python
import jax
import jax.numpy as jnp
from jax import lax
from jax.experimental import pallas as pl
from jax.experimental.pallas import tpu as pltpu
from jax.sharding import PartitionSpec as P

HD = 64
BLOCK = 64
EPSILON = 1e-06
BIG = float(2.0**100)
LOWEST = -3.0e38
TQ = 256
TK = 512
CHIPS = 16
TILE = 256
BF = jnp.bfloat16
F32 = jnp.float32
VMEM_LIMIT = 60 << 20
COST = 1.0
CUT = 320
BACK_CUT = 224


def nn(left, right):
    return lax.dot_general(left, right, (((1,), (0,)), ((), ())), preferred_element_type=F32)


def nt(left, right):
    return lax.dot_general(left, right, (((1,), (1,)), ((), ())), preferred_element_type=F32)


def tn(left, right):
    return lax.dot_general(left, right, (((0,), (0,)), ((), ())), preferred_element_type=F32)


def smem():
    return pl.BlockSpec(memory_space=pltpu.SMEM)


def anywhere():
    return pl.BlockSpec(memory_space=pl.ANY)


def cost(flops, bytes_accessed, transcendentals):
    part = lambda value: int(value * COST)
    return pl.CostEstimate(flops=part(flops), bytes_accessed=part(bytes_accessed), transcendentals=part(transcendentals))


def shape(dims, kind):
    return jax.ShapeDtypeStruct(dims, kind)


def after(value, *ready):
    if not ready:
        return value
    return lax.optimization_barrier((value,) + ready)[0]


def swap(value, dim):
    if dim == "x":
        return lax.ppermute(value, "dp", [(d, d ^ 1) for d in range(lax.axis_size("dp"))])
    bit = 1 if dim == "core" else 2
    return lax.ppermute(value, "seq", [(s, s ^ bit) for s in range(4)])


def shift_z(value, by):
    size = lax.axis_size("dp") // 2
    return lax.ppermute(value, "dp", [(2 * z + x, (z + by) % size * 2 + x) for z in range(size) for x in range(2)])


ZS = 4


def stage(*values):
    return lax.optimization_barrier(values)


def shifts_z(chunk, *by):
    return [shift_z(chunk, k) for k in by]


def scatter_z(total, *by):
    return [shift_z(total[r], ZS - r) for r in by]


def split_rows(value, cut):
    return value[:, cut:], value[:, :cut]


def added(*values):
    return sum(v.astype(F32) for v in values)


def add(*values):
    return added(*values).astype(BF)


def chip_at(order, near, index, here):
    z = lax.rem(here["z"] - index % ZS + ZS, ZS)
    near = {order[0]: near[0], order[1]: near[1]}
    return z * 4 + lax.rem(here["x"] + near["x"], 2) * 2 + lax.rem(here["y"] + near["y"], 2)


def placed(meta):
    return {"c": meta[0], "x": meta[1], "y": meta[2], "z": meta[3]}


class Plan:
    def __init__(self, sections, cut, joined=False):
        self.sections, self.cut, self.joined = sections, cut, joined
        self.rows = sum(sections)

    def pieces(self):
        if self.cut is None:
            return [(0, self.rows, None, [None] * CHIPS)]
        found = []
        if not self.joined:
            found.append((0, self.rows, "xy", [(0, 0)] * ZS))
        for first, end, order in ((self.cut, self.rows, "xy"), (0, self.cut, "yx")):
            if self.joined:
                found += [(first, end, order, [(m // ZS, last) for m in range(2 * ZS)]) for last in range(2)]
            else:
                found += [(first, end, order, [sides] * ZS) for sides in ((1, 0), (0, 1), (1, 1))]
        return found

    def shapes(self, width):
        return [shape((len(sides), end - first, width), BF) for first, end, _, sides in self.pieces()]

    def walk(self, here):
        for piece, (first, end, order, sides) in enumerate(self.pieces()):
            for m, side in enumerate(sides):
                chip = m if side is None else chip_at(order, side, m, here)
                start = 0
                for number, length in enumerate(self.sections):
                    lo, hi = max(start, first), min(start + length, end)
                    if lo < hi:
                        yield piece, m, lo - first, hi - first, chip, number, lo - start
                    start += length

    def entries(self):
        return sum(1 for _ in self.walk({"c": 0, "x": 0, "y": 0, "z": 0}))


def move(plan, here, pieces, target, sems, base, numbers=None, back=False):
    copies = []
    for i, (p, m, lo, hi, chip, number, at) in enumerate(plan.walk(here)):
        if numbers is None or number in numbers:
            near, far = pieces[p].at[m, lo:hi, :], target(number, chip, slice(at, at + hi - lo))
            if back:
                near, far = far, near
            copies.append(pltpu.make_async_copy(near, far, sems.at[base + i]))
    return copies


def run(copies):
    for copy in copies:
        copy.start()
    for copy in copies:
        copy.wait()


def spread_vectors(rows, first, second, marks, hidden_marks):
    count = rows.shape[0]
    number = lax.broadcasted_iota(jnp.int32, (9 * CHIPS, count), 0)
    entry = lax.broadcasted_iota(jnp.int32, (9 * CHIPS, count), 1)
    picker = (entry == lax.rem(number, CHIPS) * 16 + number // CHIPS).astype(F32).astype(BF)
    picked = nn(picker, rows).astype(BF)
    model = first.shape[1]
    vectors = nn(picked[: 8 * CHIPS], first).reshape(8, CHIPS, model) * marks[None]
    hidden = nn(picked[8 * CHIPS :], second).reshape(4, 4, model) * hidden_marks[None]
    return jnp.sum(vectors, axis=1), jnp.sum(hidden, axis=1)


def spread_tables(model, share, share_f, *ready):
    lane, col = jnp.arange(384)[:, None], jnp.arange(model)[None, :]
    if ready:
        lane = after(lane, *ready)
    first = (lane == 128 * (col // share % 2) + col % share).astype(BF)
    second = (lane == 128 * (col // share_f % 2) + col % share_f).astype(BF)
    marks = (jnp.arange(CHIPS)[:, None] == col // (2 * share)).astype(F32)
    hidden_marks = (jnp.arange(4)[:, None] == col // (2 * share_f)).astype(F32)
    return first, second, marks, hidden_marks


def pack_kernel(meta, qkv_ref, proj_ref, inner_ref, down_ref, mine_ref, theirs_ref):
    model = proj_ref.shape[1]
    half, share = model // 2, proj_ref.shape[0]
    for rel, out in ((0, mine_ref), (1, theirs_ref)):
        h = lax.rem(meta[0] + rel, 2)
        lanes = lambda first, n: pl.ds(pl.multiple_of(first, 128), n)
        at = 0
        for p in range(half // 128):
            for w in range(3):
                out[at : at + share, 128 * w : 128 * w + 128] = qkv_ref[:, lanes(model * w + half * h + 128 * p, 128)]
            at += share
        out[at : at + share, :] = proj_ref[:, lanes(half * h, half)]
        at += share
        for g in range(inner_ref.shape[1] // 2 // half):
            out[at : at + share, :] = inner_ref[:, lanes(inner_ref.shape[1] // 2 * h + half * g, half)]
            at += share
        out[at : at + down_ref.shape[0], :] = down_ref[:, lanes(half * h, half)]


def pack(meta, qkv, proj, inner, down):
    half = proj.shape[1] // 2
    rows = proj.shape[0] * (half // 128 + 1 + inner.shape[1] // 2 // half) + down.shape[0]
    return pl.pallas_call(
        pack_kernel,
        in_specs=[smem()] + [pl.BlockSpec(memory_space=pltpu.VMEM)] * 4,
        out_specs=[pl.BlockSpec(memory_space=pltpu.VMEM)] * 2,
        out_shape=[shape((rows, half), BF)] * 2,
        cost_estimate=cost(flops=0, bytes_accessed=8 * rows * half, transcendentals=0),
        name="pack",
    )(meta, qkv, proj, inner, down)


def qkv_kernel(plan, pieces_n, *refs):
    meta = refs[0]
    pieces = refs[1 : 1 + pieces_n]
    own_ref, oth_ref, first, second, marks, hidden_marks, out_ref, w_ref, vec_ref, rows_ref, bias_ref, sems = refs[1 + pieces_n :]
    here = placed(meta)
    wide = out_ref.shape[1]
    third = wide // 3

    @pl.when(pl.program_id(0) == 0)
    def _():
        def target(number, chip, rows):
            if number == 3:
                return rows_ref.at[chip, rows, :]
            return w_ref.at[chip, rows, third * number : third * number + third]

        run(move(plan, here, pieces, target, sems, 0))
        rows = rows_ref[...].reshape(CHIPS * 16, 384)
        vectors, hidden = spread_vectors(rows, first[...], second[...], marks[...], hidden_marks[...])
        vec_ref[0:8, :] = vectors
        vec_ref[8:12, :] = hidden
        vec_ref[12:16, :] = jnp.zeros_like(hidden)
        mine = jnp.where(here["c"] == 0, vectors[:, :third], vectors[:, third:])
        bias_ref[...] = jnp.zeros_like(bias_ref)
        for p in range(3):
            for w, source in ((0, 0), (2, 1)):
                at = third * p + 128 * w
                bias_ref[0:1, at : at + 128] = mine[source : source + 1, 128 * p : 128 * p + 128]

    weight = w_ref[...].reshape(-1, wide)
    x = jnp.where(pl.program_id(0) < 2, own_ref[...], oth_ref[...])
    out_ref[...] = (nn(x, weight) + bias_ref[0:1, :]).astype(BF)


def project_qkv(plan, meta, pieces, x_own, x_oth, tables):
    _, tile, model = x_own.shape
    rows = 4 * tile
    width, depth = model // 2, model // CHIPS
    wide = 3 * width
    full = lambda dims: pl.BlockSpec(dims, lambda i, meta: (0,) * len(dims))
    return pl.pallas_call(
        lambda *refs: qkv_kernel(plan, len(pieces), *refs),
        grid_spec=pltpu.PrefetchScalarGridSpec(
            num_scalar_prefetch=1,
            grid=(4,),
            in_specs=[anywhere()] * len(pieces)
            + [pl.BlockSpec((None, tile, model), lambda i, meta: (jnp.minimum(i, 1), 0, 0))]
            + [pl.BlockSpec((None, tile, model), lambda i, meta: (jnp.maximum(i - 2, 0), 0, 0))]
            + [full(t.shape) for t in tables],
            out_specs=[
                pl.BlockSpec((tile, wide), lambda i, meta: (2 * lax.rem(i, 2) + lax.rem(meta[0] + i // 2, 2), 0)),
                full((CHIPS, depth, wide)),
                full((16, model)),
            ],
            scratch_shapes=[
                pltpu.VMEM((CHIPS, 16, width), BF),
                pltpu.VMEM((8, wide), F32),
                pltpu.SemaphoreType.DMA((plan.entries(),)),
            ],
        ),
        out_shape=[shape((rows, wide), BF), shape((CHIPS, depth, wide), BF), shape((16, model), F32)],
        compiler_params=pltpu.CompilerParams(vmem_limit_bytes=VMEM_LIMIT),
        cost_estimate=cost(
            flops=2 * rows * model * wide, bytes_accessed=2 * rows * (model + wide), transcendentals=0
        ),
        name="project_qkv",
    )(meta, *pieces, x_own, x_oth, *tables)


def fill_features(seg_ref, rand_ref, first_global, second_global, key_ref, query_ref):
    heads, _, length = key_ref.shape
    blocks = length // BLOCK
    at = lax.broadcasted_iota(jnp.int32, (blocks, length), 1) // BLOCK
    row = lax.broadcasted_iota(jnp.int32, (blocks, length), 0)
    seen = jnp.abs(at - row) <= 1
    for chosen in (first_global, second_global):
        seen = seen | (at == chosen) | (row == chosen)
    same = lax.broadcasted_iota(jnp.int32, (HD - blocks, length), 0) == seg_ref[...]
    for h in range(heads):
        picked = seen
        for r in range(rand_ref.shape[2]):
            picked = picked | (at == rand_ref[h, :, r : r + 1])
        key_ref[h, 0:blocks, :] = jnp.where(picked, 0.0, 1.0).astype(BF)
        key_ref[h, blocks:HD, :] = jnp.where(same, 0.0, 1.0).astype(BF)
    query_ref[0:blocks, :] = jnp.where(at == row, -BIG, 0.0).astype(BF)
    query_ref[blocks:HD, :] = jnp.where(same, -BIG, 0.0).astype(BF)


def of_pair(ref, p, w):
    return ref[:, 384 * p + 128 * w : 384 * p + 128 * w + 128]


def widen_pair(p, qkv_ref, key_feat, query_feat, key_wide, query_wide):
    scaled = of_pair(qkv_ref, p, 0) * BF(HD**-0.5)
    queries, keys = scaled.T, of_pair(qkv_ref, p, 1).T
    a, b = 2 * p, 2 * p + 1
    query_wide[a, 0:HD, :] = queries[0:HD]
    query_wide[a, HD:128, :] = query_feat[...]
    query_wide[b, 0:HD, :] = query_feat[...]
    query_wide[b, HD:128, :] = queries[HD:128]
    key_wide[a] = jnp.concatenate([keys[0:HD], key_feat[a]], axis=0).T
    key_wide[b] = jnp.concatenate([key_feat[b], keys[HD:128]], axis=0).T
    return scaled, keys


def over_keys(start, n, step, carry):
    carry = lax.fori_loop(0, n // 2, lambda j, carry: step(start + j * TK, j * TK, TK, carry), carry)
    done = n // 2 * TK
    return lax.fori_loop(0, lax.rem(n, 2), lambda j, carry: step(start + done, done, TK // 2, carry), carry)


def attend_kernel(meta, lo_ref, n_ref, glob_ref, qkv_ref, seg_ref, rand_ref, own_ref, oth_ref, lse_ref,
                  key_feat, query_feat, key_wide, query_wide, values, turned, store):
    heads, length = lse_ref.shape
    fill_features(seg_ref, rand_ref, glob_ref[0], glob_ref[1], key_feat, query_feat)
    for p in range(heads // 2):
        widen_pair(p, qkv_ref, key_feat, query_feat, key_wide, query_wide)
        values[128 * p : 128 * p + 128, :] = of_pair(qkv_ref, p, 2).T

    def tile(i, _):
        qs = pl.ds(pl.multiple_of(i * TQ, TQ), TQ)

        def scan(start, at, size, tops):
            ks = pl.ds(pl.multiple_of(start, 128), size)
            to = pl.ds(pl.multiple_of(at, TK), size)
            raised = []
            for h in range(heads):
                scores = nn(key_wide[h, ks, :], query_wide[h, :, qs])
                store[h, to, :] = scores
                raised.append(jnp.maximum(tops[h], jnp.max(scores.reshape(size // 8, 8, TQ), axis=0)))
            return tuple(raised)

        tops = over_keys(lo_ref[i], n_ref[i], scan, (jnp.full((8, TQ), LOWEST, F32),) * heads)
        tops = [jnp.max(top, axis=0, keepdims=True) for top in tops]

        def collect(start, at, size, carry):
            ks = pl.ds(pl.multiple_of(start, 128), size)
            to = pl.ds(pl.multiple_of(at, TK), size)
            new = []
            for h in range(heads):
                total, summed = carry[h]
                expo = jnp.exp(store[h, to, :] - tops[h])
                total = total + jnp.sum(expo.reshape(size // 8, 8, TQ), axis=0)
                summed = summed + nn(values[HD * h : HD * h + HD, ks], expo.astype(BF))
                new.append((total, summed))
            return tuple(new)

        none = (jnp.zeros((8, TQ), F32), jnp.zeros((HD, TQ), F32))
        found = over_keys(lo_ref[i], n_ref[i], collect, (none,) * heads)
        for h in range(heads):
            total, summed = found[h]
            total = jnp.sum(total, axis=0, keepdims=True)
            turned[HD * h : HD * h + HD, qs] = (summed / total).astype(BF)
            lse_ref[h : h + 1, qs] = tops[h] + jnp.log(total)
        return 0

    lax.fori_loop(0, length // TQ, tile, 0)
    quarter = length // 4
    even = meta[0] == 0
    for p in range(heads // 2):
        result = turned[128 * p : 128 * p + 128, :].T
        for n in range(2):
            one, two = (result[quarter * k : quarter * k + quarter] for k in (2 * n, 2 * n + 1))
            where = (slice(quarter * n, quarter * n + quarter), slice(128 * p, 128 * p + 128))
            own_ref[where] = jnp.where(even, one, two)
            oth_ref[where] = jnp.where(even, two, one)


def whole(dims):
    return pl.BlockSpec(dims, lambda *_: (0,) * len(dims))


def attend(meta, qkv, number, seg_row, table, globs, lo, n):
    length = qkv.shape[0]
    heads, blocks = table.shape[:2]
    wide = heads * HD
    return pl.pallas_call(
        attend_kernel,
        grid=(1,),
        in_specs=[smem()] * 4
        + [pl.BlockSpec((length, 3 * wide), lambda i: (0, number)), whole((1, length)), whole((heads, blocks, 3))],
        out_specs=[whole((length // 2, wide))] * 2 + [whole((heads, length))],
        out_shape=[shape((length // 2, wide), BF)] * 2 + [shape((heads, length), F32)],
        scratch_shapes=[
            pltpu.VMEM((heads, HD, length), BF),
            pltpu.VMEM((HD, length), BF),
            pltpu.VMEM((heads, length, 128), BF),
            pltpu.VMEM((heads, 128, length), BF),
            pltpu.VMEM((wide, length), BF),
            pltpu.VMEM((wide, length), BF),
            pltpu.VMEM((heads, length, TQ), F32),
        ],
        compiler_params=pltpu.CompilerParams(vmem_limit_bytes=VMEM_LIMIT),
        cost_estimate=cost(
            flops=heads * length * length * 700, bytes_accessed=10 * length * wide, transcendentals=heads * length * length // 2
        ),
        name="attend",
    )(meta, lo, n, globs, qkv, seg_row, table)


def attend_back_kernel(meta, lo_ref, n_ref, glob_ref, qkv_ref, own_ref, oth_ref, ctx_own, ctx_oth, lse_ref, seg_ref,
                       rand_ref, out_ref, key_feat, query_feat, key_wide, query_wide, value_one,
                       grad_turned, keys_turned, query_one, grad_one, inner_ref, dk, dv, dqt, grads):
    heads, length = lse_ref.shape
    quarter = length // 4
    fill_features(seg_ref, rand_ref, glob_ref[0], glob_ref[1], key_feat, query_feat)
    for rel, source, ctx in ((0, own_ref, ctx_own), (1, oth_ref, ctx_oth)):
        for n in range(2):
            at = 2 * n + lax.rem(meta[0] + rel, 2)
            rows = pl.ds(pl.multiple_of(at * quarter, quarter), quarter)
            grads[0, rows, :] = source[quarter * n : quarter * n + quarter, :]
            grads[1, rows, :] = ctx[quarter * n : quarter * n + quarter, :]
    low = lax.broadcasted_iota(jnp.int32, (length, 128), 1) < HD
    zero = jnp.zeros((length, 128), BF)
    for p in range(heads // 2):
        cols = slice(128 * p, 128 * p + 128)
        scaled, keys = widen_pair(p, qkv_ref, key_feat, query_feat, key_wide, query_wide)
        keys_turned[cols, :] = keys
        grad, value = grads[0, :, cols], of_pair(qkv_ref, p, 2)
        for e in range(2):
            keep = low if e == 0 else ~low
            value_one[2 * p + e] = jnp.where(keep, value, zero)
            query_one[2 * p + e] = jnp.where(keep, scaled, zero)
            grad_one[2 * p + e] = jnp.where(keep, grad, zero)
        turned = grad.T
        grad_turned[cols, :] = turned
        product = turned.astype(F32) * grads[1, :, cols].T.astype(F32)
        for e in range(2):
            h = 2 * p + e
            inner_ref[h : h + 1, :] = jnp.sum(product[HD * e : HD * e + HD], axis=0, keepdims=True)
    dk[...] = jnp.zeros_like(dk)
    dv[...] = jnp.zeros_like(dv)

    def tile(i, _):
        qs = pl.ds(pl.multiple_of(i * TQ, TQ), TQ)

        def body(start, at, size, carry):
            ks = pl.ds(pl.multiple_of(start, 128), size)
            new = []
            for p in range(heads // 2):
                cols = slice(128 * p, 128 * p + 128)
                more_k, more_v = [], []
                for h in (2 * p, 2 * p + 1):
                    scores = nn(key_wide[h, ks, :], query_wide[h, :, qs])
                    prob = jnp.exp(scores - lse_ref[h : h + 1, qs])
                    grad_prob = nn(value_one[h, ks, :], grad_turned[cols, qs])
                    grad_scores = (prob * (grad_prob - inner_ref[h : h + 1, qs])).astype(BF)
                    new.append(carry[h] + nn(keys_turned[HD * h : HD * h + HD, ks], grad_scores))
                    more_k.append(nn(grad_scores, query_one[h, qs, :]))
                    more_v.append(nn(prob.astype(BF), grad_one[h, qs, :]))
                dk[ks, cols] += more_k[0] + more_k[1]
                dv[ks, cols] += more_v[0] + more_v[1]
            return tuple(new)

        found = over_keys(lo_ref[i], n_ref[i], body, (jnp.zeros((HD, TQ), F32),) * heads)
        for h in range(heads):
            dqt[HD * h : HD * h + HD, qs] = (found[h] * HD**-0.5).astype(BF)
        return 0

    lax.fori_loop(0, length // TQ, tile, 0)
    for p in range(heads // 2):
        cols = slice(128 * p, 128 * p + 128)
        for w, value in enumerate((dqt[cols, :].T, dk[:, cols].astype(BF), dv[:, cols].astype(BF))):
            out_ref[:, 384 * p + 128 * w : 384 * p + 128 * w + 128] = value


def attend_back(meta, qkv, number, own, oth, ctx, ctx_oth, lse, part, seg_row, table, globs, lo, n):
    length = qkv.shape[0]
    heads, blocks = table.shape[:2]
    wide = heads * HD
    group = lambda w, i=number: pl.BlockSpec((length, w), lambda _: (0, i))
    half = pl.BlockSpec((length // 2, wide), lambda _: (0, number))
    return pl.pallas_call(
        attend_back_kernel,
        grid=(1,),
        in_specs=[smem()] * 4
        + [group(3 * wide), half, half]
        + [pl.BlockSpec((length // 2, wide), lambda _: (0, part))] * 2
        + [whole((heads, length)), whole((1, length)), whole((heads, blocks, 3))],
        out_specs=whole((length, 3 * wide)),
        out_shape=shape((length, 3 * wide), BF),
        scratch_shapes=[
            pltpu.VMEM((heads, HD, length), BF),
            pltpu.VMEM((HD, length), BF),
            pltpu.VMEM((heads, length, 128), BF),
            pltpu.VMEM((heads, 128, length), BF),
            pltpu.VMEM((heads, length, 128), BF),
            pltpu.VMEM((wide, length), BF),
            pltpu.VMEM((wide, length), BF),
            pltpu.VMEM((heads, length, 128), BF),
            pltpu.VMEM((heads, length, 128), BF),
            pltpu.VMEM((heads, length), F32),
            pltpu.VMEM((length, wide), F32),
            pltpu.VMEM((length, wide), F32),
            pltpu.VMEM((wide, length), BF),
            pltpu.VMEM((2, length, wide), BF),
        ],
        compiler_params=pltpu.CompilerParams(vmem_limit_bytes=VMEM_LIMIT),
        cost_estimate=cost(
            flops=heads * length * length * 1500, bytes_accessed=20 * length * wide, transcendentals=heads * length * length // 2
        ),
        name="attend_back",
    )(meta, lo, n, globs, qkv, own, oth, ctx, ctx_oth, lse, seg_row, table)


def key_ranges(segment):
    length = segment.shape[0]
    first, last = segment[::TQ], segment[TQ - 1 :: TQ]
    lo = jnp.sum(segment[None, :] < first[:, None], axis=1, dtype=jnp.int32) // 128 * 128
    hi = jnp.sum(segment[None, :] <= last[:, None], axis=1, dtype=jnp.int32)
    n = (hi - lo + TK // 2 - 1) // (TK // 2)
    return jnp.minimum(lo, length - n * (TK // 2)), n


def centre(value):
    centred = value - jnp.mean(value, axis=1, keepdims=True)
    rate = lax.rsqrt(jnp.mean(centred * centred, axis=1, keepdims=True) + EPSILON)
    return centred * rate, rate


def norm_back(grad, normed, rate):
    return rate * (
        grad
        - jnp.mean(grad, axis=1, keepdims=True)
        - normed * jnp.mean(grad * normed, axis=1, keepdims=True)
    )


def cut(value):
    half = value.shape[1] // 2
    return value[:, :half], value[:, half:]


def wide_target(proj, inner, down, half):
    width = proj.shape[2] // 2
    groups = inner.shape[2] // 2 // width

    def target(number, chip, rows):
        if number == 0:
            return proj.at[chip, rows, pl.ds(pl.multiple_of(half * width, 128), width)]
        if number <= groups:
            first = half * (groups * width) + width * (number - 1)
            return inner.at[chip, rows, pl.ds(pl.multiple_of(first, 128), width)]
        return down.at[chip, rows, pl.ds(pl.multiple_of(half * width, 128), width)]

    return target


def ffn_kernel(plan, pieces_n, ctx_n, *refs):
    meta = refs[0]
    own_pieces = refs[1 : 1 + pieces_n]
    oth_pieces = refs[1 + pieces_n : 1 + 2 * pieces_n]
    refs = refs[1 + 2 * pieces_n :]
    ctx_own, ctx_oth = refs[:ctx_n], refs[ctx_n : 2 * ctx_n]
    (x_ref, dout_ref, vec_ref,
     kept_ref, given_ref, gr_kept, gr_given, hid_ref, gf_ref, low_ref, gp_ref, ga_ref, gc_own, gc_oth, ctx_ref, vg_ref,
     proj, inner, down, slope, sems) = refs[2 * ctx_n :]
    here = placed(meta)
    c = here["c"]
    step = pl.program_id(0)
    model = x_ref.shape[1]
    wide = hid_ref.shape[1]

    def copies(*numbers):
        found = []
        for rel, pieces in ((0, own_pieces), (1, oth_pieces)):
            target = wide_target(proj, inner, down, lax.rem(c + rel, 2))
            found += move(plan, here, pieces, target, sems, rel * plan.entries(), numbers)
        return found

    first, last = 0, len(plan.sections) - 1
    orders = [(first,), tuple(range(1, last)), (last,)]

    @pl.when(step == 0)
    def _():
        for numbers in orders:
            for copy in copies(*numbers):
                copy.start()
        vg_ref[...] = jnp.zeros_like(vg_ref)

    def arrived(which):
        @pl.when(step == 0)
        def _():
            for copy in copies(*orders[which]):
                copy.wait()

    vec = lambda n: vec_ref[n : n + 1, :]
    w_proj = lambda: proj[...].reshape(model, model)
    w_inner = lambda j: inner[:, :, model * j : model * j + model].reshape(model, model)
    span = CHIPS * model // wide
    w_down = lambda j: down[span * j : span * j + span].reshape(model, model)
    own = jnp.concatenate([ref[...] for ref in ctx_own], axis=1)
    oth = jnp.concatenate([ref[...] for ref in ctx_oth], axis=1)
    context = jnp.concatenate([jnp.where(c == 0, own, oth), jnp.where(c == 0, oth, own)], axis=1)
    ctx_ref[...] = context
    arrived(0)
    attn = nn(context, w_proj())
    n1, rate1 = centre(x_ref[...].astype(F32) + (attn + vec(2)))
    x1 = n1 * vec(3) + vec(4)
    low = x1.astype(BF)
    low_ref[...] = low
    ffn = None
    chunks = wide // model
    arrived(1)
    arrived(2)
    for j in range(chunks):
        cols = slice(model * j, model * j + model)
        pre = nn(low, w_inner(j)) + vec(8 + j)
        below = 0.5 + 0.5 * lax.erf(pre * 0.7071067811865476)
        slope[:, cols] = below + pre * (jnp.exp(-0.5 * (pre * pre)) * 0.3989422804014327)
        hidden = (pre * below).astype(BF)
        hid_ref[:, cols] = hidden
        more = nn(hidden, w_down(j))
        ffn = more if ffn is None else ffn + more
    n2, rate2 = centre(x1 + (ffn + vec(5)))
    out = (n2 * vec(6) + vec(7)).astype(BF)
    stays = step // 2 == here["y"]

    @pl.when(stays)
    def _():
        kept_ref[...] = out

    @pl.when(jnp.logical_not(stays))
    def _():
        given_ref[...] = out


    total = lambda value: jnp.sum(value, axis=0, keepdims=True)
    grad = dout_ref[...].astype(F32)
    gr2 = norm_back(grad * vec(6), n2, rate2)
    gf = gr2.astype(BF)
    gf_ref[...] = gf
    vg_ref[6:7, :] += total(grad * n2)
    vg_ref[7:8, :] += total(grad)
    vg_ref[5:6, :] += total(gf.astype(F32))
    gx1 = gr2
    for j in range(chunks):
        cols = slice(model * j, model * j + model)
        gp = (nt(gf, w_down(j)) * slope[:, cols]).astype(BF)
        gp_ref[:, cols] = gp
        vg_ref[8 + j : 9 + j, :] += total(gp.astype(F32))
        gx1 = gx1 + nt(gp, w_inner(j))
    gr1 = norm_back(gx1 * vec(3), n1, rate1)

    @pl.when(stays)
    def _():
        gr_kept[...] = gr1

    @pl.when(jnp.logical_not(stays))
    def _():
        gr_given[...] = gr1

    ga = gr1.astype(BF)
    ga_ref[...] = ga
    vg_ref[3:4, :] += total(gx1 * n1)
    vg_ref[4:5, :] += total(gx1)
    vg_ref[2:3, :] += total(ga.astype(F32))
    gc = cut(nt(ga, w_proj()))
    gc_own[...] = jnp.where(c == 0, gc[0], gc[1]).astype(BF)
    gc_oth[...] = jnp.where(c == 0, gc[1], gc[0]).astype(BF)


def feed_forward(plan, meta, own_pieces, oth_pieces, ctx, ctx_oth, x_own, d_own, vectors, wide):
    rows, model = x_own.shape
    half = model // 2
    tile = lambda n: pl.BlockSpec((TILE, n), lambda i, meta: (i, 0))
    full = lambda dims: pl.BlockSpec(dims, lambda i, meta: (0,) * len(dims))
    side = lambda mine: pl.BlockSpec(
        (TILE, model), lambda i, meta: (jnp.clip(i - (2 * meta[2] if mine else 2 - 2 * meta[2]), 0, 1), 0)
    )
    scratch = [
        pltpu.VMEM((CHIPS, model // CHIPS, model), BF),
        pltpu.VMEM((CHIPS, model // CHIPS, wide), BF),
        pltpu.VMEM((CHIPS, wide // CHIPS, model), BF),
        pltpu.VMEM((TILE, wide), F32),
        pltpu.SemaphoreType.DMA((2 * plan.entries(),)),
    ]
    outs = [(wide, BF), (model, BF), (model, BF), (wide, BF), (model, BF), (half, BF), (half, BF), (model, BF)]
    return pl.pallas_call(
        lambda *refs: ffn_kernel(plan, len(own_pieces), len(ctx), *refs),
        grid_spec=pltpu.PrefetchScalarGridSpec(
            num_scalar_prefetch=1,
            grid=(rows // TILE,),
            in_specs=[anywhere()] * (2 * len(own_pieces))
            + [tile(v.shape[1]) for v in ctx + ctx_oth]
            + [tile(model), tile(model), full(vectors.shape)],
            out_specs=[side(True), side(False)] * 2 + [tile(w) for w, _ in outs] + [full((16, model))],
            scratch_shapes=scratch,
        ),
        out_shape=[shape((rows // 2, model), BF)] * 2 + [shape((rows // 2, model), F32)] * 2 + [shape((rows, w), kind) for w, kind in outs] + [shape((16, model), F32)],
        compiler_params=pltpu.CompilerParams(vmem_limit_bytes=VMEM_LIMIT),
        cost_estimate=cost(
            flops=4 * rows * model * (model + 2 * wide), bytes_accessed=rows * (8 * wide + 20 * model), transcendentals=2 * rows * wide
        ),
        name="feed_forward",
    )(meta, *own_pieces, *oth_pieces, *ctx, *ctx_oth, x_own, d_own, vectors)


def weight_grads_kernel(plan, pieces_n, *refs):
    meta, hid_ref, gp_ref, gf_ref, low_ref, ctx_ref, ga_ref = refs[:7]
    own_pieces = refs[7 : 7 + pieces_n]
    oth_pieces = refs[7 + pieces_n : 7 + 2 * pieces_n]
    proj, inner, down, sems = refs[7 + 2 * pieces_n :]
    here = placed(meta)
    c = here["c"]
    step = pl.program_id(0)
    model = gf_ref.shape[1]
    span = CHIPS * model // inner.shape[2]
    steps = inner.shape[2] // model

    @pl.when(step == 0)
    def _():
        proj[...] = tn(ctx_ref[...], ga_ref[...]).reshape(proj.shape).astype(BF)

    more_inner = tn(low_ref[...], gp_ref[...])
    inner[:, :, pl.ds(pl.multiple_of(step * model, 128), model)] = more_inner.reshape(CHIPS, -1, model).astype(BF)
    more_down = tn(hid_ref[...], gf_ref[...])
    down[pl.ds(step * span, span)] = more_down.reshape(span, -1, model).astype(BF)

    @pl.when(step == steps - 1)
    def _():
        copies = []
        for rel, pieces in ((0, own_pieces), (1, oth_pieces)):
            target = wide_target(proj, inner, down, lax.rem(c + rel, 2))
            copies += move(plan, here, pieces, target, sems, len(copies), back=True)
        run(copies)


def weight_grads(plan, meta, hid, gp, gf, low, context, ga):
    rows, model = gf.shape
    wide, half = hid.shape[1], model // 2
    pieces = plan.shapes(half)
    cols = pl.BlockSpec((rows, model), lambda i: (0, i))
    found = pl.pallas_call(
        lambda *refs: weight_grads_kernel(plan, len(pieces), *refs),
        grid=(wide // model,),
        in_specs=[smem(), cols, cols] + [whole((rows, model))] * 4,
        out_specs=[anywhere()] * (2 * len(pieces)),
        out_shape=pieces * 2,
        scratch_shapes=[
            pltpu.VMEM((CHIPS, model // CHIPS, model), BF),
            pltpu.VMEM((CHIPS, model // CHIPS, wide), BF),
            pltpu.VMEM((CHIPS, wide // CHIPS, model), BF),
            pltpu.SemaphoreType.DMA((2 * plan.entries(),)),
        ],
        compiler_params=pltpu.CompilerParams(vmem_limit_bytes=VMEM_LIMIT),
        cost_estimate=cost(
            flops=2 * rows * model * (model + 2 * wide), bytes_accessed=rows * (4 * wide + 8 * model), transcendentals=0
        ),
        name="weight_grads",
    )(meta, hid, gp, gf, low, context, ga)
    return found[: len(pieces)], found[len(pieces) :]


def gather_vectors(vectors, hidden, first, second, marks, hidden_marks):
    model = first.shape[1]
    one = nt((vectors[:, None, :] * marks[None]).reshape(-1, model).astype(BF), first)
    two = nt((hidden[:, None, :] * hidden_marks[None]).reshape(-1, model).astype(BF), second)
    laid = jnp.concatenate([one, two], axis=0).astype(BF)
    number = lax.broadcasted_iota(jnp.int32, (9 * CHIPS, 16 * CHIPS), 0)
    entry = lax.broadcasted_iota(jnp.int32, (9 * CHIPS, 16 * CHIPS), 1)
    picker = (entry == lax.rem(number, CHIPS) * 16 + number // CHIPS).astype(F32).astype(BF)
    return tn(picker, laid)


def qkv_grads_kernel(plan, pieces_n, pairs, number, last, *refs):
    meta, own_ref, oth_ref = refs[:3]
    grads = refs[3 : 3 + pairs]
    refs = refs[3 + pairs :]
    if last:
        (known_ref, vg_ref, first, second, marks, hidden_marks), refs = refs[:6], refs[6:]
    pieces, refs = refs[:pieces_n], refs[pieces_n:]
    if last:
        g_ref, sems, rows_ref, vec_ref, sums_ref = refs
    else:
        sums_ref, g_ref, sems = refs
    here = placed(meta)
    quarter, width = own_ref.shape[1], own_ref.shape[2] // 2
    sums_ref[...] = known_ref[...] if last else jnp.zeros_like(sums_ref)
    for p, source in enumerate(grads):
        total = None
        for rel, x_ref in ((0, own_ref), (1, oth_ref)):
            for n in range(2):
                at = 2 * n + lax.rem(here["c"] + rel, 2)
                more = tn(x_ref[n], source[pl.ds(pl.multiple_of(at * quarter, quarter), quarter), :])
                total = more if total is None else total + more
        g_ref[p] = total.reshape(g_ref.shape[1:]).astype(BF)
        sums_ref[number + p : number + p + 1, :] = jnp.sum(source[...].astype(F32), axis=0, keepdims=True)
    if last:
        even = here["c"] == 0
        vec_ref[...] = vg_ref[...]
        none = jnp.zeros((1, 128), F32)
        for p in range(number + pairs):
            for row, w in ((0, 0), (1, 2)):
                value = sums_ref[p : p + 1, 128 * w : 128 * w + 128]
                vec_ref[row : row + 1, 128 * p : 128 * p + 128] = jnp.where(even, value, none)
                at = width + 128 * p
                vec_ref[row : row + 1, at : at + 128] = jnp.where(even, none, value)
        found = gather_vectors(vec_ref[0:8, :], vec_ref[8:12, :], first[...], second[...], marks[...], hidden_marks[...])
        rows_ref[...] = found.reshape(rows_ref.shape).astype(BF)

    def target(section, chip, rows):
        if section == pairs:
            return rows_ref.at[chip, rows, :]
        return g_ref.at[section, chip, rows, :]

    run(move(plan, here, pieces, target, sems, 0, back=True))


def qkv_grads(plan, meta, x_own, x_oth, grads, number, sums=None, vg=None, tables=()):
    rows, model = 4 * x_own.shape[1], x_own.shape[2]
    width, depth = grads[0].shape[1], model // CHIPS
    last = vg is not None
    pieces = plan.shapes(width)
    more = [sums, vg, *tables] if last else []
    summed = shape((8, width), F32)
    found = pl.pallas_call(
        lambda *refs: qkv_grads_kernel(plan, len(pieces), len(grads), number, last, *refs),
        grid=(1,),
        in_specs=[smem(), whole(x_own.shape), whole(x_own.shape)]
        + [whole((rows, width))] * len(grads)
        + [whole(v.shape) for v in more],
        out_specs=[anywhere()] * len(pieces) + ([] if last else [whole(summed.shape)]),
        out_shape=pieces + ([] if last else [summed]),
        scratch_shapes=[
            pltpu.VMEM((len(grads), CHIPS, depth, width), BF),
            pltpu.SemaphoreType.DMA((plan.entries(),)),
        ]
        + ([pltpu.VMEM((CHIPS, 16, width), BF), pltpu.VMEM((16, model), F32), pltpu.VMEM((8, width), F32)] if last else []),
        compiler_params=pltpu.CompilerParams(vmem_limit_bytes=VMEM_LIMIT),
        cost_estimate=cost(
            flops=2 * len(grads) * rows * model * width, bytes_accessed=2 * rows * (model + 3 * width), transcendentals=0
        ),
        name="qkv_grads",
    )(meta, x_own, x_oth, *grads, *more)
    return found if last else (found[:-1], found[-1])


def input_grads_kernel(meta, *refs):
    *grads, w_ref, own_ref, oth_ref = refs
    width = grads[0].shape[1]
    total = None
    for p, source in enumerate(grads):
        weight = w_ref[:, :, width * p : width * p + width].reshape(-1, width)
        more = nt(source[...], weight)
        total = more if total is None else total + more

    @pl.when(pl.program_id(0) == 0)
    def _():
        oth_ref[...] = total.astype(BF)

    @pl.when(pl.program_id(0) == 1)
    def _():
        own_ref[...] = total.astype(BF)


def input_grads(meta, grads, weights, given):
    rows, width = grads[0].shape
    model = weights.shape[0] * weights.shape[1]
    quarter = rows // 4
    half = lambda meta: 1 - meta[2] if given else meta[2]
    at = lambda i, meta: 2 * half(meta) + lax.rem(meta[0] + 1 + i, 2)
    return pl.pallas_call(
        input_grads_kernel,
        grid_spec=pltpu.PrefetchScalarGridSpec(
            num_scalar_prefetch=1,
            grid=(2,),
            in_specs=[pl.BlockSpec((quarter, width), lambda i, meta: (at(i, meta), 0))] * len(grads) + [whole(weights.shape)],
            out_specs=[whole((quarter, model))] * 2,
        ),
        out_shape=[shape((quarter, model), BF)] * 2,
        compiler_params=pltpu.CompilerParams(vmem_limit_bytes=VMEM_LIMIT),
        cost_estimate=cost(
            flops=3 * rows * model * width, bytes_accessed=rows * (model + 3 * width), transcendentals=0
        ),
        name="input_grads",
    )(meta, *grads, weights)


def body(
    tokens,
    qkv_weight,
    query_bias,
    value_bias,
    proj_weight,
    proj_bias,
    attn_gain,
    attn_shift,
    inner_weight,
    inner_bias,
    down_weight,
    down_bias,
    ffn_gain,
    ffn_shift,
    seg_ids,
    rand_blocks,
    glob_blocks,
    d_out,
):
    dp, seq = lax.axis_index("dp"), lax.axis_index("seq")
    members = lax.axis_size("dp") * lax.axis_size("seq")
    near = lax.axis_size("dp") == 2 * ZS
    y, c = seq // 2, seq % 2
    even, low_y = c == 0, y == 0
    meta = jnp.stack([c, dp % 2, y, dp // 2]).astype(jnp.int32)
    model = tokens.shape[3]
    half = model // 2
    ffw = inner_weight.shape[1]
    share, share_f = qkv_weight.shape[0], down_weight.shape[0]
    groups = ffw // 2 // half
    depth, deep = model // CHIPS, ffw // CHIPS
    by_parity = lambda mine, other: (jnp.where(even, mine, other), jnp.where(even, other, mine))

    pair = lambda kept, came: jnp.where(low_y, jnp.stack([kept, came]), jnp.stack([came, kept]))

    def given_kept(value):
        return jnp.where(low_y, value[1], value[0]), jnp.where(low_y, value[0], value[1])

    vectors = (query_bias, value_bias, proj_bias, attn_gain, attn_shift, down_bias, ffn_gain, ffn_shift)
    sections_a, sections_b = [depth] * 3 + [16], [depth] * (1 + groups) + [deep]
    lengths_a, lengths_b = [share] * 3, [share] * (1 + groups) + [share_f]
    segment = jnp.where(low_y, seg_ids[0, 0], seg_ids[1, 0])
    globs = jnp.where(low_y, glob_blocks[0, 0], glob_blocks[1, 0])
    lo, n = key_ranges(segment)
    blocks = rand_blocks[:, 0]
    x_given, x_kept = given_kept(tokens[:, 0])

    def pick_blocks(came):
        of_chip = by_parity(blocks, came)
        mine = jnp.where(low_y, *(jnp.concatenate([v[m] for v in of_chip]) for m in range(2)))
        return mine, jnp.where(low_y, *(jnp.concatenate([v[1 - m] for v in of_chip]) for m in range(2)))

    def attention(heads, number, qkv, table):
        return attend(meta, qkv, number, segment[None], table[heads], globs, lo, n)

    def attention_back(p, qkv, own, oth, ctx, ctx_oth, lse, table):
        part = p if p < 2 else 0
        return attend_back(meta, qkv, p, own, oth, ctx, ctx_oth, lse, part, segment[None], table[2 * p : 2 * p + 2], globs, lo, n)

    if near:
        plan_a, plan_b = Plan(sections_a, 80), Plan(sections_b, CUT)
        back_b = Plan(sections_b, BACK_CUT, True)
        back_early, back_late = Plan([depth] * 2, depth, True), Plan([depth, 16], 32, True)
        mine, theirs = pack(meta, qkv_weight, proj_weight, inner_weight, down_weight)
        came = swap(theirs, "core")
        small = jnp.concatenate([jnp.pad(jnp.stack(vectors), ((0, 0), (0, 128 - share))),
                                 jnp.pad(inner_bias[None], ((0, 7), (0, 128 - share_f)))])
        small = jnp.concatenate(by_parity(small, swap(small, "core")) + (jnp.zeros_like(small),), axis=1)
        first, second = by_parity(mine, came)
        laid, at = [], 0
        for length in lengths_a + lengths_b:
            laid += [first[at : at + length], second[at : at + length]]
            at += length
        chunk_a = jnp.concatenate(laid[:6] + [small], axis=0)
        chunk_b = jnp.concatenate(laid[6:], axis=0)
        chunk_a, chunk_b, x_given = stage(chunk_a, chunk_b, x_given)

        za = shifts_z(chunk_a, 1, 2, 3)
        x_came = swap(x_given, "y")
        blocks_came = swap(blocks, "core")
        zb = shifts_z(chunk_b, 1)
        chunk_a, chunk_b, x_came, blocks_came, *rest = stage(chunk_a, chunk_b, x_came, blocks_came, *za, *zb)
        za, zb = rest[:3], rest[3:]

        near_a = jnp.stack([chunk_a] + za)
        a, b = split_rows(near_a, plan_a.cut)
        a_x, b_y, a_y, b_x = swap(a, "x"), swap(b, "y"), swap(a, "y"), swap(b, "x")
        zb += shifts_z(chunk_b, 2)
        near_a, a_x, b_y, a_y, b_x, x_came, blocks_came, chunk_b, *zb = stage(
            near_a, a_x, b_y, a_y, b_x, x_came, blocks_came, chunk_b, *zb
        )
        x_own = pair(x_kept, x_came)
        x_oth = swap(x_own, "core")
        a_xy, b_yx = swap(a_x, "y"), swap(b_y, "x")
        zb += shifts_z(chunk_b, 3)
        blocks_mine, blocks_given = pick_blocks(blocks_came)
        blocks_came = swap(blocks_given, "y")
        tables = spread_tables(model, depth // 2, deep // 2, chunk_b)
        a_xy, b_yx, blocks_came, chunk_b, x_own, x_oth, *rest = stage(
            a_xy, b_yx, blocks_came, chunk_b, x_own, x_oth, *tables, *zb
        )
        tables, zb = rest[:4], rest[4:]
        pieces = [near_a, a_x, a_y, a_xy, b_y, b_x, b_yx]

        table = jnp.where(c == y, blocks_mine, blocks_came)
        near_b = jnp.stack([chunk_b] + zb)
        a, b = split_rows(near_b, plan_b.cut)
        a_x, b_y, a_y, b_x = swap(a, "x"), swap(b, "y"), swap(a, "y"), swap(b, "x")
        near_oth = swap(near_b, "core")
        qkv, w_qkv, spread = project_qkv(plan_a, meta, pieces, x_own, x_oth, tables)
        ctx_b, ctx_b_give, lse_b = attention(slice(4, 6), 2, qkv, table)
        d_given, d_kept = given_kept(after(d_out[:, 0], chunk_b))
        near_b, near_oth, a_x, b_y, a_y, b_x, qkv, ctx_b, ctx_b_give, d_given = stage(
            near_b, near_oth, a_x, b_y, a_y, b_x, qkv, ctx_b, ctx_b_give, d_given
        )

        a_xy, b_yx = swap(a_x, "y"), swap(b_y, "x")
        d_came = swap(d_given, "y")
        early = [a_x, a_y, b_y, b_x]
        early_oth = [swap(v, "core") for v in early]
        ctx_b_oth = swap(ctx_b_give, "core")
        ctx_a, ctx_a_give, lse_a = attention(slice(0, 4), 0, qkv, table)
        a_xy, b_yx, d_came, ctx_b_oth, ctx_a, ctx_a_give, *early_oth = stage(
            a_xy, b_yx, d_came, ctx_b_oth, ctx_a, ctx_a_give, *early_oth
        )
        own_b = [near_b] + early[:2] + [a_xy] + early[2:] + [b_yx]
        oth_b = [near_oth] + early_oth[:2] + [swap(a_xy, "core")] + early_oth[2:] + [swap(b_yx, "core")]
        ctx_a_oth = swap(ctx_a_give, "core")
        d_own = pair(d_kept, d_came).reshape(-1, model)
        found = feed_forward(plan_b, meta, own_b, oth_b, [ctx_a, ctx_b], [ctx_a_oth, ctx_b_oth], x_own.reshape(-1, model),
                             d_own, spread, ffw)
        out_kept, out_given, gr_kept, gr_given, hid, gf, x1_low, gp, ga, gc_own, gc_oth, context, vg = found

        out_came, gc_came = swap(out_given, "y"), swap(gc_oth, "core")
        grads_own, grads_oth = weight_grads(back_b, meta, hid, gp, gf, x1_low, context, ga)
        out_came, gc_came, *rest = stage(out_came, gc_came, *grads_own, *grads_oth)
        a, a_far, b, b_far, a_oth, a_far_oth, b_oth, b_far_oth = rest
        layer_out = pair(out_kept, out_came)[:, None]
        a_far, b_far = add(a_far, swap(a_far_oth, "core")), add(b_far, swap(b_far_oth, "core"))
        a_far, b_far, gc_came, a_oth, b_oth = stage(a_far, b_far, gc_came, a_oth, b_oth)

        a_came, b_came = swap(a_far, "y"), swap(b_far, "x")
        a_oth, b_oth = swap(a_oth, "core"), swap(b_oth, "core")
        back = lambda p, own, ctx, oth, lse: attention_back(p, qkv, own, gc_came, ctx, oth, lse, table)
        grad_0 = back(0, gc_own, ctx_a, ctx_a_give, lse_a[0:2])
        a_came, b_came, a_oth, b_oth, grad_0, gc_own = stage(a_came, b_came, a_oth, b_oth, grad_0, gc_own)
        a, b = add(a, a_oth, a_came), add(b, b_oth, b_came)
        a_came, b_came = swap(a[ZS:], "x"), swap(b[ZS:], "y")
        grad_1 = back(1, gc_own, ctx_a, ctx_a_give, lse_a[2:4])
        a, b, a_came, b_came, grad_1, gc_own = stage(a, b, a_came, b_came, grad_1, gc_own)
        total = jnp.concatenate([add(b[:ZS], b_came), add(a[:ZS], a_came)], axis=1)
        came_b = scatter_z(total, 1, 2, 3)
        (qa, qa_far, qb, qb_far), sums = qkv_grads(back_early, meta, x_own, x_oth, [grad_0, grad_1], 0)
        qa_came, qb_came = swap(qa_far, "y"), swap(qb_far, "x")
        grad_2 = back(2, after(gc_own, sums), ctx_b, ctx_b_give, lse_b)
        total, qa, qb, qa_came, qb_came, sums, grad_2, *came_b = stage(total, qa, qb, qa_came, qb_came, sums, grad_2, *came_b)
        ra, ra_far, rb, rb_far = qkv_grads(back_late, meta, x_own, x_oth, [grad_2], 2, sums, vg, tables)
        ra_came, rb_came = swap(ra_far, "y"), swap(rb_far, "x")
        grads = [grad_0, grad_1, after(grad_2, ra)]
        own_given, oth_given = input_grads(meta, grads, w_qkv, True)
        oth_given = swap(oth_given, "core")
        total_b = added(total[0], *came_b)
        ra, rb, ra_came, rb_came, own_given, oth_given, total_b = stage(
            ra, rb, ra_came, rb_came, own_given, oth_given, total_b
        )
        gx_came = swap(add(gr_given, own_given, oth_given), "y")
        qa = jnp.concatenate([add(qa, qa_came), add(ra, ra_came)], axis=1)
        qb = jnp.concatenate([add(qb, qb_came), add(rb, rb_came)], axis=1)
        qa_came, qb_came = swap(qa[ZS:], "x"), swap(qb[ZS:], "y")
        own_kept, oth_kept = input_grads(meta, [grad_0, grad_1, after(grad_2, qa)], w_qkv, False)
        qa, qb, qa_came, qb_came, own_kept, oth_kept = stage(qa, qb, qa_came, qb_came, own_kept, oth_kept)
        total = jnp.concatenate([add(qb[:ZS], qb_came), add(qa[:ZS], qa_came)], axis=1)
        came = scatter_z(total, 1, 2, 3)
        oth_kept = swap(oth_kept, "core")
        gx_kept = add(gr_kept, own_kept, oth_kept)

        def finish(total, lengths):
            mine, theirs, at = [], [], 0
            for length in lengths:
                kept, given = by_parity(total[at : at + length], total[at + length : at + 2 * length])
                mine.append(kept)
                theirs.append(given)
                at += 2 * length
            mine = jnp.concatenate(mine, axis=0)
            came = swap(jnp.concatenate(theirs, axis=0).astype(BF), "core").astype(F32)
            halves, cuts, at = by_parity(mine, came), [], 0
            for length in lengths:
                cuts.append([v[at : at + length] for v in halves])
                at += length
            return cuts

        cuts_b = finish(total_b, lengths_b)
        gx_came, gx_kept, total, *came = stage(gx_came, gx_kept, total, *came)
        grad_input = pair(gx_kept, gx_came)[:, None]
        total_a = added(total[0], *came)
        ends = (0, depth, depth + 32, 2 * depth + 32, 3 * depth)
        one, three, two, rest = (total_a[i:j] for i, j in zip(ends[:4], ends[1:]))
        total_a = jnp.concatenate([one, two, three, rest, total_a[3 * depth :]])
        cuts_a = finish(total_a, lengths_a)
        kept, given = by_parity(total_a[3 * depth :, :128], total_a[3 * depth :, 128:256])
        small = kept + swap(given, "core")
        small = jnp.concatenate([small[v, :share] for v in range(8)] + [small[8, :share_f]])
    else:
        plan_a, plan_b = Plan(sections_a, None), Plan(sections_b, None)
        everyone = lambda w: lax.all_gather(w, ("dp", "seq"), axis=0, tiled=True)
        full_qkv, full_proj, full_inner, full_down = map(everyone, (qkv_weight, proj_weight, inner_weight, down_weight))
        row = everyone(jnp.concatenate(list(vectors) + [inner_bias])[None])
        full_vectors = row[:, : 8 * share].reshape(members, 8, share).transpose(1, 0, 2).reshape(8, CHIPS, 2, -1)
        full_bias = row[:, 8 * share :].reshape(1, CHIPS, 2, -1)
        padded = lambda v: jnp.pad(v, ((0, 0),) * 3 + ((0, 128 - v.shape[3]),))
        rows = jnp.concatenate([padded(full_vectors), padded(full_bias)], axis=0)
        rows = jnp.pad(rows, ((0, 7), (0, 0), (0, 1), (0, 0))).transpose(1, 0, 2, 3).reshape(CHIPS, 16, 384)

        def packed(h):
            col = lambda w, at, width=half: w[:, at : at + width].reshape(CHIPS, -1, width)
            a = [
                jnp.concatenate([col(full_qkv, model * w + half * h + 128 * p, 128) for w in range(3)], axis=2)
                for p in range(3)
            ]
            b = [col(full_proj, half * h)] + [col(full_inner, ffw // 2 * h + half * g) for g in range(groups)]
            return jnp.concatenate(a + [rows], axis=1), jnp.concatenate(b + [col(full_down, half * h)], axis=1)

        zero, one = packed(0), packed(1)
        pieces_a = [jnp.where(even, zero[0], one[0])]
        own_b, oth_b = [[v] for v in by_parity(zero[1], one[1])]
        tables = spread_tables(model, depth // 2, deep // 2)
        x_own = pair(x_kept, swap(x_given, "y"))
        x_oth = swap(x_own, "core")
        d_given, d_kept = given_kept(d_out[:, 0])
        d_own = pair(d_kept, swap(d_given, "y")).reshape(-1, model)
        blocks_mine, blocks_given = pick_blocks(swap(blocks, "core"))
        table = jnp.where(c == y, blocks_mine, swap(blocks_given, "y"))
        qkv, w_qkv, spread = project_qkv(plan_a, meta, pieces_a, x_own, x_oth, tables)
        ctx_a, ctx_a_give, lse_a = attention(slice(0, 4), 0, qkv, table)
        ctx_b, ctx_b_give, lse_b = attention(slice(4, 6), 2, qkv, table)
        ctx_oth = [swap(v, "core") for v in (ctx_a_give, ctx_b_give)]
        found = feed_forward(plan_b, meta, own_b, oth_b, [ctx_a, ctx_b], ctx_oth, x_own.reshape(-1, model), d_own, spread, ffw)
        out_kept, out_given, gr_kept, gr_given, hid, gf, x1_low, gp, ga, gc_own, gc_oth, context, vg = found
        layer_out = pair(out_kept, swap(out_given, "y"))[:, None]
        gc_came = swap(gc_oth, "core")
        grads_own, grads_oth = weight_grads(plan_b, meta, hid, gp, gf, x1_low, context, ga)
        ctxs = [(ctx_a, ctx_a_give, lse_a[2 * p : 2 * p + 2]) for p in range(2)] + [(ctx_b, ctx_b_give, lse_b)]
        grads = [attention_back(p, qkv, gc_own, gc_came, *ctxs[p], table) for p in range(3)]
        pieces = qkv_grads(plan_a, meta, x_own, x_oth, grads, 0, jnp.zeros((8, 3 * 128), F32), vg, tables)
        own_given, oth_given = input_grads(meta, grads, w_qkv, True)
        own_kept, oth_kept = input_grads(meta, grads, w_qkv, False)
        gx_came = swap(add(gr_given, own_given, swap(oth_given, "core")), "y")
        grad_input = pair(add(gr_kept, own_kept, swap(oth_kept, "core")), gx_came)[:, None]
        scatter = lambda v: lax.psum_scatter(v.astype(F32), ("dp", "seq"), scatter_dimension=0, tiled=True)
        found = pieces[0][:, 3 * depth :].astype(F32)
        found = jnp.stack([found[:, :, :128], found[:, :, 128:256]], axis=1).transpose(2, 0, 1, 3)
        small = jnp.concatenate([found[v, :, :, : depth // 2].reshape(-1, 1) for v in range(8)], axis=1)
        small = jnp.concatenate([small.reshape(members, share, 8).transpose(0, 2, 1).reshape(members, -1),
                                 found[8, :, :, : deep // 2].reshape(members, share_f)], axis=1)
        small = scatter(small)[0]
        zero = jnp.zeros((model, half), BF)
        cuts_a, cuts_b = [], []
        for p in range(3):
            part = pieces[0][:, depth * p : depth * p + depth].reshape(-1, half)
            cuts_a.append([scatter(v) for v in by_parity(part, zero)])
        halves, at = by_parity(grads_own[0], grads_oth[0]), 0
        for length in sections_b:
            cuts_b.append([scatter(v[:, at : at + length].reshape(-1, half)) for v in halves])
            at += length

    cut_w = lambda h, p, w: cuts_a[p][h][:, 128 * w : 128 * w + 128]
    grad_qkv = jnp.concatenate([cut_w(h, p, w) for w in range(3) for h in range(2) for p in range(3)], axis=1)
    grad_proj = jnp.concatenate(cuts_b[0], axis=1)
    grad_inner = jnp.concatenate([cuts_b[1 + g][h] for h in range(2) for g in range(groups)], axis=1)
    grad_down = jnp.concatenate(cuts_b[1 + groups], axis=1)
    vector = [small[share * i : share * i + share] for i in range(8)]
    return (
        layer_out,
        grad_input,
        grad_qkv,
        vector[0],
        vector[1],
        grad_proj,
        vector[2],
        vector[3],
        vector[4],
        grad_inner,
        small[8 * share :],
        grad_down,
        vector[5],
        vector[6],
        vector[7],
    )


def solution(mesh):
    row, vec = P(("dp", "seq"), None), P(("dp", "seq"))
    wide = P(None, "dp", "seq", None)
    return jax.shard_map(
        body,
        mesh=mesh,
        in_specs=(wide, row, vec, vec, row, vec, vec, vec, row, vec, row, vec, vec, vec)
        + (P(None, "dp", None), P(None, "dp", "seq", None, None), P(None, "dp", None), wide),
        out_specs=(wide, wide, row, vec, vec, row, vec, vec, vec, row, vec, row, vec, vec, vec),
        check_vma=False,
    )
```

time: 422 us -> 381 us (0.903)
  waiting for transfers between devices: 103 us -> 63.8 us
  Pallas kernels: 184 us -> 198 us
  local copies, waits for them, and re-layouts: 20.5 us -> 11.6 us
  starting transfers between devices: 71.3 us -> 63.5 us
    ppermute x32 -> x39, waiting for transfers between devices: 51.7 us -> 26.4 us  [swap(): return lax.ppermute(value, 'seq', [(s, s ^ bit) for s in range(4)])]
    ppermute x8 -> x11, starting transfers between devices: 27.2 us -> 16 us  [swap(): lax.ppermute(value, 'dp', [(d, d ^ 1) for d in range(lax.axis_size('dp'))])]
    ppermute x12, waiting for transfers between devices: 38.8 us -> 28.1 us  [shift_z(): lax.ppermute(value, 'dp', [(2 * z + x, (z + by) % size * 2 + x) for z in...]
    ppermute x12, starting transfers between devices: 16.1 us -> 25.4 us  [shift_z(): lax.ppermute(value, 'dp', [(2 * z + x, (z + by) % size * 2 + x) for z in...]
    unnamed x116 -> x128, local copies, waits for them, and re-layouts: 11.5 us -> 5.4 us
    ppermute x32 -> x39, starting transfers between devices: 28 us -> 22.1 us  [swap(): return lax.ppermute(value, 'seq', [(s, s ^ bit) for s in range(4)])]
    pallas_call x1 -> x2, Pallas kernels: 9.52 us -> 13.7 us  [input_grads(): pl.pallas_call(input_grads_kernel, grid_spec=pltpu.PrefetchScalarGridSpec...]
    ppermute x8 -> x11, waiting for transfers between devices: 12.6 us -> 9.27 us  [swap(): lax.ppermute(value, 'dp', [(d, d ^ 1) for d in range(lax.axis_size('dp'))])]
  transfers between devices with their start and end apart: 52 -> 62, of which waited for: 14 -> 19; matrix products, arithmetic and copies ran while one was open for 12% -> 8% of each run, Pallas kernels for 26% -> 37%
where the time goes in v3:
time: 381 us; the launch traced here: 375 us
  Pallas kernels  198 us (52%)
  waiting for transfers between devices  63.8 us (17%)
  starting transfers between devices  63.5 us (17%)
  other arithmetic  36.9 us (10%)
  local copies, waits for them, and re-layouts  11.6 us (3%)
    pallas_call x3, Pallas kernels, attend_back(): pl.pallas_call(attend_back_kernel, grid=(1,), in_specs=[smem()] * 4 + [gr...  59.3 us
    pallas_call x1, Pallas kernels, feed_forward(): pl.pallas_call(lambda *refs: ffn_kernel(plan, len(own_pieces), len(ctx),...  43.7 us
    pallas_call x2, Pallas kernels, attend(): pl.pallas_call(attend_kernel, grid=(1,), in_specs=[smem()] * 4 + [pl.Bloc...  31.3 us
    ppermute x12, waiting for transfers between devices, shift_z(): lax.ppermute(value, 'dp', [(2 * z + x, (z + by) % size * 2 + x) for z in...  28.1 us
    ppermute x39, waiting for transfers between devices, swap(): return lax.ppermute(value, 'seq', [(s, s ^ bit) for s in range(4)])  26.4 us
    ppermute x12, starting transfers between devices, shift_z(): lax.ppermute(value, 'dp', [(2 * z + x, (z + by) % size * 2 + x) for z in...  25.4 us
    ppermute x39, starting transfers between devices, swap(): return lax.ppermute(value, 'seq', [(s, s ^ bit) for s in range(4)])  22.1 us
    pallas_call x1, Pallas kernels, weight_grads(): pl.pallas_call(lambda *refs: weight_grads_kernel(plan, len(pieces), *refs...  21.9 us
  transfers between devices with their start and end apart: 62, of which 19 were waited for; matrix products, arithmetic and copies ran while one was open for 8% of the time, Pallas kernels for 37%

profile of v3, /device:TPU:0, one launch (start us, length us, event | category | flops | bytes accessed | tf_op | source)
XLA Modules:
  0.0 375.5 jit_solution(7739888506532613440)
XLA Ops:
  3.9 1.9 pack.1
  9.9 2.6 collective-permute-start.2
  13.1 1.6 collective-permute-start.7
  15.2 2.2 collective-permute-start.6
  18.3 1.6 collective-permute-start.4
  19.9 7.6 %collective-permute-done.6 = bf16[160,384]{1,0:T(8,128)(2,1)S(1)} collective-permute-done((bf16[160,384]{1,0:T(8,128)(2,1)S(1)}, bf16[160,384]{1,0:T(8,128)(2,1)S(1)}, u32[]{:S(2)}, u32[]{:S(2)}) %collective-permute-start.6) | collective-permute-done | bytes 122912 | tf_op jit(solution)/shard_map/ppermute | solution.py:69
  27.5 7.9 %collective-permute-done.5 = bf16[160,384]{1,0:T(8,128)(2,1)S(1)} collective-permute-done((bf16[160,384]{1,0:T(8,128)(2,1)S(1)}, bf16[160,384]{1,0:T(8,128)(2,1)S(1)}, u32[]{:S(2)}, u32[]{:S(2)}) %collective-permute-start.5) | collective-permute-done | bytes 122912 | tf_op jit(solution)/shard_map/ppermute | solution.py:69
  42.5 3.7 collective-permute-done.11.refs_6_
  46.2 1.5 collective-permute-done.9.refs_5_
  47.8 4.0 %collective-permute-done.10.refs_3_ = bf16[4,80,384]{2,1,0:T(8,128)(2,1)} collective-permute-done((bf16[4,80,384]{2,1,0:T(8,128)(2,1)S(1)}, bf16[4,80,384]{2,1,0:T(8,128)(2,1)}, u32[]{:S(2)}, u32[]{:S(2)}) %collective-permute-start.10) | collective-permute-done | bytes 245792 | tf_op jit(solution)/shard_map/ppermute | solution.py:64
  51.7 3.7 collective-permute-done.12
  56.2 1.7 maximum_select_fusion.refs_8_.refs_1_
  65.8 4.4 %collective-permute-done.13.refs_4_ = bf16[4,80,384]{2,1,0:T(8,128)(2,1)S(1)} collective-permute-done((bf16[4,80,384]{2,1,0:T(8,128)(2,1)}, bf16[4,80,384]{2,1,0:T(8,128)(2,1)S(1)}, u32[]{:S(2)}, u32[]{:S(2)}) %collective-permute-start.13) | collective-permute-done | bytes 245792 | tf_op jit(solution)/shard_map/ppermute | solution.py:64
  76.7 11.3 %project_qkv.1 = (bf16[2048,1152]{1,0:T(8,128)(2,1)}, bf16[16,48,1152]{2,1,0:T(8,128)(2,1)}, f32[16,768]{1,0:T(8,128)}) custom-call(s32[4]{0:T(128)} %pad_add_fusion.2.meta.refs_0_, bf16[4,160,384]{2,1,0:T(8,128)(2,1)} %copy-done.2, bf16[4,80,384]{2,1,0:T(8,128)(2,1)} %collective-permute-done.8.refs_2_, bf16[4,80,384]{2,1,0:T(8,128)(2,1)} %collective-permute-done.10.refs_3_, ...), custom_call_target="tpu_custom_call" | custom-call | flops 3623878656 | bytes 7864320 | tf_op jit(solution)/shard_map/project_qkv/pallas_call | solution.py:257
  88.8 12.4 %attend.2 = (bf16[1024,128]{1,0:T(8,128)(2,1)}, bf16[1024,128]{1,0:T(8,128)(2,1)}, f32[2,2048]{1,0:T(2,128)}) custom-call(s32[4]{0:T(128)} %pad_add_fusion.2.meta.refs_0_, s32[8]{0:T(128)} %get-tuple-element.337.lo_ref, s32[8]{0:T(128)} %get-tuple-element.338.n_ref, s32[2]{0:T(128)} %fusion.44.glob_ref, bf16[2048,1152]{1,0:T(8,128)(2,1)} %get-tuple-element.222.qkv_ref, ...), custom_call_target="tpu_custom_call" | custom-call | flops 5872025600 | bytes 2621440 | tf_op jit(solution)/shard_map/attend/pallas_call | solution.py:393
  101.2 2.4 broadcast_select_fusion
  106.6 2.1 collective-permute-start.24
  109.8 18.9 %attend.3 = (bf16[1024,256]{1,0:T(8,128)(2,1)}, bf16[1024,256]{1,0:T(8,128)(2,1)}, f32[4,2048]{1,0:T(4,128)}) custom-call(s32[4]{0:T(128)} %pad_add_fusion.2.meta.refs_0_, s32[8]{0:T(128)} %get-tuple-element.337.lo_ref, s32[8]{0:T(128)} %get-tuple-element.338.n_ref, s32[2]{0:T(128)} %fusion.44.glob_ref, bf16[2048,1152]{1,0:T(8,128)(2,1)} %get-tuple-element.222.qkv_ref, ...), custom_call_target="tpu_custom_call" | custom-call | flops 11744051200 | bytes 5242880 | tf_op jit(solution)/shard_map/attend/pallas_call | solution.py:393
  128.8 3.8 %collective-permute-done.25 = bf16[512,768]{1,0:T(8,128)(2,1)S(1)} collective-permute-done((bf16[512,768]{1,0:T(8,128)(2,1)}, bf16[512,768]{1,0:T(8,128)(2,1)S(1)}, u32[]{:S(2)}, u32[]{:S(2)}) %collective-permute-start.25) | collective-permute-done | bytes 786464 | tf_op jit(solution)/shard_map/ppermute | solution.py:64
  134.7 2.0 collective-permute-done.31.refs_11_
  137.9 43.7 %feed_forward.1 = (bf16[512,768]{1,0:T(8,128)(2,1)}, bf16[512,768]{1,0:T(8,128)(2,1)}, f32[512,768]{1,0:T(8,128)}, f32[512,768]{1,0:T(8,128)}, bf16[1024,3072]{1...) custom-call(s32[4]{0:T(128)} %pad_add_fusion.2.meta.refs_0_, ...), custom_call_target="tpu_custom_call" | custom-call | flops 21743271936 | bytes 40894464 | tf_op jit(solution)/shard_map/feed_forward/pallas_call | solution.py:695
  182.9 21.9 %weight_grads.1 = (bf16[8,208,384]{2,1,0:T(8,128)(2,1)}, bf16[8,208,384]{2,1,0:T(8,128)(2,1)}, bf16[8,224,384]{2,1,0:T(8,128)(2,1)}, bf16[8,224,384]{2,1,0:T(8,1...) custom-call(s32[4]{0:T(128)} %pad_add_fusion.2.meta.refs_0_, ...), custom_call_target="tpu_custom_call" | custom-call | flops 10871635968 | bytes 18874368 | tf_op jit(solution)/shard_map/weight_grads/pallas_call | solution.py:750
  205.5 2.7 collective-permute-done.36
  208.3 2.7 add_convert_fusion.3
  212.4 2.3 collective-permute-start.39
  215.4 19.8 %attend_back.3.refs_3_.refs_0_ = bf16[2048,384]{1,0:T(8,128)(2,1)} custom-call(s32[4]{0:T(128)} %pad_add_fusion.2.meta.refs_0_, s32[8]{0:T(128)} %get-tuple-element.337.lo_ref, s32[8]{0:T(128)} %get-tuple-element.338.n_ref, s32[2]{0:T(128)} %fusion.44.glob_ref, bf16[2048,1152]{1,0:T(8,128)(2,1)} %get-tuple-element.222.qkv_ref, ...), custom_call_target="tpu_custom_call" | custom-call | flops 12582912000 | bytes 5242880 | tf_op jit(solution)/shard_map/attend_back/pallas_call | solution.py:489
  235.3 6.8 %collective-permute-done.38 = bf16[8,208,384]{2,1,0:T(8,128)(2,1)} collective-permute-done((bf16[8,208,384]{2,1,0:T(8,128)(2,1)}, bf16[8,208,384]{2,1,0:T(8,128)(2,1)}, u32[]{:S(2)}, u32[]{:S(2)}) %collective-permute-start.38) | collective-permute-done | bytes 1277984 | tf_op jit(solution)/shard_map/ppermute | solution.py:64
  242.1 3.3 collective-permute-done.39
  245.4 3.1 add_convert_fusion.2
  249.4 1.8 collective-permute-start.42
  251.2 2.3 add_convert_fusion
  253.9 19.6 %attend_back.4.refs_4_.refs_1_ = bf16[2048,384]{1,0:T(8,128)(2,1)} custom-call(s32[4]{0:T(128)} %pad_add_fusion.2.meta.refs_0_, s32[8]{0:T(128)} %get-tuple-element.337.lo_ref, s32[8]{0:T(128)} %get-tuple-element.338.n_ref, s32[2]{0:T(128)} %fusion.44.glob_ref, bf16[2048,1152]{1,0:T(8,128)(2,1)} %get-tuple-element.222.qkv_ref, ...), custom_call_target="tpu_custom_call" | custom-call | flops 12582912000 | bytes 5242880 | tf_op jit(solution)/shard_map/attend_back/pallas_call | solution.py:489
  275.0 4.7 %collective-permute-start.48 = (bf16[432,384]{1,0:T(8,128)(2,1)S(1)}, bf16[432,384]{1,0:T(8,128)(2,1)S(1)}, u32[]{:S(2)}, u32[]{:S(2)}) collective-permute-start(bf16[432,384]{1,0:T(8,128)(2,1)S(1)} %get-tuple-element.343), channel_id=1, source_target_pairs={{0,8},{4,12},{8,16},{12,20},{16,24},{20,28},{24,0},{28,4},{1,9},{5... | collective-permute-start | bytes 995336 | tf_op jit(solution)/shard_map/ppermute | solution.py:69
  279.7 4.4 %collective-permute-start.46 = (bf16[432,384]{1,0:T(8,128)(2,1)S(1)}, bf16[432,384]{1,0:T(8,128)(2,1)}, u32[]{:S(2)}, u32[]{:S(2)}) collective-permute-start(bf16[432,384]{1,0:T(8,128)(2,1)S(1)} %get-tuple-element.344), channel_id=1, source_target_pairs={{0,24},{4,28},{8,0},{12,4},{16,8},{20,12},{24,16},{28,20},{1,25},{... | collective-permute-start | bytes 995336 | tf_op jit(solution)/shard_map/ppermute | solution.py:69
  284.7 8.1 %qkv_grads.2 = (bf16[8,48,384]{2,1,0:T(8,128)(2,1)}, bf16[8,48,384]{2,1,0:T(8,128)(2,1)}, bf16[8,48,384]{2,1,0:T(8,128)(2,1)}, bf16[8,48,384]{2,1,0:T(8,128)(2,1)}, f32[8,384]{1,0:T(8,128)}) custom-call(s32[4]{0:T(128)} %pad_add_fusion.2.meta.refs_0_, bf16[2,512,768]{2,1,0:T(8,128)(2,1)} %copy-done, ...), custom_call_target="tpu_custom_call" | custom-call | flops 2415919104 | bytes 7864320 | tf_op jit(solution)/shard_map/qkv_grads/pallas_call | solution.py:833
  293.9 19.9 %attend_back.5.refs_3_.refs_2_ = bf16[2048,384]{1,0:T(8,128)(2,1)} custom-call(s32[4]{0:T(128)} %pad_add_fusion.2.meta.refs_0_, s32[8]{0:T(128)} %get-tuple-element.337.lo_ref, s32[8]{0:T(128)} %get-tuple-element.338.n_ref, s32[2]{0:T(128)} %fusion.44.glob_ref, bf16[2048,1152]{1,0:T(8,128)(2,1)} %get-tuple-element.222.qkv_ref, ...), custom_call_target="tpu_custom_call" | custom-call | flops 12582912000 | bytes 5242880 | tf_op jit(solution)/shard_map/attend_back/pallas_call | solution.py:489
  313.9 6.3 %qkv_grads.3 = (bf16[8,32,384]{2,1,0:T(8,128)(2,1)}, bf16[8,32,384]{2,1,0:T(8,128)(2,1)}, bf16[8,32,384]{2,1,0:T(8,128)(2,1)}, bf16[8,32,384]{2,1,0:T(8,128)(2,1)}) custom-call(s32[4]{0:T(128)} %pad_add_fusion.2.meta.refs_0_, bf16[2,512,768]{2,1,0:T(8,128)(2,1)} %copy-done, bf16[2,512,768]{2,1,0:T(8,128)(2,1)} %collective-permute-done.16.refs_9_.refs_2_, ...), custom_call_target="tpu_custom_call" | custom-call | flops 1207959552 | bytes 7864320 | tf_op jit(solution)/shard_map/qkv_grads/pallas_call | solution.py:833
  320.3 6.9 %input_grads.2 = (bf16[512,768]{1,0:T(8,128)(2,1)}, bf16[512,768]{1,0:T(8,128)(2,1)}) custom-call(s32[4]{0:T(128)} %pad_add_fusion.2.meta.refs_0_, bf16[2048,384]{1,0:T(8,128)(2,1)} %attend_back.3.refs_3_.refs_0_, bf16[2048,384]{1,0:T(8,128)(2,1)} %attend_back.4.refs_4_.refs_1_, bf16[2048,384]{1,0:T(8,128)(2,1)} %attend_back.5.refs_3_.refs_2_, ...), custom_call_target="tpu_custom_call" | custom-call | flops 1811939328 | bytes 3932160 | tf_op jit(solution)/shard_map/input_grads/pallas_call | solution.py:879
  328.5 2.5 collective-permute-start.50
  334.5 2.0 collective-permute-done.50
  340.6 1.8 collective-permute-start.53
  342.3 1.7 collective-permute-start.54
  344.8 6.8 %input_grads.3 = (bf16[512,768]{1,0:T(8,128)(2,1)}, bf16[512,768]{1,0:T(8,128)(2,1)}) custom-call(s32[4]{0:T(128)} %pad_add_fusion.2.meta.refs_0_, bf16[2048,384]{1,0:T(8,128)(2,1)} %attend_back.3.refs_3_.refs_0_, bf16[2048,384]{1,0:T(8,128)(2,1)} %attend_back.4.refs_4_.refs_1_, bf16[2048,384]{1,0:T(8,128)(2,1)} %attend_back.5.refs_3_.refs_2_, ...), custom_call_target="tpu_custom_call" | custom-call | flops 1811939328 | bytes 3932160 | tf_op jit(solution)/shard_map/input_grads/pallas_call | solution.py:879
  353.5 6.0 %collective-permute-start.58 = (bf16[160,384]{1,0:T(8,128)(2,1)S(1)}, bf16[160,384]{1,0:T(8,128)(2,1)S(1)}, u32[]{:S(2)}, u32[]{:S(2)}) collective-permute-start(bf16[160,384]{1,0:T(8,128)(2,1)S(1)} %get-tuple-element.348), channel_id=1, source_target_pairs={{0,8},{4,12},{8,16},{12,20},{16,24},{20,28},{24,0},{28,4},{1,9},{5... | collective-permute-start | bytes 368648 | tf_op jit(solution)/shard_map/ppermute | solution.py:69
  359.5 1.7 collective-permute-start.57
  363.1 2.7 collective-permute-done.56
  365.8 4.7 %collective-permute-done.57 = bf16[160,384]{1,0:T(8,128)(2,1)S(1)} collective-permute-done((bf16[160,384]{1,0:T(8,128)(2,1)S(1)}, bf16[160,384]{1,0:T(8,128)(2,1)S(1)}, u32[]{:S(2)}, u32[]{:S(2)}) %collective-permute-start.57) | collective-permute-done | bytes 122912 | tf_op jit(solution)/shard_map/ppermute | solution.py:69
  371.3 1.9 maximum_select_fusion.2
  (319 shorter events, 63.9 us)
Async XLA Ops:
  2.1 7.5 %collective-permute-start.1 = (bf16[16,128]{1,0:T(8,128)(2,1)S(1)}, bf16[16,128]{1,0:T(8,128)(2,1)S(1)}, u32[]{:S(2)}, u32[]{:S(2)}) collective-permute-start(bf16[16,128]{1,0:T(8,128)(2,1)S(1)} %fusion.40), channel_id=1, source_target_pairs={{0,1},{1,0},{2,3},{3,2},{4,5},{5,4},{6,7},{7,6},{8,9},{9,8},{10,11... | collective-permute-start | bytes 12296 | tf_op jit(solution)/shard_map/ppermute | solution.py:64
  3.3 15.0 %collective-permute-start.3 = (s32[2,3,32,3]{2,1,3,0:T(4,128)S(1)}, s32[2,3,32,3]{2,1,3,0:T(4,128)S(1)}, u32[]{:S(2)}, u32[]{:S(2)}) collective-permute-start(s32[2,3,32,3]{2,1,3,0:T(4,128)S(1)} %bitcast.112), channel_id=1, source_target_pairs={{0,1},{1,0},{2,3},{3,2},{4,5},{5,4},{6,7},{7,6},{8,9},{9,8},{10,11... | collective-permute-start | bytes 6920 | tf_op jit(solution)/shard_map/ppermute | solution.py:64
  9.9 25.5 %collective-permute-start.2 = (bf16[512,768]{1,0:T(8,128)(2,1)S(1)}, bf16[512,768]{1,0:T(8,128)(2,1)S(1)}, u32[]{:S(2)}, u32[]{:S(2)}) collective-permute-start(bf16[512,768]{1,0:T(8,128)(2,1)S(1)} %get-tuple-element.179), channel_id=1, source_target_pairs={{0,2},{1,3},{2,0},{3,1},{4,6},{5,7},{6,4},{7,5},{8,10},{9,11},{10,... | collective-permute-start | bytes 2359304 | tf_op jit(solution)/shard_map/ppermute | solution.py:64
  13.1 22.3 %collective-permute-start.7 = (bf16[432,384]{1,0:T(8,128)(2,1)S(1)}, bf16[432,384]{1,0:T(8,128)(2,1)S(1)}, u32[]{:S(2)}, u32[]{:S(2)}) collective-permute-start(bf16[432,384]{1,0:T(8,128)(2,1)S(1)} %constant_dynamic-update-slice_fusion.7), channel_id=1, source_target_pairs={{0,8},{4,12},{8,16},{12,20},{16,24},{20,28},{24,0},{28,4},{1,9},{5... | collective-permute-start | bytes 995336 | tf_op jit(solution)/shard_map/ppermute | solution.py:69
  15.2 12.3 %collective-permute-start.6 = (bf16[160,384]{1,0:T(8,128)(2,1)S(1)}, bf16[160,384]{1,0:T(8,128)(2,1)S(1)}, u32[]{:S(2)}, u32[]{:S(2)}) collective-permute-start(bf16[160,384]{1,0:T(8,128)(2,1)S(1)} %constant_dynamic-update-slice_fusion), channel_id=1, source_target_pairs={{0,24},{4,28},{8,0},{12,4},{16,8},{20,12},{24,16},{28,20},{1,25},{... | collective-permute-start | bytes 368648 | tf_op jit(solution)/shard_map/ppermute | solution.py:69
  17.5 18.0 %collective-permute-start.5 = (bf16[160,384]{1,0:T(8,128)(2,1)S(1)}, bf16[160,384]{1,0:T(8,128)(2,1)S(1)}, u32[]{:S(2)}, u32[]{:S(2)}) collective-permute-start(bf16[160,384]{1,0:T(8,128)(2,1)S(1)} %constant_dynamic-update-slice_fusion), channel_id=1, source_target_pairs={{0,16},{4,20},{8,24},{12,28},{16,0},{20,4},{24,8},{28,12},{1,17},{... | collective-permute-start | bytes 368648 | tf_op jit(solution)/shard_map/ppermute | solution.py:69
  18.3 17.2 %collective-permute-start.4 = (bf16[160,384]{1,0:T(8,128)(2,1)S(1)}, bf16[160,384]{1,0:T(8,128)(2,1)S(1)}, u32[]{:S(2)}, u32[]{:S(2)}) collective-permute-start(bf16[160,384]{1,0:T(8,128)(2,1)S(1)} %constant_dynamic-update-slice_fusion), channel_id=1, source_target_pairs={{0,8},{4,12},{8,16},{12,20},{16,24},{20,28},{24,0},{28,4},{1,9},{5... | collective-permute-start | bytes 368648 | tf_op jit(solution)/shard_map/ppermute | solution.py:69
  37.1 9.1 %collective-permute-start.11 = (bf16[4,80,384]{2,1,0:T(8,128)(2,1)}, bf16[4,80,384]{2,1,0:T(8,128)(2,1)}, u32[]{:S(2)}, u32[]{:S(2)}) collective-permute-start(bf16[4,80,384]{2,1,0:T(8,128)(2,1)} %get-tuple-element.351), channel_id=1, source_target_pairs={{0,4},{4,0},{8,12},{12,8},{16,20},{20,16},{24,28},{28,24},{1,5},{5... | collective-permute-start | bytes 737288 | tf_op jit(solution)/shard_map/ppermute | solution.py:62
  38.6 9.2 %collective-permute-start.9 = (bf16[4,80,384]{2,1,0:T(8,128)(2,1)}, bf16[4,80,384]{2,1,0:T(8,128)(2,1)}, u32[]{:S(2)}, u32[]{:S(2)}) collective-permute-start(bf16[4,80,384]{2,1,0:T(8,128)(2,1)} %get-tuple-element.351), channel_id=1, source_target_pairs={{0,2},{1,3},{2,0},{3,1},{4,6},{5,7},{6,4},{7,5},{8,10},{9,11},{10,... | collective-permute-start | bytes 737288 | tf_op jit(solution)/shard_map/ppermute | solution.py:64
  39.1 12.6 %collective-permute-start.10 = (bf16[4,80,384]{2,1,0:T(8,128)(2,1)S(1)}, bf16[4,80,384]{2,1,0:T(8,128)(2,1)}, u32[]{:S(2)}, u32[]{:S(2)}) collective-permute-start(bf16[4,80,384]{2,1,0:T(8,128)(2,1)S(1)} %get-tuple-element.352), channel_id=1, source_target_pairs={{0,2},{1,3},{2,0},{3,1},{4,6},{5,7},{6,4},{7,5},{8,10},{9,11},{10,... | collective-permute-start | bytes 737288 | tf_op jit(solution)/shard_map/ppermute | solution.py:64
  40.6 11.1 %collective-permute-start.8 = (bf16[4,80,384]{2,1,0:T(8,128)(2,1)S(1)}, bf16[4,80,384]{2,1,0:T(8,128)(2,1)}, u32[]{:S(2)}, u32[]{:S(2)}) collective-permute-start(bf16[4,80,384]{2,1,0:T(8,128)(2,1)S(1)} %get-tuple-element.352), channel_id=1, source_target_pairs={{0,4},{4,0},{8,12},{12,8},{16,20},{20,16},{24,28},{28,24},{1,5},{5... | collective-permute-start | bytes 737288 | tf_op jit(solution)/shard_map/ppermute | solution.py:62
  41.2 14.3 %collective-permute-start.12 = (bf16[432,384]{1,0:T(8,128)(2,1)S(1)}, bf16[432,384]{1,0:T(8,128)(2,1)S(1)}, u32[]{:S(2)}, u32[]{:S(2)}) collective-permute-start(bf16[432,384]{1,0:T(8,128)(2,1)S(1)} %constant_dynamic-update-slice_fusion.7), channel_id=1, source_target_pairs={{0,16},{4,20},{8,24},{12,28},{16,0},{20,4},{24,8},{28,12},{1,17},{... | collective-permute-start | bytes 995336 | tf_op jit(solution)/shard_map/ppermute | solution.py:69
  57.8 12.3 %collective-permute-start.16 = (bf16[2,512,768]{2,1,0:T(8,128)(2,1)S(1)}, bf16[2,512,768]{2,1,0:T(8,128)(2,1)}, u32[]{:S(2)}, u32[]{:S(2)}) collective-permute-start(bf16[2,512,768]{2,1,0:T(8,128)(2,1)S(1)} %maximum_select_fusion.refs_8_.refs_1_), channel_id=1, source_target_pairs={{0,1},{1,0},{2,3},{3,2},{4,5},{5,4},{6,7},{7,6},{8,9},{9,8},{10,11... | collective-permute-start | bytes 4718600 | tf_op jit(solution)/shard_map/ppermute | solution.py:64
  58.9 11.3 %collective-permute-start.17 = (bf16[432,384]{1,0:T(8,128)(2,1)S(1)}, bf16[432,384]{1,0:T(8,128)(2,1)S(1)}, u32[]{:S(2)}, u32[]{:S(2)}) collective-permute-start(bf16[432,384]{1,0:T(8,128)(2,1)S(1)} %constant_dynamic-update-slice_fusion.7), channel_id=1, source_target_pairs={{0,24},{4,28},{8,0},{12,4},{16,8},{20,12},{24,16},{28,20},{1,25},{... | collective-permute-start | bytes 995336 | tf_op jit(solution)/shard_map/ppermute | solution.py:69
  61.4 8.8 %collective-permute-start.13 = (bf16[4,80,384]{2,1,0:T(8,128)(2,1)}, bf16[4,80,384]{2,1,0:T(8,128)(2,1)S(1)}, u32[]{:S(2)}, u32[]{:S(2)}) collective-permute-start(bf16[4,80,384]{2,1,0:T(8,128)(2,1)} %collective-permute-done.8.refs_2_), channel_id=1, source_target_pairs={{0,2},{1,3},{2,0},{3,1},{4,6},{5,7},{6,4},{7,5},{8,10},{9,11},{10,... | collective-permute-start | bytes 737288 | tf_op jit(solution)/shard_map/ppermute | solution.py:64
  62.1 8.0 %collective-permute-start.14 = (bf16[4,80,384]{2,1,0:T(8,128)(2,1)}, bf16[4,80,384]{2,1,0:T(8,128)(2,1)S(1)}, u32[]{:S(2)}, u32[]{:S(2)}) collective-permute-start(bf16[4,80,384]{2,1,0:T(8,128)(2,1)} %collective-permute-done.9.refs_5_), channel_id=1, source_target_pairs={{0,4},{4,0},{8,12},{12,8},{16,20},{20,16},{24,28},{28,24},{1,5},{5... | collective-permute-start | bytes 737288 | tf_op jit(solution)/shard_map/ppermute | solution.py:62
  72.4 31.1 %collective-permute-start.21 = (bf16[4,112,384]{2,1,0:T(8,128)(2,1)S(1)}, bf16[4,112,384]{2,1,0:T(8,128)(2,1)}, u32[]{:S(2)}, u32[]{:S(2)}) collective-permute-start(bf16[4,112,384]{2,1,0:T(8,128)(2,1)S(1)} %slice.545), channel_id=1, source_target_pairs={{0,2},{1,3},{2,0},{3,1},{4,6},{5,7},{6,4},{7,5},{8,10},{9,11},{10,... | collective-permute-start | bytes 1032200 | tf_op jit(solution)/shard_map/ppermute | solution.py:64
  73.8 29.8 %collective-permute-start.19 = (bf16[4,112,384]{2,1,0:T(8,128)(2,1)S(1)}, bf16[4,112,384]{2,1,0:T(8,128)(2,1)}, u32[]{:S(2)}, u32[]{:S(2)}) collective-permute-start(bf16[4,112,384]{2,1,0:T(8,128)(2,1)S(1)} %slice.545), channel_id=1, source_target_pairs={{0,4},{4,0},{8,12},{12,8},{16,20},{20,16},{24,28},{28,24},{1,5},{5... | collective-permute-start | bytes 1032200 | tf_op jit(solution)/shard_map/ppermute | solution.py:62
  75.4 28.5 %collective-permute-start.22 = (bf16[4,320,384]{2,1,0:T(8,128)(2,1)S(1)}, bf16[4,320,384]{2,1,0:T(8,128)(2,1)}, u32[]{:S(2)}, u32[]{:S(2)}) collective-permute-start(bf16[4,320,384]{2,1,0:T(8,128)(2,1)S(1)} %slice.546), channel_id=1, source_target_pairs={{0,4},{4,0},{8,12},{12,8},{16,20},{20,16},{24,28},{28,24},{1,5},{5... | collective-permute-start | bytes 2949128 | tf_op jit(solution)/shard_map/ppermute | solution.py:62
  76.0 27.9 %collective-permute-start.20 = (bf16[4,320,384]{2,1,0:T(8,128)(2,1)S(1)}, bf16[4,320,384]{2,1,0:T(8,128)(2,1)}, u32[]{:S(2)}, u32[]{:S(2)}) collective-permute-start(bf16[4,320,384]{2,1,0:T(8,128)(2,1)S(1)} %slice.546), channel_id=1, source_target_pairs={{0,2},{1,3},{2,0},{3,1},{4,6},{5,7},{6,4},{7,5},{8,10},{9,11},{10,... | collective-permute-start | bytes 2949128 | tf_op jit(solution)/shard_map/ppermute | solution.py:64
  76.7 27.1 %collective-permute-start.18 = (bf16[4,432,384]{2,1,0:T(8,128)(2,1)S(1)}, bf16[4,432,384]{2,1,0:T(8,128)(2,1)}, u32[]{:S(2)}, u32[]{:S(2)}) collective-permute-start(bf16[4,432,384]{2,1,0:T(8,128)(2,1)S(1)} %pad_maximum_fusion.1.refs_1_), channel_id=1, source_target_pairs={{0,1},{1,0},{2,3},{3,2},{4,5},{5,4},{6,7},{7,6},{8,9},{9,8},{10,11... | collective-permute-start | bytes 3981320 | tf_op jit(solution)/shard_map/ppermute | solution.py:64
  105.4 23.4 %collective-permute-start.23 = (bf16[4,112,384]{2,1,0:T(8,128)(2,1)}, bf16[4,112,384]{2,1,0:T(8,128)(2,1)S(1)}, u32[]{:S(2)}, u32[]{:S(2)}) collective-permute-start(bf16[4,112,384]{2,1,0:T(8,128)(2,1)} %collective-permute-done.19.refs_2_), channel_id=1, source_target_pairs={{0,2},{1,3},{2,0},{3,1},{4,6},{5,7},{6,4},{7,5},{8,10},{9,11},{10,... | collective-permute-start | bytes 1032200 | tf_op jit(solution)/shard_map/ppermute | solution.py:64
  106.6 25.9 %collective-permute-start.29 = (bf16[4,320,384]{2,1,0:T(8,128)(2,1)}, bf16[4,320,384]{2,1,0:T(8,128)(2,1)S(1)}, u32[]{:S(2)}, u32[]{:S(2)}) collective-permute-start(bf16[4,320,384]{2,1,0:T(8,128)(2,1)} %collective-permute-done.20.refs_5_), channel_id=1, source_target_pairs={{0,1},{1,0},{2,3},{3,2},{4,5},{5,4},{6,7},{7,6},{8,9},{9,8},{10,11... | collective-permute-start | bytes 2949128 | tf_op jit(solution)/shard_map/ppermute | solution.py:64
  106.6 25.9 %collective-permute-start.24 = (bf16[4,320,384]{2,1,0:T(8,128)(2,1)}, bf16[4,320,384]{2,1,0:T(8,128)(2,1)S(1)}, u32[]{:S(2)}, u32[]{:S(2)}) collective-permute-start(bf16[4,320,384]{2,1,0:T(8,128)(2,1)} %collective-permute-done.20.refs_5_), channel_id=1, source_target_pairs={{0,4},{4,0},{8,12},{12,8},{16,20},{20,16},{24,28},{28,24},{1,5},{5... | collective-permute-start | bytes 2949128 | tf_op jit(solution)/shard_map/ppermute | solution.py:62
  108.7 23.8 %collective-permute-start.25 = (bf16[512,768]{1,0:T(8,128)(2,1)}, bf16[512,768]{1,0:T(8,128)(2,1)S(1)}, u32[]{:S(2)}, u32[]{:S(2)}) collective-permute-start(bf16[512,768]{1,0:T(8,128)(2,1)} %get-tuple-element.220), channel_id=1, source_target_pairs={{0,2},{1,3},{2,0},{3,1},{4,6},{5,7},{6,4},{7,5},{8,10},{9,11},{10,... | collective-permute-start | bytes 2359304 | tf_op jit(solution)/shard_map/ppermute | solution.py:64
  109.8 22.7 %collective-permute-start.30 = (bf16[4,320,384]{2,1,0:T(8,128)(2,1)}, bf16[4,320,384]{2,1,0:T(8,128)(2,1)}, u32[]{:S(2)}, u32[]{:S(2)}) collective-permute-start(bf16[4,320,384]{2,1,0:T(8,128)(2,1)} %collective-permute-done.22.refs_6_), channel_id=1, source_target_pairs={{0,1},{1,0},{2,3},{3,2},{4,5},{5,4},{6,7},{7,6},{8,9},{9,8},{10,11... | collective-permute-start | bytes 2949128 | tf_op jit(solution)/shard_map/ppermute | solution.py:64
  181.6 23.2 %collective-permute-start.34 = (bf16[512,768]{1,0:T(8,128)(2,1)}, bf16[512,768]{1,0:T(8,128)(2,1)S(1)}, u32[]{:S(2)}, u32[]{:S(2)}) collective-permute-start(bf16[512,768]{1,0:T(8,128)(2,1)} %get-tuple-element.240), channel_id=1, source_target_pairs={{0,2},{1,3},{2,0},{3,1},{4,6},{5,7},{6,4},{7,5},{8,10},{9,11},{10,... | collective-permute-start | bytes 2359304 | tf_op jit(solution)/shard_map/ppermute | solution.py:64
  182.9 22.0 %collective-permute-start.35 = (bf16[1024,384]{1,0:T(8,128)(2,1)}, bf16[1024,384]{1,0:T(8,128)(2,1)S(1)}, u32[]{:S(2)}, u32[]{:S(2)}) collective-permute-start(bf16[1024,384]{1,0:T(8,128)(2,1)} %get-tuple-element.241), channel_id=1, source_target_pairs={{0,1},{1,0},{2,3},{3,2},{4,5},{5,4},{6,7},{7,6},{8,9},{9,8},{10,11... | collective-permute-start | bytes 2359304 | tf_op jit(solution)/shard_map/ppermute | solution.py:64
  211.4 30.7 %collective-permute-start.38 = (bf16[8,208,384]{2,1,0:T(8,128)(2,1)}, bf16[8,208,384]{2,1,0:T(8,128)(2,1)}, u32[]{:S(2)}, u32[]{:S(2)}) collective-permute-start(bf16[8,208,384]{2,1,0:T(8,128)(2,1)} %add_convert_fusion.3), channel_id=1, source_target_pairs={{0,2},{1,3},{2,0},{3,1},{4,6},{5,7},{6,4},{7,5},{8,10},{9,11},{10,... | collective-permute-start | bytes 3833864 | tf_op jit(solution)/shard_map/ppermute | solution.py:64
  212.3 29.8 %collective-permute-start.40 = (bf16[8,208,384]{2,1,0:T(8,128)(2,1)}, bf16[8,208,384]{2,1,0:T(8,128)(2,1)S(1)}, u32[]{:S(2)}, u32[]{:S(2)}) collective-permute-start(bf16[8,208,384]{2,1,0:T(8,128)(2,1)} %get-tuple-element.268), channel_id=1, source_target_pairs={{0,1},{1,0},{2,3},{3,2},{4,5},{5,4},{6,7},{7,6},{8,9},{9,8},{10,11... | collective-permute-start | bytes 3833864 | tf_op jit(solution)/shard_map/ppermute | solution.py:64
  212.4 33.0 %collective-permute-start.39 = (bf16[8,224,384]{2,1,0:T(8,128)(2,1)S(1)}, bf16[8,224,384]{2,1,0:T(8,128)(2,1)S(1)}, u32[]{:S(2)}, u32[]{:S(2)}) collective-permute-start(bf16[8,224,384]{2,1,0:T(8,128)(2,1)S(1)} %add_convert_fusion.1), channel_id=1, source_target_pairs={{0,4},{4,0},{8,12},{12,8},{16,20},{20,16},{24,28},{28,24},{1,5},{5... | collective-permute-start | bytes 4128776 | tf_op jit(solution)/shard_map/ppermute | solution.py:62
  214.7 30.8 %collective-permute-start.41 = (bf16[8,224,384]{2,1,0:T(8,128)(2,1)}, bf16[8,224,384]{2,1,0:T(8,128)(2,1)}, u32[]{:S(2)}, u32[]{:S(2)}) collective-permute-start(bf16[8,224,384]{2,1,0:T(8,128)(2,1)} %get-tuple-element.269), channel_id=1, source_target_pairs={{0,1},{1,0},{2,3},{3,2},{4,5},{5,4},{6,7},{7,6},{8,9},{9,8},{10,11... | collective-permute-start | bytes 4128776 | tf_op jit(solution)/shard_map/ppermute | solution.py:64
  249.4 24.1 %collective-permute-start.42 = (bf16[4,208,384]{2,1,0:T(8,128)(2,1)}, bf16[4,208,384]{2,1,0:T(8,128)(2,1)}, u32[]{:S(2)}, u32[]{:S(2)}) collective-permute-start(bf16[4,208,384]{2,1,0:T(8,128)(2,1)} %slice.550), channel_id=1, source_target_pairs={{0,4},{4,0},{8,12},{12,8},{16,20},{20,16},{24,28},{28,24},{1,5},{5... | collective-permute-start | bytes 1916936 | tf_op jit(solution)/shard_map/ppermute | solution.py:62
  253.5 20.0 %collective-permute-start.43 = (bf16[4,224,384]{2,1,0:T(8,128)(2,1)S(1)}, bf16[4,224,384]{2,1,0:T(8,128)(2,1)S(1)}, u32[]{:S(2)}, u32[]{:S(2)}) collective-permute-start(bf16[4,224,384]{2,1,0:T(8,128)(2,1)S(1)} %slice.551), channel_id=1, source_target_pairs={{0,2},{1,3},{2,0},{3,1},{4,6},{5,7},{6,4},{7,5},{8,10},{9,11},{10,... | collective-permute-start | bytes 2064392 | tf_op jit(solution)/shard_map/ppermute | solution.py:64
  275.0 38.8 %collective-permute-start.48 = (bf16[432,384]{1,0:T(8,128)(2,1)S(1)}, bf16[432,384]{1,0:T(8,128)(2,1)S(1)}, u32[]{:S(2)}, u32[]{:S(2)}) collective-permute-start(bf16[432,384]{1,0:T(8,128)(2,1)S(1)} %get-tuple-element.343), channel_id=1, source_target_pairs={{0,8},{4,12},{8,16},{12,20},{16,24},{20,28},{24,0},{28,4},{1,9},{5... | collective-permute-start | bytes 995336 | tf_op jit(solution)/shard_map/ppermute | solution.py:69
  279.7 34.2 %collective-permute-start.46 = (bf16[432,384]{1,0:T(8,128)(2,1)S(1)}, bf16[432,384]{1,0:T(8,128)(2,1)}, u32[]{:S(2)}, u32[]{:S(2)}) collective-permute-start(bf16[432,384]{1,0:T(8,128)(2,1)S(1)} %get-tuple-element.344), channel_id=1, source_target_pairs={{0,24},{4,28},{8,0},{12,4},{16,8},{20,12},{24,16},{28,20},{1,25},{... | collective-permute-start | bytes 995336 | tf_op jit(solution)/shard_map/ppermute | solution.py:69
  284.2 29.7 %collective-permute-start.47 = (bf16[432,384]{1,0:T(8,128)(2,1)S(1)}, bf16[432,384]{1,0:T(8,128)(2,1)}, u32[]{:S(2)}, u32[]{:S(2)}) collective-permute-start(bf16[432,384]{1,0:T(8,128)(2,1)S(1)} %get-tuple-element.345), channel_id=1, source_target_pairs={{0,16},{4,20},{8,24},{12,28},{16,0},{20,4},{24,8},{28,12},{1,17},{... | collective-permute-start | bytes 995336 | tf_op jit(solution)/shard_map/ppermute | solution.py:69
  292.8 21.0 %collective-permute-start.44 = (bf16[8,48,384]{2,1,0:T(8,128)(2,1)}, bf16[8,48,384]{2,1,0:T(8,128)(2,1)}, u32[]{:S(2)}, u32[]{:S(2)}) collective-permute-start(bf16[8,48,384]{2,1,0:T(8,128)(2,1)} %get-tuple-element.287), channel_id=1, source_target_pairs={{0,2},{1,3},{2,0},{3,1},{4,6},{5,7},{6,4},{7,5},{8,10},{9,11},{10,... | collective-permute-start | bytes 884744 | tf_op jit(solution)/shard_map/ppermute | solution.py:64
  293.9 20.0 %collective-permute-start.45 = (bf16[8,48,384]{2,1,0:T(8,128)(2,1)}, bf16[8,48,384]{2,1,0:T(8,128)(2,1)}, u32[]{:S(2)}, u32[]{:S(2)}) collective-permute-start(bf16[8,48,384]{2,1,0:T(8,128)(2,1)} %get-tuple-element.288), channel_id=1, source_target_pairs={{0,4},{4,0},{8,12},{12,8},{16,20},{20,16},{24,28},{28,24},{1,5},{5... | collective-permute-start | bytes 884744 | tf_op jit(solution)/shard_map/ppermute | solution.py:62
  327.2 9.3 %collective-permute-start.51 = (bf16[512,768]{1,0:T(8,128)(2,1)}, bf16[512,768]{1,0:T(8,128)(2,1)S(1)}, u32[]{:S(2)}, u32[]{:S(2)}) collective-permute-start(bf16[512,768]{1,0:T(8,128)(2,1)} %get-tuple-element.303), channel_id=1, source_target_pairs={{0,1},{1,0},{2,3},{3,2},{4,5},{5,4},{6,7},{7,6},{8,9},{9,8},{10,11... | collective-permute-start | bytes 2359304 | tf_op jit(solution)/shard_map/ppermute | solution.py:64
  328.5 8.0 %collective-permute-start.50 = (bf16[8,32,384]{2,1,0:T(8,128)(2,1)S(1)}, bf16[8,32,384]{2,1,0:T(8,128)(2,1)S(1)}, u32[]{:S(2)}, u32[]{:S(2)}) collective-permute-start(bf16[8,32,384]{2,1,0:T(8,128)(2,1)S(1)} %copy-done.44), channel_id=1, source_target_pairs={{0,4},{4,0},{8,12},{12,8},{16,20},{20,16},{24,28},{28,24},{1,5},{5... | collective-permute-start | bytes 589832 | tf_op jit(solution)/shard_map/ppermute | solution.py:62
  340.6 11.0 %collective-permute-start.61 = (bf16[216,384]{1,0:T(8,128)(2,1)}, bf16[216,384]{1,0:T(8,128)(2,1)S(1)}, u32[]{:S(2)}, u32[]{:S(2)}) collective-permute-start(bf16[216,384]{1,0:T(8,128)(2,1)} %constant_dynamic-update-slice_fusion.42), channel_id=1, source_target_pairs={{0,1},{1,0},{2,3},{3,2},{4,5},{5,4},{6,7},{7,6},{8,9},{9,8},{10,11... | collective-permute-start | bytes 497672 | tf_op jit(solution)/shard_map/ppermute | solution.py:64
  340.6 11.9 %collective-permute-start.53 = (bf16[4,80,384]{2,1,0:T(8,128)(2,1)S(1)}, bf16[4,80,384]{2,1,0:T(8,128)(2,1)S(1)}, u32[]{:S(2)}, u32[]{:S(2)}) collective-permute-start(bf16[4,80,384]{2,1,0:T(8,128)(2,1)S(1)} %fusion.9), channel_id=1, source_target_pairs={{0,4},{4,0},{8,12},{12,8},{16,20},{20,16},{24,28},{28,24},{1,5},{5... | collective-permute-start | bytes 737288 | tf_op jit(solution)/shard_map/ppermute | solution.py:62
  342.3 10.2 %collective-permute-start.54 = (bf16[4,80,384]{2,1,0:T(8,128)(2,1)S(1)}, bf16[4,80,384]{2,1,0:T(8,128)(2,1)S(1)}, u32[]{:S(2)}, u32[]{:S(2)}) collective-permute-start(bf16[4,80,384]{2,1,0:T(8,128)(2,1)S(1)} %fusion.8), channel_id=1, source_target_pairs={{0,2},{1,3},{2,0},{3,1},{4,6},{5,7},{6,4},{7,5},{8,10},{9,11},{10,... | collective-permute-start | bytes 737288 | tf_op jit(solution)/shard_map/ppermute | solution.py:64
  344.4 26.1 %collective-permute-start.52 = (bf16[512,768]{1,0:T(8,128)(2,1)S(1)}, bf16[512,768]{1,0:T(8,128)(2,1)S(1)}, u32[]{:S(2)}, u32[]{:S(2)}) collective-permute-start(bf16[512,768]{1,0:T(8,128)(2,1)S(1)} %add_convert_fusion.5), channel_id=1, source_target_pairs={{0,2},{1,3},{2,0},{3,1},{4,6},{5,7},{6,4},{7,5},{8,10},{9,11},{10,... | collective-permute-start | bytes 2359304 | tf_op jit(solution)/shard_map/ppermute | solution.py:64
  352.7 8.6 %collective-permute-start.55 = (bf16[512,768]{1,0:T(8,128)(2,1)S(1)}, bf16[512,768]{1,0:T(8,128)(2,1)S(1)}, u32[]{:S(2)}, u32[]{:S(2)}) collective-permute-start(bf16[512,768]{1,0:T(8,128)(2,1)S(1)} %copy-done.36), channel_id=1, source_target_pairs={{0,1},{1,0},{2,3},{3,2},{4,5},{5,4},{6,7},{7,6},{8,9},{9,8},{10,11... | collective-permute-start | bytes 2359304 | tf_op jit(solution)/shard_map/ppermute | solution.py:64
  353.5 9.6 %collective-permute-start.58 = (bf16[160,384]{1,0:T(8,128)(2,1)S(1)}, bf16[160,384]{1,0:T(8,128)(2,1)S(1)}, u32[]{:S(2)}, u32[]{:S(2)}) collective-permute-start(bf16[160,384]{1,0:T(8,128)(2,1)S(1)} %get-tuple-element.348), channel_id=1, source_target_pairs={{0,8},{4,12},{8,16},{12,20},{16,24},{20,28},{24,0},{28,4},{1,9},{5... | collective-permute-start | bytes 368648 | tf_op jit(solution)/shard_map/ppermute | solution.py:69
  359.5 11.0 %collective-permute-start.57 = (bf16[160,384]{1,0:T(8,128)(2,1)S(1)}, bf16[160,384]{1,0:T(8,128)(2,1)S(1)}, u32[]{:S(2)}, u32[]{:S(2)}) collective-permute-start(bf16[160,384]{1,0:T(8,128)(2,1)S(1)} %get-tuple-element.350), channel_id=1, source_target_pairs={{0,16},{4,20},{8,24},{12,28},{16,0},{20,4},{24,8},{28,12},{1,17},{... | collective-permute-start | bytes 368648 | tf_op jit(solution)/shard_map/ppermute | solution.py:69
  (60 other events, 367.7 us)

commit v4 on v3

--- a/solution.py
+++ b/solution.py
@@ -13,13 +13,15 @@
 TQ = 256
 TK = 512
 CHIPS = 16
-TILE = 256
+TILE = 512
+SUB = 256
 BF = jnp.bfloat16
 F32 = jnp.float32
 VMEM_LIMIT = 60 << 20
 COST = 1.0
 CUT = 320
 BACK_CUT = 224
+EARLY = (160, 288)
 
 
 def nn(left, right):
@@ -60,6 +62,9 @@
 def swap(value, dim):
     if dim == "x":
         return lax.ppermute(value, "dp", [(d, d ^ 1) for d in range(lax.axis_size("dp"))])
+    if dim == "xy":
+        pairs = [(4 * d + s, 4 * (d ^ 1) + (s ^ 2)) for d in range(lax.axis_size("dp")) for s in range(4)]
+        return lax.ppermute(value, ("dp", "seq"), pairs)
     bit = 1 if dim == "core" else 2
     return lax.ppermute(value, "seq", [(s, s ^ bit) for s in range(4)])
 
@@ -107,13 +112,15 @@
 
 
 class Plan:
-    def __init__(self, sections, cut, joined=False):
-        self.sections, self.cut, self.joined = sections, cut, joined
+    def __init__(self, sections, cut, joined=False, plain=False):
+        self.sections, self.cut, self.joined, self.plain = sections, cut, joined, plain
         self.rows = sum(sections)
 
     def pieces(self):
         if self.cut is None:
             return [(0, self.rows, None, [None] * CHIPS)]
+        if self.plain:
+            return [(0, self.rows, "xy", [sides] * ZS) for sides in ((0, 0), (1, 0), (0, 1), (1, 1))]
         found = []
         if not self.joined:
             found.append((0, self.rows, "xy", [(0, 0)] * ZS))
@@ -175,7 +182,7 @@
 def spread_tables(model, share, share_f, *ready):
     lane, col = jnp.arange(384)[:, None], jnp.arange(model)[None, :]
     if ready:
-        lane = after(lane, *ready)
+        lane, col = after(lane, *ready), after(col, *ready)
     first = (lane == 128 * (col // share % 2) + col % share).astype(BF)
     second = (lane == 128 * (col // share_f % 2) + col % share_f).astype(BF)
     marks = (jnp.arange(CHIPS)[:, None] == col // (2 * share)).astype(F32)
@@ -213,6 +220,36 @@
         cost_estimate=cost(flops=0, bytes_accessed=8 * rows * half, transcendentals=0),
         name="pack",
     )(meta, qkv, proj, inner, down)
+
+
+def lay_kernel(lengths_a, lengths_b, meta, mine_ref, came_ref, small_ref, small_came, a_ref, b_ref, all_ref):
+    even = meta[0] == 0
+    order = lambda mine, came: (jnp.where(even, mine, came), jnp.where(even, came, mine))
+    at = 0
+    for lengths, out in ((lengths_a, a_ref), (lengths_b, b_ref)):
+        to = 0
+        for length in lengths:
+            for part in order(mine_ref[at : at + length, :], came_ref[at : at + length, :]):
+                out[to : to + length, :] = part
+                to += length
+            at += length
+    small = jnp.concatenate(order(small_ref[...], small_came[...]) + (jnp.zeros(small_ref.shape, BF),), axis=1)
+    a_ref[a_ref.shape[0] - small.shape[0] :, :] = small
+    all_ref[: a_ref.shape[0], :] = a_ref[...]
+    all_ref[a_ref.shape[0] :, :] = b_ref[...]
+
+
+def lay(meta, mine, came, small, small_came, lengths_a, lengths_b):
+    width = mine.shape[1]
+    rows = 2 * sum(lengths_a) + small.shape[0], 2 * sum(lengths_b)
+    return pl.pallas_call(
+        lambda *refs: lay_kernel(lengths_a, lengths_b, *refs),
+        in_specs=[smem()] + [pl.BlockSpec(memory_space=pltpu.VMEM)] * 4,
+        out_specs=[pl.BlockSpec(memory_space=pltpu.VMEM)] * 3,
+        out_shape=[shape((n, width), BF) for n in (*rows, sum(rows))],
+        cost_estimate=cost(flops=0, bytes_accessed=8 * sum(rows) * width, transcendentals=0),
+        name="lay",
+    )(meta, mine, came, small, small_came)
 
 
 def qkv_kernel(plan, pieces_n, *refs):
@@ -275,7 +312,7 @@
             ],
         ),
         out_shape=[shape((rows, wide), BF), shape((CHIPS, depth, wide), BF), shape((16, model), F32)],
-        compiler_params=pltpu.CompilerParams(vmem_limit_bytes=VMEM_LIMIT),
+        compiler_params=pltpu.CompilerParams(vmem_limit_bytes=14 << 20),
         cost_estimate=cost(
             flops=2 * rows * model * wide, bytes_accessed=2 * rows * (model + wide), transcendentals=0
         ),
@@ -406,7 +443,7 @@
             pltpu.VMEM((wide, length), BF),
             pltpu.VMEM((heads, length, TQ), F32),
         ],
-        compiler_params=pltpu.CompilerParams(vmem_limit_bytes=VMEM_LIMIT),
+        compiler_params=pltpu.CompilerParams(vmem_limit_bytes=28 << 20),
         cost_estimate=cost(
             flops=heads * length * length * 700, bytes_accessed=10 * length * wide, transcendentals=heads * length * length // 2
         ),
@@ -511,7 +548,7 @@
             pltpu.VMEM((wide, length), BF),
             pltpu.VMEM((2, length, wide), BF),
         ],
-        compiler_params=pltpu.CompilerParams(vmem_limit_bytes=VMEM_LIMIT),
+        compiler_params=pltpu.CompilerParams(vmem_limit_bytes=17 << 20),
         cost_estimate=cost(
             flops=heads * length * length * 1500, bytes_accessed=20 * length * wide, transcendentals=heads * length * length // 2
         ),
@@ -569,7 +606,7 @@
     refs = refs[1 + 2 * pieces_n :]
     ctx_own, ctx_oth = refs[:ctx_n], refs[ctx_n : 2 * ctx_n]
     (x_ref, dout_ref, vec_ref,
-     kept_ref, given_ref, gr_kept, gr_given, hid_ref, gf_ref, low_ref, gp_ref, ga_ref, gc_own, gc_oth, ctx_ref, vg_ref,
+     out_ref, gr_ref, hid_ref, gf_ref, low_ref, gp_ref, ga_ref, gc_own, gc_oth, ctx_ref, vg_ref,
      proj, inner, down, slope, sems) = refs[2 * ctx_n :]
     here = placed(meta)
     c = here["c"]
@@ -605,75 +642,65 @@
     w_inner = lambda j: inner[:, :, model * j : model * j + model].reshape(model, model)
     span = CHIPS * model // wide
     w_down = lambda j: down[span * j : span * j + span].reshape(model, model)
-    own = jnp.concatenate([ref[...] for ref in ctx_own], axis=1)
-    oth = jnp.concatenate([ref[...] for ref in ctx_oth], axis=1)
-    context = jnp.concatenate([jnp.where(c == 0, own, oth), jnp.where(c == 0, oth, own)], axis=1)
-    ctx_ref[...] = context
+    total = lambda value: jnp.sum(value, axis=0, keepdims=True)
+    chunks = wide // model
+    spans = [slice(at, at + SUB) for at in range(0, TILE, SUB)]
+    columns = [slice(model * j, model * j + model) for j in range(chunks)]
+
     arrived(0)
-    attn = nn(context, w_proj())
-    n1, rate1 = centre(x_ref[...].astype(F32) + (attn + vec(2)))
-    x1 = n1 * vec(3) + vec(4)
-    low = x1.astype(BF)
-    low_ref[...] = low
-    ffn = None
-    chunks = wide // model
+    first = []
+    for rows in spans:
+        own = jnp.concatenate([ref[rows, :] for ref in ctx_own], axis=1)
+        oth = jnp.concatenate([ref[rows, :] for ref in ctx_oth], axis=1)
+        context = jnp.concatenate([jnp.where(c == 0, own, oth), jnp.where(c == 0, oth, own)], axis=1)
+        ctx_ref[rows, :] = context
+        n1, rate1 = centre(x_ref[rows, :].astype(F32) + (nn(context, w_proj()) + vec(2)))
+        x1 = n1 * vec(3) + vec(4)
+        low = x1.astype(BF)
+        low_ref[rows, :] = low
+        first.append((n1, rate1, x1, low))
     arrived(1)
     arrived(2)
-    for j in range(chunks):
-        cols = slice(model * j, model * j + model)
-        pre = nn(low, w_inner(j)) + vec(8 + j)
-        below = 0.5 + 0.5 * lax.erf(pre * 0.7071067811865476)
-        slope[:, cols] = below + pre * (jnp.exp(-0.5 * (pre * pre)) * 0.3989422804014327)
-        hidden = (pre * below).astype(BF)
-        hid_ref[:, cols] = hidden
-        more = nn(hidden, w_down(j))
-        ffn = more if ffn is None else ffn + more
-    n2, rate2 = centre(x1 + (ffn + vec(5)))
-    out = (n2 * vec(6) + vec(7)).astype(BF)
-    stays = step // 2 == here["y"]
-
-    @pl.when(stays)
-    def _():
-        kept_ref[...] = out
-
-    @pl.when(jnp.logical_not(stays))
-    def _():
-        given_ref[...] = out
-
-
-    total = lambda value: jnp.sum(value, axis=0, keepdims=True)
-    grad = dout_ref[...].astype(F32)
-    gr2 = norm_back(grad * vec(6), n2, rate2)
-    gf = gr2.astype(BF)
-    gf_ref[...] = gf
-    vg_ref[6:7, :] += total(grad * n2)
-    vg_ref[7:8, :] += total(grad)
-    vg_ref[5:6, :] += total(gf.astype(F32))
-    gx1 = gr2
-    for j in range(chunks):
-        cols = slice(model * j, model * j + model)
-        gp = (nt(gf, w_down(j)) * slope[:, cols]).astype(BF)
-        gp_ref[:, cols] = gp
-        vg_ref[8 + j : 9 + j, :] += total(gp.astype(F32))
-        gx1 = gx1 + nt(gp, w_inner(j))
-    gr1 = norm_back(gx1 * vec(3), n1, rate1)
-
-    @pl.when(stays)
-    def _():
-        gr_kept[...] = gr1
-
-    @pl.when(jnp.logical_not(stays))
-    def _():
-        gr_given[...] = gr1
-
-    ga = gr1.astype(BF)
-    ga_ref[...] = ga
-    vg_ref[3:4, :] += total(gx1 * n1)
-    vg_ref[4:5, :] += total(gx1)
-    vg_ref[2:3, :] += total(ga.astype(F32))
-    gc = cut(nt(ga, w_proj()))
-    gc_own[...] = jnp.where(c == 0, gc[0], gc[1]).astype(BF)
-    gc_oth[...] = jnp.where(c == 0, gc[1], gc[0]).astype(BF)
+    ffn = [None] * len(spans)
+    for j, cols in enumerate(columns):
+        for k, rows in enumerate(spans):
+            pre = nn(first[k][3], w_inner(j)) + vec(8 + j)
+            below = 0.5 + 0.5 * lax.erf(pre * 0.7071067811865476)
+            slope[rows, cols] = below + pre * (jnp.exp(-0.5 * (pre * pre)) * 0.3989422804014327)
+            hidden = (pre * below).astype(BF)
+            hid_ref[rows, cols] = hidden
+            more = nn(hidden, w_down(j))
+            ffn[k] = more if ffn[k] is None else ffn[k] + more
+    second = []
+    for k, rows in enumerate(spans):
+        n2, rate2 = centre(first[k][2] + (ffn[k] + vec(5)))
+        out_ref[rows, :] = (n2 * vec(6) + vec(7)).astype(BF)
+        grad = dout_ref[rows, :].astype(F32)
+        gr2 = norm_back(grad * vec(6), n2, rate2)
+        gf = gr2.astype(BF)
+        gf_ref[rows, :] = gf
+        vg_ref[6:7, :] += total(grad * n2)
+        vg_ref[7:8, :] += total(grad)
+        vg_ref[5:6, :] += total(gf.astype(F32))
+        second.append([gr2, gf])
+    for j, cols in enumerate(columns):
+        for k, rows in enumerate(spans):
+            gp = (nt(second[k][1], w_down(j)) * slope[rows, cols]).astype(BF)
+            gp_ref[rows, cols] = gp
+            vg_ref[8 + j : 9 + j, :] += total(gp.astype(F32))
+            second[k][0] = second[k][0] + nt(gp, w_inner(j))
+    for k, rows in enumerate(spans):
+        n1, rate1, gx1 = first[k][0], first[k][1], second[k][0]
+        gr1 = norm_back(gx1 * vec(3), n1, rate1)
+        gr_ref[rows, :] = gr1
+        ga = gr1.astype(BF)
+        ga_ref[rows, :] = ga
+        vg_ref[3:4, :] += total(gx1 * n1)
+        vg_ref[4:5, :] += total(gx1)
+        vg_ref[2:3, :] += total(ga.astype(F32))
+        gc = cut(nt(ga, w_proj()))
+        gc_own[rows, :] = jnp.where(c == 0, gc[0], gc[1]).astype(BF)
+        gc_oth[rows, :] = jnp.where(c == 0, gc[1], gc[0]).astype(BF)
 
 
 def feed_forward(plan, meta, own_pieces, oth_pieces, ctx, ctx_oth, x_own, d_own, vectors, wide):
@@ -681,9 +708,8 @@
     half = model // 2
     tile = lambda n: pl.BlockSpec((TILE, n), lambda i, meta: (i, 0))
     full = lambda dims: pl.BlockSpec(dims, lambda i, meta: (0,) * len(dims))
-    side = lambda mine: pl.BlockSpec(
-        (TILE, model), lambda i, meta: (jnp.clip(i - (2 * meta[2] if mine else 2 - 2 * meta[2]), 0, 1), 0)
-    )
+    per = rows // 2 // TILE
+    side = pl.BlockSpec((None, TILE, model), lambda i, meta: (lax.rem(i // per + meta[2], 2), lax.rem(i, per), 0))
     scratch = [
         pltpu.VMEM((CHIPS, model // CHIPS, model), BF),
         pltpu.VMEM((CHIPS, model // CHIPS, wide), BF),
@@ -700,10 +726,10 @@
             in_specs=[anywhere()] * (2 * len(own_pieces))
             + [tile(v.shape[1]) for v in ctx + ctx_oth]
             + [tile(model), tile(model), full(vectors.shape)],
-            out_specs=[side(True), side(False)] * 2 + [tile(w) for w, _ in outs] + [full((16, model))],
+            out_specs=[side] * 2 + [tile(w) for w, _ in outs] + [full((16, model))],
             scratch_shapes=scratch,
         ),
-        out_shape=[shape((rows // 2, model), BF)] * 2 + [shape((rows // 2, model), F32)] * 2 + [shape((rows, w), kind) for w, kind in outs] + [shape((16, model), F32)],
+        out_shape=[shape((2, rows // 2, model), kind) for kind in (BF, F32)] + [shape((rows, w), kind) for w, kind in outs] + [shape((16, model), F32)],
         compiler_params=pltpu.CompilerParams(vmem_limit_bytes=VMEM_LIMIT),
         cost_estimate=cost(
             flops=4 * rows * model * (model + 2 * wide), bytes_accessed=rows * (8 * wide + 20 * model), transcendentals=2 * rows * wide
@@ -843,7 +869,7 @@
             pltpu.SemaphoreType.DMA((plan.entries(),)),
         ]
         + ([pltpu.VMEM((CHIPS, 16, width), BF), pltpu.VMEM((16, model), F32), pltpu.VMEM((8, width), F32)] if last else []),
-        compiler_params=pltpu.CompilerParams(vmem_limit_bytes=VMEM_LIMIT),
+        compiler_params=pltpu.CompilerParams(vmem_limit_bytes=20 << 20),
         cost_estimate=cost(
             flops=2 * len(grads) * rows * model * width, bytes_accessed=2 * rows * (model + 3 * width), transcendentals=0
         ),
@@ -885,7 +911,7 @@
             out_specs=[whole((quarter, model))] * 2,
         ),
         out_shape=[shape((quarter, model), BF)] * 2,
-        compiler_params=pltpu.CompilerParams(vmem_limit_bytes=VMEM_LIMIT),
+        compiler_params=pltpu.CompilerParams(vmem_limit_bytes=14 << 20),
         cost_estimate=cost(
             flops=3 * rows * model * width, bytes_accessed=rows * (model + 3 * width), transcendentals=0
         ),
@@ -935,9 +961,10 @@
     vectors = (query_bias, value_bias, proj_bias, attn_gain, attn_shift, down_bias, ffn_gain, ffn_shift)
     sections_a, sections_b = [depth] * 3 + [16], [depth] * (1 + groups) + [deep]
     lengths_a, lengths_b = [share] * 3, [share] * (1 + groups) + [share_f]
-    segment = jnp.where(low_y, seg_ids[0, 0], seg_ids[1, 0])
-    globs = jnp.where(low_y, glob_blocks[0, 0], glob_blocks[1, 0])
-    lo, n = key_ranges(segment)
+    def documents(seg_ids, glob_blocks):
+        segment = jnp.where(low_y, seg_ids[0, 0], seg_ids[1, 0])
+        return segment, jnp.where(low_y, glob_blocks[0, 0], glob_blocks[1, 0]), *key_ranges(segment)
+
     blocks = rand_blocks[:, 0]
     x_given, x_kept = given_kept(tokens[:, 0])
 
@@ -954,56 +981,43 @@
         return attend_back(meta, qkv, p, own, oth, ctx, ctx_oth, lse, part, segment[None], table[2 * p : 2 * p + 2], globs, lo, n)
 
     if near:
-        plan_a, plan_b = Plan(sections_a, 80), Plan(sections_b, CUT)
+        plan_a, plan_b = Plan(sections_a, 80, plain=True), Plan(sections_b, CUT)
         back_b = Plan(sections_b, BACK_CUT, True)
         back_early, back_late = Plan([depth] * 2, depth, True), Plan([depth, 16], 32, True)
         mine, theirs = pack(meta, qkv_weight, proj_weight, inner_weight, down_weight)
         came = swap(theirs, "core")
         small = jnp.concatenate([jnp.pad(jnp.stack(vectors), ((0, 0), (0, 128 - share))),
                                  jnp.pad(inner_bias[None], ((0, 7), (0, 128 - share_f)))])
-        small = jnp.concatenate(by_parity(small, swap(small, "core")) + (jnp.zeros_like(small),), axis=1)
-        first, second = by_parity(mine, came)
-        laid, at = [], 0
-        for length in lengths_a + lengths_b:
-            laid += [first[at : at + length], second[at : at + length]]
-            at += length
-        chunk_a = jnp.concatenate(laid[:6] + [small], axis=0)
-        chunk_b = jnp.concatenate(laid[6:], axis=0)
-        chunk_a, chunk_b, x_given = stage(chunk_a, chunk_b, x_given)
-
-        za = shifts_z(chunk_a, 1, 2, 3)
+        blocks_came = swap(blocks, "core")
+        chunk_a, chunk_b, chunk = lay(meta, mine, came, small, swap(small, "core"), lengths_a, lengths_b)
+        chunk_a, chunk_b, chunk, seg_ids, glob_blocks, blocks_came = stage(
+            chunk_a, chunk_b, chunk, seg_ids, glob_blocks, blocks_came
+        )
+        blocks_mine, blocks_given = pick_blocks(blocks_came)
+        segment, globs, lo, n = documents(seg_ids, glob_blocks)
+
+        za = shifts_z(chunk_a, 2, 3)
+        both = shift_z(chunk, 1)
         x_came = swap(x_given, "y")
-        blocks_came = swap(blocks, "core")
-        zb = shifts_z(chunk_b, 1)
-        chunk_a, chunk_b, x_came, blocks_came, *rest = stage(chunk_a, chunk_b, x_came, blocks_came, *za, *zb)
-        za, zb = rest[:3], rest[3:]
-
-        near_a = jnp.stack([chunk_a] + za)
-        a, b = split_rows(near_a, plan_a.cut)
-        a_x, b_y, a_y, b_x = swap(a, "x"), swap(b, "y"), swap(a, "y"), swap(b, "x")
-        zb += shifts_z(chunk_b, 2)
-        near_a, a_x, b_y, a_y, b_x, x_came, blocks_came, chunk_b, *zb = stage(
-            near_a, a_x, b_y, a_y, b_x, x_came, blocks_came, chunk_b, *zb
-        )
+        blocks_came = swap(blocks_given, "y")
+        chunk_a, chunk_b, x_came, blocks_came, both, *za = stage(chunk_a, chunk_b, x_came, blocks_came, both, *za)
+
+        near_a = jnp.stack([chunk_a, both[: plan_a.rows]] + za)
+        far_a = [swap(near_a, dim) for dim in ("x", "y", "xy")]
         x_own = pair(x_kept, x_came)
         x_oth = swap(x_own, "core")
-        a_xy, b_yx = swap(a_x, "y"), swap(b_y, "x")
-        zb += shifts_z(chunk_b, 3)
-        blocks_mine, blocks_given = pick_blocks(blocks_came)
-        blocks_came = swap(blocks_given, "y")
+        zb = [both[plan_a.rows :]] + shifts_z(chunk_b, 2) + shifts_z(after(chunk_b, x_oth), 3)
         tables = spread_tables(model, depth // 2, deep // 2, chunk_b)
-        a_xy, b_yx, blocks_came, chunk_b, x_own, x_oth, *rest = stage(
-            a_xy, b_yx, blocks_came, chunk_b, x_own, x_oth, *tables, *zb
-        )
-        tables, zb = rest[:4], rest[4:]
-        pieces = [near_a, a_x, a_y, a_xy, b_y, b_x, b_yx]
-
-        table = jnp.where(c == y, blocks_mine, blocks_came)
+        near_a, chunk_b, x_own, x_oth, *rest = stage(near_a, chunk_b, x_own, x_oth, *tables, *far_a, *zb)
+        tables, far_a, zb = rest[:4], rest[4:7], rest[7:]
+        pieces = [near_a] + far_a
+
         near_b = jnp.stack([chunk_b] + zb)
         a, b = split_rows(near_b, plan_b.cut)
         a_x, b_y, a_y, b_x = swap(a, "x"), swap(b, "y"), swap(a, "y"), swap(b, "x")
         near_oth = swap(near_b, "core")
         qkv, w_qkv, spread = project_qkv(plan_a, meta, pieces, x_own, x_oth, tables)
+        table = jnp.where(c == y, blocks_mine, blocks_came)
         ctx_b, ctx_b_give, lse_b = attention(slice(4, 6), 2, qkv, table)
         d_given, d_kept = given_kept(after(d_out[:, 0], chunk_b))
         near_b, near_oth, a_x, b_y, a_y, b_x, qkv, ctx_b, ctx_b_give, d_given = stage(
@@ -1025,13 +1039,13 @@
         d_own = pair(d_kept, d_came).reshape(-1, model)
         found = feed_forward(plan_b, meta, own_b, oth_b, [ctx_a, ctx_b], [ctx_a_oth, ctx_b_oth], x_own.reshape(-1, model),
                              d_own, spread, ffw)
-        out_kept, out_given, gr_kept, gr_given, hid, gf, x1_low, gp, ga, gc_own, gc_oth, context, vg = found
-
-        out_came, gc_came = swap(out_given, "y"), swap(gc_oth, "core")
+        out, gr, hid, gf, x1_low, gp, ga, gc_own, gc_oth, context, vg = found
+
+        out_came, gc_came = swap(out[1], "y"), swap(gc_oth, "core")
         grads_own, grads_oth = weight_grads(back_b, meta, hid, gp, gf, x1_low, context, ga)
         out_came, gc_came, *rest = stage(out_came, gc_came, *grads_own, *grads_oth)
         a, a_far, b, b_far, a_oth, a_far_oth, b_oth, b_far_oth = rest
-        layer_out = pair(out_kept, out_came)[:, None]
+        layer_out = pair(out[0], out_came)[:, None]
         a_far, b_far = add(a_far, swap(a_far_oth, "core")), add(b_far, swap(b_far_oth, "core"))
         a_far, b_far, gc_came, a_oth, b_oth = stage(a_far, b_far, gc_came, a_oth, b_oth)
 
@@ -1050,25 +1064,30 @@
         qa_came, qb_came = swap(qa_far, "y"), swap(qb_far, "x")
         grad_2 = back(2, after(gc_own, sums), ctx_b, ctx_b_give, lse_b)
         total, qa, qb, qa_came, qb_came, sums, grad_2, *came_b = stage(total, qa, qb, qa_came, qb_came, sums, grad_2, *came_b)
-        ra, ra_far, rb, rb_far = qkv_grads(back_late, meta, x_own, x_oth, [grad_2], 2, sums, vg, tables)
+        own_given, oth_given = input_grads(meta, [grad_0, grad_1, grad_2], w_qkv, True)
+        oth_given = swap(oth_given, "core")
+        last = after(grad_2, own_given)
+        ra, ra_far, rb, rb_far = qkv_grads(back_late, meta, x_own, x_oth, [last], 2, sums, vg, tables)
         ra_came, rb_came = swap(ra_far, "y"), swap(rb_far, "x")
-        grads = [grad_0, grad_1, after(grad_2, ra)]
-        own_given, oth_given = input_grads(meta, grads, w_qkv, True)
-        oth_given = swap(oth_given, "core")
+        gx_given = add(gr[1], own_given, oth_given)
+        gx_came = [swap(gx_given[: EARLY[0]], "y")]
         total_b = added(total[0], *came_b)
-        ra, rb, ra_came, rb_came, own_given, oth_given, total_b = stage(
-            ra, rb, ra_came, rb_came, own_given, oth_given, total_b
+        ra, rb, ra_came, rb_came, gx_given, total_b, *gx_came = stage(
+            ra, rb, ra_came, rb_came, gx_given, total_b, *gx_came
         )
-        gx_came = swap(add(gr_given, own_given, oth_given), "y")
+        gx_came.append(swap(gx_given[EARLY[0] : EARLY[1]], "y"))
         qa = jnp.concatenate([add(qa, qa_came), add(ra, ra_came)], axis=1)
         qb = jnp.concatenate([add(qb, qb_came), add(rb, rb_came)], axis=1)
         qa_came, qb_came = swap(qa[ZS:], "x"), swap(qb[ZS:], "y")
         own_kept, oth_kept = input_grads(meta, [grad_0, grad_1, after(grad_2, qa)], w_qkv, False)
-        qa, qb, qa_came, qb_came, own_kept, oth_kept = stage(qa, qb, qa_came, qb_came, own_kept, oth_kept)
+        qa, qb, qa_came, qb_came, own_kept, oth_kept, gx_given, *gx_came = stage(
+            qa, qb, qa_came, qb_came, own_kept, oth_kept, gx_given, *gx_came
+        )
+        gx_came.append(swap(gx_given[EARLY[1] :], "y"))
         total = jnp.concatenate([add(qb[:ZS], qb_came), add(qa[:ZS], qa_came)], axis=1)
         came = scatter_z(total, 1, 2, 3)
         oth_kept = swap(oth_kept, "core")
-        gx_kept = add(gr_kept, own_kept, oth_kept)
+        gx_kept = add(gr[0], own_kept, oth_kept)
 
         def finish(total, lengths):
             mine, theirs, at = [], [], 0
@@ -1085,9 +1104,10 @@
                 at += length
             return cuts
 
-        cuts_b = finish(total_b, lengths_b)
-        gx_came, gx_kept, total, *came = stage(gx_came, gx_kept, total, *came)
-        grad_input = pair(gx_kept, gx_came)[:, None]
+        cuts_b = finish(after(total_b, total), lengths_b)
+        total, *rest = stage(total, *came, *gx_came)
+        came, gx_came = rest[:3], rest[3:]
+        grad_input = pair(gx_kept, jnp.concatenate(gx_came))[:, None]
         total_a = added(total[0], *came)
         ends = (0, depth, depth + 32, 2 * depth + 32, 3 * depth)
         one, three, two, rest = (total_a[i:j] for i, j in zip(ends[:4], ends[1:]))
@@ -1116,6 +1136,7 @@
             b = [col(full_proj, half * h)] + [col(full_inner, ffw // 2 * h + half * g) for g in range(groups)]
             return jnp.concatenate(a + [rows], axis=1), jnp.concatenate(b + [col(full_down, half * h)], axis=1)
 
+        segment, globs, lo, n = documents(seg_ids, glob_blocks)
         zero, one = packed(0), packed(1)
         pieces_a = [jnp.where(even, zero[0], one[0])]
         own_b, oth_b = [[v] for v in by_parity(zero[1], one[1])]
@@ -1131,8 +1152,8 @@
         ctx_b, ctx_b_give, lse_b = attention(slice(4, 6), 2, qkv, table)
         ctx_oth = [swap(v, "core") for v in (ctx_a_give, ctx_b_give)]
         found = feed_forward(plan_b, meta, own_b, oth_b, [ctx_a, ctx_b], ctx_oth, x_own.reshape(-1, model), d_own, spread, ffw)
-        out_kept, out_given, gr_kept, gr_given, hid, gf, x1_low, gp, ga, gc_own, gc_oth, context, vg = found
-        layer_out = pair(out_kept, swap(out_given, "y"))[:, None]
+        out, gr, hid, gf, x1_low, gp, ga, gc_own, gc_oth, context, vg = found
+        layer_out = pair(out[0], swap(out[1], "y"))[:, None]
         gc_came = swap(gc_oth, "core")
         grads_own, grads_oth = weight_grads(plan_b, meta, hid, gp, gf, x1_low, context, ga)
         ctxs = [(ctx_a, ctx_a_give, lse_a[2 * p : 2 * p + 2]) for p in range(2)] + [(ctx_b, ctx_b_give, lse_b)]
@@ -1140,8 +1161,8 @@
         pieces = qkv_grads(plan_a, meta, x_own, x_oth, grads, 0, jnp.zeros((8, 3 * 128), F32), vg, tables)
         own_given, oth_given = input_grads(meta, grads, w_qkv, True)
         own_kept, oth_kept = input_grads(meta, grads, w_qkv, False)
-        gx_came = swap(add(gr_given, own_given, swap(oth_given, "core")), "y")
-        grad_input = pair(add(gr_kept, own_kept, swap(oth_kept, "core")), gx_came)[:, None]
+        gx_came = swap(add(gr[1], own_given, swap(oth_given, "core")), "y")
+        grad_input = pair(add(gr[0], own_kept, swap(oth_kept, "core")), gx_came)[:, None]
         scatter = lambda v: lax.psum_scatter(v.astype(F32), ("dp", "seq"), scatter_dimension=0, tiled=True)
         found = pieces[0][:, 3 * depth :].astype(F32)
         found = jnp.stack([found[:, :, :128], found[:, :, 128:256]], axis=1).transpose(2, 0, 1, 3)

time: 381 us -> 358 us (0.940)
  Pallas kernels: 198 us -> 177 us
  other arithmetic: 36.9 us -> 20.7 us
  waiting for transfers between devices: 63.8 us -> 72.7 us
  local copies, waits for them, and re-layouts: 11.6 us -> 17.3 us
    ppermute x39, waiting for transfers between devices: 26.4 us -> 35.9 us  [swap(): return lax.ppermute(value, 'seq', [(s, s ^ bit) for s in range(4)])]
    convert_element_type x14 -> x13, other arithmetic: 12.8 us -> 4.29 us  [add(): return added(*values).astype(BF)]
    pallas_call x2, Pallas kernels: 13.7 us -> 7.02 us  [input_grads(): pl.pallas_call(input_grads_kernel, grid_spec=pltpu.PrefetchScalarGridSpec...]
    unnamed x128 -> x131, local copies, waits for them, and re-layouts: 5.4 us -> 11.4 us
    pallas_call x1, Pallas kernels: 43.7 us -> 39 us  [feed_forward(): pl.pallas_call(lambda *refs: ffn_kernel(plan, len(own_pieces), len(ctx),...]
    ppermute x12 -> x11, waiting for transfers between devices: 28.1 us -> 24.7 us  [shift_z(): lax.ppermute(value, 'dp', [(2 * z + x, (z + by) % size * 2 + x) for z in...]
    ppermute x11 -> x9, waiting for transfers between devices: 9.27 us -> 12.1 us  [swap(): lax.ppermute(value, 'dp', [(d, d ^ 1) for d in range(lax.axis_size('dp'))])]
    ppermute x12 -> x11, starting transfers between devices: 25.4 us -> 23.3 us  [shift_z(): lax.ppermute(value, 'dp', [(2 * z + x, (z + by) % size * 2 + x) for z in...]
  transfers between devices with their start and end apart: 62 -> 60, of which waited for: 19 -> 19; matrix products, arithmetic and copies ran while one was open for 8% -> 5% of each run, Pallas kernels for 37% -> 38%
where the time goes in v4:
time: 358 us; the launch traced here: 355 us
  Pallas kernels  177 us (49%)
  waiting for transfers between devices  72.7 us (20%)
  starting transfers between devices  65 us (18%)
  other arithmetic  20.7 us (6%)
  local copies, waits for them, and re-layouts  17.3 us (5%)
    pallas_call x3, Pallas kernels, attend_back(): pl.pallas_call(attend_back_kernel, grid=(1,), in_specs=[smem()] * 4 + [gr...  57.1 us
    pallas_call x1, Pallas kernels, feed_forward(): pl.pallas_call(lambda *refs: ffn_kernel(plan, len(own_pieces), len(ctx),...  39 us
    ppermute x39, waiting for transfers between devices, swap(): return lax.ppermute(value, 'seq', [(s, s ^ bit) for s in range(4)])  35.9 us
    pallas_call x2, Pallas kernels, attend(): pl.pallas_call(attend_kernel, grid=(1,), in_specs=[smem()] * 4 + [pl.Bloc...  29.6 us
    ppermute x11, waiting for transfers between devices, shift_z(): lax.ppermute(value, 'dp', [(2 * z + x, (z + by) % size * 2 + x) for z in...  24.7 us
    ppermute x39, starting transfers between devices, swap(): return lax.ppermute(value, 'seq', [(s, s ^ bit) for s in range(4)])  24.3 us
    ppermute x11, starting transfers between devices, shift_z(): lax.ppermute(value, 'dp', [(2 * z + x, (z + by) % size * 2 + x) for z in...  23.3 us
    pallas_call x1, Pallas kernels, weight_grads(): pl.pallas_call(lambda *refs: weight_grads_kernel(plan, len(pieces), *refs...  21.8 us
  transfers between devices with their start and end apart: 60, of which 19 were waited for; matrix products, arithmetic and copies ran while one was open for 5% of the time, Pallas kernels for 38%

profile of v4, /device:TPU:0, one launch (start us, length us, event | category | flops | bytes accessed | tf_op | source)
XLA Modules:
  0.0 355.2 jit_solution(14884107659470283563)
XLA Ops:
  3.9 1.9 pack.1
  7.8 2.6 collective-permute-start.3
  11.1 2.0 lay.1
  13.3 3.6 %collective-permute-start.7 = (bf16[160,384]{1,0:T(8,128)(2,1)}, bf16[160,384]{1,0:T(8,128)(2,1)S(1)}, u32[]{:S(2)}, u32[]{:S(2)}) collective-permute-start(bf16[160,384]{1,0:T(8,128)(2,1)} %get-tuple-element.185), channel_id=1, source_target_pairs={{0,24},{4,28},{8,0},{12,4},{16,8},{20,12},{24,16},{28,20},{1,25},{... | collective-permute-start | bytes 368648 | tf_op jit(solution)/shard_map/ppermute | solution.py:74
  19.1 11.6 %collective-permute-done.4 = s32[6,32,3]{2,1,0:T(8,128)S(1)} collective-permute-done((s32[6,32,3]{2,1,0:T(8,128)S(1)}, s32[6,32,3]{2,1,0:T(8,128)S(1)}, u32[]{:S(2)}, u32[]{:S(2)}) %collective-permute-start.4) | collective-permute-done | bytes 2336 | tf_op jit(solution)/shard_map/ppermute | solution.py:69
  30.7 4.7 %collective-permute-done.6 = bf16[160,384]{1,0:T(8,128)(2,1)S(1)} collective-permute-done((bf16[160,384]{1,0:T(8,128)(2,1)}, bf16[160,384]{1,0:T(8,128)(2,1)S(1)}, u32[]{:S(2)}, u32[]{:S(2)}) %collective-permute-start.6) | collective-permute-done | bytes 122912 | tf_op jit(solution)/shard_map/ppermute | solution.py:74
  36.3 1.9 maximum_select_fusion.refs_5_.refs_1_
  41.0 1.5 collective-permute-start.10
  43.1 2.3 collective-permute-start.12
  48.8 11.8 %collective-permute-done.12 = bf16[432,384]{1,0:T(8,128)(2,1)} collective-permute-done((bf16[432,384]{1,0:T(8,128)(2,1)}, bf16[432,384]{1,0:T(8,128)(2,1)}, u32[]{:S(2)}, u32[]{:S(2)}) %collective-permute-start.12) | collective-permute-done | bytes 331808 | tf_op jit(solution)/shard_map/ppermute | solution.py:74
  60.6 3.9 %collective-permute-done.10.refs_3_ = bf16[4,160,384]{2,1,0:T(8,128)(2,1)} collective-permute-done((bf16[4,160,384]{2,1,0:T(8,128)(2,1)S(1)}, bf16[4,160,384]{2,1,0:T(8,128)(2,1)}, u32[]{:S(2)}, u32[]{:S(2)}) %collective-permute-start.10) | collective-permute-done | bytes 491552 | tf_op jit(solution)/shard_map/ppermute | solution.py:69
  70.5 8.0 %project_qkv.1 = (bf16[2048,1152]{1,0:T(8,128)(2,1)S(1)}, bf16[16,48,1152]{2,1,0:T(8,128)(2,1)S(1)}, f32[16,768]{1,0:T(8,128)S(1)}) custom-call(s32[4]{0:T(128)S(1)} %copy-done.6, bf16[4,160,384]{2,1,0:T(8,128)(2,1)S(1)} %pad_maximum_fusion.5.refs_1_, bf16[4,160,384]{2,1,0:T(8,128)(2,1)} %collective-permute-done.9.refs_2_, ...), custom_call_target="tpu_custom_call" | custom-call | flops 3623878656 | bytes 7864320 | tf_op jit(solution)/shard_map/project_qkv/pallas_call | solution.py:294
  79.8 11.6 %attend.2 = (bf16[1024,128]{1,0:T(8,128)(2,1)S(1)}, bf16[1024,128]{1,0:T(8,128)(2,1)S(1)}, f32[2,2048]{1,0:T(2,128)S(1)}) custom-call(s32[4]{0:T(128)S(1)} %copy-done.6, s32[8]{0:T(128)S(1)} %get-tuple-element.343.lo_ref, s32[8]{0:T(128)S(1)} %get-tuple-element.344.n_ref, s32[2]{0:T(128)S(1)} %fusion.38.glob_ref, ...), custom_call_target="tpu_custom_call" | custom-call | flops 5872025600 | bytes 2621440 | tf_op jit(solution)/shard_map/attend/pallas_call | solution.py:430
  92.1 6.0 %collective-permute-done.18.refs_6_ = bf16[4,320,384]{2,1,0:T(8,128)(2,1)S(1)} collective-permute-done((bf16[4,320,384]{2,1,0:T(8,128)(2,1)S(1)}, bf16[4,320,384]{2,1,0:T(8,128)(2,1)S(1)}, u32[]{:S(2)}, u32[]{:S(2)}) %collective-permute-start.18) | collective-permute-done | bytes 983072 | tf_op jit(solution)/shard_map/ppermute | solution.py:64
  103.7 18.0 %attend.3 = (bf16[1024,256]{1,0:T(8,128)(2,1)S(1)}, bf16[1024,256]{1,0:T(8,128)(2,1)S(1)}, f32[4,2048]{1,0:T(4,128)S(1)}) custom-call(s32[4]{0:T(128)S(1)} %copy-done.6, s32[8]{0:T(128)S(1)} %get-tuple-element.343.lo_ref, s32[8]{0:T(128)S(1)} %get-tuple-element.344.n_ref, s32[2]{0:T(128)S(1)} %fusion.38.glob_ref, ...), custom_call_target="tpu_custom_call" | custom-call | flops 11744051200 | bytes 5242880 | tf_op jit(solution)/shard_map/attend/pallas_call | solution.py:430
  121.8 4.3 %collective-permute-done.21 = bf16[512,768]{1,0:T(8,128)(2,1)S(1)} collective-permute-done((bf16[512,768]{1,0:T(8,128)(2,1)S(1)}, bf16[512,768]{1,0:T(8,128)(2,1)S(1)}, u32[]{:S(2)}, u32[]{:S(2)}) %collective-permute-start.21) | collective-permute-done | bytes 786464 | tf_op jit(solution)/shard_map/ppermute | solution.py:69
  128.2 1.8 collective-permute-done.27.refs_11_
  131.2 39.0 %feed_forward.1 = (bf16[2,512,768]{2,1,0:T(8,128)(2,1)}, f32[2,512,768]{2,1,0:T(8,128)}, bf16[1024,3072]{1,0:T(8,128)(2,1)}, bf16[1024,768]{1,0:T(8,128)(2,1)}, ...) custom-call(s32[4]{0:T(128)} %pad_add_fusion.2.meta.refs_0_, ...), custom_call_target="tpu_custom_call" | custom-call | flops 21743271936 | bytes 40894464 | tf_op jit(solution)/shard_map/feed_forward/pallas_call | solution.py:721
  170.2 2.4 slice_bitcast_fusion.1
  174.1 21.8 %weight_grads.1 = (bf16[8,208,384]{2,1,0:T(8,128)(2,1)}, bf16[8,208,384]{2,1,0:T(8,128)(2,1)}, bf16[8,224,384]{2,1,0:T(8,128)(2,1)}, bf16[8,224,384]{2,1,0:T(8,1...) custom-call(s32[4]{0:T(128)} %pad_add_fusion.2.meta.refs_0_, ...), custom_call_target="tpu_custom_call" | custom-call | flops 10871635968 | bytes 18874368 | tf_op jit(solution)/shard_map/weight_grads/pallas_call | solution.py:776
  196.6 2.7 collective-permute-done.32
  199.3 1.8 add_convert_fusion.3
  202.4 1.5 collective-permute-start.35
  204.1 2.3 copy-done.11
  206.5 19.3 %attend_back.3.refs_3_.refs_0_ = bf16[2048,384]{1,0:T(8,128)(2,1)S(1)} custom-call(s32[4]{0:T(128)S(1)} %copy-done.7, s32[8]{0:T(128)S(1)} %get-tuple-element.343.lo_ref, s32[8]{0:T(128)S(1)} %get-tuple-element.344.n_ref, s32[2]{0:T(128)S(1)} %fusion.38.glob_ref, bf16[2048,1152]{1,0:T(8,128)(2,1)S(1)} %copy-done.11, bf16[1024,384]{1,0:T(8,128)(2,1)S(1)} %copy-done.15, ...), custom_call_target="tpu_custom_call" | custom-call | flops 12582912000 | bytes 5242880 | tf_op jit(solution)/shard_map/attend_back/pallas_call | solution.py:526
  225.8 6.3 %collective-permute-done.34 = bf16[8,208,384]{2,1,0:T(8,128)(2,1)S(1)} collective-permute-done((bf16[8,208,384]{2,1,0:T(8,128)(2,1)S(1)}, bf16[8,208,384]{2,1,0:T(8,128)(2,1)S(1)}, u32[]{:S(2)}, u32[]{:S(2)}) %collective-permute-start.34) | collective-permute-done | bytes 1277984 | tf_op jit(solution)/shard_map/ppermute | solution.py:69
  232.1 2.9 collective-permute-done.35
  235.6 1.6 collective-permute-start.38
  238.5 18.9 %attend_back.4.refs_4_.refs_1_ = bf16[2048,384]{1,0:T(8,128)(2,1)S(1)} custom-call(s32[4]{0:T(128)S(1)} %copy-done.7, s32[8]{0:T(128)S(1)} %get-tuple-element.343.lo_ref, s32[8]{0:T(128)S(1)} %get-tuple-element.344.n_ref, s32[2]{0:T(128)S(1)} %fusion.38.glob_ref, bf16[2048,1152]{1,0:T(8,128)(2,1)S(1)} %bitcast.114, bf16[1024,384]{1,0:T(8,128)(2,1)S(1)} %copy-done.15, ...), custom_call_target="tpu_custom_call" | custom-call | flops 12582912000 | bytes 5242880 | tf_op jit(solution)/shard_map/attend_back/pallas_call | solution.py:526
  257.9 7.3 %collective-permute-start.44 = (bf16[432,384]{1,0:T(8,128)(2,1)S(1)}, bf16[432,384]{1,0:T(8,128)(2,1)S(1)}, u32[]{:S(2)}, u32[]{:S(2)}) collective-permute-start(bf16[432,384]{1,0:T(8,128)(2,1)S(1)} %get-tuple-element.351), channel_id=1, source_target_pairs={{0,8},{4,12},{8,16},{12,20},{16,24},{20,28},{24,0},{28,4},{1,9},{5... | collective-permute-start | bytes 995336 | tf_op jit(solution)/shard_map/ppermute | solution.py:74
  265.2 1.5 collective-permute-start.43
  266.8 6.2 %qkv_grads.2 = (bf16[8,48,384]{2,1,0:T(8,128)(2,1)S(1)}, bf16[8,48,384]{2,1,0:T(8,128)(2,1)S(1)}, bf16[8,48,384]{2,1,0:T(8,128)(2,1)S(1)}, bf16[8,48,384]{2,1,0:T(8,128)(2,1)S(1)}, f32[8,384]{1,0:T(8,128)S(1)}) custom-call(s32[4]{0:T(128)S(1)} %copy-done.7, bf16[2,512,768]{2,1,0:T(8,128)(2,1)S(1)} %copy-done.1, bf16[2,512,768]{2,1,0:T(8,128)(2,1)S(1)} %copy-done.4, ...), custom_call_target="tpu_custom_call" | custom-call | flops 2415919104 | bytes 7864320 | tf_op jit(solution)/shard_map/qkv_grads/pallas_call | solution.py:859
  274.2 18.9 %attend_back.5.refs_2_.refs_3_ = bf16[2048,384]{1,0:T(8,128)(2,1)S(1)} custom-call(s32[4]{0:T(128)S(1)} %copy-done.7, s32[8]{0:T(128)S(1)} %get-tuple-element.343.lo_ref, s32[8]{0:T(128)S(1)} %get-tuple-element.344.n_ref, s32[2]{0:T(128)S(1)} %fusion.38.glob_ref, bf16[2048,1152]{1,0:T(8,128)(2,1)S(1)} %bitcast.114, bf16[1024,384]{1,0:T(8,128)(2,1)S(1)} %copy-done.15, ...), custom_call_target="tpu_custom_call" | custom-call | flops 12582912000 | bytes 5242880 | tf_op jit(solution)/shard_map/attend_back/pallas_call | solution.py:526
  294.6 3.5 input_grads.2
  298.2 2.8 maximum_select_fusion.2
  301.1 4.6 %qkv_grads.3 = (bf16[8,32,384]{2,1,0:T(8,128)(2,1)S(1)}, bf16[8,32,384]{2,1,0:T(8,128)(2,1)S(1)}, bf16[8,32,384]{2,1,0:T(8,128)(2,1)S(1)}, bf16[8,32,384]{2,1,0:T(8,128)(2,1)S(1)}) custom-call(s32[4]{0:T(128)S(1)} %copy-done.7, bf16[2,512,768]{2,1,0:T(8,128)(2,1)S(1)} %copy-done.1, bf16[2,512,768]{2,1,0:T(8,128)(2,1)S(1)} %copy-done.4, ...), custom_call_target="tpu_custom_call" | custom-call | flops 1207959552 | bytes 7864320 | tf_op jit(solution)/shard_map/qkv_grads/pallas_call | solution.py:859
  306.3 5.8 %collective-permute-start.46 = (bf16[8,32,384]{2,1,0:T(8,128)(2,1)S(1)}, bf16[8,32,384]{2,1,0:T(8,128)(2,1)S(1)}, u32[]{:S(2)}, u32[]{:S(2)}) collective-permute-start(bf16[8,32,384]{2,1,0:T(8,128)(2,1)S(1)} %get-tuple-element.302), channel_id=1, source_target_pairs={{0,4},{4,0},{8,12},{12,8},{16,20},{20,16},{24,28},{28,24},{1,5},{5... | collective-permute-start | bytes 589832 | tf_op jit(solution)/shard_map/ppermute | solution.py:64
  312.7 2.0 collective-permute-start.48
  314.8 2.8 collective-permute-done.46
  317.6 3.2 collective-permute-done.48
  321.0 1.7 collective-permute-start.51
  322.8 2.4 collective-permute-start.49
  325.2 1.7 collective-permute-start.50
  327.0 3.5 input_grads.3
  330.9 1.5 collective-permute-done.50
  335.3 3.9 %collective-permute-start.53 = (bf16[160,384]{1,0:T(8,128)(2,1)S(1)}, bf16[160,384]{1,0:T(8,128)(2,1)S(1)}, u32[]{:S(2)}, u32[]{:S(2)}) collective-permute-start(bf16[160,384]{1,0:T(8,128)(2,1)S(1)} %get-tuple-element.357), channel_id=1, source_target_pairs={{0,24},{4,28},{8,0},{12,4},{16,8},{20,12},{24,16},{28,20},{1,25},{... | collective-permute-start | bytes 368648 | tf_op jit(solution)/shard_map/ppermute | solution.py:74
  341.0 2.4 collective-permute-done.55
  344.0 5.2 %collective-permute-done.54 = bf16[160,384]{1,0:T(8,128)(2,1)S(1)} collective-permute-done((bf16[160,384]{1,0:T(8,128)(2,1)S(1)}, bf16[160,384]{1,0:T(8,128)(2,1)S(1)}, u32[]{:S(2)}, u32[]{:S(2)}) %collective-permute-start.54) | collective-permute-done | bytes 122912 | tf_op jit(solution)/shard_map/ppermute | solution.py:74
  (318 shorter events, 53.8 us)
Async XLA Ops:
  2.1 8.3 %collective-permute-start.1 = (bf16[16,128]{1,0:T(8,128)(2,1)S(1)}, bf16[16,128]{1,0:T(8,128)(2,1)S(1)}, u32[]{:S(2)}, u32[]{:S(2)}) collective-permute-start(bf16[16,128]{1,0:T(8,128)(2,1)S(1)} %fusion.27.refs_3_), channel_id=1, source_target_pairs={{0,1},{1,0},{2,3},{3,2},{4,5},{5,4},{6,7},{7,6},{8,9},{9,8},{10,11... | collective-permute-start | bytes 12296 | tf_op jit(solution)/shard_map/ppermute | solution.py:69
  3.3 9.8 %collective-permute-start.2 = (s32[2,3,32,3]{2,1,3,0:T(4,128)S(1)}, s32[2,3,32,3]{2,1,3,0:T(4,128)S(1)}, u32[]{:S(2)}, u32[]{:S(2)}) collective-permute-start(s32[2,3,32,3]{2,1,3,0:T(4,128)S(1)} %bitcast.126), channel_id=1, source_target_pairs={{0,1},{1,0},{2,3},{3,2},{4,5},{5,4},{6,7},{7,6},{8,9},{9,8},{10,11... | collective-permute-start | bytes 6920 | tf_op jit(solution)/shard_map/ppermute | solution.py:69
  7.8 27.6 %collective-permute-start.3 = (bf16[512,768]{1,0:T(8,128)(2,1)S(1)}, bf16[512,768]{1,0:T(8,128)(2,1)S(1)}, u32[]{:S(2)}, u32[]{:S(2)}) collective-permute-start(bf16[512,768]{1,0:T(8,128)(2,1)S(1)} %get-tuple-element.350), channel_id=1, source_target_pairs={{0,2},{1,3},{2,0},{3,1},{4,6},{5,7},{6,4},{7,5},{8,10},{9,11},{10,... | collective-permute-start | bytes 2359304 | tf_op jit(solution)/shard_map/ppermute | solution.py:69
  13.3 17.4 %collective-permute-start.7 = (bf16[160,384]{1,0:T(8,128)(2,1)}, bf16[160,384]{1,0:T(8,128)(2,1)S(1)}, u32[]{:S(2)}, u32[]{:S(2)}) collective-permute-start(bf16[160,384]{1,0:T(8,128)(2,1)} %get-tuple-element.185), channel_id=1, source_target_pairs={{0,24},{4,28},{8,0},{12,4},{16,8},{20,12},{24,16},{28,20},{1,25},{... | collective-permute-start | bytes 368648 | tf_op jit(solution)/shard_map/ppermute | solution.py:74
  16.9 18.5 %collective-permute-start.6 = (bf16[160,384]{1,0:T(8,128)(2,1)}, bf16[160,384]{1,0:T(8,128)(2,1)S(1)}, u32[]{:S(2)}, u32[]{:S(2)}) collective-permute-start(bf16[160,384]{1,0:T(8,128)(2,1)} %get-tuple-element.185), channel_id=1, source_target_pairs={{0,16},{4,20},{8,24},{12,28},{16,0},{20,4},{24,8},{28,12},{1,17},{... | collective-permute-start | bytes 368648 | tf_op jit(solution)/shard_map/ppermute | solution.py:74
  17.2 18.2 %collective-permute-start.5 = (bf16[592,384]{1,0:T(8,128)(2,1)}, bf16[592,384]{1,0:T(8,128)(2,1)S(1)}, u32[]{:S(2)}, u32[]{:S(2)}) collective-permute-start(bf16[592,384]{1,0:T(8,128)(2,1)} %get-tuple-element.184), channel_id=1, source_target_pairs={{0,8},{4,12},{8,16},{12,20},{16,24},{20,28},{24,0},{28,4},{1,9},{5... | collective-permute-start | bytes 1363976 | tf_op jit(solution)/shard_map/ppermute | solution.py:74
  18.3 12.4 %collective-permute-start.4 = (s32[6,32,3]{2,1,0:T(8,128)S(1)}, s32[6,32,3]{2,1,0:T(8,128)S(1)}, u32[]{:S(2)}, u32[]{:S(2)}) collective-permute-start(s32[6,32,3]{2,1,0:T(8,128)S(1)} %broadcast_select_fusion.1), channel_id=1, source_target_pairs={{0,2},{1,3},{2,0},{3,1},{4,6},{5,7},{6,4},{7,5},{8,10},{9,11},{10,... | collective-permute-start | bytes 6920 | tf_op jit(solution)/shard_map/ppermute | solution.py:69
  38.2 7.3 %collective-permute-start.8 = (bf16[2,512,768]{2,1,0:T(8,128)(2,1)S(1)}, bf16[2,512,768]{2,1,0:T(8,128)(2,1)S(1)}, u32[]{:S(2)}, u32[]{:S(2)}) collective-permute-start(bf16[2,512,768]{2,1,0:T(8,128)(2,1)S(1)} %maximum_select_fusion.refs_5_.refs_1_), channel_id=1, source_target_pairs={{0,1},{1,0},{2,3},{3,2},{4,5},{5,4},{6,7},{7,6},{8,9},{9,8},{10,11... | collective-permute-start | bytes 4718600 | tf_op jit(solution)/shard_map/ppermute | solution.py:69
  39.5 21.1 %collective-permute-start.11 = (bf16[4,160,384]{2,1,0:T(8,128)(2,1)S(1)}, bf16[4,160,384]{2,1,0:T(8,128)(2,1)}, u32[]{:S(2)}, u32[]{:S(2)}) collective-permute-start(bf16[4,160,384]{2,1,0:T(8,128)(2,1)S(1)} %pad_maximum_fusion.5.refs_1_), channel_id=1, source_target_pairs={{0,6},{1,7},{2,4},{3,5},{4,2},{5,3},{6,0},{7,1},{8,14},{9,15},{10,... | collective-permute-start | bytes 1474568 | tf_op jit(solution)/shard_map/ppermute | solution.py:67
  41.0 23.5 %collective-permute-start.10 = (bf16[4,160,384]{2,1,0:T(8,128)(2,1)S(1)}, bf16[4,160,384]{2,1,0:T(8,128)(2,1)}, u32[]{:S(2)}, u32[]{:S(2)}) collective-permute-start(bf16[4,160,384]{2,1,0:T(8,128)(2,1)S(1)} %pad_maximum_fusion.5.refs_1_), channel_id=1, source_target_pairs={{0,2},{1,3},{2,0},{3,1},{4,6},{5,7},{6,4},{7,5},{8,10},{9,11},{10,... | collective-permute-start | bytes 1474568 | tf_op jit(solution)/shard_map/ppermute | solution.py:69
  42.5 22.0 %collective-permute-start.9 = (bf16[4,160,384]{2,1,0:T(8,128)(2,1)S(1)}, bf16[4,160,384]{2,1,0:T(8,128)(2,1)}, u32[]{:S(2)}, u32[]{:S(2)}) collective-permute-start(bf16[4,160,384]{2,1,0:T(8,128)(2,1)S(1)} %pad_maximum_fusion.5.refs_1_), channel_id=1, source_target_pairs={{0,4},{4,0},{8,12},{12,8},{16,20},{20,16},{24,28},{28,24},{1,5},{5... | collective-permute-start | bytes 1474568 | tf_op jit(solution)/shard_map/ppermute | solution.py:64
  43.1 17.6 %collective-permute-start.12 = (bf16[432,384]{1,0:T(8,128)(2,1)}, bf16[432,384]{1,0:T(8,128)(2,1)}, u32[]{:S(2)}, u32[]{:S(2)}) collective-permute-start(bf16[432,384]{1,0:T(8,128)(2,1)} %get-tuple-element.194), channel_id=1, source_target_pairs={{0,16},{4,20},{8,24},{12,28},{16,0},{20,4},{24,8},{28,12},{1,17},{... | collective-permute-start | bytes 995336 | tf_op jit(solution)/shard_map/ppermute | solution.py:74
  46.7 17.9 %collective-permute-start.13 = (bf16[432,384]{1,0:T(8,128)(2,1)}, bf16[432,384]{1,0:T(8,128)(2,1)}, u32[]{:S(2)}, u32[]{:S(2)}) collective-permute-start(bf16[432,384]{1,0:T(8,128)(2,1)} %get-tuple-element.194), channel_id=1, source_target_pairs={{0,24},{4,28},{8,0},{12,4},{16,8},{20,12},{24,16},{28,20},{1,25},{... | collective-permute-start | bytes 995336 | tf_op jit(solution)/shard_map/ppermute | solution.py:74
  66.1 32.1 %collective-permute-start.14 = (bf16[4,432,384]{2,1,0:T(8,128)(2,1)S(1)}, bf16[4,432,384]{2,1,0:T(8,128)(2,1)S(1)}, u32[]{:S(2)}, u32[]{:S(2)}) collective-permute-start(bf16[4,432,384]{2,1,0:T(8,128)(2,1)S(1)} %pad_maximum_fusion.1.refs_1_), channel_id=1, source_target_pairs={{0,1},{1,0},{2,3},{3,2},{4,5},{5,4},{6,7},{7,6},{8,9},{9,8},{10,11... | collective-permute-start | bytes 3981320 | tf_op jit(solution)/shard_map/ppermute | solution.py:69
  66.2 25.9 %collective-permute-start.17 = (bf16[4,112,384]{2,1,0:T(8,128)(2,1)S(1)}, bf16[4,112,384]{2,1,0:T(8,128)(2,1)S(1)}, u32[]{:S(2)}, u32[]{:S(2)}) collective-permute-start(bf16[4,112,384]{2,1,0:T(8,128)(2,1)S(1)} %slice.481), channel_id=1, source_target_pairs={{0,2},{1,3},{2,0},{3,1},{4,6},{5,7},{6,4},{7,5},{8,10},{9,11},{10,... | collective-permute-start | bytes 1032200 | tf_op jit(solution)/shard_map/ppermute | solution.py:69
  66.9 25.2 %collective-permute-start.15 = (bf16[4,112,384]{2,1,0:T(8,128)(2,1)S(1)}, bf16[4,112,384]{2,1,0:T(8,128)(2,1)S(1)}, u32[]{:S(2)}, u32[]{:S(2)}) collective-permute-start(bf16[4,112,384]{2,1,0:T(8,128)(2,1)S(1)} %slice.481), channel_id=1, source_target_pairs={{0,4},{4,0},{8,12},{12,8},{16,20},{20,16},{24,28},{28,24},{1,5},{5... | collective-permute-start | bytes 1032200 | tf_op jit(solution)/shard_map/ppermute | solution.py:64
  68.5 29.6 %collective-permute-start.18 = (bf16[4,320,384]{2,1,0:T(8,128)(2,1)S(1)}, bf16[4,320,384]{2,1,0:T(8,128)(2,1)S(1)}, u32[]{:S(2)}, u32[]{:S(2)}) collective-permute-start(bf16[4,320,384]{2,1,0:T(8,128)(2,1)S(1)} %slice.482), channel_id=1, source_target_pairs={{0,4},{4,0},{8,12},{12,8},{16,20},{20,16},{24,28},{28,24},{1,5},{5... | collective-permute-start | bytes 2949128 | tf_op jit(solution)/shard_map/ppermute | solution.py:64
  69.1 29.0 %collective-permute-start.16 = (bf16[4,320,384]{2,1,0:T(8,128)(2,1)S(1)}, bf16[4,320,384]{2,1,0:T(8,128)(2,1)S(1)}, u32[]{:S(2)}, u32[]{:S(2)}) collective-permute-start(bf16[4,320,384]{2,1,0:T(8,128)(2,1)S(1)} %slice.482), channel_id=1, source_target_pairs={{0,2},{1,3},{2,0},{3,1},{4,6},{5,7},{6,4},{7,5},{8,10},{9,11},{10,... | collective-permute-start | bytes 2949128 | tf_op jit(solution)/shard_map/ppermute | solution.py:69
  98.8 23.0 %collective-permute-start.19 = (bf16[4,112,384]{2,1,0:T(8,128)(2,1)S(1)}, bf16[4,112,384]{2,1,0:T(8,128)(2,1)S(1)}, u32[]{:S(2)}, u32[]{:S(2)}) collective-permute-start(bf16[4,112,384]{2,1,0:T(8,128)(2,1)S(1)} %collective-permute-done.15.refs_2_), channel_id=1, source_target_pairs={{0,2},{1,3},{2,0},{3,1},{4,6},{5,7},{6,4},{7,5},{8,10},{9,11},{10,... | collective-permute-start | bytes 1032200 | tf_op jit(solution)/shard_map/ppermute | solution.py:69
  100.2 25.9 %collective-permute-start.25 = (bf16[4,320,384]{2,1,0:T(8,128)(2,1)S(1)}, bf16[4,320,384]{2,1,0:T(8,128)(2,1)S(1)}, u32[]{:S(2)}, u32[]{:S(2)}) collective-permute-start(bf16[4,320,384]{2,1,0:T(8,128)(2,1)S(1)} %collective-permute-done.16.refs_5_), channel_id=1, source_target_pairs={{0,1},{1,0},{2,3},{3,2},{4,5},{5,4},{6,7},{7,6},{8,9},{9,8},{10,11... | collective-permute-start | bytes 2949128 | tf_op jit(solution)/shard_map/ppermute | solution.py:69
  100.7 25.4 %collective-permute-start.20 = (bf16[4,320,384]{2,1,0:T(8,128)(2,1)S(1)}, bf16[4,320,384]{2,1,0:T(8,128)(2,1)S(1)}, u32[]{:S(2)}, u32[]{:S(2)}) collective-permute-start(bf16[4,320,384]{2,1,0:T(8,128)(2,1)S(1)} %collective-permute-done.16.refs_5_), channel_id=1, source_target_pairs={{0,4},{4,0},{8,12},{12,8},{16,20},{20,16},{24,28},{28,24},{1,5},{5... | collective-permute-start | bytes 2949128 | tf_op jit(solution)/shard_map/ppermute | solution.py:64
  102.2 23.8 %collective-permute-start.21 = (bf16[512,768]{1,0:T(8,128)(2,1)S(1)}, bf16[512,768]{1,0:T(8,128)(2,1)S(1)}, u32[]{:S(2)}, u32[]{:S(2)}) collective-permute-start(bf16[512,768]{1,0:T(8,128)(2,1)S(1)} %get-tuple-element.219), channel_id=1, source_target_pairs={{0,2},{1,3},{2,0},{3,1},{4,6},{5,7},{6,4},{7,5},{8,10},{9,11},{10,... | collective-permute-start | bytes 2359304 | tf_op jit(solution)/shard_map/ppermute | solution.py:69
  103.7 22.4 %collective-permute-start.26 = (bf16[4,320,384]{2,1,0:T(8,128)(2,1)S(1)}, bf16[4,320,384]{2,1,0:T(8,128)(2,1)S(1)}, u32[]{:S(2)}, u32[]{:S(2)}) collective-permute-start(bf16[4,320,384]{2,1,0:T(8,128)(2,1)S(1)} %collective-permute-done.18.refs_6_), channel_id=1, source_target_pairs={{0,1},{1,0},{2,3},{3,2},{4,5},{5,4},{6,7},{7,6},{8,9},{9,8},{10,11... | collective-permute-start | bytes 2949128 | tf_op jit(solution)/shard_map/ppermute | solution.py:69
  172.6 23.2 %collective-permute-start.30 = (bf16[512,768]{1,0:T(8,128)(2,1)S(1)}, bf16[512,768]{1,0:T(8,128)(2,1)}, u32[]{:S(2)}, u32[]{:S(2)}) collective-permute-start(bf16[512,768]{1,0:T(8,128)(2,1)S(1)} %get-tuple-element.346), channel_id=1, source_target_pairs={{0,2},{1,3},{2,0},{3,1},{4,6},{5,7},{6,4},{7,5},{8,10},{9,11},{10,... | collective-permute-start | bytes 2359304 | tf_op jit(solution)/shard_map/ppermute | solution.py:69
  174.1 21.8 %collective-permute-start.31 = (bf16[1024,384]{1,0:T(8,128)(2,1)}, bf16[1024,384]{1,0:T(8,128)(2,1)S(1)}, u32[]{:S(2)}, u32[]{:S(2)}) collective-permute-start(bf16[1024,384]{1,0:T(8,128)(2,1)} %get-tuple-element.239), channel_id=1, source_target_pairs={{0,1},{1,0},{2,3},{3,2},{4,5},{5,4},{6,7},{7,6},{8,9},{9,8},{10,11... | collective-permute-start | bytes 2359304 | tf_op jit(solution)/shard_map/ppermute | solution.py:69
  201.6 30.4 %collective-permute-start.34 = (bf16[8,208,384]{2,1,0:T(8,128)(2,1)S(1)}, bf16[8,208,384]{2,1,0:T(8,128)(2,1)S(1)}, u32[]{:S(2)}, u32[]{:S(2)}) collective-permute-start(bf16[8,208,384]{2,1,0:T(8,128)(2,1)S(1)} %add_convert_fusion.3), channel_id=1, source_target_pairs={{0,2},{1,3},{2,0},{3,1},{4,6},{5,7},{6,4},{7,5},{8,10},{9,11},{10,... | collective-permute-start | bytes 3833864 | tf_op jit(solution)/shard_map/ppermute | solution.py:69
  202.3 29.7 %collective-permute-start.36 = (bf16[8,208,384]{2,1,0:T(8,128)(2,1)}, bf16[8,208,384]{2,1,0:T(8,128)(2,1)S(1)}, u32[]{:S(2)}, u32[]{:S(2)}) collective-permute-start(bf16[8,208,384]{2,1,0:T(8,128)(2,1)} %get-tuple-element.266), channel_id=1, source_target_pairs={{0,1},{1,0},{2,3},{3,2},{4,5},{5,4},{6,7},{7,6},{8,9},{9,8},{10,11... | collective-permute-start | bytes 3833864 | tf_op jit(solution)/shard_map/ppermute | solution.py:69
  202.4 32.5 %collective-permute-start.35 = (bf16[8,224,384]{2,1,0:T(8,128)(2,1)S(1)}, bf16[8,224,384]{2,1,0:T(8,128)(2,1)S(1)}, u32[]{:S(2)}, u32[]{:S(2)}) collective-permute-start(bf16[8,224,384]{2,1,0:T(8,128)(2,1)S(1)} %add_convert_fusion.1), channel_id=1, source_target_pairs={{0,4},{4,0},{8,12},{12,8},{16,20},{20,16},{24,28},{28,24},{1,5},{5... | collective-permute-start | bytes 4128776 | tf_op jit(solution)/shard_map/ppermute | solution.py:64
  203.9 31.0 %collective-permute-start.37 = (bf16[8,224,384]{2,1,0:T(8,128)(2,1)}, bf16[8,224,384]{2,1,0:T(8,128)(2,1)S(1)}, u32[]{:S(2)}, u32[]{:S(2)}) collective-permute-start(bf16[8,224,384]{2,1,0:T(8,128)(2,1)} %get-tuple-element.267), channel_id=1, source_target_pairs={{0,1},{1,0},{2,3},{3,2},{4,5},{5,4},{6,7},{7,6},{8,9},{9,8},{10,11... | collective-permute-start | bytes 4128776 | tf_op jit(solution)/shard_map/ppermute | solution.py:69
  235.6 21.9 %collective-permute-start.38 = (bf16[4,208,384]{2,1,0:T(8,128)(2,1)S(1)}, bf16[4,208,384]{2,1,0:T(8,128)(2,1)S(1)}, u32[]{:S(2)}, u32[]{:S(2)}) collective-permute-start(bf16[4,208,384]{2,1,0:T(8,128)(2,1)S(1)} %slice.486), channel_id=1, source_target_pairs={{0,4},{4,0},{8,12},{12,8},{16,20},{20,16},{24,28},{28,24},{1,5},{5... | collective-permute-start | bytes 1916936 | tf_op jit(solution)/shard_map/ppermute | solution.py:64
  237.7 19.7 %collective-permute-start.39 = (bf16[4,224,384]{2,1,0:T(8,128)(2,1)S(1)}, bf16[4,224,384]{2,1,0:T(8,128)(2,1)S(1)}, u32[]{:S(2)}, u32[]{:S(2)}) collective-permute-start(bf16[4,224,384]{2,1,0:T(8,128)(2,1)S(1)} %slice.487), channel_id=1, source_target_pairs={{0,2},{1,3},{2,0},{3,1},{4,6},{5,7},{6,4},{7,5},{8,10},{9,11},{10,... | collective-permute-start | bytes 2064392 | tf_op jit(solution)/shard_map/ppermute | solution.py:69
  257.9 35.4 %collective-permute-start.44 = (bf16[432,384]{1,0:T(8,128)(2,1)S(1)}, bf16[432,384]{1,0:T(8,128)(2,1)S(1)}, u32[]{:S(2)}, u32[]{:S(2)}) collective-permute-start(bf16[432,384]{1,0:T(8,128)(2,1)S(1)} %get-tuple-element.351), channel_id=1, source_target_pairs={{0,8},{4,12},{8,16},{12,20},{16,24},{20,28},{24,0},{28,4},{1,9},{5... | collective-permute-start | bytes 995336 | tf_op jit(solution)/shard_map/ppermute | solution.py:74
  265.2 28.1 %collective-permute-start.42 = (bf16[432,384]{1,0:T(8,128)(2,1)S(1)}, bf16[432,384]{1,0:T(8,128)(2,1)S(1)}, u32[]{:S(2)}, u32[]{:S(2)}) collective-permute-start(bf16[432,384]{1,0:T(8,128)(2,1)S(1)} %get-tuple-element.352), channel_id=1, source_target_pairs={{0,24},{4,28},{8,0},{12,4},{16,8},{20,12},{24,16},{28,20},{1,25},{... | collective-permute-start | bytes 995336 | tf_op jit(solution)/shard_map/ppermute | solution.py:74
  265.2 28.1 %collective-permute-start.43 = (bf16[432,384]{1,0:T(8,128)(2,1)S(1)}, bf16[432,384]{1,0:T(8,128)(2,1)S(1)}, u32[]{:S(2)}, u32[]{:S(2)}) collective-permute-start(bf16[432,384]{1,0:T(8,128)(2,1)S(1)} %get-tuple-element.353), channel_id=1, source_target_pairs={{0,16},{4,20},{8,24},{12,28},{16,0},{20,4},{24,8},{28,12},{1,17},{... | collective-permute-start | bytes 995336 | tf_op jit(solution)/shard_map/ppermute | solution.py:74
  273.0 20.3 %collective-permute-start.40 = (bf16[8,48,384]{2,1,0:T(8,128)(2,1)S(1)}, bf16[8,48,384]{2,1,0:T(8,128)(2,1)S(1)}, u32[]{:S(2)}, u32[]{:S(2)}) collective-permute-start(bf16[8,48,384]{2,1,0:T(8,128)(2,1)S(1)} %get-tuple-element.285), channel_id=1, source_target_pairs={{0,2},{1,3},{2,0},{3,1},{4,6},{5,7},{6,4},{7,5},{8,10},{9,11},{10,... | collective-permute-start | bytes 884744 | tf_op jit(solution)/shard_map/ppermute | solution.py:69
  273.7 19.6 %collective-permute-start.41 = (bf16[8,48,384]{2,1,0:T(8,128)(2,1)S(1)}, bf16[8,48,384]{2,1,0:T(8,128)(2,1)S(1)}, u32[]{:S(2)}, u32[]{:S(2)}) collective-permute-start(bf16[8,48,384]{2,1,0:T(8,128)(2,1)S(1)} %get-tuple-element.286), channel_id=1, source_target_pairs={{0,4},{4,0},{8,12},{12,8},{16,20},{20,16},{24,28},{28,24},{1,5},{5... | collective-permute-start | bytes 884744 | tf_op jit(solution)/shard_map/ppermute | solution.py:64
  298.1 14.2 %collective-permute-start.47 = (bf16[512,768]{1,0:T(8,128)(2,1)S(1)}, bf16[512,768]{1,0:T(8,128)(2,1)S(1)}, u32[]{:S(2)}, u32[]{:S(2)}) collective-permute-start(bf16[512,768]{1,0:T(8,128)(2,1)S(1)} %get-tuple-element.303), channel_id=1, source_target_pairs={{0,1},{1,0},{2,3},{3,2},{4,5},{5,4},{6,7},{7,6},{8,9},{9,8},{10,11... | collective-permute-start | bytes 2359304 | tf_op jit(solution)/shard_map/ppermute | solution.py:69
  305.6 9.2 %collective-permute-start.45 = (bf16[8,32,384]{2,1,0:T(8,128)(2,1)S(1)}, bf16[8,32,384]{2,1,0:T(8,128)(2,1)S(1)}, u32[]{:S(2)}, u32[]{:S(2)}) collective-permute-start(bf16[8,32,384]{2,1,0:T(8,128)(2,1)S(1)} %get-tuple-element.301), channel_id=1, source_target_pairs={{0,2},{1,3},{2,0},{3,1},{4,6},{5,7},{6,4},{7,5},{8,10},{9,11},{10,... | collective-permute-start | bytes 589832 | tf_op jit(solution)/shard_map/ppermute | solution.py:69
  306.3 11.3 %collective-permute-start.46 = (bf16[8,32,384]{2,1,0:T(8,128)(2,1)S(1)}, bf16[8,32,384]{2,1,0:T(8,128)(2,1)S(1)}, u32[]{:S(2)}, u32[]{:S(2)}) collective-permute-start(bf16[8,32,384]{2,1,0:T(8,128)(2,1)S(1)} %get-tuple-element.302), channel_id=1, source_target_pairs={{0,4},{4,0},{8,12},{12,8},{16,20},{20,16},{24,28},{28,24},{1,5},{5... | collective-permute-start | bytes 589832 | tf_op jit(solution)/shard_map/ppermute | solution.py:64
  312.7 8.1 %collective-permute-start.48 = (bf16[160,768]{1,0:T(8,128)(2,1)S(1)}, bf16[160,768]{1,0:T(8,128)(2,1)S(1)}, u32[]{:S(2)}, u32[]{:S(2)}) collective-permute-start(bf16[160,768]{1,0:T(8,128)(2,1)S(1)} %slice.495), channel_id=1, source_target_pairs={{0,2},{1,3},{2,0},{3,1},{4,6},{5,7},{6,4},{7,5},{8,10},{9,11},{10,... | collective-permute-start | bytes 737288 | tf_op jit(solution)/shard_map/ppermute | solution.py:69
  321.0 9.5 %collective-permute-start.51 = (bf16[128,768]{1,0:T(8,128)(2,1)S(1)}, bf16[128,768]{1,0:T(8,128)(2,1)S(1)}, u32[]{:S(2)}, u32[]{:S(2)}) collective-permute-start(bf16[128,768]{1,0:T(8,128)(2,1)S(1)} %slice.408), channel_id=1, source_target_pairs={{0,2},{1,3},{2,0},{3,1},{4,6},{5,7},{6,4},{7,5},{8,10},{9,11},{10,... | collective-permute-start | bytes 589832 | tf_op jit(solution)/shard_map/ppermute | solution.py:69
  322.8 8.1 %collective-permute-start.49 = (bf16[4,80,384]{2,1,0:T(8,128)(2,1)S(1)}, bf16[4,80,384]{2,1,0:T(8,128)(2,1)S(1)}, u32[]{:S(2)}, u32[]{:S(2)}) collective-permute-start(bf16[4,80,384]{2,1,0:T(8,128)(2,1)S(1)} %fusion.14), channel_id=1, source_target_pairs={{0,4},{4,0},{8,12},{12,8},{16,20},{20,16},{24,28},{28,24},{1,5},{5... | collective-permute-start | bytes 737288 | tf_op jit(solution)/shard_map/ppermute | solution.py:64
  332.8 16.3 %collective-permute-start.56 = (bf16[224,768]{1,0:T(8,128)(2,1)S(1)}, bf16[224,768]{1,0:T(8,128)(2,1)S(1)}, u32[]{:S(2)}, u32[]{:S(2)}) collective-permute-start(bf16[224,768]{1,0:T(8,128)(2,1)S(1)} %slice.414), channel_id=1, source_target_pairs={{0,2},{1,3},{2,0},{3,1},{4,6},{5,7},{6,4},{7,5},{8,10},{9,11},{10,... | collective-permute-start | bytes 1032200 | tf_op jit(solution)/shard_map/ppermute | solution.py:69
  334.3 9.0 %collective-permute-start.55 = (bf16[160,384]{1,0:T(8,128)(2,1)S(1)}, bf16[160,384]{1,0:T(8,128)(2,1)S(1)}, u32[]{:S(2)}, u32[]{:S(2)}) collective-permute-start(bf16[160,384]{1,0:T(8,128)(2,1)S(1)} %get-tuple-element.356), channel_id=1, source_target_pairs={{0,8},{4,12},{8,16},{12,20},{16,24},{20,28},{24,0},{28,4},{1,9},{5... | collective-permute-start | bytes 368648 | tf_op jit(solution)/shard_map/ppermute | solution.py:74
  335.3 8.7 %collective-permute-start.53 = (bf16[160,384]{1,0:T(8,128)(2,1)S(1)}, bf16[160,384]{1,0:T(8,128)(2,1)S(1)}, u32[]{:S(2)}, u32[]{:S(2)}) collective-permute-start(bf16[160,384]{1,0:T(8,128)(2,1)S(1)} %get-tuple-element.357), channel_id=1, source_target_pairs={{0,24},{4,28},{8,0},{12,4},{16,8},{20,12},{24,16},{28,20},{1,25},{... | collective-permute-start | bytes 368648 | tf_op jit(solution)/shard_map/ppermute | solution.py:74
  339.2 9.9 %collective-permute-start.54 = (bf16[160,384]{1,0:T(8,128)(2,1)S(1)}, bf16[160,384]{1,0:T(8,128)(2,1)S(1)}, u32[]{:S(2)}, u32[]{:S(2)}) collective-permute-start(bf16[160,384]{1,0:T(8,128)(2,1)S(1)} %get-tuple-element.358), channel_id=1, source_target_pairs={{0,16},{4,20},{8,24},{12,28},{16,0},{20,4},{24,8},{28,12},{1,17},{... | collective-permute-start | bytes 368648 | tf_op jit(solution)/shard_map/ppermute | solution.py:74
  340.8 8.5 %collective-permute-start.59 = (bf16[216,384]{1,0:T(8,128)(2,1)S(1)}, bf16[216,384]{1,0:T(8,128)(2,1)S(1)}, u32[]{:S(2)}, u32[]{:S(2)}) collective-permute-start(bf16[216,384]{1,0:T(8,128)(2,1)S(1)} %constant_dynamic-update-slice_fusion.23), channel_id=1, source_target_pairs={{0,1},{1,0},{2,3},{3,2},{4,5},{5,4},{6,7},{7,6},{8,9},{9,8},{10,11... | collective-permute-start | bytes 497672 | tf_op jit(solution)/shard_map/ppermute | solution.py:69
  343.4 9.6 %collective-permute-start.52 = (bf16[512,768]{1,0:T(8,128)(2,1)S(1)}, bf16[512,768]{1,0:T(8,128)(2,1)S(1)}, u32[]{:S(2)}, u32[]{:S(2)}) collective-permute-start(bf16[512,768]{1,0:T(8,128)(2,1)S(1)} %get-tuple-element.320), channel_id=1, source_target_pairs={{0,1},{1,0},{2,3},{3,2},{4,5},{5,4},{6,7},{7,6},{8,9},{9,8},{10,11... | collective-permute-start | bytes 2359304 | tf_op jit(solution)/shard_map/ppermute | solution.py:69
  (65 other events, 547.2 us)

commit v5 on v4

--- a/solution.py
+++ b/solution.py
@@ -13,15 +13,14 @@
 TQ = 256
 TK = 512
 CHIPS = 16
-TILE = 512
 SUB = 256
 BF = jnp.bfloat16
 F32 = jnp.float32
 VMEM_LIMIT = 60 << 20
-COST = 1.0
+COST = 0.3
 CUT = 320
 BACK_CUT = 224
-EARLY = (160, 288)
+EARLY = 224
 
 
 def nn(left, right):
@@ -313,7 +312,7 @@
         ),
         out_shape=[shape((rows, wide), BF), shape((CHIPS, depth, wide), BF), shape((16, model), F32)],
         compiler_params=pltpu.CompilerParams(vmem_limit_bytes=14 << 20),
-        cost_estimate=cost(
+        cost_estimate=pl.CostEstimate(
             flops=2 * rows * model * wide, bytes_accessed=2 * rows * (model + wide), transcendentals=0
         ),
         name="project_qkv",
@@ -353,7 +352,7 @@
     query_wide[b, HD:128, :] = queries[HD:128]
     key_wide[a] = jnp.concatenate([keys[0:HD], key_feat[a]], axis=0).T
     key_wide[b] = jnp.concatenate([key_feat[b], keys[HD:128]], axis=0).T
-    return scaled, keys
+    return keys
 
 
 def over_keys(start, n, step, carry):
@@ -444,7 +443,7 @@
             pltpu.VMEM((heads, length, TQ), F32),
         ],
         compiler_params=pltpu.CompilerParams(vmem_limit_bytes=28 << 20),
-        cost_estimate=cost(
+        cost_estimate=pl.CostEstimate(
             flops=heads * length * length * 700, bytes_accessed=10 * length * wide, transcendentals=heads * length * length // 2
         ),
         name="attend",
@@ -453,7 +452,7 @@
 
 def attend_back_kernel(meta, lo_ref, n_ref, glob_ref, qkv_ref, own_ref, oth_ref, ctx_own, ctx_oth, lse_ref, seg_ref,
                        rand_ref, out_ref, key_feat, query_feat, key_wide, query_wide, value_one,
-                       grad_turned, keys_turned, query_one, grad_one, inner_ref, dk, dv, dqt, grads):
+                       grad_turned, keys_turned, inner_ref, dkt, dvt, dqt, grads):
     heads, length = lse_ref.shape
     quarter = length // 4
     fill_features(seg_ref, rand_ref, glob_ref[0], glob_ref[1], key_feat, query_feat)
@@ -467,22 +466,20 @@
     zero = jnp.zeros((length, 128), BF)
     for p in range(heads // 2):
         cols = slice(128 * p, 128 * p + 128)
-        scaled, keys = widen_pair(p, qkv_ref, key_feat, query_feat, key_wide, query_wide)
+        keys = widen_pair(p, qkv_ref, key_feat, query_feat, key_wide, query_wide)
         keys_turned[cols, :] = keys
         grad, value = grads[0, :, cols], of_pair(qkv_ref, p, 2)
         for e in range(2):
             keep = low if e == 0 else ~low
             value_one[2 * p + e] = jnp.where(keep, value, zero)
-            query_one[2 * p + e] = jnp.where(keep, scaled, zero)
-            grad_one[2 * p + e] = jnp.where(keep, grad, zero)
         turned = grad.T
         grad_turned[cols, :] = turned
         product = turned.astype(F32) * grads[1, :, cols].T.astype(F32)
         for e in range(2):
             h = 2 * p + e
             inner_ref[h : h + 1, :] = jnp.sum(product[HD * e : HD * e + HD], axis=0, keepdims=True)
-    dk[...] = jnp.zeros_like(dk)
-    dv[...] = jnp.zeros_like(dv)
+    dkt[...] = jnp.zeros_like(dkt)
+    dvt[...] = jnp.zeros_like(dvt)
 
     def tile(i, _):
         qs = pl.ds(pl.multiple_of(i * TQ, TQ), TQ)
@@ -490,19 +487,23 @@
         def body(start, at, size, carry):
             ks = pl.ds(pl.multiple_of(start, 128), size)
             new = []
-            for p in range(heads // 2):
-                cols = slice(128 * p, 128 * p + 128)
-                more_k, more_v = [], []
-                for h in (2 * p, 2 * p + 1):
-                    scores = nn(key_wide[h, ks, :], query_wide[h, :, qs])
-                    prob = jnp.exp(scores - lse_ref[h : h + 1, qs])
-                    grad_prob = nn(value_one[h, ks, :], grad_turned[cols, qs])
-                    grad_scores = (prob * (grad_prob - inner_ref[h : h + 1, qs])).astype(BF)
-                    new.append(carry[h] + nn(keys_turned[HD * h : HD * h + HD, ks], grad_scores))
-                    more_k.append(nn(grad_scores, query_one[h, qs, :]))
-                    more_v.append(nn(prob.astype(BF), grad_one[h, qs, :]))
-                dk[ks, cols] += more_k[0] + more_k[1]
-                dv[ks, cols] += more_v[0] + more_v[1]
+            scores = [nn(key_wide[h, ks, :], query_wide[h, :, qs]) for h in range(heads)]
+            grad_probs = [nn(value_one[h, ks, :], grad_turned[128 * (h // 2) : 128 * (h // 2) + 128, qs]) for h in range(heads)]
+            probs = [jnp.exp(scores[h] - lse_ref[h : h + 1, qs]) for h in range(heads)]
+            low = [prob.astype(BF) for prob in probs]
+            for h in range(heads):
+                rows = slice(HD * h, HD * h + HD)
+                mine = slice(HD * (h % 2), HD * (h % 2) + HD)
+                dvt[rows, ks] += nt(grad_turned[rows, qs], low[h])
+            grad_scores = [(probs[h] * (grad_probs[h] - inner_ref[h : h + 1, qs])).astype(BF) for h in range(heads)]
+            for h in range(heads):
+                rows = slice(HD * h, HD * h + HD)
+                mine = slice(HD * (h % 2), HD * (h % 2) + HD)
+                new.append(carry[h] + nn(keys_turned[rows, ks], grad_scores[h]))
+            for h in range(heads):
+                rows = slice(HD * h, HD * h + HD)
+                mine = slice(HD * (h % 2), HD * (h % 2) + HD)
+                dkt[rows, ks] += nt(query_wide[h, mine, qs], grad_scores[h])
             return tuple(new)
 
         found = over_keys(lo_ref[i], n_ref[i], body, (jnp.zeros((HD, TQ), F32),) * heads)
@@ -513,8 +514,8 @@
     lax.fori_loop(0, length // TQ, tile, 0)
     for p in range(heads // 2):
         cols = slice(128 * p, 128 * p + 128)
-        for w, value in enumerate((dqt[cols, :].T, dk[:, cols].astype(BF), dv[:, cols].astype(BF))):
-            out_ref[:, 384 * p + 128 * w : 384 * p + 128 * w + 128] = value
+        for w, value in enumerate((dqt[cols, :], dkt[cols, :].astype(BF), dvt[cols, :].astype(BF))):
+            out_ref[:, 384 * p + 128 * w : 384 * p + 128 * w + 128] = value.T
 
 
 def attend_back(meta, qkv, number, own, oth, ctx, ctx_oth, lse, part, seg_row, table, globs, lo, n):
@@ -540,11 +541,9 @@
             pltpu.VMEM((heads, length, 128), BF),
             pltpu.VMEM((wide, length), BF),
             pltpu.VMEM((wide, length), BF),
-            pltpu.VMEM((heads, length, 128), BF),
-            pltpu.VMEM((heads, length, 128), BF),
             pltpu.VMEM((heads, length), F32),
-            pltpu.VMEM((length, wide), F32),
-            pltpu.VMEM((length, wide), F32),
+            pltpu.VMEM((wide, length), F32),
+            pltpu.VMEM((wide, length), F32),
             pltpu.VMEM((wide, length), BF),
             pltpu.VMEM((2, length, wide), BF),
         ],
@@ -605,8 +604,8 @@
     oth_pieces = refs[1 + pieces_n : 1 + 2 * pieces_n]
     refs = refs[1 + 2 * pieces_n :]
     ctx_own, ctx_oth = refs[:ctx_n], refs[ctx_n : 2 * ctx_n]
-    (x_ref, dout_ref, vec_ref,
-     out_ref, gr_ref, hid_ref, gf_ref, low_ref, gp_ref, ga_ref, gc_own, gc_oth, ctx_ref, vg_ref,
+    (x_ref, d_came, d_kept, vec_ref,
+     given_ref, out_ref, gr_ref, hid_ref, gf_ref, low_ref, gp_ref, ga_ref, gc_own, gc_oth, ctx_ref, vg_ref,
      proj, inner, down, slope, sems) = refs[2 * ctx_n :]
     here = placed(meta)
     c = here["c"]
@@ -644,7 +643,7 @@
     w_down = lambda j: down[span * j : span * j + span].reshape(model, model)
     total = lambda value: jnp.sum(value, axis=0, keepdims=True)
     chunks = wide // model
-    spans = [slice(at, at + SUB) for at in range(0, TILE, SUB)]
+    spans = [slice(at, at + SUB) for at in range(0, x_ref.shape[0], SUB)]
     columns = [slice(model * j, model * j + model) for j in range(chunks)]
 
     arrived(0)
@@ -675,7 +674,7 @@
     for k, rows in enumerate(spans):
         n2, rate2 = centre(first[k][2] + (ffn[k] + vec(5)))
         out_ref[rows, :] = (n2 * vec(6) + vec(7)).astype(BF)
-        grad = dout_ref[rows, :].astype(F32)
+        grad = jnp.where(step == 0, d_came[rows, :], d_kept[rows, :]).astype(F32)
         gr2 = norm_back(grad * vec(6), n2, rate2)
         gf = gr2.astype(BF)
         gf_ref[rows, :] = gf
@@ -702,19 +701,21 @@
         gc_own[rows, :] = jnp.where(c == 0, gc[0], gc[1]).astype(BF)
         gc_oth[rows, :] = jnp.where(c == 0, gc[1], gc[0]).astype(BF)
 
-
-def feed_forward(plan, meta, own_pieces, oth_pieces, ctx, ctx_oth, x_own, d_own, vectors, wide):
+    @pl.when(step == 0)
+    def _():
+        given_ref[...] = out_ref[...]
+
+
+def feed_forward(plan, meta, own_pieces, oth_pieces, ctx, ctx_oth, x_own, d_came, d_out, vectors, wide):
     rows, model = x_own.shape
-    half = model // 2
-    tile = lambda n: pl.BlockSpec((TILE, n), lambda i, meta: (i, 0))
+    half, tall = model // 2, rows // 2
+    tile = lambda n: pl.BlockSpec((tall, n), lambda i, meta: (lax.rem(i + 1 + meta[2], 2), 0))
     full = lambda dims: pl.BlockSpec(dims, lambda i, meta: (0,) * len(dims))
-    per = rows // 2 // TILE
-    side = pl.BlockSpec((None, TILE, model), lambda i, meta: (lax.rem(i // per + meta[2], 2), lax.rem(i, per), 0))
     scratch = [
         pltpu.VMEM((CHIPS, model // CHIPS, model), BF),
         pltpu.VMEM((CHIPS, model // CHIPS, wide), BF),
         pltpu.VMEM((CHIPS, wide // CHIPS, model), BF),
-        pltpu.VMEM((TILE, wide), F32),
+        pltpu.VMEM((tall, wide), F32),
         pltpu.SemaphoreType.DMA((2 * plan.entries(),)),
     ]
     outs = [(wide, BF), (model, BF), (model, BF), (wide, BF), (model, BF), (half, BF), (half, BF), (model, BF)]
@@ -722,20 +723,27 @@
         lambda *refs: ffn_kernel(plan, len(own_pieces), len(ctx), *refs),
         grid_spec=pltpu.PrefetchScalarGridSpec(
             num_scalar_prefetch=1,
-            grid=(rows // TILE,),
+            grid=(2,),
             in_specs=[anywhere()] * (2 * len(own_pieces))
             + [tile(v.shape[1]) for v in ctx + ctx_oth]
-            + [tile(model), tile(model), full(vectors.shape)],
-            out_specs=[side] * 2 + [tile(w) for w, _ in outs] + [full((16, model))],
+            + [tile(model), full((tall, model)), pl.BlockSpec((None, tall, model), lambda i, meta: (meta[2], 0, 0))]
+            + [full(vectors.shape)],
+            out_specs=[full((tall, model))] * 2
+            + [pl.BlockSpec((None, tall, model), lambda i, meta: (i, 0, 0))]
+            + [tile(w) for w, _ in outs]
+            + [full((16, model))],
             scratch_shapes=scratch,
         ),
-        out_shape=[shape((2, rows // 2, model), kind) for kind in (BF, F32)] + [shape((rows, w), kind) for w, kind in outs] + [shape((16, model), F32)],
+        out_shape=[shape((tall, model), BF)] * 2
+        + [shape((2, tall, model), F32)]
+        + [shape((rows, w), kind) for w, kind in outs]
+        + [shape((16, model), F32)],
         compiler_params=pltpu.CompilerParams(vmem_limit_bytes=VMEM_LIMIT),
         cost_estimate=cost(
             flops=4 * rows * model * (model + 2 * wide), bytes_accessed=rows * (8 * wide + 20 * model), transcendentals=2 * rows * wide
         ),
         name="feed_forward",
-    )(meta, *own_pieces, *oth_pieces, *ctx, *ctx_oth, x_own, d_own, vectors)
+    )(meta, *own_pieces, *oth_pieces, *ctx, *ctx_oth, x_own, d_came, d_out, vectors)
 
 
 def weight_grads_kernel(plan, pieces_n, *refs):
@@ -986,6 +994,7 @@
         back_early, back_late = Plan([depth] * 2, depth, True), Plan([depth, 16], 32, True)
         mine, theirs = pack(meta, qkv_weight, proj_weight, inner_weight, down_weight)
         came = swap(theirs, "core")
+        mine, inner_bias, blocks, *vectors = stage(mine, inner_bias, blocks, *vectors)
         small = jnp.concatenate([jnp.pad(jnp.stack(vectors), ((0, 0), (0, 128 - share))),
                                  jnp.pad(inner_bias[None], ((0, 7), (0, 128 - share_f)))])
         blocks_came = swap(blocks, "core")
@@ -1004,7 +1013,7 @@
 
         near_a = jnp.stack([chunk_a, both[: plan_a.rows]] + za)
         far_a = [swap(near_a, dim) for dim in ("x", "y", "xy")]
-        x_own = pair(x_kept, x_came)
+        x_own = pair(x_kept, after(x_came, near_a))
         x_oth = swap(x_own, "core")
         zb = [both[plan_a.rows :]] + shifts_z(chunk_b, 2) + shifts_z(after(chunk_b, x_oth), 3)
         tables = spread_tables(model, depth // 2, deep // 2, chunk_b)
@@ -1019,7 +1028,7 @@
         qkv, w_qkv, spread = project_qkv(plan_a, meta, pieces, x_own, x_oth, tables)
         table = jnp.where(c == y, blocks_mine, blocks_came)
         ctx_b, ctx_b_give, lse_b = attention(slice(4, 6), 2, qkv, table)
-        d_given, d_kept = given_kept(after(d_out[:, 0], chunk_b))
+        d_given, _ = given_kept(after(d_out[:, 0], chunk_b))
         near_b, near_oth, a_x, b_y, a_y, b_x, qkv, ctx_b, ctx_b_give, d_given = stage(
             near_b, near_oth, a_x, b_y, a_y, b_x, qkv, ctx_b, ctx_b_give, d_given
         )
@@ -1036,16 +1045,14 @@
         own_b = [near_b] + early[:2] + [a_xy] + early[2:] + [b_yx]
         oth_b = [near_oth] + early_oth[:2] + [swap(a_xy, "core")] + early_oth[2:] + [swap(b_yx, "core")]
         ctx_a_oth = swap(ctx_a_give, "core")
-        d_own = pair(d_kept, d_came).reshape(-1, model)
         found = feed_forward(plan_b, meta, own_b, oth_b, [ctx_a, ctx_b], [ctx_a_oth, ctx_b_oth], x_own.reshape(-1, model),
-                             d_own, spread, ffw)
-        out, gr, hid, gf, x1_low, gp, ga, gc_own, gc_oth, context, vg = found
-
-        out_came, gc_came = swap(out[1], "y"), swap(gc_oth, "core")
+                             d_came, d_out[:, 0], spread, ffw)
+        out_given, out_kept, gr, hid, gf, x1_low, gp, ga, gc_own, gc_oth, context, vg = found
+
+        out_came, gc_came = swap(out_given, "y"), swap(gc_oth, "core")
         grads_own, grads_oth = weight_grads(back_b, meta, hid, gp, gf, x1_low, context, ga)
         out_came, gc_came, *rest = stage(out_came, gc_came, *grads_own, *grads_oth)
         a, a_far, b, b_far, a_oth, a_far_oth, b_oth, b_far_oth = rest
-        layer_out = pair(out[0], out_came)[:, None]
         a_far, b_far = add(a_far, swap(a_far_oth, "core")), add(b_far, swap(b_far_oth, "core"))
         a_far, b_far, gc_came, a_oth, b_oth = stage(a_far, b_far, gc_came, a_oth, b_oth)
 
@@ -1053,41 +1060,43 @@
         a_oth, b_oth = swap(a_oth, "core"), swap(b_oth, "core")
         back = lambda p, own, ctx, oth, lse: attention_back(p, qkv, own, gc_came, ctx, oth, lse, table)
         grad_0 = back(0, gc_own, ctx_a, ctx_a_give, lse_a[0:2])
-        a_came, b_came, a_oth, b_oth, grad_0, gc_own = stage(a_came, b_came, a_oth, b_oth, grad_0, gc_own)
+        grad_1 = back(1, after(gc_own, grad_0), ctx_a, ctx_a_give, lse_a[2:4])
+        layer_out = pair(out_kept, after(out_came, grad_1))[:, None]
+        a_came, b_came, a_oth, b_oth, grad_0, grad_1, gc_own, layer_out = stage(
+            a_came, b_came, a_oth, b_oth, grad_0, grad_1, gc_own, layer_out
+        )
         a, b = add(a, a_oth, a_came), add(b, b_oth, b_came)
         a_came, b_came = swap(a[ZS:], "x"), swap(b[ZS:], "y")
-        grad_1 = back(1, gc_own, ctx_a, ctx_a_give, lse_a[2:4])
-        a, b, a_came, b_came, grad_1, gc_own = stage(a, b, a_came, b_came, grad_1, gc_own)
-        total = jnp.concatenate([add(b[:ZS], b_came), add(a[:ZS], a_came)], axis=1)
-        came_b = scatter_z(total, 1, 2, 3)
         (qa, qa_far, qb, qb_far), sums = qkv_grads(back_early, meta, x_own, x_oth, [grad_0, grad_1], 0)
         qa_came, qb_came = swap(qa_far, "y"), swap(qb_far, "x")
         grad_2 = back(2, after(gc_own, sums), ctx_b, ctx_b_give, lse_b)
-        total, qa, qb, qa_came, qb_came, sums, grad_2, *came_b = stage(total, qa, qb, qa_came, qb_came, sums, grad_2, *came_b)
-        own_given, oth_given = input_grads(meta, [grad_0, grad_1, grad_2], w_qkv, True)
-        oth_given = swap(oth_given, "core")
-        last = after(grad_2, own_given)
-        ra, ra_far, rb, rb_far = qkv_grads(back_late, meta, x_own, x_oth, [last], 2, sums, vg, tables)
+        a, b, a_came, b_came, qa, qb, qa_came, qb_came, sums, grad_2 = stage(
+            a, b, a_came, b_came, qa, qb, qa_came, qb_came, sums, grad_2
+        )
+        total = jnp.concatenate([add(b[:ZS], b_came), add(a[:ZS], a_came)], axis=1)
+        came_b = scatter_z(total, 1)
+        ra, ra_far, rb, rb_far = qkv_grads(back_late, meta, x_own, x_oth, [grad_2], 2, sums, vg, tables)
         ra_came, rb_came = swap(ra_far, "y"), swap(rb_far, "x")
-        gx_given = add(gr[1], own_given, oth_given)
-        gx_came = [swap(gx_given[: EARLY[0]], "y")]
-        total_b = added(total[0], *came_b)
-        ra, rb, ra_came, rb_came, gx_given, total_b, *gx_came = stage(
-            ra, rb, ra_came, rb_came, gx_given, total_b, *gx_came
+        own_given, oth_given = input_grads(meta, [grad_0, grad_1, after(grad_2, ra)], w_qkv, True)
+        total, ra, rb, ra_came, rb_came, own_given, oth_given, *came_b = stage(
+            total, ra, rb, ra_came, rb_came, own_given, oth_given, *came_b
         )
-        gx_came.append(swap(gx_given[EARLY[0] : EARLY[1]], "y"))
+        came_b += scatter_z(total, 2)
         qa = jnp.concatenate([add(qa, qa_came), add(ra, ra_came)], axis=1)
         qb = jnp.concatenate([add(qb, qb_came), add(rb, rb_came)], axis=1)
         qa_came, qb_came = swap(qa[ZS:], "x"), swap(qb[ZS:], "y")
+        gx_given = add(gr[0], own_given, swap(oth_given, "core"))
+        gx_came = [swap(gx_given[:EARLY], "y")]
         own_kept, oth_kept = input_grads(meta, [grad_0, grad_1, after(grad_2, qa)], w_qkv, False)
-        qa, qb, qa_came, qb_came, own_kept, oth_kept, gx_given, *gx_came = stage(
-            qa, qb, qa_came, qb_came, own_kept, oth_kept, gx_given, *gx_came
+        qa, qb, qa_came, qb_came, own_kept, oth_kept, gx_given, total, *rest = stage(
+            qa, qb, qa_came, qb_came, own_kept, oth_kept, gx_given, total, *came_b, *gx_came
         )
-        gx_came.append(swap(gx_given[EARLY[1] :], "y"))
+        came_b, gx_came = rest[:2] + scatter_z(total, 3), [rest[2], swap(gx_given[EARLY:], "y")]
+        total_b = total[0]
         total = jnp.concatenate([add(qb[:ZS], qb_came), add(qa[:ZS], qa_came)], axis=1)
         came = scatter_z(total, 1, 2, 3)
         oth_kept = swap(oth_kept, "core")
-        gx_kept = add(gr[0], own_kept, oth_kept)
+        gx_kept = add(gr[1], own_kept, oth_kept)
 
         def finish(total, lengths):
             mine, theirs, at = [], [], 0
@@ -1104,9 +1113,9 @@
                 at += length
             return cuts
 
-        cuts_b = finish(after(total_b, total), lengths_b)
-        total, *rest = stage(total, *came, *gx_came)
-        came, gx_came = rest[:3], rest[3:]
+        total, total_b, *rest = stage(total, total_b, *came, *came_b, *gx_came)
+        came, came_b, gx_came = rest[:3], rest[3:6], rest[6:]
+        cuts_b = finish(added(total_b, *came_b), lengths_b)
         grad_input = pair(gx_kept, jnp.concatenate(gx_came))[:, None]
         total_a = added(total[0], *came)
         ends = (0, depth, depth + 32, 2 * depth + 32, 3 * depth)
@@ -1143,17 +1152,16 @@
         tables = spread_tables(model, depth // 2, deep // 2)
         x_own = pair(x_kept, swap(x_given, "y"))
         x_oth = swap(x_own, "core")
-        d_given, d_kept = given_kept(d_out[:, 0])
-        d_own = pair(d_kept, swap(d_given, "y")).reshape(-1, model)
+        d_came = swap(given_kept(d_out[:, 0])[0], "y")
         blocks_mine, blocks_given = pick_blocks(swap(blocks, "core"))
         table = jnp.where(c == y, blocks_mine, swap(blocks_given, "y"))
         qkv, w_qkv, spread = project_qkv(plan_a, meta, pieces_a, x_own, x_oth, tables)
         ctx_a, ctx_a_give, lse_a = attention(slice(0, 4), 0, qkv, table)
         ctx_b, ctx_b_give, lse_b = attention(slice(4, 6), 2, qkv, table)
         ctx_oth = [swap(v, "core") for v in (ctx_a_give, ctx_b_give)]
-        found = feed_forward(plan_b, meta, own_b, oth_b, [ctx_a, ctx_b], ctx_oth, x_own.reshape(-1, model), d_own, spread, ffw)
-        out, gr, hid, gf, x1_low, gp, ga, gc_own, gc_oth, context, vg = found
-        layer_out = pair(out[0], swap(out[1], "y"))[:, None]
+        found = feed_forward(plan_b, meta, own_b, oth_b, [ctx_a, ctx_b], ctx_oth, x_own.reshape(-1, model), d_came, d_out[:, 0], spread, ffw)
+        out_given, out_kept, gr, hid, gf, x1_low, gp, ga, gc_own, gc_oth, context, vg = found
+        layer_out = pair(out_kept, swap(out_given, "y"))[:, None]
         gc_came = swap(gc_oth, "core")
         grads_own, grads_oth = weight_grads(plan_b, meta, hid, gp, gf, x1_low, context, ga)
         ctxs = [(ctx_a, ctx_a_give, lse_a[2 * p : 2 * p + 2]) for p in range(2)] + [(ctx_b, ctx_b_give, lse_b)]
@@ -1161,8 +1169,8 @@
         pieces = qkv_grads(plan_a, meta, x_own, x_oth, grads, 0, jnp.zeros((8, 3 * 128), F32), vg, tables)
         own_given, oth_given = input_grads(meta, grads, w_qkv, True)
         own_kept, oth_kept = input_grads(meta, grads, w_qkv, False)
-        gx_came = swap(add(gr[1], own_given, swap(oth_given, "core")), "y")
-        grad_input = pair(add(gr[0], own_kept, swap(oth_kept, "core")), gx_came)[:, None]
+        gx_came = swap(add(gr[0], own_given, swap(oth_given, "core")), "y")
+        grad_input = pair(add(gr[1], own_kept, swap(oth_kept, "core")), gx_came)[:, None]
         scatter = lambda v: lax.psum_scatter(v.astype(F32), ("dp", "seq"), scatter_dimension=0, tiled=True)
         found = pieces[0][:, 3 * depth :].astype(F32)
         found = jnp.stack([found[:, :, :128], found[:, :, 128:256]], axis=1).transpose(2, 0, 1, 3)

time: 358 us -> 342 us (0.955)
  Pallas kernels: 177 us -> 161 us
  waiting for transfers between devices: 72.7 us -> 84.3 us
  local copies, waits for them, and re-layouts: 17.3 us -> 12.5 us
  starting transfers between devices: 65 us -> 60.4 us
    ppermute x11, waiting for transfers between devices: 24.7 us -> 39.6 us  [shift_z(): lax.ppermute(value, 'dp', [(2 * z + x, (z + by) % size * 2 + x) for z in...]
    pallas_call x3, Pallas kernels: 57.1 us -> 42.3 us  [attend_back(): pl.pallas_call(attend_back_kernel, grid=(1,), in_specs=[smem()] * 4 + [gr...]
    ppermute x11, starting transfers between devices: 23.3 us -> 14.5 us  [shift_z(): lax.ppermute(value, 'dp', [(2 * z + x, (z + by) % size * 2 + x) for z in...]
    ppermute x9, starting transfers between devices: 16 us -> 24.3 us  [swap(): lax.ppermute(value, 'dp', [(d, d ^ 1) for d in range(lax.axis_size('dp'))])]
    ppermute x9, waiting for transfers between devices: 12.1 us -> 7.27 us  [swap(): lax.ppermute(value, 'dp', [(d, d ^ 1) for d in range(lax.axis_size('dp'))])]
    ppermute x39 -> x38, starting transfers between devices: 24.3 us -> 20.1 us  [swap(): return lax.ppermute(value, 'seq', [(s, s ^ bit) for s in range(4)])]
    unnamed x131 -> x147, local copies, waits for them, and re-layouts: 11.4 us -> 8.93 us
    ppermute x39 -> x38, waiting for transfers between devices: 35.9 us -> 37.4 us  [swap(): return lax.ppermute(value, 'seq', [(s, s ^ bit) for s in range(4)])]
  transfers between devices with their start and end apart: 60 -> 59, of which waited for: 19 -> 19; matrix products, arithmetic and copies ran while one was open for 5% -> 4% of each run, Pallas kernels for 38% -> 34%
where the time goes in v5:
time: 342 us; the launch traced here: 340 us
  Pallas kernels  161 us (47%)
  waiting for transfers between devices  84.3 us (25%)
  starting transfers between devices  60.4 us (18%)
  other arithmetic  19.2 us (6%)
  local copies, waits for them, and re-layouts  12.5 us (4%)
    pallas_call x3, Pallas kernels, attend_back(): pl.pallas_call(attend_back_kernel, grid=(1,), in_specs=[smem()] * 4 + [gr...  42.3 us
    pallas_call x1, Pallas kernels, feed_forward(): pl.pallas_call(lambda *refs: ffn_kernel(plan, len(own_pieces), len(ctx),...  41 us
    ppermute x11, waiting for transfers between devices, shift_z(): lax.ppermute(value, 'dp', [(2 * z + x, (z + by) % size * 2 + x) for z in...  39.6 us
    ppermute x38, waiting for transfers between devices, swap(): return lax.ppermute(value, 'seq', [(s, s ^ bit) for s in range(4)])  37.4 us
    pallas_call x2, Pallas kernels, attend(): pl.pallas_call(attend_kernel, grid=(1,), in_specs=[smem()] * 4 + [pl.Bloc...  27.3 us
    ppermute x9, starting transfers between devices, swap(): lax.ppermute(value, 'dp', [(d, d ^ 1) for d in range(lax.axis_size('dp'))])  24.3 us
    pallas_call x1, Pallas kernels, weight_grads(): pl.pallas_call(lambda *refs: weight_grads_kernel(plan, len(pieces), *refs...  21.8 us
    ppermute x38, starting transfers between devices, swap(): return lax.ppermute(value, 'seq', [(s, s ^ bit) for s in range(4)])  20.1 us
  transfers between devices with their start and end apart: 59, of which 19 were waited for; matrix products, arithmetic and copies ran while one was open for 4% of the time, Pallas kernels for 34%

profile of v5, /device:TPU:0, one launch (start us, length us, event | category | flops | bytes accessed | tf_op | source)
XLA Modules:
  0.0 340.3 jit_solution(12692879867935042840)
XLA Ops:
  2.0 1.9 pack.1
  6.3 1.5 select_bitcast_fusion.1
  7.8 2.7 collective-permute-start.3
  11.7 2.0 lay.1
  13.7 3.6 %collective-permute-start.7 = (bf16[160,384]{1,0:T(8,128)(2,1)}, bf16[160,384]{1,0:T(8,128)(2,1)S(1)}, u32[]{:S(2)}, u32[]{:S(2)}) collective-permute-start(bf16[160,384]{1,0:T(8,128)(2,1)} %get-tuple-element.212), channel_id=1, source_target_pairs={{0,24},{4,28},{8,0},{12,4},{16,8},{20,12},{24,16},{28,20},{1,25},{... | collective-permute-start | bytes 368648 | tf_op jit(solution)/shard_map/ppermute | solution.py:73
  19.5 11.2 %collective-permute-done.4 = s32[6,32,3]{2,1,0:T(8,128)S(1)} collective-permute-done((s32[6,32,3]{2,1,0:T(8,128)S(1)}, s32[6,32,3]{2,1,0:T(8,128)S(1)}, u32[]{:S(2)}, u32[]{:S(2)}) %collective-permute-start.4) | collective-permute-done | bytes 2336 | tf_op jit(solution)/shard_map/ppermute | solution.py:68
  30.7 5.1 %collective-permute-done.6 = bf16[160,384]{1,0:T(8,128)(2,1)S(1)} collective-permute-done((bf16[160,384]{1,0:T(8,128)(2,1)}, bf16[160,384]{1,0:T(8,128)(2,1)S(1)}, u32[]{:S(2)}, u32[]{:S(2)}) %collective-permute-start.6) | collective-permute-done | bytes 122912 | tf_op jit(solution)/shard_map/ppermute | solution.py:73
  37.6 1.8 maximum_select_fusion.refs_5_.refs_1_
  39.8 1.5 collective-permute-start.11
  41.3 1.5 collective-permute-start.10
  43.3 2.4 collective-permute-start.12
  49.2 12.0 %collective-permute-done.12 = bf16[432,384]{1,0:T(8,128)(2,1)} collective-permute-done((bf16[432,384]{1,0:T(8,128)(2,1)}, bf16[432,384]{1,0:T(8,128)(2,1)}, u32[]{:S(2)}, u32[]{:S(2)}) %collective-permute-start.12) | collective-permute-done | bytes 331808 | tf_op jit(solution)/shard_map/ppermute | solution.py:73
  61.2 3.8 %collective-permute-done.10.refs_3_ = bf16[4,160,384]{2,1,0:T(8,128)(2,1)S(1)} collective-permute-done((bf16[4,160,384]{2,1,0:T(8,128)(2,1)S(1)}, bf16[4,160,384]{2,1,0:T(8,128)(2,1)S(1)}, u32[]{:S(2)}, u32[]{:S(2)}) %collective-permute-start.10) | collective-permute-done | bytes 491552 | tf_op jit(solution)/shard_map/ppermute | solution.py:68
  64.9 1.7 pad_maximum_fusion.1.refs_1_
  67.5 1.5 collective-permute-start.15
  69.7 1.4 collective-permute-start.16
  72.2 7.8 %project_qkv.1 = (bf16[2048,1152]{1,0:T(8,128)(2,1)S(1)}, bf16[16,48,1152]{2,1,0:T(8,128)(2,1)S(1)}, f32[16,768]{1,0:T(8,128)S(1)}) custom-call(s32[4]{0:T(128)S(1)} %copy-done.12, bf16[4,160,384]{2,1,0:T(8,128)(2,1)S(1)} %copy-done.10, bf16[4,160,384]{2,1,0:T(8,128)(2,1)} %collective-permute-done.9.refs_2_, bf16[4,160,384]{2,1,0:T(8,128)(2,1)S(1)} %copy-done.17, ...), custom_call_target="tpu_custom_call" | custom-call | flops 3623878656 | bytes 7864320 | tf_op jit(solution)/shard_map/project_qkv/pallas_call | solution.py:293
  80.6 10.7 %attend.2 = (bf16[1024,128]{1,0:T(8,128)(2,1)S(1)}, bf16[1024,128]{1,0:T(8,128)(2,1)S(1)}, f32[2,2048]{1,0:T(2,128)S(1)}) custom-call(s32[4]{0:T(128)S(1)} %copy-done.12, s32[8]{0:T(128)S(1)} %get-tuple-element.375.lo_ref, s32[8]{0:T(128)S(1)} %get-tuple-element.376.n_ref, s32[2]{0:T(128)S(1)} %fusion.32.glob_ref, ...), custom_call_target="tpu_custom_call" | custom-call | flops 5872025600 | bytes 2621440 | tf_op jit(solution)/shard_map/attend/pallas_call | solution.py:429
  91.5 7.2 %collective-permute-done.18.refs_6_ = bf16[4,320,384]{2,1,0:T(8,128)(2,1)S(1)} collective-permute-done((bf16[4,320,384]{2,1,0:T(8,128)(2,1)S(1)}, bf16[4,320,384]{2,1,0:T(8,128)(2,1)S(1)}, u32[]{:S(2)}, u32[]{:S(2)}) %collective-permute-start.18) | collective-permute-done | bytes 983072 | tf_op jit(solution)/shard_map/ppermute | solution.py:63
  99.3 1.5 collective-permute-start.19
  101.2 1.5 collective-permute-start.20
  103.6 16.6 %attend.3 = (bf16[1024,256]{1,0:T(8,128)(2,1)S(1)}, bf16[1024,256]{1,0:T(8,128)(2,1)S(1)}, f32[4,2048]{1,0:T(4,128)S(1)}) custom-call(s32[4]{0:T(128)S(1)} %copy-done.12, s32[8]{0:T(128)S(1)} %get-tuple-element.375.lo_ref, s32[8]{0:T(128)S(1)} %get-tuple-element.376.n_ref, s32[2]{0:T(128)S(1)} %fusion.32.glob_ref, ...), custom_call_target="tpu_custom_call" | custom-call | flops 11744051200 | bytes 5242880 | tf_op jit(solution)/shard_map/attend/pallas_call | solution.py:429
  121.1 5.5 %collective-permute-done.21.refs_20_ = bf16[512,768]{1,0:T(8,128)(2,1)S(1)} collective-permute-done((bf16[512,768]{1,0:T(8,128)(2,1)S(1)}, bf16[512,768]{1,0:T(8,128)(2,1)S(1)}, u32[]{:S(2)}, u32[]{:S(2)}) %collective-permute-start.21) | collective-permute-done | bytes 786464 | tf_op jit(solution)/shard_map/ppermute | solution.py:68
  127.3 3.2 collective-permute-done.27.refs_11_
  131.7 41.0 %feed_forward.1 = (bf16[512,768]{1,0:T(8,128)(2,1)}, bf16[512,768]{1,0:T(8,128)(2,1)}, f32[2,512,768]{2,1,0:T(8,128)}, bf16[1024,3072]{1,0:T(8,128)(2,1)}, bf16[...) custom-call(s32[4]{0:T(128)} %pad_add_fusion.2.meta.refs_0_, ...), custom_call_target="tpu_custom_call" | custom-call | flops 6522981376 | bytes 12268339 | tf_op jit(solution)/shard_map/feed_forward/pallas_call | solution.py:722
  172.7 1.6 collective-permute-start.30
  174.3 21.8 %weight_grads.1 = (bf16[8,208,384]{2,1,0:T(8,128)(2,1)}, bf16[8,208,384]{2,1,0:T(8,128)(2,1)}, bf16[8,224,384]{2,1,0:T(8,128)(2,1)}, bf16[8,224,384]{2,1,0:T(8,1...) custom-call(s32[4]{0:T(128)} %pad_add_fusion.2.meta.refs_0_, ...), custom_call_target="tpu_custom_call" | custom-call | flops 3261490688 | bytes 5662310 | tf_op jit(solution)/shard_map/weight_grads/pallas_call | solution.py:784
  196.8 2.7 collective-permute-done.32
  199.5 1.8 add_convert_fusion.3
  204.2 14.0 %attend_back.3.refs_3_.refs_0_ = bf16[2048,384]{1,0:T(8,128)(2,1)S(1)} custom-call(s32[4]{0:T(128)S(1)} %copy-done.13, s32[8]{0:T(128)S(1)} %get-tuple-element.375.lo_ref, s32[8]{0:T(128)S(1)} %get-tuple-element.376.n_ref, s32[2]{0:T(128)S(1)} %fusion.32.glob_ref, bf16[2048,1152]{1,0:T(8,128)(2,1)S(1)} %copy-done.19, bf16[1024,384]{1,0:T(8,128)(2,1)S(1)} %copy-done.20, ...), custom_call_target="tpu_custom_call" | custom-call | flops 3774873600 | bytes 1572864 | tf_op jit(solution)/shard_map/attend_back/pallas_call | solution.py:527
  218.3 14.2 %attend_back.4.refs_4_.refs_1_ = bf16[2048,384]{1,0:T(8,128)(2,1)S(1)} custom-call(s32[4]{0:T(128)S(1)} %copy-done.13, s32[8]{0:T(128)S(1)} %get-tuple-element.375.lo_ref, s32[8]{0:T(128)S(1)} %get-tuple-element.376.n_ref, s32[2]{0:T(128)S(1)} %fusion.32.glob_ref, bf16[2048,1152]{1,0:T(8,128)(2,1)S(1)} %copy-done.19, bf16[1024,384]{1,0:T(8,128)(2,1)S(1)} %copy-done.20, ...), custom_call_target="tpu_custom_call" | custom-call | flops 3774873600 | bytes 1572864 | tf_op jit(solution)/shard_map/attend_back/pallas_call | solution.py:527
  232.5 2.9 maximum_select_fusion.1
  237.9 11.0 %collective-permute-start.38 = (bf16[4,208,384]{2,1,0:T(8,128)(2,1)S(1)}, bf16[4,208,384]{2,1,0:T(8,128)(2,1)S(1)}, u32[]{:S(2)}, u32[]{:S(2)}) collective-permute-start(bf16[4,208,384]{2,1,0:T(8,128)(2,1)S(1)} %slice.473), channel_id=1, source_target_pairs={{0,4},{4,0},{8,12},{12,8},{16,20},{20,16},{24,28},{28,24},{1,5},{5... | collective-permute-start | bytes 1916936 | tf_op jit(solution)/shard_map/ppermute | solution.py:63
  248.8 6.0 %qkv_grads.2 = (bf16[8,48,384]{2,1,0:T(8,128)(2,1)S(1)}, bf16[8,48,384]{2,1,0:T(8,128)(2,1)S(1)}, bf16[8,48,384]{2,1,0:T(8,128)(2,1)S(1)}, bf16[8,48,384]{2,1,0:T(8,128)(2,1)S(1)}, f32[8,384]{1,0:T(8,128)S(1)}) custom-call(s32[4]{0:T(128)S(1)} %copy-done.13, bf16[2,512,768]{2,1,0:T(8,128)(2,1)S(1)} %copy-done.1, bf16[2,512,768]{2,1,0:T(8,128)(2,1)S(1)} %copy-done.4, ...), custom_call_target="tpu_custom_call" | custom-call | flops 724775744 | bytes 2359296 | tf_op jit(solution)/shard_map/qkv_grads/pallas_call | solution.py:867
  254.8 1.2 collective-permute-start.40
  257.2 14.0 %attend_back.5.refs_3_.refs_2_ = bf16[2048,384]{1,0:T(8,128)(2,1)S(1)} custom-call(s32[4]{0:T(128)S(1)} %copy-done.13, s32[8]{0:T(128)S(1)} %get-tuple-element.375.lo_ref, s32[8]{0:T(128)S(1)} %get-tuple-element.376.n_ref, s32[2]{0:T(128)S(1)} %fusion.32.glob_ref, bf16[2048,1152]{1,0:T(8,128)(2,1)S(1)} %copy-done.19, bf16[1024,384]{1,0:T(8,128)(2,1)S(1)} %copy-done.20, ...), custom_call_target="tpu_custom_call" | custom-call | flops 3774873600 | bytes 1572864 | tf_op jit(solution)/shard_map/attend_back/pallas_call | solution.py:527
  271.3 4.6 %qkv_grads.3 = (bf16[8,32,384]{2,1,0:T(8,128)(2,1)S(1)}, bf16[8,32,384]{2,1,0:T(8,128)(2,1)S(1)}, bf16[8,32,384]{2,1,0:T(8,128)(2,1)S(1)}, bf16[8,32,384]{2,1,0:T(8,128)(2,1)S(1)}) custom-call(s32[4]{0:T(128)S(1)} %copy-done.13, bf16[2,512,768]{2,1,0:T(8,128)(2,1)S(1)} %copy-done.1, bf16[2,512,768]{2,1,0:T(8,128)(2,1)S(1)} %copy-done.4, ...), custom_call_target="tpu_custom_call" | custom-call | flops 362387872 | bytes 2359296 | tf_op jit(solution)/shard_map/qkv_grads/pallas_call | solution.py:867
  276.0 6.7 %collective-permute-start.43 = (bf16[8,32,384]{2,1,0:T(8,128)(2,1)S(1)}, bf16[8,32,384]{2,1,0:T(8,128)(2,1)S(1)}, u32[]{:S(2)}, u32[]{:S(2)}) collective-permute-start(bf16[8,32,384]{2,1,0:T(8,128)(2,1)S(1)} %get-tuple-element.330), channel_id=1, source_target_pairs={{0,4},{4,0},{8,12},{12,8},{16,20},{20,16},{24,28},{28,24},{1,5},{5... | collective-permute-start | bytes 589832 | tf_op jit(solution)/shard_map/ppermute | solution.py:63
  283.6 3.5 %input_grads.2 = (bf16[512,768]{1,0:T(8,128)(2,1)S(1)}, bf16[512,768]{1,0:T(8,128)(2,1)S(1)}) custom-call(s32[4]{0:T(128)S(1)} %copy-done.13, bf16[2048,384]{1,0:T(8,128)(2,1)S(1)} %attend_back.3.refs_3_.refs_0_, bf16[2048,384]{1,0:T(8,128)(2,1)S(1)} %attend_back.4.refs_4_.refs_1_, bf16[2048,384]{1,0:T(8,128)(2,1)S(1)} %attend_back.5.refs_3_.refs_2_, ...), custom_call_target="tpu_custom_call" | custom-call | flops 543581824 | bytes 1179648 | tf_op jit(solution)/shard_map/input_grads/pallas_call | solution.py:913
  287.2 6.4 %collective-permute-done.44 = bf16[432,384]{1,0:T(8,128)(2,1)S(1)} collective-permute-done((bf16[432,384]{1,0:T(8,128)(2,1)S(1)}, bf16[432,384]{1,0:T(8,128)(2,1)S(1)}, u32[]{:S(2)}, u32[]{:S(2)}) %collective-permute-start.44) | collective-permute-done | bytes 331808 | tf_op jit(solution)/shard_map/ppermute | solution.py:73
  296.7 1.7 collective-permute-start.46
  298.5 3.5 %input_grads.3 = (bf16[512,768]{1,0:T(8,128)(2,1)S(1)}, bf16[512,768]{1,0:T(8,128)(2,1)S(1)}) custom-call(s32[4]{0:T(128)S(1)} %copy-done.13, bf16[2048,384]{1,0:T(8,128)(2,1)S(1)} %attend_back.3.refs_3_.refs_0_, bf16[2048,384]{1,0:T(8,128)(2,1)S(1)} %attend_back.4.refs_4_.refs_1_, bf16[2048,384]{1,0:T(8,128)(2,1)S(1)} %attend_back.5.refs_3_.refs_2_, ...), custom_call_target="tpu_custom_call" | custom-call | flops 543581824 | bytes 1179648 | tf_op jit(solution)/shard_map/input_grads/pallas_call | solution.py:913
  302.1 9.5 %collective-permute-done.46 = bf16[4,80,384]{2,1,0:T(8,128)(2,1)S(1)} collective-permute-done((bf16[4,80,384]{2,1,0:T(8,128)(2,1)S(1)}, bf16[4,80,384]{2,1,0:T(8,128)(2,1)S(1)}, u32[]{:S(2)}, u32[]{:S(2)}) %collective-permute-start.46) | collective-permute-done | bytes 245792 | tf_op jit(solution)/shard_map/ppermute | solution.py:68
  312.6 1.4 collective-permute-start.54
  314.3 3.8 %collective-permute-start.51 = (bf16[160,384]{1,0:T(8,128)(2,1)S(1)}, bf16[160,384]{1,0:T(8,128)(2,1)S(1)}, u32[]{:S(2)}, u32[]{:S(2)}) collective-permute-start(bf16[160,384]{1,0:T(8,128)(2,1)S(1)} %get-tuple-element.384), channel_id=1, source_target_pairs={{0,24},{4,28},{8,0},{12,4},{16,8},{20,12},{24,16},{28,20},{1,25},{... | collective-permute-start | bytes 368648 | tf_op jit(solution)/shard_map/ppermute | solution.py:73
  318.1 9.8 %collective-permute-done.53 = bf16[160,384]{1,0:T(8,128)(2,1)S(1)} collective-permute-done((bf16[160,384]{1,0:T(8,128)(2,1)S(1)}, bf16[160,384]{1,0:T(8,128)(2,1)S(1)}, u32[]{:S(2)}, u32[]{:S(2)}) %collective-permute-start.53) | collective-permute-done | bytes 122912 | tf_op jit(solution)/shard_map/ppermute | solution.py:73
  328.0 5.8 %collective-permute-done.52 = bf16[160,384]{1,0:T(8,128)(2,1)S(1)} collective-permute-done((bf16[160,384]{1,0:T(8,128)(2,1)S(1)}, bf16[160,384]{1,0:T(8,128)(2,1)S(1)}, u32[]{:S(2)}, u32[]{:S(2)}) %collective-permute-start.52) | collective-permute-done | bytes 122912 | tf_op jit(solution)/shard_map/ppermute | solution.py:73
  338.7 1.4 maximum_select_fusion.2
  (330 shorter events, 38.4 us)
Async XLA Ops:
  5.3 5.1 %collective-permute-start.1 = (bf16[16,128]{1,0:T(8,128)(2,1)S(1)}, bf16[16,128]{1,0:T(8,128)(2,1)S(1)}, u32[]{:S(2)}, u32[]{:S(2)}) collective-permute-start(bf16[16,128]{1,0:T(8,128)(2,1)S(1)} %fusion.21.refs_3_), channel_id=1, source_target_pairs={{0,1},{1,0},{2,3},{3,2},{4,5},{5,4},{6,7},{7,6},{8,9},{9,8},{10,11... | collective-permute-start | bytes 12296 | tf_op jit(solution)/shard_map/ppermute | solution.py:68
  5.8 8.0 %collective-permute-start.2 = (s32[2,3,32,3]{2,1,3,0:T(4,128)S(1)}, s32[2,3,32,3]{2,1,3,0:T(4,128)S(1)}, u32[]{:S(2)}, u32[]{:S(2)}) collective-permute-start(s32[2,3,32,3]{2,1,3,0:T(4,128)S(1)} %bitcast.111), channel_id=1, source_target_pairs={{0,1},{1,0},{2,3},{3,2},{4,5},{5,4},{6,7},{7,6},{8,9},{9,8},{10,11... | collective-permute-start | bytes 6920 | tf_op jit(solution)/shard_map/ppermute | solution.py:68
  7.8 28.0 %collective-permute-start.3 = (bf16[512,768]{1,0:T(8,128)(2,1)S(1)}, bf16[512,768]{1,0:T(8,128)(2,1)S(1)}, u32[]{:S(2)}, u32[]{:S(2)}) collective-permute-start(bf16[512,768]{1,0:T(8,128)(2,1)S(1)} %get-tuple-element.378), channel_id=1, source_target_pairs={{0,2},{1,3},{2,0},{3,1},{4,6},{5,7},{6,4},{7,5},{8,10},{9,11},{10,... | collective-permute-start | bytes 2359304 | tf_op jit(solution)/shard_map/ppermute | solution.py:68
  13.7 17.0 %collective-permute-start.7 = (bf16[160,384]{1,0:T(8,128)(2,1)}, bf16[160,384]{1,0:T(8,128)(2,1)S(1)}, u32[]{:S(2)}, u32[]{:S(2)}) collective-permute-start(bf16[160,384]{1,0:T(8,128)(2,1)} %get-tuple-element.212), channel_id=1, source_target_pairs={{0,24},{4,28},{8,0},{12,4},{16,8},{20,12},{24,16},{28,20},{1,25},{... | collective-permute-start | bytes 368648 | tf_op jit(solution)/shard_map/ppermute | solution.py:73
  17.3 18.4 %collective-permute-start.6 = (bf16[160,384]{1,0:T(8,128)(2,1)}, bf16[160,384]{1,0:T(8,128)(2,1)S(1)}, u32[]{:S(2)}, u32[]{:S(2)}) collective-permute-start(bf16[160,384]{1,0:T(8,128)(2,1)} %get-tuple-element.212), channel_id=1, source_target_pairs={{0,16},{4,20},{8,24},{12,28},{16,0},{20,4},{24,8},{28,12},{1,17},{... | collective-permute-start | bytes 368648 | tf_op jit(solution)/shard_map/ppermute | solution.py:73
  17.6 18.1 %collective-permute-start.5 = (bf16[592,384]{1,0:T(8,128)(2,1)}, bf16[592,384]{1,0:T(8,128)(2,1)S(1)}, u32[]{:S(2)}, u32[]{:S(2)}) collective-permute-start(bf16[592,384]{1,0:T(8,128)(2,1)} %get-tuple-element.211), channel_id=1, source_target_pairs={{0,8},{4,12},{8,16},{12,20},{16,24},{20,28},{24,0},{28,4},{1,9},{5... | collective-permute-start | bytes 1363976 | tf_op jit(solution)/shard_map/ppermute | solution.py:73
  18.7 12.0 %collective-permute-start.4 = (s32[6,32,3]{2,1,0:T(8,128)S(1)}, s32[6,32,3]{2,1,0:T(8,128)S(1)}, u32[]{:S(2)}, u32[]{:S(2)}) collective-permute-start(s32[6,32,3]{2,1,0:T(8,128)S(1)} %broadcast_select_fusion), channel_id=1, source_target_pairs={{0,2},{1,3},{2,0},{3,1},{4,6},{5,7},{6,4},{7,5},{8,10},{9,11},{10,... | collective-permute-start | bytes 6920 | tf_op jit(solution)/shard_map/ppermute | solution.py:68
  39.4 6.5 %collective-permute-start.8 = (bf16[2,512,768]{2,1,0:T(8,128)(2,1)S(1)}, bf16[2,512,768]{2,1,0:T(8,128)(2,1)S(1)}, u32[]{:S(2)}, u32[]{:S(2)}) collective-permute-start(bf16[2,512,768]{2,1,0:T(8,128)(2,1)S(1)} %maximum_select_fusion.refs_5_.refs_1_), channel_id=1, source_target_pairs={{0,1},{1,0},{2,3},{3,2},{4,5},{5,4},{6,7},{7,6},{8,9},{9,8},{10,11... | collective-permute-start | bytes 4718600 | tf_op jit(solution)/shard_map/ppermute | solution.py:68
  39.8 21.4 %collective-permute-start.11 = (bf16[4,160,384]{2,1,0:T(8,128)(2,1)S(1)}, bf16[4,160,384]{2,1,0:T(8,128)(2,1)S(1)}, u32[]{:S(2)}, u32[]{:S(2)}) collective-permute-start(bf16[4,160,384]{2,1,0:T(8,128)(2,1)S(1)} %pad_maximum_fusion.5.refs_1_), channel_id=1, source_target_pairs={{0,6},{1,7},{2,4},{3,5},{4,2},{5,3},{6,0},{7,1},{8,14},{9,15},{10,... | collective-permute-start | bytes 1474568 | tf_op jit(solution)/shard_map/ppermute | solution.py:66
  41.3 23.6 %collective-permute-start.10 = (bf16[4,160,384]{2,1,0:T(8,128)(2,1)S(1)}, bf16[4,160,384]{2,1,0:T(8,128)(2,1)S(1)}, u32[]{:S(2)}, u32[]{:S(2)}) collective-permute-start(bf16[4,160,384]{2,1,0:T(8,128)(2,1)S(1)} %pad_maximum_fusion.5.refs_1_), channel_id=1, source_target_pairs={{0,2},{1,3},{2,0},{3,1},{4,6},{5,7},{6,4},{7,5},{8,10},{9,11},{10,... | collective-permute-start | bytes 1474568 | tf_op jit(solution)/shard_map/ppermute | solution.py:68
  42.8 22.1 %collective-permute-start.9 = (bf16[4,160,384]{2,1,0:T(8,128)(2,1)S(1)}, bf16[4,160,384]{2,1,0:T(8,128)(2,1)}, u32[]{:S(2)}, u32[]{:S(2)}) collective-permute-start(bf16[4,160,384]{2,1,0:T(8,128)(2,1)S(1)} %pad_maximum_fusion.5.refs_1_), channel_id=1, source_target_pairs={{0,4},{4,0},{8,12},{12,8},{16,20},{20,16},{24,28},{28,24},{1,5},{5... | collective-permute-start | bytes 1474568 | tf_op jit(solution)/shard_map/ppermute | solution.py:63
  43.3 17.8 %collective-permute-start.12 = (bf16[432,384]{1,0:T(8,128)(2,1)}, bf16[432,384]{1,0:T(8,128)(2,1)}, u32[]{:S(2)}, u32[]{:S(2)}) collective-permute-start(bf16[432,384]{1,0:T(8,128)(2,1)} %get-tuple-element.222), channel_id=1, source_target_pairs={{0,16},{4,20},{8,24},{12,28},{16,0},{20,4},{24,8},{28,12},{1,17},{... | collective-permute-start | bytes 995336 | tf_op jit(solution)/shard_map/ppermute | solution.py:73
  47.0 17.9 %collective-permute-start.13 = (bf16[432,384]{1,0:T(8,128)(2,1)}, bf16[432,384]{1,0:T(8,128)(2,1)}, u32[]{:S(2)}, u32[]{:S(2)}) collective-permute-start(bf16[432,384]{1,0:T(8,128)(2,1)} %get-tuple-element.222), channel_id=1, source_target_pairs={{0,24},{4,28},{8,0},{12,4},{16,8},{20,12},{24,16},{28,20},{1,25},{... | collective-permute-start | bytes 995336 | tf_op jit(solution)/shard_map/ppermute | solution.py:73
  66.6 32.0 %collective-permute-start.14 = (bf16[4,432,384]{2,1,0:T(8,128)(2,1)S(1)}, bf16[4,432,384]{2,1,0:T(8,128)(2,1)S(1)}, u32[]{:S(2)}, u32[]{:S(2)}) collective-permute-start(bf16[4,432,384]{2,1,0:T(8,128)(2,1)S(1)} %pad_maximum_fusion.1.refs_1_), channel_id=1, source_target_pairs={{0,1},{1,0},{2,3},{3,2},{4,5},{5,4},{6,7},{7,6},{8,9},{9,8},{10,11... | collective-permute-start | bytes 3981320 | tf_op jit(solution)/shard_map/ppermute | solution.py:68
  66.8 24.6 %collective-permute-start.17 = (bf16[4,112,384]{2,1,0:T(8,128)(2,1)S(1)}, bf16[4,112,384]{2,1,0:T(8,128)(2,1)S(1)}, u32[]{:S(2)}, u32[]{:S(2)}) collective-permute-start(bf16[4,112,384]{2,1,0:T(8,128)(2,1)S(1)} %slice.467), channel_id=1, source_target_pairs={{0,2},{1,3},{2,0},{3,1},{4,6},{5,7},{6,4},{7,5},{8,10},{9,11},{10,... | collective-permute-start | bytes 1032200 | tf_op jit(solution)/shard_map/ppermute | solution.py:68
  67.5 23.9 %collective-permute-start.15 = (bf16[4,112,384]{2,1,0:T(8,128)(2,1)S(1)}, bf16[4,112,384]{2,1,0:T(8,128)(2,1)S(1)}, u32[]{:S(2)}, u32[]{:S(2)}) collective-permute-start(bf16[4,112,384]{2,1,0:T(8,128)(2,1)S(1)} %slice.467), channel_id=1, source_target_pairs={{0,4},{4,0},{8,12},{12,8},{16,20},{20,16},{24,28},{28,24},{1,5},{5... | collective-permute-start | bytes 1032200 | tf_op jit(solution)/shard_map/ppermute | solution.py:63
  69.1 29.5 %collective-permute-start.18 = (bf16[4,320,384]{2,1,0:T(8,128)(2,1)S(1)}, bf16[4,320,384]{2,1,0:T(8,128)(2,1)S(1)}, u32[]{:S(2)}, u32[]{:S(2)}) collective-permute-start(bf16[4,320,384]{2,1,0:T(8,128)(2,1)S(1)} %slice.468), channel_id=1, source_target_pairs={{0,4},{4,0},{8,12},{12,8},{16,20},{20,16},{24,28},{28,24},{1,5},{5... | collective-permute-start | bytes 2949128 | tf_op jit(solution)/shard_map/ppermute | solution.py:63
  69.7 28.9 %collective-permute-start.16 = (bf16[4,320,384]{2,1,0:T(8,128)(2,1)S(1)}, bf16[4,320,384]{2,1,0:T(8,128)(2,1)S(1)}, u32[]{:S(2)}, u32[]{:S(2)}) collective-permute-start(bf16[4,320,384]{2,1,0:T(8,128)(2,1)S(1)} %slice.468), channel_id=1, source_target_pairs={{0,2},{1,3},{2,0},{3,1},{4,6},{5,7},{6,4},{7,5},{8,10},{9,11},{10,... | collective-permute-start | bytes 2949128 | tf_op jit(solution)/shard_map/ppermute | solution.py:68
  98.7 4.8 %collective-permute-start.23 = (bf16[4,112,384]{2,1,0:T(8,128)(2,1)S(1)}, bf16[4,112,384]{2,1,0:T(8,128)(2,1)S(1)}, u32[]{:S(2)}, u32[]{:S(2)}) collective-permute-start(bf16[4,112,384]{2,1,0:T(8,128)(2,1)S(1)} %collective-permute-done.15.refs_2_), channel_id=1, source_target_pairs={{0,1},{1,0},{2,3},{3,2},{4,5},{5,4},{6,7},{7,6},{8,9},{9,8},{10,11... | collective-permute-start | bytes 1032200 | tf_op jit(solution)/shard_map/ppermute | solution.py:68
  99.3 21.8 %collective-permute-start.19 = (bf16[4,112,384]{2,1,0:T(8,128)(2,1)S(1)}, bf16[4,112,384]{2,1,0:T(8,128)(2,1)S(1)}, u32[]{:S(2)}, u32[]{:S(2)}) collective-permute-start(bf16[4,112,384]{2,1,0:T(8,128)(2,1)S(1)} %collective-permute-done.15.refs_2_), channel_id=1, source_target_pairs={{0,2},{1,3},{2,0},{3,1},{4,6},{5,7},{6,4},{7,5},{8,10},{9,11},{10,... | collective-permute-start | bytes 1032200 | tf_op jit(solution)/shard_map/ppermute | solution.py:68
  100.8 25.8 %collective-permute-start.25 = (bf16[4,320,384]{2,1,0:T(8,128)(2,1)S(1)}, bf16[4,320,384]{2,1,0:T(8,128)(2,1)S(1)}, u32[]{:S(2)}, u32[]{:S(2)}) collective-permute-start(bf16[4,320,384]{2,1,0:T(8,128)(2,1)S(1)} %collective-permute-done.16.refs_5_), channel_id=1, source_target_pairs={{0,1},{1,0},{2,3},{3,2},{4,5},{5,4},{6,7},{7,6},{8,9},{9,8},{10,11... | collective-permute-start | bytes 2949128 | tf_op jit(solution)/shard_map/ppermute | solution.py:68
  101.2 25.4 %collective-permute-start.20 = (bf16[4,320,384]{2,1,0:T(8,128)(2,1)S(1)}, bf16[4,320,384]{2,1,0:T(8,128)(2,1)S(1)}, u32[]{:S(2)}, u32[]{:S(2)}) collective-permute-start(bf16[4,320,384]{2,1,0:T(8,128)(2,1)S(1)} %collective-permute-done.16.refs_5_), channel_id=1, source_target_pairs={{0,4},{4,0},{8,12},{12,8},{16,20},{20,16},{24,28},{28,24},{1,5},{5... | collective-permute-start | bytes 2949128 | tf_op jit(solution)/shard_map/ppermute | solution.py:63
  102.7 23.8 %collective-permute-start.21 = (bf16[512,768]{1,0:T(8,128)(2,1)S(1)}, bf16[512,768]{1,0:T(8,128)(2,1)S(1)}, u32[]{:S(2)}, u32[]{:S(2)}) collective-permute-start(bf16[512,768]{1,0:T(8,128)(2,1)S(1)} %select_bitcast_fusion), channel_id=1, source_target_pairs={{0,2},{1,3},{2,0},{3,1},{4,6},{5,7},{6,4},{7,5},{8,10},{9,11},{10,... | collective-permute-start | bytes 2359304 | tf_op jit(solution)/shard_map/ppermute | solution.py:68
  103.5 23.0 %collective-permute-start.26 = (bf16[4,320,384]{2,1,0:T(8,128)(2,1)S(1)}, bf16[4,320,384]{2,1,0:T(8,128)(2,1)S(1)}, u32[]{:S(2)}, u32[]{:S(2)}) collective-permute-start(bf16[4,320,384]{2,1,0:T(8,128)(2,1)S(1)} %collective-permute-done.18.refs_6_), channel_id=1, source_target_pairs={{0,1},{1,0},{2,3},{3,2},{4,5},{5,4},{6,7},{7,6},{8,9},{9,8},{10,11... | collective-permute-start | bytes 2949128 | tf_op jit(solution)/shard_map/ppermute | solution.py:68
  172.7 23.3 %collective-permute-start.30 = (bf16[512,768]{1,0:T(8,128)(2,1)}, bf16[512,768]{1,0:T(8,128)(2,1)}, u32[]{:S(2)}, u32[]{:S(2)}) collective-permute-start(bf16[512,768]{1,0:T(8,128)(2,1)} %get-tuple-element.266), channel_id=1, source_target_pairs={{0,2},{1,3},{2,0},{3,1},{4,6},{5,7},{6,4},{7,5},{8,10},{9,11},{10,... | collective-permute-start | bytes 2359304 | tf_op jit(solution)/shard_map/ppermute | solution.py:68
  174.3 21.8 %collective-permute-start.31 = (bf16[1024,384]{1,0:T(8,128)(2,1)}, bf16[1024,384]{1,0:T(8,128)(2,1)S(1)}, u32[]{:S(2)}, u32[]{:S(2)}) collective-permute-start(bf16[1024,384]{1,0:T(8,128)(2,1)} %get-tuple-element.267), channel_id=1, source_target_pairs={{0,1},{1,0},{2,3},{3,2},{4,5},{5,4},{6,7},{7,6},{8,9},{9,8},{10,11... | collective-permute-start | bytes 2359304 | tf_op jit(solution)/shard_map/ppermute | solution.py:68
  196.7 4.8 %collective-permute-start.33 = (bf16[8,224,384]{2,1,0:T(8,128)(2,1)}, bf16[8,224,384]{2,1,0:T(8,128)(2,1)S(1)}, u32[]{:S(2)}, u32[]{:S(2)}) collective-permute-start(bf16[8,224,384]{2,1,0:T(8,128)(2,1)} %get-tuple-element.285), channel_id=1, source_target_pairs={{0,1},{1,0},{2,3},{3,2},{4,5},{5,4},{6,7},{7,6},{8,9},{9,8},{10,11... | collective-permute-start | bytes 4128776 | tf_op jit(solution)/shard_map/ppermute | solution.py:68
  201.8 33.6 %collective-permute-start.35 = (bf16[8,224,384]{2,1,0:T(8,128)(2,1)S(1)}, bf16[8,224,384]{2,1,0:T(8,128)(2,1)S(1)}, u32[]{:S(2)}, u32[]{:S(2)}) collective-permute-start(bf16[8,224,384]{2,1,0:T(8,128)(2,1)S(1)} %add_convert_fusion.1), channel_id=1, source_target_pairs={{0,4},{4,0},{8,12},{12,8},{16,20},{20,16},{24,28},{28,24},{1,5},{5... | collective-permute-start | bytes 4128776 | tf_op jit(solution)/shard_map/ppermute | solution.py:63
  202.8 32.6 %collective-permute-start.37 = (bf16[8,224,384]{2,1,0:T(8,128)(2,1)}, bf16[8,224,384]{2,1,0:T(8,128)(2,1)S(1)}, u32[]{:S(2)}, u32[]{:S(2)}) collective-permute-start(bf16[8,224,384]{2,1,0:T(8,128)(2,1)} %get-tuple-element.292), channel_id=1, source_target_pairs={{0,1},{1,0},{2,3},{3,2},{4,5},{5,4},{6,7},{7,6},{8,9},{9,8},{10,11... | collective-permute-start | bytes 4128776 | tf_op jit(solution)/shard_map/ppermute | solution.py:68
  202.9 32.5 %collective-permute-start.34 = (bf16[8,208,384]{2,1,0:T(8,128)(2,1)S(1)}, bf16[8,208,384]{2,1,0:T(8,128)(2,1)S(1)}, u32[]{:S(2)}, u32[]{:S(2)}) collective-permute-start(bf16[8,208,384]{2,1,0:T(8,128)(2,1)S(1)} %add_convert_fusion.3), channel_id=1, source_target_pairs={{0,2},{1,3},{2,0},{3,1},{4,6},{5,7},{6,4},{7,5},{8,10},{9,11},{10,... | collective-permute-start | bytes 3833864 | tf_op jit(solution)/shard_map/ppermute | solution.py:68
  204.0 31.4 %collective-permute-start.36 = (bf16[8,208,384]{2,1,0:T(8,128)(2,1)}, bf16[8,208,384]{2,1,0:T(8,128)(2,1)S(1)}, u32[]{:S(2)}, u32[]{:S(2)}) collective-permute-start(bf16[8,208,384]{2,1,0:T(8,128)(2,1)} %get-tuple-element.291), channel_id=1, source_target_pairs={{0,1},{1,0},{2,3},{3,2},{4,5},{5,4},{6,7},{7,6},{8,9},{9,8},{10,11... | collective-permute-start | bytes 3833864 | tf_op jit(solution)/shard_map/ppermute | solution.py:68
  236.0 35.3 %collective-permute-start.39 = (bf16[4,224,384]{2,1,0:T(8,128)(2,1)S(1)}, bf16[4,224,384]{2,1,0:T(8,128)(2,1)S(1)}, u32[]{:S(2)}, u32[]{:S(2)}) collective-permute-start(bf16[4,224,384]{2,1,0:T(8,128)(2,1)S(1)} %slice.474), channel_id=1, source_target_pairs={{0,2},{1,3},{2,0},{3,1},{4,6},{5,7},{6,4},{7,5},{8,10},{9,11},{10,... | collective-permute-start | bytes 2064392 | tf_op jit(solution)/shard_map/ppermute | solution.py:68
  237.9 33.4 %collective-permute-start.38 = (bf16[4,208,384]{2,1,0:T(8,128)(2,1)S(1)}, bf16[4,208,384]{2,1,0:T(8,128)(2,1)S(1)}, u32[]{:S(2)}, u32[]{:S(2)}) collective-permute-start(bf16[4,208,384]{2,1,0:T(8,128)(2,1)S(1)} %slice.473), channel_id=1, source_target_pairs={{0,4},{4,0},{8,12},{12,8},{16,20},{20,16},{24,28},{28,24},{1,5},{5... | collective-permute-start | bytes 1916936 | tf_op jit(solution)/shard_map/ppermute | solution.py:63
  254.8 16.5 %collective-permute-start.40 = (bf16[8,48,384]{2,1,0:T(8,128)(2,1)S(1)}, bf16[8,48,384]{2,1,0:T(8,128)(2,1)S(1)}, u32[]{:S(2)}, u32[]{:S(2)}) collective-permute-start(bf16[8,48,384]{2,1,0:T(8,128)(2,1)S(1)} %get-tuple-element.312), channel_id=1, source_target_pairs={{0,2},{1,3},{2,0},{3,1},{4,6},{5,7},{6,4},{7,5},{8,10},{9,11},{10,... | collective-permute-start | bytes 884744 | tf_op jit(solution)/shard_map/ppermute | solution.py:68
  256.0 15.3 %collective-permute-start.41 = (bf16[8,48,384]{2,1,0:T(8,128)(2,1)S(1)}, bf16[8,48,384]{2,1,0:T(8,128)(2,1)S(1)}, u32[]{:S(2)}, u32[]{:S(2)}) collective-permute-start(bf16[8,48,384]{2,1,0:T(8,128)(2,1)S(1)} %get-tuple-element.313), channel_id=1, source_target_pairs={{0,4},{4,0},{8,12},{12,8},{16,20},{20,16},{24,28},{28,24},{1,5},{5... | collective-permute-start | bytes 884744 | tf_op jit(solution)/shard_map/ppermute | solution.py:63
  275.9 11.3 %collective-permute-start.42 = (bf16[8,32,384]{2,1,0:T(8,128)(2,1)S(1)}, bf16[8,32,384]{2,1,0:T(8,128)(2,1)S(1)}, u32[]{:S(2)}, u32[]{:S(2)}) collective-permute-start(bf16[8,32,384]{2,1,0:T(8,128)(2,1)S(1)} %get-tuple-element.329), channel_id=1, source_target_pairs={{0,2},{1,3},{2,0},{3,1},{4,6},{5,7},{6,4},{7,5},{8,10},{9,11},{10,... | collective-permute-start | bytes 589832 | tf_op jit(solution)/shard_map/ppermute | solution.py:68
  276.0 11.2 %collective-permute-start.43 = (bf16[8,32,384]{2,1,0:T(8,128)(2,1)S(1)}, bf16[8,32,384]{2,1,0:T(8,128)(2,1)S(1)}, u32[]{:S(2)}, u32[]{:S(2)}) collective-permute-start(bf16[8,32,384]{2,1,0:T(8,128)(2,1)S(1)} %get-tuple-element.330), channel_id=1, source_target_pairs={{0,4},{4,0},{8,12},{12,8},{16,20},{20,16},{24,28},{28,24},{1,5},{5... | collective-permute-start | bytes 589832 | tf_op jit(solution)/shard_map/ppermute | solution.py:63
  283.1 10.5 %collective-permute-start.44 = (bf16[432,384]{1,0:T(8,128)(2,1)S(1)}, bf16[432,384]{1,0:T(8,128)(2,1)S(1)}, u32[]{:S(2)}, u32[]{:S(2)}) collective-permute-start(bf16[432,384]{1,0:T(8,128)(2,1)S(1)} %fusion.6), channel_id=1, source_target_pairs={{0,24},{4,28},{8,0},{12,4},{16,8},{20,12},{24,16},{28,20},{1,25},{... | collective-permute-start | bytes 995336 | tf_op jit(solution)/shard_map/ppermute | solution.py:73
  293.7 8.4 %collective-permute-start.45 = (bf16[4,80,384]{2,1,0:T(8,128)(2,1)S(1)}, bf16[4,80,384]{2,1,0:T(8,128)(2,1)S(1)}, u32[]{:S(2)}, u32[]{:S(2)}) collective-permute-start(bf16[4,80,384]{2,1,0:T(8,128)(2,1)S(1)} %fusion.8), channel_id=1, source_target_pairs={{0,4},{4,0},{8,12},{12,8},{16,20},{20,16},{24,28},{28,24},{1,5},{5... | collective-permute-start | bytes 737288 | tf_op jit(solution)/shard_map/ppermute | solution.py:63
  294.1 18.0 %collective-permute-start.48 = (bf16[432,384]{1,0:T(8,128)(2,1)S(1)}, bf16[432,384]{1,0:T(8,128)(2,1)S(1)}, u32[]{:S(2)}, u32[]{:S(2)}) collective-permute-start(bf16[432,384]{1,0:T(8,128)(2,1)S(1)} %slice_bitcast_fusion.2), channel_id=1, source_target_pairs={{0,16},{4,20},{8,24},{12,28},{16,0},{20,4},{24,8},{28,12},{1,17},{... | collective-permute-start | bytes 995336 | tf_op jit(solution)/shard_map/ppermute | solution.py:73
  296.2 15.9 %collective-permute-start.49 = (bf16[224,768]{1,0:T(8,128)(2,1)S(1)}, bf16[224,768]{1,0:T(8,128)(2,1)S(1)}, u32[]{:S(2)}, u32[]{:S(2)}) collective-permute-start(bf16[224,768]{1,0:T(8,128)(2,1)S(1)} %slice.481), channel_id=1, source_target_pairs={{0,2},{1,3},{2,0},{3,1},{4,6},{5,7},{6,4},{7,5},{8,10},{9,11},{10,... | collective-permute-start | bytes 1032200 | tf_op jit(solution)/shard_map/ppermute | solution.py:68
  296.7 15.0 %collective-permute-start.46 = (bf16[4,80,384]{2,1,0:T(8,128)(2,1)S(1)}, bf16[4,80,384]{2,1,0:T(8,128)(2,1)S(1)}, u32[]{:S(2)}, u32[]{:S(2)}) collective-permute-start(bf16[4,80,384]{2,1,0:T(8,128)(2,1)S(1)} %fusion.7), channel_id=1, source_target_pairs={{0,2},{1,3},{2,0},{3,1},{4,6},{5,7},{6,4},{7,5},{8,10},{9,11},{10,... | collective-permute-start | bytes 737288 | tf_op jit(solution)/shard_map/ppermute | solution.py:68
  312.1 21.7 %collective-permute-start.55 = (bf16[288,768]{1,0:T(8,128)(2,1)S(1)}, bf16[288,768]{1,0:T(8,128)(2,1)S(1)}, u32[]{:S(2)}, u32[]{:S(2)}) collective-permute-start(bf16[288,768]{1,0:T(8,128)(2,1)S(1)} %slice.400), channel_id=1, source_target_pairs={{0,2},{1,3},{2,0},{3,1},{4,6},{5,7},{6,4},{7,5},{8,10},{9,11},{10,... | collective-permute-start | bytes 1327112 | tf_op jit(solution)/shard_map/ppermute | solution.py:68
  312.6 21.2 %collective-permute-start.54 = (bf16[432,384]{1,0:T(8,128)(2,1)S(1)}, bf16[432,384]{1,0:T(8,128)(2,1)S(1)}, u32[]{:S(2)}, u32[]{:S(2)}) collective-permute-start(bf16[432,384]{1,0:T(8,128)(2,1)S(1)} %get-tuple-element.379), channel_id=1, source_target_pairs={{0,8},{4,12},{8,16},{12,20},{16,24},{20,28},{24,0},{28,4},{1,9},{5... | collective-permute-start | bytes 995336 | tf_op jit(solution)/shard_map/ppermute | solution.py:73
  314.2 13.8 %collective-permute-start.53 = (bf16[160,384]{1,0:T(8,128)(2,1)S(1)}, bf16[160,384]{1,0:T(8,128)(2,1)S(1)}, u32[]{:S(2)}, u32[]{:S(2)}) collective-permute-start(bf16[160,384]{1,0:T(8,128)(2,1)S(1)} %get-tuple-element.383), channel_id=1, source_target_pairs={{0,8},{4,12},{8,16},{12,20},{16,24},{20,28},{24,0},{28,4},{1,9},{5... | collective-permute-start | bytes 368648 | tf_op jit(solution)/shard_map/ppermute | solution.py:73
  314.3 13.8 %collective-permute-start.51 = (bf16[160,384]{1,0:T(8,128)(2,1)S(1)}, bf16[160,384]{1,0:T(8,128)(2,1)S(1)}, u32[]{:S(2)}, u32[]{:S(2)}) collective-permute-start(bf16[160,384]{1,0:T(8,128)(2,1)S(1)} %get-tuple-element.384), channel_id=1, source_target_pairs={{0,24},{4,28},{8,0},{12,4},{16,8},{20,12},{24,16},{28,20},{1,25},{... | collective-permute-start | bytes 368648 | tf_op jit(solution)/shard_map/ppermute | solution.py:73
  318.1 15.8 %collective-permute-start.52 = (bf16[160,384]{1,0:T(8,128)(2,1)S(1)}, bf16[160,384]{1,0:T(8,128)(2,1)S(1)}, u32[]{:S(2)}, u32[]{:S(2)}) collective-permute-start(bf16[160,384]{1,0:T(8,128)(2,1)S(1)} %get-tuple-element.385), channel_id=1, source_target_pairs={{0,16},{4,20},{8,24},{12,28},{16,0},{20,4},{24,8},{28,12},{1,17},{... | collective-permute-start | bytes 368648 | tf_op jit(solution)/shard_map/ppermute | solution.py:73
  328.0 10.4 %collective-permute-start.50 = (bf16[512,768]{1,0:T(8,128)(2,1)S(1)}, bf16[512,768]{1,0:T(8,128)(2,1)S(1)}, u32[]{:S(2)}, u32[]{:S(2)}) collective-permute-start(bf16[512,768]{1,0:T(8,128)(2,1)S(1)} %get-tuple-element.349), channel_id=1, source_target_pairs={{0,1},{1,0},{2,3},{3,2},{4,5},{5,4},{6,7},{7,6},{8,9},{9,8},{10,11... | collective-permute-start | bytes 2359304 | tf_op jit(solution)/shard_map/ppermute | solution.py:68
  (72 other events, 568.4 us)
